TPU v7x, 256 devices: a whole 4x4x8 slice. The times are simulated.
256 devices in a mesh: segment: 2 (over core), tensor: 16 (over x, z_hi), dp: 8 (over z_lo, y).
Axes of the slice: x: 4, y: 4, z: 8 (z_hi: 4, z_lo: 2; z = z_hi * 2 + z_lo), core: 2. Of those that a mesh axis runs over, the one named last changes fastest.
Arguments:
- tokens: bfloat16 [1024, 1536], P('dp', 'tensor'), may hold values from -6 to 6
- w_gate: bfloat16 [2, 1536, 12288], P('segment', None, 'tensor'), may hold values from -0.15625 to 0.15625
- w_up: bfloat16 [2, 1536, 12288], P('segment', None, 'tensor'), may hold values from -0.15625 to 0.15625
- w_down: bfloat16 [2, 12288, 1536], P('segment', 'tensor'), may hold values from -0.0546875 to 0.0546875
- cotangent: bfloat16 [1024, 1536], P('dp', 'tensor'), may hold values from -0.1796875 to 0.1796875
Outputs:
- grad_gate: float32 [2, 1536, 12288], P('segment', 'dp', 'tensor')
- grad_up: float32 [2, 1536, 12288], P('segment', 'dp', 'tensor')
- grad_down: float32 [2, 12288, 1536], P('segment', 'tensor', 'dp')
All inputs are finite; a program needn't handle non-finite values.
Results may differ from a plain program's by a relative error of at most 0.023.
Values may be sent and summed in bfloat16 or wider, within the bound.
No kernel may reach another device: no remote copies, remote signals or barrier semaphores. Data moves between devices by JAX's collectives and lax.ppermute only.
A program may use at most 64 MiB of HBM per device.

v0:
```python
import jax
import jax.numpy as jnp
from jax import lax
from jax.sharding import PartitionSpec as P

MICRO = 2


def sent_to_all(value, axis):
    copies = jnp.broadcast_to(value, (lax.axis_size(axis), *value.shape))
    return lax.all_to_all(copies, axis, split_axis=0, concat_axis=0, tiled=True)


def joined_along(blocks, dim):
    shape = list(blocks.shape[1:])
    shape[dim] *= blocks.shape[0]
    return jnp.moveaxis(blocks, 0, dim).reshape(shape)


def gather_directly(value, axis, dim):
    blocks = sent_to_all(value, axis)
    return joined_along(blocks, dim)


def in_blocks(value, dim, peers):
    shape = value.shape
    blocks = value.reshape(*shape[:dim], peers, shape[dim] // peers, *shape[dim + 1 :])
    return jnp.moveaxis(blocks, dim, 0)


def sent_and_summed(value, axis, dim):
    peers = lax.axis_size(axis)
    blocks = lax.all_to_all(in_blocks(value, dim, peers), axis, 0, 0, tiled=True)
    return jnp.sum(blocks.astype(jnp.float32), axis=0)


def from_behind(block, axis, distance):
    devices = range(lax.axis_size(axis))
    route = [(i - distance, i) for i in devices if i - distance in devices]
    return lax.ppermute(block, axis, route)


def select_tick(stored, position):
    if 0 <= position < len(stored):
        return stored[position]
    return jnp.zeros_like(stored[0])


def inner_rows(left, right):
    return lax.dot_general(
        left, right, (((0,), (0,)), ((), ())), preferred_element_type=jnp.float32
    )


def against_cols(left, right):
    return lax.dot_general(
        left, right, (((1,), (1,)), ((), ())), preferred_element_type=jnp.float32
    )


def local(tokens, w_gate, w_up, w_down, cotangent):
    gate_weight = w_gate[0]
    up_weight = w_up[0]
    down_weight = w_down[0]
    leading = lax.axis_index("segment") == 0
    row_count = tokens.shape[0] // MICRO
    hidden_cols = gate_weight.shape[1]
    blank_rows = jnp.zeros((row_count, tokens.shape[1]), jnp.bfloat16)
    received = blank_rows
    gathers = []
    gates = []
    ups = []
    for moment in range(MICRO + 1):
        fresh_rows = (
            tokens[moment * row_count : (moment + 1) * row_count] if moment < MICRO else blank_rows
        )
        inputs = jnp.where(leading, fresh_rows, received)
        gathered = gather_directly(inputs, "tensor", 1)
        gate_store = jnp.dot(gathered, gate_weight, preferred_element_type=jnp.float32).astype(
            jnp.bfloat16
        )
        up_store = jnp.dot(gathered, up_weight, preferred_element_type=jnp.float32).astype(
            jnp.bfloat16
        )
        hidden = (
            jax.nn.silu(gate_store.astype(jnp.float32)) * up_store.astype(jnp.float32)
        ).astype(jnp.bfloat16)
        partial_value = jnp.dot(hidden, down_weight, preferred_element_type=jnp.float32)
        mixed_sum = sent_and_summed(partial_value.astype(jnp.bfloat16), "tensor", 1)
        output = (inputs.astype(jnp.float32) + mixed_sum).astype(jnp.bfloat16)
        gathers.append(gathered)
        gates.append(gate_store)
        ups.append(up_store)
        if moment < MICRO:
            received = from_behind(output, "segment", 1)
    received_back = blank_rows
    records = []
    for moment in range(MICRO + 1):
        fresh_rows = (
            cotangent[moment * row_count : (moment + 1) * row_count]
            if moment < MICRO
            else blank_rows
        )
        upstream = jnp.where(leading, received_back, fresh_rows)
        gathered = jnp.where(
            leading, select_tick(gathers, moment - 1), select_tick(gathers, moment + 1)
        )
        gate_store = jnp.where(
            leading, select_tick(gates, moment - 1), select_tick(gates, moment + 1)
        )
        up_store = jnp.where(leading, select_tick(ups, moment - 1), select_tick(ups, moment + 1))
        gate_value = gate_store.astype(jnp.float32)
        up_value = up_store.astype(jnp.float32)
        hidden = (jax.nn.silu(gate_value) * up_value).astype(jnp.bfloat16)
        cot_full = gather_directly(upstream, "tensor", 1)
        d_hidden = against_cols(cot_full, down_weight)
        sigma = jax.nn.sigmoid(gate_value)
        d_gate = (d_hidden * up_value * sigma * (1.0 + gate_value * (1.0 - sigma))).astype(
            jnp.bfloat16
        )
        d_up = (d_hidden * gate_value * sigma).astype(jnp.bfloat16)
        records.append((gathered, d_gate, d_up, cot_full, hidden))
        if moment < MICRO:
            partial_value = against_cols(d_gate, gate_weight) + against_cols(d_up, up_weight)
            summed = sent_and_summed(partial_value.astype(jnp.bfloat16), "tensor", 1)
            d_input = (upstream.astype(jnp.float32) + summed).astype(jnp.bfloat16)
            received_back = from_behind(d_input, "segment", -1)
    all_gathered = jnp.concatenate([entry[0] for entry in records], axis=0)
    all_gate = jnp.concatenate([entry[1] for entry in records], axis=0)
    all_up = jnp.concatenate([entry[2] for entry in records], axis=0)
    all_cot = jnp.concatenate([entry[3] for entry in records], axis=0)
    all_hidden = jnp.concatenate([entry[4] for entry in records], axis=0)
    reduced = lax.psum_scatter(
        jnp.concatenate(
            [
                inner_rows(all_gathered, all_gate),
                inner_rows(all_gathered, all_up),
                inner_rows(all_cot, all_hidden),
            ],
            axis=1,
        ).astype(jnp.bfloat16),
        "dp",
        scatter_dimension=0,
        tiled=True,
    ).astype(jnp.float32)
    grad_gate = reduced[:, :hidden_cols][None]
    grad_up = reduced[:, hidden_cols : 2 * hidden_cols][None]
    grad_down = reduced[:, 2 * hidden_cols :].T[None]
    return (grad_gate, grad_up, grad_down)


def solution(mesh):
    in_specs = (
        P("dp", "tensor"),
        P("segment", None, "tensor"),
        P("segment", None, "tensor"),
        P("segment", "tensor", None),
        P("dp", "tensor"),
    )
    out_specs = (
        P("segment", "dp", "tensor"),
        P("segment", "dp", "tensor"),
        P("segment", "tensor", "dp"),
    )
    return jax.shard_map(local, mesh=mesh, in_specs=in_specs, out_specs=out_specs, check_vma=False)
```

profile of v0, /device:TPU:1, one launch (start us, length us, event | category | flops | bytes accessed | tf_op | source)
XLA Modules:
  0.0 312.5 jit_solution(10562688644457806110)
XLA Ops:
  8.3 23.8 %all_to_all.50 = bf16[16,64,96]{2,1,0:T(8,128)(2,1)S(1)} all-to-all(bf16[16,64,96]{2,1,0:T(8,128)(2,1)S(1)} %broadcast_in_dim.31), channel_id=1, replica_groups=mesh['segment'=2,'tensor'=16,'dp'=8] {'tensor'}, dimensions={0} | all-to-all | bytes 393216 | tf_op jit(solution)/shard_map/all_to_all | solution.py:11
  32.6 2.3 fusion.57
  37.8 3.5 %all-to-all-start.1 = ((bf16[16,64,96]{2,1,0:T(8,128)(2,1)}), bf16[16,64,96]{2,1,0:T(8,128)(2,1)S(1)}, u32[]{:S(2)}, u32[]{:S(2)}) async-start(bf16[16,64,96]{2,1,0:T(8,128)(2,1)} %bitcast.110), calls=%async_computation.1 | async-start | bytes 524288 | tf_op jit(solution)/shard_map/all_to_all | solution.py:33
  42.1 10.5 %all-to-all-done.1 = bf16[16,64,96]{2,1,0:T(8,128)(2,1)S(1)} async-done(((bf16[16,64,96]{2,1,0:T(8,128)(2,1)}), bf16[16,64,96]{2,1,0:T(8,128)(2,1)S(1)}, u32[]{:S(2)}, u32[]{:S(2)}) %all-to-all-start.1) | async-done | bytes 196640 | tf_op jit(solution)/shard_map/all_to_all | solution.py:33
  53.3 3.5 %all-to-all-start.5 = ((bf16[16,64,96]{2,1,0:T(8,128)(2,1)}), bf16[16,64,96]{2,1,0:T(8,128)(2,1)S(1)}, u32[]{:S(2)}, u32[]{:S(2)}) async-start(bf16[16,64,96]{2,1,0:T(8,128)(2,1)} %broadcast_in_dim.34), calls=%async_computation.5 | async-start | bytes 524288 | tf_op jit(solution)/shard_map/all_to_all | solution.py:11
  58.4 3.5 %collective-permute-done = bf16[64,96]{1,0:T(8,128)(2,1)S(1)} collective-permute-done((bf16[64,96]{1,0:T(8,128)(2,1)S(1)}, bf16[64,96]{1,0:T(8,128)(2,1)S(1)}, u32[]{:S(2)}, u32[]{:S(2)}) %collective-permute-start) | collective-permute-done | bytes 12320 | tf_op jit(solution)/shard_map/ppermute | solution.py:40
  61.9 5.7 %all-to-all-done.5 = bf16[16,64,96]{2,1,0:T(8,128)(2,1)S(1)} async-done(((bf16[16,64,96]{2,1,0:T(8,128)(2,1)}), bf16[16,64,96]{2,1,0:T(8,128)(2,1)S(1)}, u32[]{:S(2)}, u32[]{:S(2)}) %all-to-all-start.5) | async-done | bytes 196640 | tf_op jit(solution)/shard_map/all_to_all | solution.py:11
  68.3 3.6 %all-to-all-start.2 = ((bf16[16,64,96]{2,1,0:T(8,128)(2,1)}), bf16[16,64,96]{2,1,0:T(8,128)(2,1)S(1)}, u32[]{:S(2)}, u32[]{:S(2)}) async-start(bf16[16,64,96]{2,1,0:T(8,128)(2,1)} %broadcast_in_dim.32), calls=%async_computation.2 | async-start | bytes 524288 | tf_op jit(solution)/shard_map/all_to_all | solution.py:11
  73.0 9.8 %all-to-all-done.2 = bf16[16,64,96]{2,1,0:T(8,128)(2,1)S(1)} async-done(((bf16[16,64,96]{2,1,0:T(8,128)(2,1)}), bf16[16,64,96]{2,1,0:T(8,128)(2,1)S(1)}, u32[]{:S(2)}, u32[]{:S(2)}) %all-to-all-start.2) | async-done | bytes 196640 | tf_op jit(solution)/shard_map/all_to_all | solution.py:11
  83.3 2.3 fusion.60
  88.5 3.5 %all-to-all-start.3 = ((bf16[16,64,96]{2,1,0:T(8,128)(2,1)}), bf16[16,64,96]{2,1,0:T(8,128)(2,1)S(1)}, u32[]{:S(2)}, u32[]{:S(2)}) async-start(bf16[16,64,96]{2,1,0:T(8,128)(2,1)} %bitcast.114), calls=%async_computation.3 | async-start | bytes 524288 | tf_op jit(solution)/shard_map/all_to_all | solution.py:33
  92.0 2.0 fusion.108
  96.8 6.1 %all-to-all-done.3 = bf16[16,64,96]{2,1,0:T(8,128)(2,1)S(1)} async-done(((bf16[16,64,96]{2,1,0:T(8,128)(2,1)}), bf16[16,64,96]{2,1,0:T(8,128)(2,1)S(1)}, u32[]{:S(2)}, u32[]{:S(2)}) %all-to-all-start.3) | async-done | bytes 196640 | tf_op jit(solution)/shard_map/all_to_all | solution.py:33
  102.9 3.5 %all-to-all-start.6 = ((bf16[16,64,96]{2,1,0:T(8,128)(2,1)}), bf16[16,64,96]{2,1,0:T(8,128)(2,1)S(1)}, u32[]{:S(2)}, u32[]{:S(2)}) async-start(bf16[16,64,96]{2,1,0:T(8,128)(2,1)} %bitcast.113), calls=%async_computation.6 | async-start | bytes 524288 | tf_op jit(solution)/shard_map/all_to_all | solution.py:33
  107.9 9.4 %all-to-all-done.6 = bf16[16,64,96]{2,1,0:T(8,128)(2,1)S(1)} async-done(((bf16[16,64,96]{2,1,0:T(8,128)(2,1)}), bf16[16,64,96]{2,1,0:T(8,128)(2,1)S(1)}, u32[]{:S(2)}, u32[]{:S(2)}) %all-to-all-start.6) | async-done | bytes 196640 | tf_op jit(solution)/shard_map/all_to_all | solution.py:33
  118.1 6.6 %all-to-all-start.4 = ((bf16[16,64,96]{2,1,0:T(8,128)(2,1)}), bf16[16,64,96]{2,1,0:T(8,128)(2,1)S(1)}, u32[]{:S(2)}, u32[]{:S(2)}) async-start(bf16[16,64,96]{2,1,0:T(8,128)(2,1)} %broadcast_in_dim.33), calls=%async_computation.4 | async-start | bytes 524288 | tf_op jit(solution)/shard_map/all_to_all | solution.py:11
  124.8 5.9 %collective-permute-start.2 = (bf16[64,96]{1,0:T(8,128)(2,1)S(1)}, bf16[64,96]{1,0:T(8,128)(2,1)S(1)}, u32[]{:S(2)}, u32[]{:S(2)}) collective-permute-start(bf16[64,96]{1,0:T(8,128)(2,1)S(1)} %add_convert_fusion.1), channel_id=1, source_target_pairs={{128,0},{129,1},{130,2},{131,3},{132,4},{133,5},{134,6},{135,7},{1... | collective-permute-start | bytes 36872 | tf_op jit(solution)/shard_map/ppermute | solution.py:40
  131.5 4.0 %all-to-all-done.4 = bf16[16,64,96]{2,1,0:T(8,128)(2,1)S(1)} async-done(((bf16[16,64,96]{2,1,0:T(8,128)(2,1)}), bf16[16,64,96]{2,1,0:T(8,128)(2,1)S(1)}, u32[]{:S(2)}, u32[]{:S(2)}) %all-to-all-start.4) | async-done | bytes 196640 | tf_op jit(solution)/shard_map/all_to_all | solution.py:11
  136.2 5.4 %all-to-all-start.7 = ((bf16[16,64,96]{2,1,0:T(8,128)(2,1)}), bf16[16,64,96]{2,1,0:T(8,128)(2,1)}, u32[]{:S(2)}, u32[]{:S(2)}) async-start(bf16[16,64,96]{2,1,0:T(8,128)(2,1)} %broadcast_in_dim.35), calls=%async_computation.7 | async-start | bytes 524288 | tf_op jit(solution)/shard_map/all_to_all | solution.py:11
  142.1 2.2 fusion.75
  144.3 8.3 %all-to-all-done.7 = bf16[16,64,96]{2,1,0:T(8,128)(2,1)} async-done(((bf16[16,64,96]{2,1,0:T(8,128)(2,1)}), bf16[16,64,96]{2,1,0:T(8,128)(2,1)}, u32[]{:S(2)}, u32[]{:S(2)}) %all-to-all-start.7) | async-done | bytes 196640 | tf_op jit(solution)/shard_map/all_to_all | solution.py:11
  154.7 1.9 fusion.2
  159.8 13.5 %all_to_all.51 = bf16[16,64,96]{2,1,0:T(8,128)(2,1)S(1)} all-to-all(bf16[16,64,96]{2,1,0:T(8,128)(2,1)S(1)} %bitcast.118), channel_id=1, replica_groups=mesh['segment'=2,'tensor'=16,'dp'=8] {'tensor'}, dimensions={0} | all-to-all | bytes 393216 | tf_op jit(solution)/shard_map/all_to_all | solution.py:33
  173.4 8.4 %collective-permute-start.3 = (bf16[64,96]{1,0:T(8,128)(2,1)S(1)}, bf16[64,96]{1,0:T(8,128)(2,1)S(1)}, u32[]{:S(2)}, u32[]{:S(2)}) collective-permute-start(bf16[64,96]{1,0:T(8,128)(2,1)S(1)} %add_convert_fusion), channel_id=1, source_target_pairs={{128,0},{129,1},{130,2},{131,3},{132,4},{133,5},{134,6},{135,7},{1... | collective-permute-start | bytes 36872 | tf_op jit(solution)/shard_map/ppermute | solution.py:40
  183.4 3.5 %all-to-all-start.9 = ((bf16[16,64,96]{2,1,0:T(8,128)(2,1)}), bf16[16,64,96]{2,1,0:T(8,128)(2,1)S(1)}, u32[]{:S(2)}, u32[]{:S(2)}) async-start(bf16[16,64,96]{2,1,0:T(8,128)(2,1)} %broadcast_in_dim.36), calls=%async_computation.9 | async-start | bytes 524288 | tf_op jit(solution)/shard_map/all_to_all | solution.py:11
  187.8 11.7 %all-to-all-done.9 = bf16[16,64,96]{2,1,0:T(8,128)(2,1)S(1)} async-done(((bf16[16,64,96]{2,1,0:T(8,128)(2,1)}), bf16[16,64,96]{2,1,0:T(8,128)(2,1)S(1)}, u32[]{:S(2)}, u32[]{:S(2)}) %all-to-all-start.9) | async-done | bytes 196640 | tf_op jit(solution)/shard_map/all_to_all | solution.py:11
  203.8 3.6 %pad_maximum_fusion = bf16[1536,2304]{0,1:T(8,128)(2,1)} fusion(bf16[1536,768]{0,1:T(8,128)(2,1)S(1)} %convolution_convert_fusion, bf16[1536,768]{0,1:T(8,128)(2,1)S(1)} %convolution_convert_fusion.1, bf16[1536,768]{0,1:T(8,128)(2,1)S(1)} %convolution_convert_fusion.2), kind=kLoop, calls=%fused_computation | loop fusion | flops 21233664 | bytes 14155776 | tf_op jit(solution)/shard_map/concatenate | solution.py:134
  207.4 10.4 %copy.65 = bf16[1536,2304]{1,0:T(8,128)(2,1)} copy(bf16[1536,2304]{0,1:T(8,128)(2,1)} %pad_maximum_fusion) | data formatting | bytes 14155776
  217.7 79.5 %reduce-scatter.4.cloned.1.call-done = bf16[192,2304]{1,0:T(8,128)(2,1)} async-done(((bf16[1536,2304]{1,0:T(8,128)(2,1)}), bf16[192,2304]{1,0:T(8,128)(2,1)}) %reduce-scatter.4.cloned.1.call-update) | async-done | bytes 884752
  297.2 1.5 copy.66
  300.2 2.2 copy.64
  302.4 2.2 copy.63
  (131 shorter events, 33.9 us)
Async XLA Ops:
  7.2 29.1 %copy-start = (bf16[1,768,1536]{2,1,0:T(8,128)(2,1)S(1)}, bf16[1,768,1536]{2,1,0:T(8,128)(2,1)}, u32[]{:S(2)}) copy-start(bf16[1,768,1536]{2,1,0:T(8,128)(2,1)} %param.8) | copy-start | bytes 7077892
  32.6 2.4 copy-start.3
  36.2 5.1 %copy-start.29 = (bf16[128,96]{0,1:T(8,128)(2,1)S(1)}, bf16[128,96]{0,1:T(8,128)(2,1)}, u32[]{:S(2)}) copy-start(bf16[128,96]{0,1:T(8,128)(2,1)} %param.9) | copy-start | bytes 73732
  37.8 14.8 %all-to-all-start.1 = ((bf16[16,64,96]{2,1,0:T(8,128)(2,1)}), bf16[16,64,96]{2,1,0:T(8,128)(2,1)S(1)}, u32[]{:S(2)}, u32[]{:S(2)}) async-start(bf16[16,64,96]{2,1,0:T(8,128)(2,1)} %bitcast.110), calls=%async_computation.1 | async-start | bytes 524288 | tf_op jit(solution)/shard_map/all_to_all | solution.py:33
  42.1 43.6 %copy-start.22 = (bf16[64,96]{1,0:T(8,128)(2,1)}, bf16[64,96]{1,0:T(8,128)(2,1)S(1)}, u32[]{:S(2)}) copy-start(bf16[64,96]{1,0:T(8,128)(2,1)S(1)} %copy.73) | copy-start | bytes 36868
  53.3 14.2 %all-to-all-start.5 = ((bf16[16,64,96]{2,1,0:T(8,128)(2,1)}), bf16[16,64,96]{2,1,0:T(8,128)(2,1)S(1)}, u32[]{:S(2)}, u32[]{:S(2)}) async-start(bf16[16,64,96]{2,1,0:T(8,128)(2,1)} %broadcast_in_dim.34), calls=%async_computation.5 | async-start | bytes 524288 | tf_op jit(solution)/shard_map/all_to_all | solution.py:11
  57.0 4.9 %collective-permute-start = (bf16[64,96]{1,0:T(8,128)(2,1)S(1)}, bf16[64,96]{1,0:T(8,128)(2,1)S(1)}, u32[]{:S(2)}, u32[]{:S(2)}) collective-permute-start(bf16[64,96]{1,0:T(8,128)(2,1)S(1)} %add_convert_fusion.3), channel_id=1, source_target_pairs={{0,128},{1,129},{2,130},{3,131},{4,132},{5,133},{6,134},{7,135},{8... | collective-permute-start | bytes 36872 | tf_op jit(solution)/shard_map/ppermute | solution.py:40
  68.3 14.6 %all-to-all-start.2 = ((bf16[16,64,96]{2,1,0:T(8,128)(2,1)}), bf16[16,64,96]{2,1,0:T(8,128)(2,1)S(1)}, u32[]{:S(2)}, u32[]{:S(2)}) async-start(bf16[16,64,96]{2,1,0:T(8,128)(2,1)} %broadcast_in_dim.32), calls=%async_computation.2 | async-start | bytes 524288 | tf_op jit(solution)/shard_map/all_to_all | solution.py:11
  83.3 2.4 copy-start.4
  88.5 14.5 %all-to-all-start.3 = ((bf16[16,64,96]{2,1,0:T(8,128)(2,1)}), bf16[16,64,96]{2,1,0:T(8,128)(2,1)S(1)}, u32[]{:S(2)}, u32[]{:S(2)}) async-start(bf16[16,64,96]{2,1,0:T(8,128)(2,1)} %bitcast.114), calls=%async_computation.3 | async-start | bytes 524288 | tf_op jit(solution)/shard_map/all_to_all | solution.py:33
  92.0 2.1 copy-start.1
  92.0 2.9 copy-start.5
  95.0 29.8 %copy-start.23 = (bf16[64,96]{1,0:T(8,128)(2,1)S(1)}, bf16[64,96]{1,0:T(8,128)(2,1)}, u32[]{:S(2)}) copy-start(bf16[64,96]{1,0:T(8,128)(2,1)} %copy-done.22) | copy-start | bytes 36868
  102.9 14.4 %all-to-all-start.6 = ((bf16[16,64,96]{2,1,0:T(8,128)(2,1)}), bf16[16,64,96]{2,1,0:T(8,128)(2,1)S(1)}, u32[]{:S(2)}, u32[]{:S(2)}) async-start(bf16[16,64,96]{2,1,0:T(8,128)(2,1)} %bitcast.113), calls=%async_computation.6 | async-start | bytes 524288 | tf_op jit(solution)/shard_map/all_to_all | solution.py:33
  106.6 10.8 %collective-permute-start.1 = (bf16[64,96]{1,0:T(8,128)(2,1)S(1)}, bf16[64,96]{1,0:T(8,128)(2,1)S(1)}, u32[]{:S(2)}, u32[]{:S(2)}) collective-permute-start(bf16[64,96]{1,0:T(8,128)(2,1)S(1)} %add_convert_fusion.2), channel_id=1, source_target_pairs={{0,128},{1,129},{2,130},{3,131},{4,132},{5,133},{6,134},{7,135},{8... | collective-permute-start | bytes 36872 | tf_op jit(solution)/shard_map/ppermute | solution.py:40
  118.1 17.3 %all-to-all-start.4 = ((bf16[16,64,96]{2,1,0:T(8,128)(2,1)}), bf16[16,64,96]{2,1,0:T(8,128)(2,1)S(1)}, u32[]{:S(2)}, u32[]{:S(2)}) async-start(bf16[16,64,96]{2,1,0:T(8,128)(2,1)} %broadcast_in_dim.33), calls=%async_computation.4 | async-start | bytes 524288 | tf_op jit(solution)/shard_map/all_to_all | solution.py:11
  124.8 6.7 %collective-permute-start.2 = (bf16[64,96]{1,0:T(8,128)(2,1)S(1)}, bf16[64,96]{1,0:T(8,128)(2,1)S(1)}, u32[]{:S(2)}, u32[]{:S(2)}) collective-permute-start(bf16[64,96]{1,0:T(8,128)(2,1)S(1)} %add_convert_fusion.1), channel_id=1, source_target_pairs={{128,0},{129,1},{130,2},{131,3},{132,4},{133,5},{134,6},{135,7},{1... | collective-permute-start | bytes 36872 | tf_op jit(solution)/shard_map/ppermute | solution.py:40
  136.2 16.4 %all-to-all-start.7 = ((bf16[16,64,96]{2,1,0:T(8,128)(2,1)}), bf16[16,64,96]{2,1,0:T(8,128)(2,1)}, u32[]{:S(2)}, u32[]{:S(2)}) async-start(bf16[16,64,96]{2,1,0:T(8,128)(2,1)} %broadcast_in_dim.35), calls=%async_computation.7 | async-start | bytes 524288 | tf_op jit(solution)/shard_map/all_to_all | solution.py:11
  144.3 12.3 %copy-start.8 = (bf16[64,768]{1,0:T(8,128)(2,1)S(1)}, bf16[64,768]{1,0:T(8,128)(2,1)}, u32[]{:S(2)}) copy-start(bf16[64,768]{1,0:T(8,128)(2,1)} %copy-done.7) | copy-start | bytes 294916
  154.6 1.9 copy-start.2
  156.6 2.1 copy-start.6
  159.5 40.5 %copy-start.16 = (bf16[64,768]{1,0:T(8,128)(2,1)S(1)}, bf16[64,768]{1,0:T(8,128)(2,1)}, u32[]{:S(2)}) copy-start(bf16[64,768]{1,0:T(8,128)(2,1)} %copy-done.15) | copy-start | bytes 294916
  159.7 40.3 %copy-start.18 = (bf16[64,768]{1,0:T(8,128)(2,1)S(1)}, bf16[64,768]{1,0:T(8,128)(2,1)}, u32[]{:S(2)}) copy-start(bf16[64,768]{1,0:T(8,128)(2,1)} %copy-done.17) | copy-start | bytes 294916
  173.4 9.2 %collective-permute-start.3 = (bf16[64,96]{1,0:T(8,128)(2,1)S(1)}, bf16[64,96]{1,0:T(8,128)(2,1)S(1)}, u32[]{:S(2)}, u32[]{:S(2)}) collective-permute-start(bf16[64,96]{1,0:T(8,128)(2,1)S(1)} %add_convert_fusion), channel_id=1, source_target_pairs={{128,0},{129,1},{130,2},{131,3},{132,4},{133,5},{134,6},{135,7},{1... | collective-permute-start | bytes 36872 | tf_op jit(solution)/shard_map/ppermute | solution.py:40
  183.4 16.2 %all-to-all-start.9 = ((bf16[16,64,96]{2,1,0:T(8,128)(2,1)}), bf16[16,64,96]{2,1,0:T(8,128)(2,1)S(1)}, u32[]{:S(2)}, u32[]{:S(2)}) async-start(bf16[16,64,96]{2,1,0:T(8,128)(2,1)} %broadcast_in_dim.36), calls=%async_computation.9 | async-start | bytes 524288 | tf_op jit(solution)/shard_map/all_to_all | solution.py:11
  186.9 110.3 %reduce-scatter.4.cloned.1.call-start = ((), (), s32[]{:S(2)}) async-start(), calls=%async_computation.11 | async-start | bytes 7962624
  199.7 1.2 copy-start.14
  199.7 1.2 copy-start.27
  200.0 1.0 copy-start.21
  200.9 1.0 copy-start.12
  201.9 1.0 copy-start.19
  201.9 1.1 copy-start.28
  (11 other events, 8.8 us)
Sparse Core Ops, SparseCore 0:
  217.9 79.2 reduce-scatter.3
where the time goes:
time: 314 us; the launch traced here: 313 us
  waiting for transfers between devices  149 us (47%)
  starting transfers between devices  50.3 us (16%)
  blocking collectives  37.3 us (12%)
  local copies, waits for them, and re-layouts  35.4 us (11%)
  matrix products  20.8 us (7%)
  between operations  14.8 us (5%)
  other arithmetic  5.48 us (2%)
    unnamed x2, waiting for transfers between devices  79.5 us
    all_to_all x5, waiting for transfers between devices, sent_to_all(): return lax.all_to_all(copies, axis, split_axis=0, concat_axis=0, tiled=True)  39.5 us
    all_to_all x3, waiting for transfers between devices, sent_and_summed(): lax.all_to_all(in_blocks(value, dim, peers), axis, 0, 0, tiled=True)  26 us
    all_to_all x1, blocking collectives, sent_to_all(): return lax.all_to_all(copies, axis, split_axis=0, concat_axis=0, tiled=True)  23.8 us
    all_to_all x5, starting transfers between devices, sent_to_all(): return lax.all_to_all(copies, axis, split_axis=0, concat_axis=0, tiled=True)  22.7 us
    unnamed x69, local copies, waits for them, and re-layouts  20.3 us
    ppermute x4, starting transfers between devices, from_behind(): return lax.ppermute(block, axis, route)  16.8 us
    all_to_all x1, blocking collectives, sent_and_summed(): lax.all_to_all(in_blocks(value, dim, peers), axis, 0, 0, tiled=True)  13.5 us
  transfers between devices with their start and end apart: 13, of which 11 were waited for; matrix products, arithmetic and copies ran while one was open for 4% of the time, Pallas kernels for 0%

commit v1 on v0

--- a/solution.py
+++ b/solution.py
@@ -3,7 +3,7 @@
 from jax import lax
 from jax.sharding import PartitionSpec as P
 
-MICRO = 2
+MICRO = 1
 
 
 def sent_to_all(value, axis):

time: 314 us -> 259 us (0.82)
  starting transfers between devices: 50.3 us -> 28.1 us
  waiting for transfers between devices: 149 us -> 127 us
  local copies, waits for them, and re-layouts: 35.4 us -> 24.3 us
  matrix products: 20.8 us -> 16.5 us
  blocking collectives: 37.3 us -> 40.9 us
    all_to_all x3 -> x1, waiting for transfers between devices: 26 us -> 12.7 us  [sent_and_summed(): lax.all_to_all(in_blocks(value, dim, peers), axis, 0, 0, tiled=True)]
    all_to_all x5 -> x3, starting transfers between devices: 22.7 us -> 11.3 us  [sent_to_all(): return lax.all_to_all(copies, axis, split_axis=0, concat_axis=0, tiled=True)]
    all_to_all x5 -> x3, waiting for transfers between devices: 39.5 us -> 28.5 us  [sent_to_all(): return lax.all_to_all(copies, axis, split_axis=0, concat_axis=0, tiled=True)]
    all_to_all x3 -> x1, starting transfers between devices: 10.6 us -> 3.55 us  [sent_and_summed(): lax.all_to_all(in_blocks(value, dim, peers), axis, 0, 0, tiled=True)]
    reshape x14 -> x0, local copies, waits for them, and re-layouts: 6.24 us -> none  [the longest x8 3.33 us: in_blocks(): value.reshape(*shape[:dim], peers, shape[dim] // peers, *shape[dim + 1:])]
    dot_general x3 -> x2, matrix products: 5.9 us -> 1.81 us  [local(): jnp.dot(gathered, up_weight, preferred_element_type=jnp.float32)]
    ppermute x4 -> x2, starting transfers between devices: 16.8 us -> 13.2 us  [from_behind(): return lax.ppermute(block, axis, route)]
    unnamed x69 -> x31, local copies, waits for them, and re-layouts: 20.3 us -> 18.7 us
  transfers between devices with their start and end apart: 13 -> 7, of which waited for: 11 -> 7; matrix products, arithmetic and copies ran while one was open for 4% -> 2% of each run, Pallas kernels for 0% -> 0%
where the time goes in v1:
time: 259 us; the launch traced here: 258 us
  waiting for transfers between devices  127 us (49%)
  blocking collectives  40.9 us (16%)
  starting transfers between devices  28.1 us (11%)
  local copies, waits for them, and re-layouts  24.3 us (9%)
  matrix products  16.5 us (6%)
  between operations  14.3 us (6%)
  other arithmetic  6.48 us (3%)
    unnamed x2, waiting for transfers between devices  80.8 us
    all_to_all x3, waiting for transfers between devices, sent_to_all(): return lax.all_to_all(copies, axis, split_axis=0, concat_axis=0, tiled=True)  28.5 us
    all_to_all x1, blocking collectives, sent_to_all(): return lax.all_to_all(copies, axis, split_axis=0, concat_axis=0, tiled=True)  26 us
    unnamed x31, local copies, waits for them, and re-layouts  18.7 us
    all_to_all x1, blocking collectives, sent_and_summed(): lax.all_to_all(in_blocks(value, dim, peers), axis, 0, 0, tiled=True)  15 us
    ppermute x2, starting transfers between devices, from_behind(): return lax.ppermute(block, axis, route)  13.2 us
    all_to_all x1, waiting for transfers between devices, sent_and_summed(): lax.all_to_all(in_blocks(value, dim, peers), axis, 0, 0, tiled=True)  12.7 us
    all_to_all x3, starting transfers between devices, sent_to_all(): return lax.all_to_all(copies, axis, split_axis=0, concat_axis=0, tiled=True)  11.3 us
  transfers between devices with their start and end apart: 7, of which 7 were waited for; matrix products, arithmetic and copies ran while one was open for 2% of the time, Pallas kernels for 0%

profile of v1, /device:TPU:1, one launch (start us, length us, event | category | flops | bytes accessed | tf_op | source)
XLA Modules:
  0.0 257.7 jit_solution(8687394638904730587)
XLA Ops:
  7.3 26.0 %all_to_all.30 = bf16[16,128,96]{1,2,0:T(8,128)(2,1)S(1)} all-to-all(bf16[16,128,96]{1,2,0:T(8,128)(2,1)S(1)} %broadcast_in_dim.25), channel_id=1, replica_groups=mesh['segment'=2,'tensor'=16,'dp'=8] {'tensor'}, dimensions={0} | all-to-all | bytes 786432 | tf_op jit(solution)/shard_map/all_to_all | solution.py:11
  35.7 0.9 copy.20
  36.6 3.6 %all-to-all-start.1 = ((bf16[16,128,96]{1,2,0:T(8,128)(2,1)}), bf16[16,128,96]{1,2,0:T(8,128)(2,1)S(1)}, u32[]{:S(2)}, u32[]{:S(2)}) async-start(bf16[16,128,96]{1,2,0:T(8,128)(2,1)} %bitcast.7), calls=%async_computation.1 | async-start | bytes 786432 | tf_op jit(solution)/shard_map/all_to_all | solution.py:33
  40.9 12.7 %all-to-all-done.1 = bf16[16,128,96]{1,2,0:T(8,128)(2,1)S(1)} async-done(((bf16[16,128,96]{1,2,0:T(8,128)(2,1)}), bf16[16,128,96]{1,2,0:T(8,128)(2,1)S(1)}, u32[]{:S(2)}, u32[]{:S(2)}) %all-to-all-start.1) | async-done | bytes 393248 | tf_op jit(solution)/shard_map/all_to_all | solution.py:33
  54.4 3.6 %all-to-all-start.3 = ((bf16[16,128,96]{1,2,0:T(8,128)(2,1)}), bf16[16,128,96]{1,2,0:T(8,128)(2,1)S(1)}, u32[]{:S(2)}, u32[]{:S(2)}) async-start(bf16[16,128,96]{1,2,0:T(8,128)(2,1)} %broadcast_in_dim.27), calls=%async_computation.3 | async-start | bytes 786432 | tf_op jit(solution)/shard_map/all_to_all | solution.py:11
  58.1 1.3 collective-permute-start
  59.4 4.2 %collective-permute-done = bf16[128,96]{0,1:T(8,128)(2,1)S(1)} collective-permute-done((bf16[128,96]{0,1:T(8,128)(2,1)S(1)}, bf16[128,96]{0,1:T(8,128)(2,1)S(1)}, u32[]{:S(2)}, u32[]{:S(2)}) %collective-permute-start) | collective-permute-done | bytes 24608 | tf_op jit(solution)/shard_map/ppermute | solution.py:40
  63.6 7.6 %all-to-all-done.3 = bf16[16,128,96]{1,2,0:T(8,128)(2,1)S(1)} async-done(((bf16[16,128,96]{1,2,0:T(8,128)(2,1)}), bf16[16,128,96]{1,2,0:T(8,128)(2,1)S(1)}, u32[]{:S(2)}, u32[]{:S(2)}) %all-to-all-start.3) | async-done | bytes 393248 | tf_op jit(solution)/shard_map/all_to_all | solution.py:11
  72.0 3.6 %all-to-all-start.2 = ((bf16[16,128,96]{1,2,0:T(8,128)(2,1)}), bf16[16,128,96]{1,2,0:T(8,128)(2,1)S(1)}, u32[]{:S(2)}, u32[]{:S(2)}) async-start(bf16[16,128,96]{1,2,0:T(8,128)(2,1)} %broadcast_in_dim.26), calls=%async_computation.2 | async-start | bytes 786432 | tf_op jit(solution)/shard_map/all_to_all | solution.py:11
  75.6 3.3 %fusion.3 = f32[128,768]{1,0:T(8,128)} fusion(bf16[128,1536]{0,1:T(8,128)(2,1)S(1)} %bitcast.80, bf16[1,768,1536]{2,1,0:T(8,128)(2,1)} %param.8), kind=kOutput, calls=%fused_computation.9 | convolution fusion | flops 301989888 | bytes 3145728 | tf_op jit(solution)/shard_map/dot_general | solution.py:56
  78.9 8.2 %all-to-all-done.2 = bf16[16,128,96]{1,2,0:T(8,128)(2,1)S(1)} async-done(((bf16[16,128,96]{1,2,0:T(8,128)(2,1)}), bf16[16,128,96]{1,2,0:T(8,128)(2,1)S(1)}, u32[]{:S(2)}, u32[]{:S(2)}) %all-to-all-start.2) | async-done | bytes 393248 | tf_op jit(solution)/shard_map/all_to_all | solution.py:11
  87.1 2.3 fusion.38
  89.5 1.3 multiply_convert_fusion
  91.2 0.9 fusion.11
  92.1 0.9 fusion
  93.0 0.9 copy.21
  93.9 15.0 %all_to_all.31 = bf16[16,128,96]{1,2,0:T(8,128)(2,1)S(1)} all-to-all(bf16[16,128,96]{1,2,0:T(8,128)(2,1)} %bitcast.84), channel_id=1, replica_groups=mesh['segment'=2,'tensor'=16,'dp'=8] {'tensor'}, dimensions={0} | all-to-all | bytes 786432 | tf_op jit(solution)/shard_map/all_to_all | solution.py:33
  109.7 11.9 %collective-permute-start.1 = (bf16[128,96]{0,1:T(8,128)(2,1)S(1)}, bf16[128,96]{0,1:T(8,128)(2,1)S(1)}, u32[]{:S(2)}, u32[]{:S(2)}) collective-permute-start(bf16[128,96]{0,1:T(8,128)(2,1)S(1)} %add_convert_fusion), channel_id=1, source_target_pairs={{128,0},{129,1},{130,2},{131,3},{132,4},{133,5},{134,6},{135,7},{1... | collective-permute-start | bytes 73736 | tf_op jit(solution)/shard_map/ppermute | solution.py:40
  123.3 4.2 %all-to-all-start.5 = ((bf16[16,128,96]{1,2,0:T(8,128)(2,1)}), bf16[16,128,96]{1,2,0:T(8,128)(2,1)}, u32[]{:S(2)}, u32[]{:S(2)}) async-start(bf16[16,128,96]{1,2,0:T(8,128)(2,1)} %broadcast_in_dim.28), calls=%async_computation.5 | async-start | bytes 786432 | tf_op jit(solution)/shard_map/all_to_all | solution.py:11
  127.6 1.0 broadcast_select_fusion.1
  128.6 12.7 %all-to-all-done.5 = bf16[16,128,96]{1,2,0:T(8,128)(2,1)} async-done(((bf16[16,128,96]{1,2,0:T(8,128)(2,1)}), bf16[16,128,96]{1,2,0:T(8,128)(2,1)}, u32[]{:S(2)}, u32[]{:S(2)}) %all-to-all-start.5) | async-done | bytes 393248 | tf_op jit(solution)/shard_map/all_to_all | solution.py:11
  141.3 2.8 %fusion.50 = (bf16[128,768]{1,0:T(8,128)(2,1)S(1)}, bf16[128,768]{1,0:T(8,128)(2,1)S(1)}, bf16[128,768]{1,0:T(8,128)(2,1)S(1)}) fusion(bf16[128,768]{1,0:T(8,128)(2,1)} %copy-done.10, pred[]{:T(512)S(6)} %eq.3, bf16[128,768]{1,0:T(8,128)(2,1)} %copy-done.11, bf16[128,1536]{0,1:T(8,128)(2,1)} %bitcast.16, bf16[1,768,1536]{2,1,0:T(8,128)(2,1)} %param.8), kind=kOutput, calls=%fused_computation.54 | convolution fusion | flops 303955968 | bytes 3735553 | tf_op jit(solution)/shard_map/dot_general | solution.py:56
  145.1 0.8 convolution_convert_fusion.1
  145.9 1.8 convolution_convert_fusion
  147.8 3.5 %pad_maximum_fusion = bf16[1536,2304]{0,1:T(8,128)(2,1)} fusion(bf16[1536,768]{0,1:T(8,128)(2,1)S(1)} %convolution_convert_fusion, bf16[1536,768]{0,1:T(8,128)(2,1)S(1)} %convolution_convert_fusion.1, bf16[1536,768]{0,1:T(8,128)(2,1)S(1)} %convolution_convert_fusion.2), kind=kLoop, calls=%fused_computation | loop fusion | flops 21233664 | bytes 14155776 | tf_op jit(solution)/shard_map/concatenate | solution.py:134
  151.3 10.3 %copy.25 = bf16[1536,2304]{1,0:T(8,128)(2,1)} copy(bf16[1536,2304]{0,1:T(8,128)(2,1)} %pad_maximum_fusion) | data formatting | bytes 14155776
  161.6 80.8 %reduce-scatter.4.cloned.1.call-done = bf16[192,2304]{1,0:T(8,128)(2,1)} async-done(((bf16[1536,2304]{1,0:T(8,128)(2,1)}), bf16[192,2304]{1,0:T(8,128)(2,1)}) %reduce-scatter.4.cloned.1.call-update) | async-done | bytes 884752
  242.4 1.5 copy.26
  244.1 1.3 slice_bitcast_fusion
  245.4 2.2 copy.24
  247.6 2.2 copy.23
  249.8 1.1 copy.22
  (47 shorter events, 9.0 us)
Async XLA Ops:
  7.2 26.1 %copy-start = (bf16[1,1536,768]{2,1,0:T(8,128)(2,1)S(1)}, bf16[1,1536,768]{2,1,0:T(8,128)(2,1)}, u32[]{:S(2)}) copy-start(bf16[1,1536,768]{2,1,0:T(8,128)(2,1)} %param.7) | copy-start | bytes 7077892
  7.2 26.6 %copy-start.1 = (bf16[1,1536,768]{2,1,0:T(8,128)(2,1)S(1)}, bf16[1,1536,768]{2,1,0:T(8,128)(2,1)}, u32[]{:S(2)}) copy-start(bf16[1,1536,768]{2,1,0:T(8,128)(2,1)} %param.6) | copy-start | bytes 7077892
  33.3 1.9 copy-start.4
  33.8 0.7 copy-start.10
  34.5 0.7 copy-start.11
  36.6 17.0 %all-to-all-start.1 = ((bf16[16,128,96]{1,2,0:T(8,128)(2,1)}), bf16[16,128,96]{1,2,0:T(8,128)(2,1)S(1)}, u32[]{:S(2)}, u32[]{:S(2)}) async-start(bf16[16,128,96]{1,2,0:T(8,128)(2,1)} %bitcast.7), calls=%async_computation.1 | async-start | bytes 786432 | tf_op jit(solution)/shard_map/all_to_all | solution.py:33
  54.4 16.8 %all-to-all-start.3 = ((bf16[16,128,96]{1,2,0:T(8,128)(2,1)}), bf16[16,128,96]{1,2,0:T(8,128)(2,1)S(1)}, u32[]{:S(2)}, u32[]{:S(2)}) async-start(bf16[16,128,96]{1,2,0:T(8,128)(2,1)} %broadcast_in_dim.27), calls=%async_computation.3 | async-start | bytes 786432 | tf_op jit(solution)/shard_map/all_to_all | solution.py:11
  58.1 5.5 %collective-permute-start = (bf16[128,96]{0,1:T(8,128)(2,1)S(1)}, bf16[128,96]{0,1:T(8,128)(2,1)S(1)}, u32[]{:S(2)}, u32[]{:S(2)}) collective-permute-start(bf16[128,96]{0,1:T(8,128)(2,1)S(1)} %add_convert_fusion.1), channel_id=1, source_target_pairs={{0,128},{1,129},{2,130},{3,131},{4,132},{5,133},{6,134},{7,135},{8... | collective-permute-start | bytes 73736 | tf_op jit(solution)/shard_map/ppermute | solution.py:40
  72.0 15.1 %all-to-all-start.2 = ((bf16[16,128,96]{1,2,0:T(8,128)(2,1)}), bf16[16,128,96]{1,2,0:T(8,128)(2,1)S(1)}, u32[]{:S(2)}, u32[]{:S(2)}) async-start(bf16[16,128,96]{1,2,0:T(8,128)(2,1)} %broadcast_in_dim.26), calls=%async_computation.2 | async-start | bytes 786432 | tf_op jit(solution)/shard_map/all_to_all | solution.py:11
  87.1 3.7 %copy-start.3 = (bf16[16,128,96]{1,2,0:T(8,128)(2,1)}, bf16[16,128,96]{1,2,0:T(8,128)(2,1)S(1)}, u32[]{:S(2)}) copy-start(bf16[16,128,96]{1,2,0:T(8,128)(2,1)S(1)} %all-to-all-done.2) | copy-start | bytes 1179652
  87.1 2.4 copy-start.9
  89.4 1.7 copy-start.2
  90.8 1.3 copy-start.7
  90.8 1.3 copy-start.5
  109.7 12.8 %collective-permute-start.1 = (bf16[128,96]{0,1:T(8,128)(2,1)S(1)}, bf16[128,96]{0,1:T(8,128)(2,1)S(1)}, u32[]{:S(2)}, u32[]{:S(2)}) collective-permute-start(bf16[128,96]{0,1:T(8,128)(2,1)S(1)} %add_convert_fusion), channel_id=1, source_target_pairs={{128,0},{129,1},{130,2},{131,3},{132,4},{133,5},{134,6},{135,7},{1... | collective-permute-start | bytes 73736 | tf_op jit(solution)/shard_map/ppermute | solution.py:40
  123.3 18.1 %all-to-all-start.5 = ((bf16[16,128,96]{1,2,0:T(8,128)(2,1)}), bf16[16,128,96]{1,2,0:T(8,128)(2,1)}, u32[]{:S(2)}, u32[]{:S(2)}) async-start(bf16[16,128,96]{1,2,0:T(8,128)(2,1)} %broadcast_in_dim.28), calls=%async_computation.5 | async-start | bytes 786432 | tf_op jit(solution)/shard_map/all_to_all | solution.py:11
  127.5 114.9 %reduce-scatter.4.cloned.1.call-start = ((), (), s32[]{:S(2)}) async-start(), calls=%async_computation.7 | async-start | bytes 7962624
  141.3 2.8 %copy-start.8 = (bf16[128,768]{1,0:T(8,128)(2,1)S(1)}, bf16[128,768]{1,0:T(8,128)(2,1)}, u32[]{:S(2)}) copy-start(bf16[128,768]{1,0:T(8,128)(2,1)} %copy-done.7) | copy-start | bytes 589828
  144.1 0.9 copy-start.6
  145.0 0.9 copy-start.12
Sparse Core Ops, SparseCore 0:
  161.8 80.5 reduce-scatter.3

commit v2 on v1

v2 whole, which is shorter than its diff:
```python
import jax
import jax.numpy as jnp
from jax import lax
from jax.experimental import pallas as pl
from jax.experimental.pallas import tpu as pltpu
from jax.sharding import Mesh, PartitionSpec as P

CORES = 2
XS = 4
ZH = 4
ZL = 2
YS = 4
PEERS = ZL * YS
LANES = 128
TENSOR = ("x", "zh")
DP = ("zl", "y")
BF16 = jnp.bfloat16
F32 = jnp.float32


def shifted(value, axis, distance):
    size = lax.axis_size(axis)
    return lax.ppermute(value, axis, [(i, (i + distance) % size) for i in range(size)])


def one_way(value, source):
    return lax.ppermute(value, "segment", [(source, 1 - source)])


def exchanged(value, axes):
    return lax.all_to_all(value, axes, 0, 0, tiled=True)


def dot_tn(left, right):
    return lax.dot_general(left, right, (((0,), (0,)), ((), ())), preferred_element_type=F32)


def dot_nt(left, right):
    return lax.dot_general(left, right, (((1,), (1,)), ((), ())), preferred_element_type=F32)


def dot_nn(left, right):
    return jnp.dot(left, right, preferred_element_type=F32)


def whole(memory_space=pltpu.VMEM):
    return pl.BlockSpec(memory_space=memory_space)


def hidden_of(gate, up):
    gate = gate.astype(F32)
    return (jax.nn.silu(gate) * up.astype(F32)).astype(BF16)


def gate_grads(d_hidden, gate, up):
    gate = gate.astype(F32)
    up = up.astype(F32)
    sigma = jax.nn.sigmoid(gate)
    d_gate = (d_hidden * up * sigma * (1.0 + gate * (1.0 - sigma))).astype(BF16)
    d_up = (d_hidden * gate * sigma).astype(BF16)
    return d_gate, d_up


def limits(mebibytes):
    return pltpu.CompilerParams(vmem_limit_bytes=mebibytes * 2**20)


def columns_at(value, index, width):
    return lax.dynamic_slice_in_dim(value, index * width, width, 1)


def assemble(blocks, x):
    rows, width = blocks[0].shape

    def body(x_ref, *refs):
        out_ref = refs[-1]
        for k in range(XS):
            start = pl.multiple_of(((x_ref[0] + k) % XS) * width, LANES)
            out_ref[:, pl.ds(start, width)] = refs[k][...]

    return pl.pallas_call(
        body,
        in_specs=[whole(pltpu.SMEM)] + [whole()] * XS,
        out_specs=whole(),
        out_shape=jax.ShapeDtypeStruct((rows, width * XS), BF16),
        compiler_params=limits(2),
        name="assemble",
    )(x, *blocks)


def merge(own, other, core):
    rows, width = own.shape

    def body(core_ref, own_ref, other_ref, out_ref):
        start = pl.multiple_of(core_ref[0] * rows, 16)
        out_ref[pl.ds(start, rows), :] = own_ref[...]
        start = pl.multiple_of((1 - core_ref[0]) * rows, 16)
        out_ref[pl.ds(start, rows), :] = other_ref[...]

    return pl.pallas_call(
        body,
        in_specs=[whole(pltpu.SMEM), whole(), whole()],
        out_specs=whole(),
        out_shape=jax.ShapeDtypeStruct((rows * CORES, width), BF16),
        compiler_params=limits(2),
        name="merge",
    )(core, own, other)


def packed(choices, acts, core):
    rows, half = choices[0][1].shape
    tiles = half // LANES
    shard = acts.shape[0] // PEERS
    count = len(choices)
    height = count * tiles * rows + shard

    def body(core_ref, *refs):
        acts_ref = refs[2 * count]
        out_ref = refs[-1]
        for c in range(count):
            source = choices[c][0]

            def fill(ref, c=c):
                for t in range(tiles):
                    base = (c * tiles + t) * rows
                    out_ref[0, base : base + rows, :] = ref[:, t * LANES : (t + 1) * LANES]

            pl.when(core_ref[0] == source)(lambda: fill(refs[2 * c]))
            pl.when(core_ref[0] != source)(lambda: fill(refs[2 * c + 1]))
        out_ref[0, count * tiles * rows :, :] = acts_ref[...]

    values = [v for choice in choices for v in choice[1:]]
    return pl.pallas_call(
        body,
        grid=(PEERS,),
        in_specs=[whole(pltpu.SMEM)]
        + [pl.BlockSpec((rows, half), lambda p: (0, 0))] * (2 * count)
        + [pl.BlockSpec((shard, rows), lambda p: (p, 0))],
        out_specs=pl.BlockSpec((1, height, rows), lambda p: (p, 0, 0)),
        out_shape=jax.ShapeDtypeStruct((PEERS, height, rows), BF16),
        compiler_params=limits(8),
        name="packed",
    )(core, *values, acts)


def weight_grads(stored, d_hidden, acts, upstream, core):
    arrays = []

    def ref_of(array):
        for i, known in enumerate(arrays):
            if known is array:
                return i
        arrays.append(array)
        return len(arrays) - 1

    step = 2
    lanes = stored[0].shape[2]
    half = 3 * lanes
    shard = 192
    stored_at = ref_of(stored[0])
    grad_at = ref_of(d_hidden[0])
    plans = []
    for plan in (acts, upstream):
        if plan[0] == "own":
            plans.append((ref_of(plan[1]), plan[2], None, None))
        else:
            plans.append((ref_of(plan[2]), plan[3], plan[1], ref_of(plan[4])))

    def body(core_ref, *refs):
        ins = refs[: len(arrays)]
        out_ref, low_ref, acc_ref = refs[len(arrays) :]
        index = pl.program_id(0)

        @pl.when(index == 0)
        def _():
            acc_ref[...] = jnp.zeros_like(acc_ref)

        def wide(ref, base):
            rows = [
                jnp.concatenate(
                    [ref[r, base + t * lanes : base + (t + 1) * lanes, :] for t in range(3)],
                    axis=1,
                )
                for r in range(step)
            ]
            return jnp.concatenate(rows, axis=0)

        def features(plan):
            at, base, when, other = plan
            blocks = []
            for r in range(step):
                block = ins[at][r, base : base + shard, :]
                if other is not None:
                    block = jnp.where(core_ref[0] == when, block, ins[other][r])
                blocks.append(block)
            return jnp.concatenate(blocks, axis=1)

        gate = wide(ins[stored_at], stored[1]).astype(F32)
        up = wide(ins[stored_at], stored[1] + half).astype(F32)
        grad = wide(ins[grad_at], d_hidden[1]).astype(F32)
        sigma = jax.nn.sigmoid(gate)
        silu = gate * sigma
        d_gate = (grad * up * sigma * (1.0 + gate * (1.0 - sigma))).astype(BF16)
        d_up = (grad * silu).astype(BF16)
        acts_t = features(plans[0])
        acc_ref[0] += dot_nn(acts_t, d_gate)
        acc_ref[1] += dot_nn(acts_t, d_up)
        acc_ref[2] += dot_nn(features(plans[1]), (silu * up).astype(BF16))

        @pl.when(index == PEERS // step - 1)
        def _():
            out_ref[...] = acc_ref[...]
            low_ref[...] = acc_ref[...].astype(BF16)

    shape = (3, shard, half)
    return pl.pallas_call(
        body,
        grid=(PEERS // step,),
        in_specs=[whole(pltpu.SMEM)]
        + [pl.BlockSpec((step, *a.shape[1:]), lambda p: (p, 0, 0)) for a in arrays],
        out_specs=[
            pl.BlockSpec(shape, lambda p: (0, 0, 0)),
            pl.BlockSpec(shape, lambda p: (0, 0, 0)),
        ],
        out_shape=[jax.ShapeDtypeStruct(shape, F32), jax.ShapeDtypeStruct(shape, BF16)],
        scratch_shapes=[pltpu.VMEM(shape, F32)],
        compiler_params=limits(16),
    )(core, *arrays)


def finish(own_0, own_1, got_0, got_1, core):
    count, shard, half = own_0.shape

    def body(core_ref, own_0_ref, own_1_ref, got_0_ref, got_1_ref, *outs):
        @pl.when(core_ref[0] == 0)
        def _():
            for i in range(count):
                outs[i][:, :half] = own_0_ref[i]
                outs[i][:, half:] = got_0_ref[i].astype(F32)

        @pl.when(core_ref[0] != 0)
        def _():
            for i in range(count):
                outs[i][:, :half] = got_1_ref[i].astype(F32)
                outs[i][:, half:] = own_1_ref[i]

    shape = jax.ShapeDtypeStruct((shard, half * CORES), F32)
    return pl.pallas_call(
        body,
        in_specs=[whole(pltpu.SMEM)] + [whole()] * 4,
        out_specs=[whole()] * count,
        out_shape=[shape] * count,
        compiler_params=limits(8),
        name="finish",
    )(core, own_0, own_1, got_0, got_1)


def crossing(sent, kept, residual, source, core, x, core_id, x_id):
    received = one_way(sent.astype(BF16), source)
    mine = jnp.where(core == source, kept.astype(BF16), received)
    width = mine.shape[1] // XS
    pieces = [
        shifted(columns_at(mine, (x + k) % XS, width), "x", k) for k in range(1, XS)
    ]
    total = columns_at(mine, x, width).astype(F32)
    for piece in pieces:
        total = total + piece.astype(F32)
    summed = total.astype(BF16)
    pieces = [shifted(summed, "zh", k) for k in range(1, ZH)]
    total = summed.astype(F32)
    for piece in pieces:
        total = total + piece.astype(F32)
    half_rows = lax.dynamic_slice(
        residual, (core * sent.shape[0], x * width), (sent.shape[0], width)
    )
    out = (half_rows.astype(F32) + total).astype(BF16)
    blocks = [out] + [shifted(out, "x", XS - k) for k in range(1, XS)]
    own = assemble(blocks, x_id)
    other = shifted(own, "segment", 1)
    return merge(own, other, core_id)


def local(tokens, w_gate, w_up, w_down, cotangent):
    return step(tokens, w_gate[0], w_up[0], w_down[0], cotangent)


def step(tokens, gate_w, up_w, down_w, cotangent):
    core = lax.axis_index("segment")
    x = lax.axis_index("x")
    core_id = core.astype(jnp.int32)[None]
    x_id = x.astype(jnp.int32)[None]
    rows = tokens.shape[0]
    features, hidden = gate_w.shape
    half = hidden // CORES
    split = rows // CORES

    def split_of(value):
        return value[:, :half], value[:, half:]

    own = jnp.where(core == 0, tokens.T, cotangent.T)
    gathered = exchanged(jnp.broadcast_to(own, (XS * ZH, *own.shape)), TENSOR)
    entered = gathered.reshape(features, rows)

    gate_a = dot_tn(entered, gate_w).astype(BF16)
    up_a = dot_tn(entered, up_w).astype(BF16)
    hidden_a = hidden_of(gate_a, up_a)
    sent = dot_nn(hidden_a[split:], down_w)
    kept = dot_nn(hidden_a[:split], down_w)
    swapped = shifted(entered, "segment", 1)
    tokens_t = jnp.where(core == 0, entered, swapped)
    cot_t = jnp.where(core == 0, swapped, entered)
    middle = crossing(sent, kept, tokens_t.T, 0, core, x, core_id, x_id)

    d_hidden_a = lax.optimization_barrier(
        lax.dot_general(
            entered, down_w, (((0,), (1,)), ((), ())), preferred_element_type=F32
        ).astype(BF16)
    )
    gate_l, gate_r = split_of(gate_a)
    up_l, up_r = split_of(up_a)
    grad_l, grad_r = split_of(d_hidden_a)
    choices = [
        (0, gate_l, one_way(gate_r, 0)),
        (0, up_l, one_way(up_r, 0)),
        (1, grad_r, one_way(grad_l, 1)),
    ]
    load = packed(choices, entered, core_id)
    wide = exchanged(load, DP)

    wide_a = wide
    entered_all = wide[:, 3 * half :]
    entered_other = shifted(entered_all, "segment", 1)

    gate_b = dot_nn(middle, gate_w).astype(BF16)
    up_b = dot_nn(middle, up_w).astype(BF16)
    d_gate_b, d_up_b = gate_grads(d_hidden_a.astype(F32), gate_b, up_b)
    sent = dot_nt(d_gate_b[:split], gate_w) + dot_nt(d_up_b[:split], up_w)
    kept = dot_nt(d_gate_b[split:], gate_w) + dot_nt(d_up_b[split:], up_w)
    upstream = crossing(sent, kept, cot_t.T, 1, core, x, core_id, x_id)

    gate_l, gate_r = split_of(gate_b)
    up_l, up_r = split_of(up_b)
    choices = [(1, gate_r, one_way(gate_l, 1)), (1, up_r, one_way(up_l, 1))]
    load = packed(choices, middle.T, core_id)
    load, wide_a = lax.optimization_barrier((load, wide_a))
    wide_b = exchanged(load, DP)

    d_hidden_b = dot_nt(upstream, down_w).astype(BF16)
    grad_l, grad_r = split_of(d_hidden_b)
    choices = [(0, grad_l, one_way(grad_r, 0))]
    load = packed(choices, upstream.T, core_id)
    load, wide_b = lax.optimization_barrier((load, wide_b))
    wide_c = exchanged(load, DP)

    own_1, low_1 = weight_grads(
        (wide_b, 0),
        (wide_a, 2 * half),
        ("own", wide_b, 2 * half),
        ("pick", 1, wide_a, 3 * half, entered_other),
        core_id,
    )
    got_1 = one_way(low_1, 0)
    own_0, low_0 = weight_grads(
        (wide_a, 0),
        (wide_c, 0),
        ("pick", 0, wide_a, 3 * half, entered_other),
        ("own", wide_c, half),
        core_id,
    )
    got_0 = one_way(low_0, 1)
    grad_gate, grad_up, grad_down = finish(own_0, own_1, got_0, got_1, core_id)
    return (grad_gate[None], grad_up[None], grad_down.T[None])


def solution(mesh):
    fine = Mesh(
        mesh.devices.reshape(CORES, XS, ZH, ZL, YS), ("segment", "x", "zh", "zl", "y")
    )
    in_specs = (
        P(DP, TENSOR),
        P("segment", None, TENSOR),
        P("segment", None, TENSOR),
        P("segment", TENSOR, None),
        P(DP, TENSOR),
    )
    out_specs = (
        P("segment", DP, TENSOR),
        P("segment", DP, TENSOR),
        P("segment", TENSOR, DP),
    )
    return jax.shard_map(
        local, mesh=fine, in_specs=in_specs, out_specs=out_specs, check_vma=False
    )
```

time: 259 us -> 188 us (0.73)
  waiting for transfers between devices: 127 us -> 50.4 us
  starting transfers between devices: 28.1 us -> 68 us
  local copies, waits for them, and re-layouts: 24.3 us -> 9.06 us
  blocking collectives: 40.9 us -> 26.2 us
  between operations: 14.3 us -> 1.16 us
  Pallas kernels: 0 us -> 13.1 us
  other arithmetic: 6.48 us -> 2.68 us
    unnamed x2 -> x0, waiting for transfers between devices: 80.8 us -> none
    ppermute x2 -> x32, starting transfers between devices: 13.2 us -> 52.5 us  [the longest x22 32.9 us: shifted(): lax.ppermute(value, axis, [(i, (i + distance) % size) for i in range(size)])]
    ppermute x2 -> x32, waiting for transfers between devices: 5.05 us -> 44.3 us  [the longest x22 37.6 us: shifted(): lax.ppermute(value, axis, [(i, (i + distance) % size) for i in range(size)])]
    all_to_all x4 -> x3, waiting for transfers between devices: 41.2 us -> 6.19 us  [exchanged(): return lax.all_to_all(value, axes, 0, 0, tiled=True)]
    all_to_all x2 -> x1, blocking collectives: 40.9 us -> 26.2 us  [exchanged(): return lax.all_to_all(value, axes, 0, 0, tiled=True)]
    pallas_call x0 -> x10, Pallas kernels: none -> 13.1 us  [the longest x2 9.04 us: weight_grads(): pl.pallas_call(body, grid=(PEERS // step,), in_specs=[whole(pltpu.SMEM)]...]
    unnamed x31 -> x32, local copies, waits for them, and re-layouts: 18.7 us -> 5.91 us
    broadcast_in_dim x5 -> x1, local copies, waits for them, and re-layouts: 3.77 us -> 0.05 us  [step(): gathered = exchanged(jnp.broadcast_to(own, (XS * ZH, *own.shape)), TENSOR)]
  transfers between devices with their start and end apart: 7 -> 35, of which waited for: 7 -> 25; matrix products, arithmetic and copies ran while one was open for 2% -> 11% of each run, Pallas kernels for 0% -> 5%
where the time goes in v2:
time: 188 us; the launch traced here: 187 us
  starting transfers between devices  68 us (36%)
  waiting for transfers between devices  50.4 us (27%)
  blocking collectives  26.2 us (14%)
  matrix products  16.6 us (9%)
  Pallas kernels  13.1 us (7%)
  local copies, waits for them, and re-layouts  9.06 us (5%)
  other arithmetic  2.68 us (1%)
    ppermute x22, waiting for transfers between devices, shifted(): lax.ppermute(value, axis, [(i, (i + distance) % size) for i in range(size)])  37.6 us
    ppermute x22, starting transfers between devices, shifted(): lax.ppermute(value, axis, [(i, (i + distance) % size) for i in range(size)])  32.9 us
    all_to_all x1, blocking collectives, exchanged(): return lax.all_to_all(value, axes, 0, 0, tiled=True)  26.2 us
    ppermute x10, starting transfers between devices, one_way(): return lax.ppermute(value, 'segment', [(source, 1 - source)])  19.6 us
    all_to_all x3, starting transfers between devices, exchanged(): return lax.all_to_all(value, axes, 0, 0, tiled=True)  15.5 us
    pallas_call x2, Pallas kernels, weight_grads(): pl.pallas_call(body, grid=(PEERS // step,), in_specs=[whole(pltpu.SMEM)]...  9.04 us
    dot_general x4, matrix products, dot_nn(): return jnp.dot(left, right, preferred_element_type=F32)  8.65 us
    ppermute x10, waiting for transfers between devices, one_way(): return lax.ppermute(value, 'segment', [(source, 1 - source)])  6.61 us
  transfers between devices with their start and end apart: 35, of which 25 were waited for; matrix products, arithmetic and copies ran while one was open for 11% of the time, Pallas kernels for 5%

profile of v2, /device:TPU:1, one launch (start us, length us, event | category | flops | bytes accessed | tf_op | source)
XLA Modules:
  0.0 187.3 jit_solution(1032098618771924658)
XLA Ops:
  1.6 26.2 %all_to_all.20 = bf16[16,96,128]{2,1,0:T(8,128)(2,1)S(1)} all-to-all(bf16[16,96,128]{2,1,0:T(8,128)(2,1)S(1)} %broadcast_in_dim.20), channel_id=1, replica_groups=mesh['segment'=2,'x'=4,'zh'=4,'zl'=2,'y'=4] {'x','zh'}, dimensions={0} | all-to-all | bytes 786432 | tf_op jit(solution)/shard_map/all_to_all | solution.py:31
  29.4 4.1 %collective-permute-start.16 = (bf16[128,384]{1,0:T(8,128)(2,1)S(1)}, bf16[128,384]{1,0:T(8,128)(2,1)S(1)}, u32[]{:S(2)}, u32[]{:S(2)}) collective-permute-start(bf16[128,384]{1,0:T(8,128)(2,1)S(1)} %get-tuple-element.32), channel_id=1, source_target_pairs={{128,0},{129,1},{130,2},{131,3},{132,4},{133,5},{134,6},{135,7},{1... | collective-permute-start | bytes 294920 | tf_op jit(solution)/shard_map/ppermute | solution.py:27
  36.7 1.9 %collective-permute-done.15.refs_3_ = bf16[128,384]{1,0:T(8,128)(2,1)S(1)} collective-permute-done((bf16[128,384]{1,0:T(8,128)(2,1)S(1)}, bf16[128,384]{1,0:T(8,128)(2,1)S(1)}, u32[]{:S(2)}, u32[]{:S(2)}) %collective-permute-start.15) | collective-permute-done | bytes 98336 | tf_op jit(solution)/shard_map/ppermute | solution.py:27
  41.0 4.7 %all-to-all-start.1 = ((bf16[8,1344,128]{2,1,0:T(8,128)(2,1)}), bf16[8,1344,128]{2,1,0:T(8,128)(2,1)}, u32[]{:S(2)}, u32[]{:S(2)}) async-start(bf16[8,1344,128]{2,1,0:T(8,128)(2,1)} %copy-done.1), calls=%async_computation.1 | async-start | bytes 5505024 | tf_op jit(solution)/shard_map/all_to_all | solution.py:31
  45.7 2.9 %fusion.39 = bf16[64,1536]{1,0:T(8,128)(2,1)} fusion(bf16[1,768,1536]{2,1,0:T(8,128)(2,1)} %param.8, bf16[128,768]{1,0:T(8,128)(2,1)S(1)} %get-tuple-element.45), kind=kOutput, calls=%fused_computation.29 | convolution fusion | flops 151093248 | bytes 2654208 | tf_op jit(solution)/shard_map/dot_general | solution.py:43
  52.1 2.3 %fusion.42 = bf16[64,1536]{1,0:T(8,128)(2,1)S(1)} fusion(bf16[64,1536]{1,0:T(8,128)(2,1)S(1)} %collective-permute-done.1, bf16[1,768,1536]{2,1,0:T(8,128)(2,1)} %param.8, pred[]{:T(512)S(6)} %eq.16, bf16[128,768]{1,0:T(8,128)(2,1)} %copy-done.15), kind=kOutput, calls=%fused_computation.30 | convolution fusion | flops 151191552 | bytes 2850817 | tf_op jit(solution)/shard_map/dot_general | solution.py:43
  54.5 2.7 %collective-permute-start.4 = (bf16[64,384]{1,0:T(8,128)(2,1)S(1)}, bf16[64,384]{1,0:T(8,128)(2,1)S(1)}, u32[]{:S(2)}, u32[]{:S(2)}) collective-permute-start(bf16[64,384]{1,0:T(8,128)(2,1)S(1)} %get-tuple-element.43), channel_id=1, source_target_pairs={{0,96},{32,0},{64,32},{96,64},{1,97},{33,1},{65,33},{97,65},{2,98}... | collective-permute-start | bytes 147464 | tf_op jit(solution)/shard_map/ppermute | solution.py:23
  57.1 1.9 collective-permute-done.2
  59.0 3.0 %collective-permute-done.3 = bf16[64,384]{1,0:T(8,128)(2,1)S(1)} collective-permute-done((bf16[64,384]{1,0:T(8,128)(2,1)S(1)}, bf16[64,384]{1,0:T(8,128)(2,1)S(1)}, u32[]{:S(2)}, u32[]{:S(2)}) %collective-permute-start.3) | collective-permute-done | bytes 49184 | tf_op jit(solution)/shard_map/ppermute | solution.py:23
  62.3 3.7 %collective-permute-start.6 = (bf16[64,384]{1,0:T(8,128)(2,1)S(1)}, bf16[64,384]{1,0:T(8,128)(2,1)S(1)}, u32[]{:S(2)}, u32[]{:S(2)}) collective-permute-start(bf16[64,384]{1,0:T(8,128)(2,1)S(1)} %add_convert_fusion.1), channel_id=1, source_target_pairs={{0,16},{8,24},{16,0},{24,8},{1,17},{9,25},{17,1},{25,9},{2,18},{10... | collective-permute-start | bytes 147464 | tf_op jit(solution)/shard_map/ppermute | solution.py:23
  66.3 11.8 %collective-permute-done.6 = bf16[64,384]{1,0:T(8,128)(2,1)S(1)} collective-permute-done((bf16[64,384]{1,0:T(8,128)(2,1)S(1)}, bf16[64,384]{1,0:T(8,128)(2,1)S(1)}, u32[]{:S(2)}, u32[]{:S(2)}) %collective-permute-start.6) | collective-permute-done | bytes 49184 | tf_op jit(solution)/shard_map/ppermute | solution.py:23
  78.1 2.1 %collective-permute-done.5 = bf16[64,384]{1,0:T(8,128)(2,1)S(1)} collective-permute-done((bf16[64,384]{1,0:T(8,128)(2,1)S(1)}, bf16[64,384]{1,0:T(8,128)(2,1)S(1)}, u32[]{:S(2)}, u32[]{:S(2)}) %collective-permute-start.5) | collective-permute-done | bytes 49184 | tf_op jit(solution)/shard_map/ppermute | solution.py:23
  86.4 2.9 %collective-permute-start.11 = (bf16[64,1536]{1,0:T(8,128)(2,1)S(1)}, bf16[64,1536]{1,0:T(8,128)(2,1)S(1)}, u32[]{:S(2)}, u32[]{:S(2)}) collective-permute-start(bf16[64,1536]{1,0:T(8,128)(2,1)S(1)} %assemble.2.own_ref), channel_id=1, source_target_pairs={{0,128},{128,0},{1,129},{129,1},{2,130},{130,2},{3,131},{131,3},{4... | collective-permute-start | bytes 589832 | tf_op jit(solution)/shard_map/ppermute | solution.py:23
  90.4 2.1 %fusion.57 = bf16[128,768]{1,0:T(8,128)(2,1)S(1)} fusion(bf16[128,1536]{1,0:T(8,128)(2,1)S(1)} %merge.2, bf16[1,1536,768]{2,1,0:T(8,128)(2,1)} %param.7), kind=kOutput, calls=%fused_computation.35 | convolution fusion | flops 302088192 | bytes 2949120 | tf_op jit(solution)/shard_map/dot_general | solution.py:43
  93.2 2.3 %collective-permute-start.13 = (bf16[128,384]{1,0:T(8,128)(2,1)}, bf16[128,384]{1,0:T(8,128)(2,1)S(1)}, u32[]{:S(2)}, u32[]{:S(2)}) collective-permute-start(bf16[128,384]{1,0:T(8,128)(2,1)} %get-tuple-element.38), channel_id=1, source_target_pairs={{128,0},{129,1},{130,2},{131,3},{132,4},{133,5},{134,6},{135,7},{1... | collective-permute-start | bytes 294920 | tf_op jit(solution)/shard_map/ppermute | solution.py:27
  101.9 5.2 %all-to-all-start.2 = ((bf16[8,960,128]{2,1,0:T(8,128)(2,1)}), bf16[8,960,128]{2,1,0:T(8,128)(2,1)}, u32[]{:S(2)}, u32[]{:S(2)}) async-start(bf16[8,960,128]{2,1,0:T(8,128)(2,1)} %copy-done.2), calls=%async_computation.2 | async-start | bytes 3932160 | tf_op jit(solution)/shard_map/all_to_all | solution.py:31
  107.1 2.6 %fusion.8 = f32[64,1536]{1,0:T(8,128)S(1)} fusion(bf16[1,1536,768]{2,1,0:T(8,128)(2,1)} %param.7, bf16[128,768]{1,0:T(8,128)(2,1)S(1)} %copy-done.14), kind=kOutput, calls=%fused_computation.8 | convolution fusion | flops 150994944 | bytes 2850816 | tf_op jit(solution)/shard_map/dot_general | solution.py:39
  110.6 2.5 %collective-permute-start.17 = (bf16[64,1536]{1,0:T(8,128)(2,1)S(1)}, bf16[64,1536]{1,0:T(8,128)(2,1)S(1)}, u32[]{:S(2)}, u32[]{:S(2)}) collective-permute-start(bf16[64,1536]{1,0:T(8,128)(2,1)S(1)} %fusion.30), channel_id=1, source_target_pairs={{128,0},{129,1},{130,2},{131,3},{132,4},{133,5},{134,6},{135,7},{1... | collective-permute-start | bytes 589832 | tf_op jit(solution)/shard_map/ppermute | solution.py:27
  119.6 3.0 %collective-permute-done.19 = bf16[64,384]{1,0:T(8,128)(2,1)S(1)} collective-permute-done((bf16[64,384]{1,0:T(8,128)(2,1)S(1)}, bf16[64,384]{1,0:T(8,128)(2,1)S(1)}, u32[]{:S(2)}, u32[]{:S(2)}) %collective-permute-start.19) | collective-permute-done | bytes 49184 | tf_op jit(solution)/shard_map/ppermute | solution.py:23
  122.6 3.9 %collective-permute-start.23 = (bf16[64,384]{1,0:T(8,128)(2,1)S(1)}, bf16[64,384]{1,0:T(8,128)(2,1)S(1)}, u32[]{:S(2)}, u32[]{:S(2)}) collective-permute-start(bf16[64,384]{1,0:T(8,128)(2,1)S(1)} %add_convert_fusion), channel_id=1, source_target_pairs={{0,24},{8,0},{16,8},{24,16},{1,25},{9,1},{17,9},{25,17},{2,26},{10... | collective-permute-start | bytes 147464 | tf_op jit(solution)/shard_map/ppermute | solution.py:23
  127.6 2.3 %collective-permute-start.21 = (bf16[64,384]{1,0:T(8,128)(2,1)S(1)}, bf16[64,384]{1,0:T(8,128)(2,1)S(1)}, u32[]{:S(2)}, u32[]{:S(2)}) collective-permute-start(bf16[64,384]{1,0:T(8,128)(2,1)S(1)} %add_convert_fusion), channel_id=1, source_target_pairs={{0,8},{8,16},{16,24},{24,0},{1,9},{9,17},{17,25},{25,1},{2,10},{10... | collective-permute-start | bytes 147464 | tf_op jit(solution)/shard_map/ppermute | solution.py:23
  129.9 5.0 %collective-permute-done.22 = bf16[64,384]{1,0:T(8,128)(2,1)S(1)} collective-permute-done((bf16[64,384]{1,0:T(8,128)(2,1)S(1)}, bf16[64,384]{1,0:T(8,128)(2,1)S(1)}, u32[]{:S(2)}, u32[]{:S(2)}) %collective-permute-start.22) | collective-permute-done | bytes 49184 | tf_op jit(solution)/shard_map/ppermute | solution.py:23
  136.7 2.0 %collective-permute-start.26 = (bf16[64,384]{1,0:T(8,128)(2,1)S(1)}, bf16[64,384]{1,0:T(8,128)(2,1)S(1)}, u32[]{:S(2)}, u32[]{:S(2)}) collective-permute-start(bf16[64,384]{1,0:T(8,128)(2,1)S(1)} %fusion.86.refs_0_), channel_id=1, source_target_pairs={{0,32},{32,64},{64,96},{96,0},{1,33},{33,65},{65,97},{97,1},{2,34}... | collective-permute-start | bytes 147464 | tf_op jit(solution)/shard_map/ppermute | solution.py:23
  138.7 2.4 %collective-permute-start.25 = (bf16[64,384]{1,0:T(8,128)(2,1)S(1)}, bf16[64,384]{1,0:T(8,128)(2,1)S(1)}, u32[]{:S(2)}, u32[]{:S(2)}) collective-permute-start(bf16[64,384]{1,0:T(8,128)(2,1)S(1)} %fusion.86.refs_0_), channel_id=1, source_target_pairs={{0,64},{32,96},{64,0},{96,32},{1,65},{33,97},{65,1},{97,33},{2,66}... | collective-permute-start | bytes 147464 | tf_op jit(solution)/shard_map/ppermute | solution.py:23
  141.4 1.8 collective-permute-done.25.refs_2_
  144.8 2.5 %collective-permute-start.27 = (bf16[64,1536]{1,0:T(8,128)(2,1)S(1)}, bf16[64,1536]{1,0:T(8,128)(2,1)S(1)}, u32[]{:S(2)}, u32[]{:S(2)}) collective-permute-start(bf16[64,1536]{1,0:T(8,128)(2,1)S(1)} %assemble.3.own_ref), channel_id=1, source_target_pairs={{0,128},{128,0},{1,129},{129,1},{2,130},{130,2},{3,131},{131,3},{4... | collective-permute-start | bytes 589832 | tf_op jit(solution)/shard_map/ppermute | solution.py:23
  153.9 5.6 %all-to-all-start.3 = ((bf16[8,576,128]{2,1,0:T(8,128)(2,1)}), bf16[8,576,128]{2,1,0:T(8,128)(2,1)S(1)}, u32[]{:S(2)}, u32[]{:S(2)}) async-start(bf16[8,576,128]{2,1,0:T(8,128)(2,1)} %copy-done.3), calls=%async_computation.3 | async-start | bytes 2359296 | tf_op jit(solution)/shard_map/all_to_all | solution.py:31
  162.4 5.1 %shard_map.77 = (f32[3,192,384]{2,1,0:T(8,128)S(1)}, bf16[3,192,384]{2,1,0:T(8,128)(2,1)}) custom-call(s32[1]{0:T(128)} %bitcast.core_ref, bf16[8,960,128]{2,1,0:T(8,128)(2,1)} %all-to-all-done.2.refs_0_, bf16[8,1344,128]{2,1,0:T(8,128)(2,1)} %all-to-all-done.1.refs_0_.refs_1_, bf16[8,192,128]{2,1,0:T(8,128)(2,1)S(1)} %collective-permute-done.29.refs_2_), custom_call_target="tpu_custom_call" | custom-call | tf_op jit(solution)/shard_map/pallas_call | solution.py:216
  169.7 6.2 %all-to-all-done.3.refs_1_ = bf16[8,576,128]{2,1,0:T(8,128)(2,1)S(1)} async-done(((bf16[8,576,128]{2,1,0:T(8,128)(2,1)}), bf16[8,576,128]{2,1,0:T(8,128)(2,1)S(1)}, u32[]{:S(2)}, u32[]{:S(2)}) %all-to-all-start.3) | async-done | bytes 1179680 | tf_op jit(solution)/shard_map/all_to_all | solution.py:31
  176.9 4.0 %shard_map.76 = (f32[3,192,384]{2,1,0:T(8,128)S(1)}, bf16[3,192,384]{2,1,0:T(8,128)(2,1)S(1)}) custom-call(s32[1]{0:T(128)} %bitcast.core_ref, bf16[8,1344,128]{2,1,0:T(8,128)(2,1)} %all-to-all-done.1.refs_0_.refs_1_, bf16[8,576,128]{2,1,0:T(8,128)(2,1)S(1)} %all-to-all-done.3.refs_1_, bf16[8,192,128]{2,1,0:T(8,128)(2,1)S(1)} %copy-done.5), custom_call_target="tpu_custom_call" | custom-call | tf_op jit(solution)/shard_map/pallas_call | solution.py:216
  180.9 2.7 %collective-permute-start.30 = (bf16[3,192,384]{2,1,0:T(8,128)(2,1)S(1)}, bf16[3,192,384]{2,1,0:T(8,128)(2,1)S(1)}, u32[]{:S(2)}, u32[]{:S(2)}) collective-permute-start(bf16[3,192,384]{2,1,0:T(8,128)(2,1)S(1)} %get-tuple-element.20), channel_id=1, source_target_pairs={{128,0},{129,1},{130,2},{131,3},{132,4},{133,5},{134,6},{135,7},{1... | collective-permute-start | bytes 1327112 | tf_op jit(solution)/shard_map/ppermute | solution.py:27
  185.0 2.3 %finish.1 = (f32[192,768]{1,0:T(8,128)}, f32[192,768]{1,0:T(8,128)}, f32[192,768]{1,0:T(8,128)}) custom-call(s32[1]{0:T(128)} %bitcast.core_ref, f32[3,192,384]{2,1,0:T(8,128)S(1)} %get-tuple-element.17.own_0_ref, f32[3,192,384]{2,1,0:T(8,128)S(1)} %copy-done.7, bf16[3,192,384]{2,1,0:T(8,128)(2,1)S(1)} %collective-permute-done.30.got_0_ref, ...), custom_call_target="tpu_custom_call" | custom-call | tf_op jit(solution)/shard_map/finish/pallas_call | solution.py:248
  (111 shorter events, 52.7 us)
Async XLA Ops:
  29.4 7.4 %collective-permute-start.16 = (bf16[128,384]{1,0:T(8,128)(2,1)S(1)}, bf16[128,384]{1,0:T(8,128)(2,1)S(1)}, u32[]{:S(2)}, u32[]{:S(2)}) collective-permute-start(bf16[128,384]{1,0:T(8,128)(2,1)S(1)} %get-tuple-element.32), channel_id=1, source_target_pairs={{128,0},{129,1},{130,2},{131,3},{132,4},{133,5},{134,6},{135,7},{1... | collective-permute-start | bytes 294920 | tf_op jit(solution)/shard_map/ppermute | solution.py:27
  33.5 3.2 %collective-permute-start.14 = (bf16[128,384]{1,0:T(8,128)(2,1)S(1)}, bf16[128,384]{1,0:T(8,128)(2,1)S(1)}, u32[]{:S(2)}, u32[]{:S(2)}) collective-permute-start(bf16[128,384]{1,0:T(8,128)(2,1)S(1)} %get-tuple-element.36), channel_id=1, source_target_pairs={{0,128},{1,129},{2,130},{3,131},{4,132},{5,133},{6,134},{7,135},{8... | collective-permute-start | bytes 294920 | tf_op jit(solution)/shard_map/ppermute | solution.py:27
  35.4 3.2 %collective-permute-start.15 = (bf16[128,384]{1,0:T(8,128)(2,1)S(1)}, bf16[128,384]{1,0:T(8,128)(2,1)S(1)}, u32[]{:S(2)}, u32[]{:S(2)}) collective-permute-start(bf16[128,384]{1,0:T(8,128)(2,1)S(1)} %get-tuple-element.34), channel_id=1, source_target_pairs={{0,128},{1,129},{2,130},{3,131},{4,132},{5,133},{6,134},{7,135},{8... | collective-permute-start | bytes 294920 | tf_op jit(solution)/shard_map/ppermute | solution.py:27
  41.0 60.9 %all-to-all-start.1 = ((bf16[8,1344,128]{2,1,0:T(8,128)(2,1)}), bf16[8,1344,128]{2,1,0:T(8,128)(2,1)}, u32[]{:S(2)}, u32[]{:S(2)}) async-start(bf16[8,1344,128]{2,1,0:T(8,128)(2,1)} %copy-done.1), calls=%async_computation.1 | async-start | bytes 5505024 | tf_op jit(solution)/shard_map/all_to_all | solution.py:31
  48.5 3.5 %collective-permute-start.1 = (bf16[64,1536]{1,0:T(8,128)(2,1)}, bf16[64,1536]{1,0:T(8,128)(2,1)S(1)}, u32[]{:S(2)}, u32[]{:S(2)}) collective-permute-start(bf16[64,1536]{1,0:T(8,128)(2,1)} %fusion.39), channel_id=1, source_target_pairs={{0,128},{1,129},{2,130},{3,131},{4,132},{5,133},{6,134},{7,135},{8... | collective-permute-start | bytes 589832 | tf_op jit(solution)/shard_map/ppermute | solution.py:27
  50.1 30.1 %collective-permute-start = (bf16[1536,128]{0,1:T(8,128)(2,1)S(1)}, bf16[1536,128]{0,1:T(8,128)(2,1)}, u32[]{:S(2)}, u32[]{:S(2)}) collective-permute-start(bf16[1536,128]{0,1:T(8,128)(2,1)S(1)} %copy.13), channel_id=1, source_target_pairs={{0,128},{128,0},{1,129},{129,1},{2,130},{130,2},{3,131},{131,3},{4... | collective-permute-start | bytes 1179656 | tf_op jit(solution)/shard_map/ppermute | solution.py:23
  54.4 4.6 %collective-permute-start.2 = (bf16[64,384]{1,0:T(8,128)(2,1)S(1)}, bf16[64,384]{1,0:T(8,128)(2,1)S(1)}, u32[]{:S(2)}, u32[]{:S(2)}) collective-permute-start(bf16[64,384]{1,0:T(8,128)(2,1)S(1)} %get-tuple-element.42), channel_id=1, source_target_pairs={{0,32},{32,64},{64,96},{96,0},{1,33},{33,65},{65,97},{97,1},{2,34}... | collective-permute-start | bytes 147464 | tf_op jit(solution)/shard_map/ppermute | solution.py:23
  54.5 4.5 %collective-permute-start.4 = (bf16[64,384]{1,0:T(8,128)(2,1)S(1)}, bf16[64,384]{1,0:T(8,128)(2,1)S(1)}, u32[]{:S(2)}, u32[]{:S(2)}) collective-permute-start(bf16[64,384]{1,0:T(8,128)(2,1)S(1)} %get-tuple-element.43), channel_id=1, source_target_pairs={{0,96},{32,0},{64,32},{96,64},{1,97},{33,1},{65,33},{97,65},{2,98}... | collective-permute-start | bytes 147464 | tf_op jit(solution)/shard_map/ppermute | solution.py:23
  57.1 4.8 %collective-permute-start.3 = (bf16[64,384]{1,0:T(8,128)(2,1)S(1)}, bf16[64,384]{1,0:T(8,128)(2,1)S(1)}, u32[]{:S(2)}, u32[]{:S(2)}) collective-permute-start(bf16[64,384]{1,0:T(8,128)(2,1)S(1)} %get-tuple-element.44), channel_id=1, source_target_pairs={{0,64},{32,96},{64,0},{96,32},{1,65},{33,97},{65,1},{97,33},{2,66}... | collective-permute-start | bytes 147464 | tf_op jit(solution)/shard_map/ppermute | solution.py:23
  62.0 4.3 %collective-permute-start.7 = (bf16[64,384]{1,0:T(8,128)(2,1)S(1)}, bf16[64,384]{1,0:T(8,128)(2,1)S(1)}, u32[]{:S(2)}, u32[]{:S(2)}) collective-permute-start(bf16[64,384]{1,0:T(8,128)(2,1)S(1)} %add_convert_fusion.1), channel_id=1, source_target_pairs={{0,24},{8,0},{16,8},{24,16},{1,25},{9,1},{17,9},{25,17},{2,26},{10... | collective-permute-start | bytes 147464 | tf_op jit(solution)/shard_map/ppermute | solution.py:23
  62.3 15.8 %collective-permute-start.6 = (bf16[64,384]{1,0:T(8,128)(2,1)S(1)}, bf16[64,384]{1,0:T(8,128)(2,1)S(1)}, u32[]{:S(2)}, u32[]{:S(2)}) collective-permute-start(bf16[64,384]{1,0:T(8,128)(2,1)S(1)} %add_convert_fusion.1), channel_id=1, source_target_pairs={{0,16},{8,24},{16,0},{24,8},{1,17},{9,25},{17,1},{25,9},{2,18},{10... | collective-permute-start | bytes 147464 | tf_op jit(solution)/shard_map/ppermute | solution.py:23
  65.9 14.2 %collective-permute-start.5 = (bf16[64,384]{1,0:T(8,128)(2,1)S(1)}, bf16[64,384]{1,0:T(8,128)(2,1)S(1)}, u32[]{:S(2)}, u32[]{:S(2)}) collective-permute-start(bf16[64,384]{1,0:T(8,128)(2,1)S(1)} %add_convert_fusion.1), channel_id=1, source_target_pairs={{0,8},{8,16},{16,24},{24,0},{1,9},{9,17},{17,25},{25,1},{2,10},{10... | collective-permute-start | bytes 147464 | tf_op jit(solution)/shard_map/ppermute | solution.py:23
  81.0 4.2 %collective-permute-start.10 = (bf16[64,384]{1,0:T(8,128)(2,1)S(1)}, bf16[64,384]{1,0:T(8,128)(2,1)S(1)}, u32[]{:S(2)}, u32[]{:S(2)}) collective-permute-start(bf16[64,384]{1,0:T(8,128)(2,1)S(1)} %fusion.87.refs_0_), channel_id=1, source_target_pairs={{0,32},{32,64},{64,96},{96,0},{1,33},{33,65},{65,97},{97,1},{2,34}... | collective-permute-start | bytes 147464 | tf_op jit(solution)/shard_map/ppermute | solution.py:23
  81.6 4.5 %collective-permute-start.9 = (bf16[64,384]{1,0:T(8,128)(2,1)S(1)}, bf16[64,384]{1,0:T(8,128)(2,1)S(1)}, u32[]{:S(2)}, u32[]{:S(2)}) collective-permute-start(bf16[64,384]{1,0:T(8,128)(2,1)S(1)} %fusion.87.refs_0_), channel_id=1, source_target_pairs={{0,64},{32,96},{64,0},{96,32},{1,65},{33,97},{65,1},{97,33},{2,66}... | collective-permute-start | bytes 147464 | tf_op jit(solution)/shard_map/ppermute | solution.py:23
  86.4 4.0 %collective-permute-start.11 = (bf16[64,1536]{1,0:T(8,128)(2,1)S(1)}, bf16[64,1536]{1,0:T(8,128)(2,1)S(1)}, u32[]{:S(2)}, u32[]{:S(2)}) collective-permute-start(bf16[64,1536]{1,0:T(8,128)(2,1)S(1)} %assemble.2.own_ref), channel_id=1, source_target_pairs={{0,128},{128,0},{1,129},{129,1},{2,130},{130,2},{3,131},{131,3},{4... | collective-permute-start | bytes 589832 | tf_op jit(solution)/shard_map/ppermute | solution.py:23
  93.2 6.0 %collective-permute-start.13 = (bf16[128,384]{1,0:T(8,128)(2,1)}, bf16[128,384]{1,0:T(8,128)(2,1)S(1)}, u32[]{:S(2)}, u32[]{:S(2)}) collective-permute-start(bf16[128,384]{1,0:T(8,128)(2,1)} %get-tuple-element.38), channel_id=1, source_target_pairs={{128,0},{129,1},{130,2},{131,3},{132,4},{133,5},{134,6},{135,7},{1... | collective-permute-start | bytes 294920 | tf_op jit(solution)/shard_map/ppermute | solution.py:27
  101.9 52.0 %all-to-all-start.2 = ((bf16[8,960,128]{2,1,0:T(8,128)(2,1)}), bf16[8,960,128]{2,1,0:T(8,128)(2,1)}, u32[]{:S(2)}, u32[]{:S(2)}) async-start(bf16[8,960,128]{2,1,0:T(8,128)(2,1)} %copy-done.2), calls=%async_computation.2 | async-start | bytes 3932160 | tf_op jit(solution)/shard_map/all_to_all | solution.py:31
  110.6 3.6 %collective-permute-start.17 = (bf16[64,1536]{1,0:T(8,128)(2,1)S(1)}, bf16[64,1536]{1,0:T(8,128)(2,1)S(1)}, u32[]{:S(2)}, u32[]{:S(2)}) collective-permute-start(bf16[64,1536]{1,0:T(8,128)(2,1)S(1)} %fusion.30), channel_id=1, source_target_pairs={{128,0},{129,1},{130,2},{131,3},{132,4},{133,5},{134,6},{135,7},{1... | collective-permute-start | bytes 589832 | tf_op jit(solution)/shard_map/ppermute | solution.py:27
  115.0 4.6 %collective-permute-start.18 = (bf16[64,384]{1,0:T(8,128)(2,1)S(1)}, bf16[64,384]{1,0:T(8,128)(2,1)S(1)}, u32[]{:S(2)}, u32[]{:S(2)}) collective-permute-start(bf16[64,384]{1,0:T(8,128)(2,1)S(1)} %get-tuple-element.29), channel_id=1, source_target_pairs={{0,32},{32,64},{64,96},{96,0},{1,33},{33,65},{65,97},{97,1},{2,34}... | collective-permute-start | bytes 147464 | tf_op jit(solution)/shard_map/ppermute | solution.py:23
  116.3 3.3 %collective-permute-start.20 = (bf16[64,384]{1,0:T(8,128)(2,1)S(1)}, bf16[64,384]{1,0:T(8,128)(2,1)S(1)}, u32[]{:S(2)}, u32[]{:S(2)}) collective-permute-start(bf16[64,384]{1,0:T(8,128)(2,1)S(1)} %get-tuple-element.30), channel_id=1, source_target_pairs={{0,96},{32,0},{64,32},{96,64},{1,97},{33,1},{65,33},{97,65},{2,98}... | collective-permute-start | bytes 147464 | tf_op jit(solution)/shard_map/ppermute | solution.py:23
  117.8 4.8 %collective-permute-start.19 = (bf16[64,384]{1,0:T(8,128)(2,1)S(1)}, bf16[64,384]{1,0:T(8,128)(2,1)S(1)}, u32[]{:S(2)}, u32[]{:S(2)}) collective-permute-start(bf16[64,384]{1,0:T(8,128)(2,1)S(1)} %get-tuple-element.31), channel_id=1, source_target_pairs={{0,64},{32,96},{64,0},{96,32},{1,65},{33,97},{65,1},{97,33},{2,66}... | collective-permute-start | bytes 147464 | tf_op jit(solution)/shard_map/ppermute | solution.py:23
  122.6 7.2 %collective-permute-start.23 = (bf16[64,384]{1,0:T(8,128)(2,1)S(1)}, bf16[64,384]{1,0:T(8,128)(2,1)S(1)}, u32[]{:S(2)}, u32[]{:S(2)}) collective-permute-start(bf16[64,384]{1,0:T(8,128)(2,1)S(1)} %add_convert_fusion), channel_id=1, source_target_pairs={{0,24},{8,0},{16,8},{24,16},{1,25},{9,1},{17,9},{25,17},{2,26},{10... | collective-permute-start | bytes 147464 | tf_op jit(solution)/shard_map/ppermute | solution.py:23
  126.5 8.4 %collective-permute-start.22 = (bf16[64,384]{1,0:T(8,128)(2,1)S(1)}, bf16[64,384]{1,0:T(8,128)(2,1)S(1)}, u32[]{:S(2)}, u32[]{:S(2)}) collective-permute-start(bf16[64,384]{1,0:T(8,128)(2,1)S(1)} %add_convert_fusion), channel_id=1, source_target_pairs={{0,16},{8,24},{16,0},{24,8},{1,17},{9,25},{17,1},{25,9},{2,18},{10... | collective-permute-start | bytes 147464 | tf_op jit(solution)/shard_map/ppermute | solution.py:23
  127.6 8.2 %collective-permute-start.21 = (bf16[64,384]{1,0:T(8,128)(2,1)S(1)}, bf16[64,384]{1,0:T(8,128)(2,1)S(1)}, u32[]{:S(2)}, u32[]{:S(2)}) collective-permute-start(bf16[64,384]{1,0:T(8,128)(2,1)S(1)} %add_convert_fusion), channel_id=1, source_target_pairs={{0,8},{8,16},{16,24},{24,0},{1,9},{9,17},{17,25},{25,1},{2,10},{10... | collective-permute-start | bytes 147464 | tf_op jit(solution)/shard_map/ppermute | solution.py:23
  136.7 4.7 %collective-permute-start.26 = (bf16[64,384]{1,0:T(8,128)(2,1)S(1)}, bf16[64,384]{1,0:T(8,128)(2,1)S(1)}, u32[]{:S(2)}, u32[]{:S(2)}) collective-permute-start(bf16[64,384]{1,0:T(8,128)(2,1)S(1)} %fusion.86.refs_0_), channel_id=1, source_target_pairs={{0,32},{32,64},{64,96},{96,0},{1,33},{33,65},{65,97},{97,1},{2,34}... | collective-permute-start | bytes 147464 | tf_op jit(solution)/shard_map/ppermute | solution.py:23
  138.7 4.5 %collective-permute-start.25 = (bf16[64,384]{1,0:T(8,128)(2,1)S(1)}, bf16[64,384]{1,0:T(8,128)(2,1)S(1)}, u32[]{:S(2)}, u32[]{:S(2)}) collective-permute-start(bf16[64,384]{1,0:T(8,128)(2,1)S(1)} %fusion.86.refs_0_), channel_id=1, source_target_pairs={{0,64},{32,96},{64,0},{96,32},{1,65},{33,97},{65,1},{97,33},{2,66}... | collective-permute-start | bytes 147464 | tf_op jit(solution)/shard_map/ppermute | solution.py:23
  141.1 3.7 %collective-permute-start.24 = (bf16[64,384]{1,0:T(8,128)(2,1)S(1)}, bf16[64,384]{1,0:T(8,128)(2,1)S(1)}, u32[]{:S(2)}, u32[]{:S(2)}) collective-permute-start(bf16[64,384]{1,0:T(8,128)(2,1)S(1)} %fusion.86.refs_0_), channel_id=1, source_target_pairs={{0,96},{32,0},{64,32},{96,64},{1,97},{33,1},{65,33},{97,65},{2,98}... | collective-permute-start | bytes 147464 | tf_op jit(solution)/shard_map/ppermute | solution.py:23
  144.8 3.6 %collective-permute-start.27 = (bf16[64,1536]{1,0:T(8,128)(2,1)S(1)}, bf16[64,1536]{1,0:T(8,128)(2,1)S(1)}, u32[]{:S(2)}, u32[]{:S(2)}) collective-permute-start(bf16[64,1536]{1,0:T(8,128)(2,1)S(1)} %assemble.3.own_ref), channel_id=1, source_target_pairs={{0,128},{128,0},{1,129},{129,1},{2,130},{130,2},{3,131},{131,3},{4... | collective-permute-start | bytes 589832 | tf_op jit(solution)/shard_map/ppermute | solution.py:23
  149.3 3.2 %collective-permute-start.28 = (bf16[128,384]{1,0:T(8,128)(2,1)S(1)}, bf16[128,384]{1,0:T(8,128)(2,1)S(1)}, u32[]{:S(2)}, u32[]{:S(2)}) collective-permute-start(bf16[128,384]{1,0:T(8,128)(2,1)S(1)} %get-tuple-element.27), channel_id=1, source_target_pairs={{0,128},{1,129},{2,130},{3,131},{4,132},{5,133},{6,134},{7,135},{8... | collective-permute-start | bytes 294920 | tf_op jit(solution)/shard_map/ppermute | solution.py:27
  153.9 22.0 %all-to-all-start.3 = ((bf16[8,576,128]{2,1,0:T(8,128)(2,1)}), bf16[8,576,128]{2,1,0:T(8,128)(2,1)S(1)}, u32[]{:S(2)}, u32[]{:S(2)}) async-start(bf16[8,576,128]{2,1,0:T(8,128)(2,1)} %copy-done.3), calls=%async_computation.3 | async-start | bytes 2359296 | tf_op jit(solution)/shard_map/all_to_all | solution.py:31
  168.4 15.2 %collective-permute-start.31 = (bf16[3,192,384]{2,1,0:T(8,128)(2,1)}, bf16[3,192,384]{2,1,0:T(8,128)(2,1)}, u32[]{:S(2)}, u32[]{:S(2)}) collective-permute-start(bf16[3,192,384]{2,1,0:T(8,128)(2,1)} %get-tuple-element.21), channel_id=1, source_target_pairs={{0,128},{1,129},{2,130},{3,131},{4,132},{5,133},{6,134},{7,135},{8... | collective-permute-start | bytes 1327112 | tf_op jit(solution)/shard_map/ppermute | solution.py:27
  180.9 4.1 %collective-permute-start.30 = (bf16[3,192,384]{2,1,0:T(8,128)(2,1)S(1)}, bf16[3,192,384]{2,1,0:T(8,128)(2,1)S(1)}, u32[]{:S(2)}, u32[]{:S(2)}) collective-permute-start(bf16[3,192,384]{2,1,0:T(8,128)(2,1)S(1)} %get-tuple-element.20), channel_id=1, source_target_pairs={{128,0},{129,1},{130,2},{131,3},{132,4},{133,5},{134,6},{135,7},{1... | collective-permute-start | bytes 1327112 | tf_op jit(solution)/shard_map/ppermute | solution.py:27
  (19 other events, 186.9 us)

commit v3 on v2

--- a/solution.py
+++ b/solution.py
@@ -107,40 +107,68 @@
     )(core, own, other)
 
 
-def packed(choices, acts, core):
-    rows, half = choices[0][1].shape
+def picked(by_core, core):
+    rows, width = by_core[0][0][0].shape
+    half = width // CORES
+    count = max(len(picks) for picks in by_core)
+    values = []
+    for picks in by_core:
+        for value, _ in picks:
+            if not any(value is known for known in values):
+                values.append(value)
+
+    def body(core_ref, *refs):
+        out_ref = refs[-1]
+        for c, picks in enumerate(by_core):
+
+            @pl.when(core_ref[0] == c)
+            def _(picks=picks):
+                for slot in range(count):
+                    value, side = picks[min(slot, len(picks) - 1)]
+                    at = [value is known for known in values].index(True)
+                    out_ref[slot] = refs[at][:, side * half : (side + 1) * half]
+
+    return pl.pallas_call(
+        body,
+        in_specs=[whole(pltpu.SMEM)] + [whole()] * len(values),
+        out_specs=whole(),
+        out_shape=jax.ShapeDtypeStruct((count, rows, half), BF16),
+        compiler_params=limits(4),
+        name="picked",
+    )(core, *values)
+
+
+def packed(choices, given, acts, core):
+    rows, width = choices[0][0].shape
+    half = width // CORES
     tiles = half // LANES
     shard = acts.shape[0] // PEERS
     count = len(choices)
     height = count * tiles * rows + shard
 
     def body(core_ref, *refs):
-        acts_ref = refs[2 * count]
-        out_ref = refs[-1]
-        for c in range(count):
-            source = choices[c][0]
-
-            def fill(ref, c=c):
-                for t in range(tiles):
-                    base = (c * tiles + t) * rows
-                    out_ref[0, base : base + rows, :] = ref[:, t * LANES : (t + 1) * LANES]
-
-            pl.when(core_ref[0] == source)(lambda: fill(refs[2 * c]))
-            pl.when(core_ref[0] != source)(lambda: fill(refs[2 * c + 1]))
+        given_ref, acts_ref, out_ref = refs[count:]
+        for c, (_, source, slot) in enumerate(choices):
+            for t in range(tiles):
+                base = (c * tiles + t) * rows
+                first = source * half + t * LANES
+                own = refs[c][:, first : first + LANES]
+                other = given_ref[slot, :, t * LANES : (t + 1) * LANES]
+                out_ref[0, base : base + rows, :] = jnp.where(core_ref[0] == source, own, other)
         out_ref[0, count * tiles * rows :, :] = acts_ref[...]
 
-    values = [v for choice in choices for v in choice[1:]]
     return pl.pallas_call(
         body,
         grid=(PEERS,),
         in_specs=[whole(pltpu.SMEM)]
-        + [pl.BlockSpec((rows, half), lambda p: (0, 0))] * (2 * count)
+        + [pl.BlockSpec((rows, width), lambda p: (0, 0))] * count
+        + [pl.BlockSpec(given.shape, lambda p: (0, 0, 0))]
         + [pl.BlockSpec((shard, rows), lambda p: (p, 0))],
         out_specs=pl.BlockSpec((1, height, rows), lambda p: (p, 0, 0)),
-        out_shape=jax.ShapeDtypeStruct((PEERS, height, rows), BF16),
+        out_shape=pltpu.HBM((PEERS, height, rows), BF16),
         compiler_params=limits(8),
         name="packed",
-    )(core, *values, acts)
+    )(core, *[choice[0] for choice in choices], given, acts)
 
 
 def weight_grads(stored, d_hidden, acts, upstream, core):
@@ -255,9 +283,11 @@
     )(core, own_0, own_1, got_0, got_1)
 
 
-def crossing(sent, kept, residual, source, core, x, core_id, x_id):
-    received = one_way(sent.astype(BF16), source)
-    mine = jnp.where(core == source, kept.astype(BF16), received)
+def crossing(partial, residual, source, core, x, core_id, x_id):
+    split = partial.shape[0] // CORES
+    halves = [partial[:split], partial[split:]]
+    received = one_way(halves[1 - source], source)
+    mine = jnp.where(core == source, halves[source], received)
     width = mine.shape[1] // XS
     pieces = [
         shifted(columns_at(mine, (x + k) % XS, width), "x", k) for k in range(1, XS)
@@ -270,9 +300,7 @@
     total = summed.astype(F32)
     for piece in pieces:
         total = total + piece.astype(F32)
-    half_rows = lax.dynamic_slice(
-        residual, (core * sent.shape[0], x * width), (sent.shape[0], width)
-    )
+    half_rows = lax.dynamic_slice(residual, (core * split, x * width), (split, width))
     out = (half_rows.astype(F32) + total).astype(BF16)
     blocks = [out] + [shifted(out, "x", XS - k) for k in range(1, XS)]
     own = assemble(blocks, x_id)
@@ -292,10 +320,6 @@
     rows = tokens.shape[0]
     features, hidden = gate_w.shape
     half = hidden // CORES
-    split = rows // CORES
-
-    def split_of(value):
-        return value[:, :half], value[:, half:]
 
     own = jnp.where(core == 0, tokens.T, cotangent.T)
     gathered = exchanged(jnp.broadcast_to(own, (XS * ZH, *own.shape)), TENSOR)
@@ -304,27 +328,20 @@
     gate_a = dot_tn(entered, gate_w).astype(BF16)
     up_a = dot_tn(entered, up_w).astype(BF16)
     hidden_a = hidden_of(gate_a, up_a)
-    sent = dot_nn(hidden_a[split:], down_w)
-    kept = dot_nn(hidden_a[:split], down_w)
+    partial_a = dot_nn(hidden_a, down_w).astype(BF16)
     swapped = shifted(entered, "segment", 1)
     tokens_t = jnp.where(core == 0, entered, swapped)
     cot_t = jnp.where(core == 0, swapped, entered)
-    middle = crossing(sent, kept, tokens_t.T, 0, core, x, core_id, x_id)
+    middle = crossing(partial_a, tokens_t.T, 0, core, x, core_id, x_id)
 
     d_hidden_a = lax.optimization_barrier(
         lax.dot_general(
             entered, down_w, (((0,), (1,)), ((), ())), preferred_element_type=F32
         ).astype(BF16)
     )
-    gate_l, gate_r = split_of(gate_a)
-    up_l, up_r = split_of(up_a)
-    grad_l, grad_r = split_of(d_hidden_a)
-    choices = [
-        (0, gate_l, one_way(gate_r, 0)),
-        (0, up_l, one_way(up_r, 0)),
-        (1, grad_r, one_way(grad_l, 1)),
-    ]
-    load = packed(choices, entered, core_id)
+    outgoing = picked([[(gate_a, 1), (up_a, 1)], [(d_hidden_a, 0)]], core_id)
+    given = shifted(outgoing, "segment", 1)
+    load = packed([(gate_a, 0, 0), (up_a, 0, 1), (d_hidden_a, 1, 0)], given, entered, core_id)
     wide = exchanged(load, DP)
 
     wide_a = wide
@@ -334,21 +351,20 @@
     gate_b = dot_nn(middle, gate_w).astype(BF16)
     up_b = dot_nn(middle, up_w).astype(BF16)
     d_gate_b, d_up_b = gate_grads(d_hidden_a.astype(F32), gate_b, up_b)
-    sent = dot_nt(d_gate_b[:split], gate_w) + dot_nt(d_up_b[:split], up_w)
-    kept = dot_nt(d_gate_b[split:], gate_w) + dot_nt(d_up_b[split:], up_w)
-    upstream = crossing(sent, kept, cot_t.T, 1, core, x, core_id, x_id)
-
-    gate_l, gate_r = split_of(gate_b)
-    up_l, up_r = split_of(up_b)
-    choices = [(1, gate_r, one_way(gate_l, 1)), (1, up_r, one_way(up_l, 1))]
-    load = packed(choices, middle.T, core_id)
+    partial_b = (dot_nt(d_gate_b, gate_w) + dot_nt(d_up_b, up_w)).astype(BF16)
+    upstream = crossing(partial_b, cot_t.T, 1, core, x, core_id, x_id)
+
+    picks = [(gate_b, 0), (up_b, 0)]
+    outgoing = picked([picks, picks], core_id)
+    given = one_way(outgoing, 1)
+    load = packed([(gate_b, 1, 0), (up_b, 1, 1)], given, middle.T, core_id)
     load, wide_a = lax.optimization_barrier((load, wide_a))
     wide_b = exchanged(load, DP)
 
     d_hidden_b = dot_nt(upstream, down_w).astype(BF16)
-    grad_l, grad_r = split_of(d_hidden_b)
-    choices = [(0, grad_l, one_way(grad_r, 0))]
-    load = packed(choices, upstream.T, core_id)
+    outgoing = d_hidden_b[:, half:][None]
+    given = one_way(outgoing, 0)
+    load = packed([(d_hidden_b, 0, 0)], given, upstream.T, core_id)
     load, wide_b = lax.optimization_barrier((load, wide_b))
     wide_c = exchanged(load, DP)
 

time: 188 us -> 185 us (0.984)
  Pallas kernels: 13.1 us -> 21.6 us
  matrix products: 16.6 us -> 9.54 us
  starting transfers between devices: 68 us -> 63.1 us
  local copies, waits for them, and re-layouts: 9.06 us -> 6.97 us
    ppermute x10 -> x6, starting transfers between devices: 19.6 us -> 11.4 us  [one_way(): return lax.ppermute(value, 'segment', [(source, 1 - source)])]
    pallas_call x3, Pallas kernels: 1.67 us -> 9.37 us  [packed(): pl.pallas_call(body, grid=(PEERS,), in_specs=[whole(pltpu.SMEM)] + [pl.Bl...]
    dot_general x4 -> x3, matrix products: 8.65 us -> 3.12 us  [dot_nn(): return jnp.dot(left, right, preferred_element_type=F32)]
    ppermute x22 -> x23, waiting for transfers between devices: 37.6 us -> 41.2 us  [shifted(): lax.ppermute(value, axis, [(i, (i + distance) % size) for i in range(size)])]
    dot_general x5 -> x3, matrix products: 6 us -> 2.65 us  [dot_nt(): lax.dot_general(left, right, (((1,), (1,)), ((), ())), preferred_element_...]
    ppermute x22 -> x23, starting transfers between devices: 32.9 us -> 36.1 us  [shifted(): lax.ppermute(value, axis, [(i, (i + distance) % size) for i in range(size)])]
    ppermute x10 -> x6, waiting for transfers between devices: 6.61 us -> 4.47 us  [one_way(): return lax.ppermute(value, 'segment', [(source, 1 - source)])]
    unnamed x32 -> x24, local copies, waits for them, and re-layouts: 5.91 us -> 4.49 us
  transfers between devices with their start and end apart: 35 -> 32, of which waited for: 25 -> 25; matrix products, arithmetic and copies ran while one was open for 11% -> 6% of each run, Pallas kernels for 5% -> 9%
where the time goes in v3:
time: 185 us; the launch traced here: 184 us
  starting transfers between devices  63.1 us (34%)
  waiting for transfers between devices  51.9 us (28%)
  blocking collectives  26.1 us (14%)
  Pallas kernels  21.6 us (12%)
  matrix products  9.54 us (5%)
  local copies, waits for them, and re-layouts  6.97 us (4%)
  other arithmetic  3.74 us (2%)
    ppermute x23, waiting for transfers between devices, shifted(): lax.ppermute(value, axis, [(i, (i + distance) % size) for i in range(size)])  41.2 us
    ppermute x23, starting transfers between devices, shifted(): lax.ppermute(value, axis, [(i, (i + distance) % size) for i in range(size)])  36.1 us
    all_to_all x1, blocking collectives, exchanged(): return lax.all_to_all(value, axes, 0, 0, tiled=True)  26.1 us
    all_to_all x3, starting transfers between devices, exchanged(): return lax.all_to_all(value, axes, 0, 0, tiled=True)  15.6 us
    ppermute x6, starting transfers between devices, one_way(): return lax.ppermute(value, 'segment', [(source, 1 - source)])  11.4 us
    pallas_call x3, Pallas kernels, packed(): pl.pallas_call(body, grid=(PEERS,), in_specs=[whole(pltpu.SMEM)] + [pl.Bl...  9.37 us
    pallas_call x2, Pallas kernels, weight_grads(): pl.pallas_call(body, grid=(PEERS // step,), in_specs=[whole(pltpu.SMEM)]...  9.04 us
    all_to_all x3, waiting for transfers between devices, exchanged(): return lax.all_to_all(value, axes, 0, 0, tiled=True)  6.18 us
  transfers between devices with their start and end apart: 32, of which 25 were waited for; matrix products, arithmetic and copies ran while one was open for 6% of the time, Pallas kernels for 9%

profile of v3, /device:TPU:1, one launch (start us, length us, event | category | flops | bytes accessed | tf_op | source)
XLA Modules:
  0.0 183.9 jit_solution(10424064841721070599)
XLA Ops:
  1.6 26.1 %all_to_all.20 = bf16[16,96,128]{2,1,0:T(8,128)(2,1)S(1)} all-to-all(bf16[16,96,128]{2,1,0:T(8,128)(2,1)S(1)} %broadcast_in_dim.23), channel_id=1, replica_groups=mesh['segment'=2,'x'=4,'zh'=4,'zl'=2,'y'=4] {'x','zh'}, dimensions={0} | all-to-all | bytes 786432 | tf_op jit(solution)/shard_map/all_to_all | solution.py:31
  27.7 2.3 %fusion.23.refs_1_ = bf16[128,768]{1,0:T(8,128)(2,1)S(1)} fusion(bf16[1536,128]{1,0:T(8,128)(2,1)S(1)} %bitcast.61, bf16[1,1536,768]{2,1,0:T(8,128)(2,1)} %param.7), kind=kOutput, calls=%fused_computation.21 | convolution fusion | flops 302088192 | bytes 2949120 | tf_op jit(solution)/shard_map/dot_general | solution.py:35
  31.6 2.3 %collective-permute-start.13 = (bf16[2,128,384]{2,1,0:T(8,128)(2,1)S(1)}, bf16[2,128,384]{2,1,0:T(8,128)(2,1)S(1)}, u32[]{:S(2)}, u32[]{:S(2)}) collective-permute-start(bf16[2,128,384]{2,1,0:T(8,128)(2,1)S(1)} %picked.3), channel_id=1, source_target_pairs={{0,128},{128,0},{1,129},{129,1},{2,130},{130,2},{3,131},{131,3},{4... | collective-permute-start | bytes 589832 | tf_op jit(solution)/shard_map/ppermute | solution.py:23
  34.9 3.4 %packed.4 = bf16[8,1344,128]{2,1,0:T(8,128)(2,1)} custom-call(s32[1]{0:T(128)} %bitcast.core_ref, bf16[128,768]{1,0:T(8,128)(2,1)S(1)} %fusion.17.refs_0_, bf16[128,768]{1,0:T(8,128)(2,1)S(1)} %fusion.23.refs_1_, bf16[128,768]{1,0:T(8,128)(2,1)S(1)} %fusion.29.refs_2_, bf16[2,128,384]{2,1,0:T(8,128)(2,1)S(1)} %collective-permute-done.13.refs_3_, ...), custom_call_target="tpu_custom_call" | custom-call | tf_op jit(solution)/shard_map/packed/pallas_call | solution.py:160
  38.3 4.7 %all-to-all-start.1 = ((bf16[8,1344,128]{2,1,0:T(8,128)(2,1)}), bf16[8,1344,128]{2,1,0:T(8,128)(2,1)}, u32[]{:S(2)}, u32[]{:S(2)}) async-start(bf16[8,1344,128]{2,1,0:T(8,128)(2,1)} %packed.4), calls=%async_computation.1 | async-start | bytes 5505024 | tf_op jit(solution)/shard_map/all_to_all | solution.py:31
  43.0 2.2 %convolution_convert_fusion = bf16[128,1536]{1,0:T(8,128)(2,1)S(1)} fusion(bf16[1,768,1536]{2,1,0:T(8,128)(2,1)} %param.8, bf16[128,768]{1,0:T(8,128)(2,1)S(1)} %fusion.23.refs_1_, bf16[128,768]{1,0:T(8,128)(2,1)S(1)} %fusion.17.refs_0_), kind=kOutput, calls=%fused_computation.2 | convolution fusion | flops 302972928 | bytes 3145728 | tf_op jit(solution)/shard_map/dot_general | solution.py:43
  47.5 1.8 %collective-permute-start = (bf16[1536,128]{0,1:T(8,128)(2,1)S(1)}, bf16[1536,128]{0,1:T(8,128)(2,1)}, u32[]{:S(2)}, u32[]{:S(2)}) collective-permute-start(bf16[1536,128]{0,1:T(8,128)(2,1)S(1)} %copy.13), channel_id=1, source_target_pairs={{0,128},{128,0},{1,129},{129,1},{2,130},{130,2},{3,131},{131,3},{4... | collective-permute-start | bytes 1179656 | tf_op jit(solution)/shard_map/ppermute | solution.py:23
  50.6 2.7 %collective-permute-start.4 = (bf16[64,384]{1,0:T(8,128)(2,1)S(1)}, bf16[64,384]{1,0:T(8,128)(2,1)S(1)}, u32[]{:S(2)}, u32[]{:S(2)}) collective-permute-start(bf16[64,384]{1,0:T(8,128)(2,1)S(1)} %get-tuple-element.29), channel_id=1, source_target_pairs={{0,96},{32,0},{64,32},{96,64},{1,97},{33,1},{65,33},{97,65},{2,98}... | collective-permute-start | bytes 147464 | tf_op jit(solution)/shard_map/ppermute | solution.py:23
  53.3 1.9 %collective-permute-done.2 = bf16[64,384]{1,0:T(8,128)(2,1)S(1)} collective-permute-done((bf16[64,384]{1,0:T(8,128)(2,1)S(1)}, bf16[64,384]{1,0:T(8,128)(2,1)S(1)}, u32[]{:S(2)}, u32[]{:S(2)}) %collective-permute-start.2) | collective-permute-done | bytes 49184 | tf_op jit(solution)/shard_map/ppermute | solution.py:23
  55.1 3.0 %collective-permute-done.3 = bf16[64,384]{1,0:T(8,128)(2,1)S(1)} collective-permute-done((bf16[64,384]{1,0:T(8,128)(2,1)S(1)}, bf16[64,384]{1,0:T(8,128)(2,1)S(1)}, u32[]{:S(2)}, u32[]{:S(2)}) %collective-permute-start.3) | collective-permute-done | bytes 49184 | tf_op jit(solution)/shard_map/ppermute | solution.py:23
  58.4 3.7 %collective-permute-start.6 = (bf16[64,384]{1,0:T(8,128)(2,1)S(1)}, bf16[64,384]{1,0:T(8,128)(2,1)S(1)}, u32[]{:S(2)}, u32[]{:S(2)}) collective-permute-start(bf16[64,384]{1,0:T(8,128)(2,1)S(1)} %add_convert_fusion.1), channel_id=1, source_target_pairs={{0,16},{8,24},{16,0},{24,8},{1,17},{9,25},{17,1},{25,9},{2,18},{10... | collective-permute-start | bytes 147464 | tf_op jit(solution)/shard_map/ppermute | solution.py:23
  62.4 12.8 %collective-permute-done.6 = bf16[64,384]{1,0:T(8,128)(2,1)S(1)} collective-permute-done((bf16[64,384]{1,0:T(8,128)(2,1)S(1)}, bf16[64,384]{1,0:T(8,128)(2,1)S(1)}, u32[]{:S(2)}, u32[]{:S(2)}) %collective-permute-start.6) | collective-permute-done | bytes 49184 | tf_op jit(solution)/shard_map/ppermute | solution.py:23
  75.2 2.1 %collective-permute-done.5 = bf16[64,384]{1,0:T(8,128)(2,1)S(1)} collective-permute-done((bf16[64,384]{1,0:T(8,128)(2,1)S(1)}, bf16[64,384]{1,0:T(8,128)(2,1)S(1)}, u32[]{:S(2)}, u32[]{:S(2)}) %collective-permute-start.5) | collective-permute-done | bytes 49184 | tf_op jit(solution)/shard_map/ppermute | solution.py:23
  83.6 3.1 %collective-permute-start.11 = (bf16[64,1536]{1,0:T(8,128)(2,1)S(1)}, bf16[64,1536]{1,0:T(8,128)(2,1)S(1)}, u32[]{:S(2)}, u32[]{:S(2)}) collective-permute-start(bf16[64,1536]{1,0:T(8,128)(2,1)S(1)} %assemble.2.own_ref), channel_id=1, source_target_pairs={{0,128},{128,0},{1,129},{129,1},{2,130},{130,2},{3,131},{131,3},{4... | collective-permute-start | bytes 589832 | tf_op jit(solution)/shard_map/ppermute | solution.py:23
  89.4 2.3 %collective-permute-start.12 = (bf16[2,128,384]{2,1,0:T(8,128)(2,1)}, bf16[2,128,384]{2,1,0:T(8,128)(2,1)S(1)}, u32[]{:S(2)}, u32[]{:S(2)}) collective-permute-start(bf16[2,128,384]{2,1,0:T(8,128)(2,1)} %picked.2), channel_id=1, source_target_pairs={{128,0},{129,1},{130,2},{131,3},{132,4},{133,5},{134,6},{135,7},{1... | collective-permute-start | bytes 589832 | tf_op jit(solution)/shard_map/ppermute | solution.py:27
  94.0 3.1 %packed.3 = bf16[8,960,128]{2,1,0:T(8,128)(2,1)} custom-call(s32[1]{0:T(128)} %bitcast.core_ref, bf16[128,768]{1,0:T(8,128)(2,1)S(1)} %fusion.20.refs_0_, bf16[128,768]{1,0:T(8,128)(2,1)S(1)} %fusion.26.refs_1_, bf16[2,128,384]{2,1,0:T(8,128)(2,1)S(1)} %collective-permute-done.12.refs_2_, bf16[1536,128]{1,0:T(8,128)(2,1)S(1)} %bitcast.66), custom_call_target="tpu_custom_call" | custom-call | tf_op jit(solution)/shard_map/packed/pallas_call | solution.py:160
  97.1 5.0 %all-to-all-start.2 = ((bf16[8,960,128]{2,1,0:T(8,128)(2,1)}), bf16[8,960,128]{2,1,0:T(8,128)(2,1)}, u32[]{:S(2)}, u32[]{:S(2)}) async-start(bf16[8,960,128]{2,1,0:T(8,128)(2,1)} %packed.3), calls=%async_computation.2 | async-start | bytes 3932160 | tf_op jit(solution)/shard_map/all_to_all | solution.py:31
  104.8 2.6 %collective-permute-start.14 = (bf16[64,1536]{1,0:T(8,128)(2,1)S(1)}, bf16[64,1536]{1,0:T(8,128)(2,1)S(1)}, u32[]{:S(2)}, u32[]{:S(2)}) collective-permute-start(bf16[64,1536]{1,0:T(8,128)(2,1)S(1)} %slice.27), channel_id=1, source_target_pairs={{128,0},{129,1},{130,2},{131,3},{132,4},{133,5},{134,6},{135,7},{1... | collective-permute-start | bytes 589832 | tf_op jit(solution)/shard_map/ppermute | solution.py:27
  113.1 3.0 %collective-permute-done.16 = bf16[64,384]{1,0:T(8,128)(2,1)S(1)} collective-permute-done((bf16[64,384]{1,0:T(8,128)(2,1)S(1)}, bf16[64,384]{1,0:T(8,128)(2,1)S(1)}, u32[]{:S(2)}, u32[]{:S(2)}) %collective-permute-start.16) | collective-permute-done | bytes 49184 | tf_op jit(solution)/shard_map/ppermute | solution.py:23
  116.1 3.9 %collective-permute-start.20 = (bf16[64,384]{1,0:T(8,128)(2,1)S(1)}, bf16[64,384]{1,0:T(8,128)(2,1)S(1)}, u32[]{:S(2)}, u32[]{:S(2)}) collective-permute-start(bf16[64,384]{1,0:T(8,128)(2,1)S(1)} %add_convert_fusion), channel_id=1, source_target_pairs={{0,24},{8,0},{16,8},{24,16},{1,25},{9,1},{17,9},{25,17},{2,26},{10... | collective-permute-start | bytes 147464 | tf_op jit(solution)/shard_map/ppermute | solution.py:23
  121.1 2.2 %collective-permute-start.18 = (bf16[64,384]{1,0:T(8,128)(2,1)S(1)}, bf16[64,384]{1,0:T(8,128)(2,1)S(1)}, u32[]{:S(2)}, u32[]{:S(2)}) collective-permute-start(bf16[64,384]{1,0:T(8,128)(2,1)S(1)} %add_convert_fusion), channel_id=1, source_target_pairs={{0,8},{8,16},{16,24},{24,0},{1,9},{9,17},{17,25},{25,1},{2,10},{10... | collective-permute-start | bytes 147464 | tf_op jit(solution)/shard_map/ppermute | solution.py:23
  123.3 6.7 %collective-permute-done.19 = bf16[64,384]{1,0:T(8,128)(2,1)S(1)} collective-permute-done((bf16[64,384]{1,0:T(8,128)(2,1)S(1)}, bf16[64,384]{1,0:T(8,128)(2,1)S(1)}, u32[]{:S(2)}, u32[]{:S(2)}) %collective-permute-start.19) | collective-permute-done | bytes 49184 | tf_op jit(solution)/shard_map/ppermute | solution.py:23
  133.3 2.1 %collective-permute-start.22 = (bf16[64,384]{1,0:T(8,128)(2,1)S(1)}, bf16[64,384]{1,0:T(8,128)(2,1)S(1)}, u32[]{:S(2)}, u32[]{:S(2)}) collective-permute-start(bf16[64,384]{1,0:T(8,128)(2,1)S(1)} %fusion.55.refs_0_), channel_id=1, source_target_pairs={{0,64},{32,96},{64,0},{96,32},{1,65},{33,97},{65,1},{97,33},{2,66}... | collective-permute-start | bytes 147464 | tf_op jit(solution)/shard_map/ppermute | solution.py:23
  138.7 3.6 %collective-permute-start.24 = (bf16[64,1536]{1,0:T(8,128)(2,1)S(1)}, bf16[64,1536]{1,0:T(8,128)(2,1)S(1)}, u32[]{:S(2)}, u32[]{:S(2)}) collective-permute-start(bf16[64,1536]{1,0:T(8,128)(2,1)S(1)} %assemble.3.own_ref), channel_id=1, source_target_pairs={{0,128},{128,0},{1,129},{129,1},{2,130},{130,2},{3,131},{131,3},{4... | collective-permute-start | bytes 589832 | tf_op jit(solution)/shard_map/ppermute | solution.py:23
  145.8 1.7 collective-permute-done.25.refs_1_
  147.5 2.9 %packed.5 = bf16[8,576,128]{2,1,0:T(8,128)(2,1)} custom-call(s32[1]{0:T(128)} %bitcast.core_ref, bf16[128,768]{1,0:T(8,128)(2,1)S(1)} %fusion.32.refs_0_, bf16[1,128,384]{2,1,0:T(8,128)(2,1)S(1)} %collective-permute-done.25.refs_1_, bf16[1536,128]{1,0:T(8,128)(2,1)S(1)} %bitcast.67), custom_call_target="tpu_custom_call" | custom-call | tf_op jit(solution)/shard_map/packed/pallas_call | solution.py:160
  150.3 5.8 %all-to-all-start.3 = ((bf16[8,576,128]{2,1,0:T(8,128)(2,1)}), bf16[8,576,128]{2,1,0:T(8,128)(2,1)S(1)}, u32[]{:S(2)}, u32[]{:S(2)}) async-start(bf16[8,576,128]{2,1,0:T(8,128)(2,1)} %packed.5), calls=%async_computation.3 | async-start | bytes 2359296 | tf_op jit(solution)/shard_map/all_to_all | solution.py:31
  159.1 5.1 %shard_map.77 = (f32[3,192,384]{2,1,0:T(8,128)S(1)}, bf16[3,192,384]{2,1,0:T(8,128)(2,1)}) custom-call(s32[1]{0:T(128)} %bitcast.core_ref, bf16[8,960,128]{2,1,0:T(8,128)(2,1)} %all-to-all-done.2.refs_0_, bf16[8,1344,128]{2,1,0:T(8,128)(2,1)} %all-to-all-done.1.refs_0_.refs_1_, bf16[8,192,128]{2,1,0:T(8,128)(2,1)S(1)} %collective-permute-done.26.refs_2_), custom_call_target="tpu_custom_call" | custom-call | tf_op jit(solution)/shard_map/pallas_call | solution.py:244
  166.3 6.2 %all-to-all-done.3.refs_1_ = bf16[8,576,128]{2,1,0:T(8,128)(2,1)S(1)} async-done(((bf16[8,576,128]{2,1,0:T(8,128)(2,1)}), bf16[8,576,128]{2,1,0:T(8,128)(2,1)S(1)}, u32[]{:S(2)}, u32[]{:S(2)}) %all-to-all-start.3) | async-done | bytes 1179680 | tf_op jit(solution)/shard_map/all_to_all | solution.py:31
  173.5 4.0 %shard_map.76 = (f32[3,192,384]{2,1,0:T(8,128)S(1)}, bf16[3,192,384]{2,1,0:T(8,128)(2,1)S(1)}) custom-call(s32[1]{0:T(128)} %bitcast.core_ref, bf16[8,1344,128]{2,1,0:T(8,128)(2,1)} %all-to-all-done.1.refs_0_.refs_1_, bf16[8,576,128]{2,1,0:T(8,128)(2,1)S(1)} %all-to-all-done.3.refs_1_, bf16[8,192,128]{2,1,0:T(8,128)(2,1)S(1)} %copy-done.3), custom_call_target="tpu_custom_call" | custom-call | tf_op jit(solution)/shard_map/pallas_call | solution.py:244
  177.5 2.7 %collective-permute-start.27 = (bf16[3,192,384]{2,1,0:T(8,128)(2,1)S(1)}, bf16[3,192,384]{2,1,0:T(8,128)(2,1)S(1)}, u32[]{:S(2)}, u32[]{:S(2)}) collective-permute-start(bf16[3,192,384]{2,1,0:T(8,128)(2,1)S(1)} %get-tuple-element.20), channel_id=1, source_target_pairs={{128,0},{129,1},{130,2},{131,3},{132,4},{133,5},{134,6},{135,7},{1... | collective-permute-start | bytes 1327112 | tf_op jit(solution)/shard_map/ppermute | solution.py:27
  181.6 2.3 %finish.1 = (f32[192,768]{1,0:T(8,128)}, f32[192,768]{1,0:T(8,128)}, f32[192,768]{1,0:T(8,128)}) custom-call(s32[1]{0:T(128)} %bitcast.core_ref, f32[3,192,384]{2,1,0:T(8,128)S(1)} %get-tuple-element.17.own_0_ref, f32[3,192,384]{2,1,0:T(8,128)S(1)} %copy-done.5, bf16[3,192,384]{2,1,0:T(8,128)(2,1)S(1)} %collective-permute-done.27.got_0_ref, ...), custom_call_target="tpu_custom_call" | custom-call | tf_op jit(solution)/shard_map/finish/pallas_call | solution.py:276
  (95 shorter events, 45.9 us)
Async XLA Ops:
  31.6 3.4 %collective-permute-start.13 = (bf16[2,128,384]{2,1,0:T(8,128)(2,1)S(1)}, bf16[2,128,384]{2,1,0:T(8,128)(2,1)S(1)}, u32[]{:S(2)}, u32[]{:S(2)}) collective-permute-start(bf16[2,128,384]{2,1,0:T(8,128)(2,1)S(1)} %picked.3), channel_id=1, source_target_pairs={{0,128},{128,0},{1,129},{129,1},{2,130},{130,2},{3,131},{131,3},{4... | collective-permute-start | bytes 589832 | tf_op jit(solution)/shard_map/ppermute | solution.py:23
  38.3 58.8 %all-to-all-start.1 = ((bf16[8,1344,128]{2,1,0:T(8,128)(2,1)}), bf16[8,1344,128]{2,1,0:T(8,128)(2,1)}, u32[]{:S(2)}, u32[]{:S(2)}) async-start(bf16[8,1344,128]{2,1,0:T(8,128)(2,1)} %packed.4), calls=%async_computation.1 | async-start | bytes 5505024 | tf_op jit(solution)/shard_map/all_to_all | solution.py:31
  45.9 3.5 %collective-permute-start.1 = (bf16[64,1536]{1,0:T(8,128)(2,1)S(1)}, bf16[64,1536]{1,0:T(8,128)(2,1)}, u32[]{:S(2)}, u32[]{:S(2)}) collective-permute-start(bf16[64,1536]{1,0:T(8,128)(2,1)S(1)} %slice.25), channel_id=1, source_target_pairs={{0,128},{1,129},{2,130},{3,131},{4,132},{5,133},{6,134},{7,135},{8... | collective-permute-start | bytes 589832 | tf_op jit(solution)/shard_map/ppermute | solution.py:27
  47.5 29.9 %collective-permute-start = (bf16[1536,128]{0,1:T(8,128)(2,1)S(1)}, bf16[1536,128]{0,1:T(8,128)(2,1)}, u32[]{:S(2)}, u32[]{:S(2)}) collective-permute-start(bf16[1536,128]{0,1:T(8,128)(2,1)S(1)} %copy.13), channel_id=1, source_target_pairs={{0,128},{128,0},{1,129},{129,1},{2,130},{130,2},{3,131},{131,3},{4... | collective-permute-start | bytes 1179656 | tf_op jit(solution)/shard_map/ppermute | solution.py:23
  50.5 4.6 %collective-permute-start.2 = (bf16[64,384]{1,0:T(8,128)(2,1)S(1)}, bf16[64,384]{1,0:T(8,128)(2,1)S(1)}, u32[]{:S(2)}, u32[]{:S(2)}) collective-permute-start(bf16[64,384]{1,0:T(8,128)(2,1)S(1)} %get-tuple-element.28), channel_id=1, source_target_pairs={{0,32},{32,64},{64,96},{96,0},{1,33},{33,65},{65,97},{97,1},{2,34}... | collective-permute-start | bytes 147464 | tf_op jit(solution)/shard_map/ppermute | solution.py:23
  50.6 4.6 %collective-permute-start.4 = (bf16[64,384]{1,0:T(8,128)(2,1)S(1)}, bf16[64,384]{1,0:T(8,128)(2,1)S(1)}, u32[]{:S(2)}, u32[]{:S(2)}) collective-permute-start(bf16[64,384]{1,0:T(8,128)(2,1)S(1)} %get-tuple-element.29), channel_id=1, source_target_pairs={{0,96},{32,0},{64,32},{96,64},{1,97},{33,1},{65,33},{97,65},{2,98}... | collective-permute-start | bytes 147464 | tf_op jit(solution)/shard_map/ppermute | solution.py:23
  53.3 4.8 %collective-permute-start.3 = (bf16[64,384]{1,0:T(8,128)(2,1)S(1)}, bf16[64,384]{1,0:T(8,128)(2,1)S(1)}, u32[]{:S(2)}, u32[]{:S(2)}) collective-permute-start(bf16[64,384]{1,0:T(8,128)(2,1)S(1)} %get-tuple-element.30), channel_id=1, source_target_pairs={{0,64},{32,96},{64,0},{96,32},{1,65},{33,97},{65,1},{97,33},{2,66}... | collective-permute-start | bytes 147464 | tf_op jit(solution)/shard_map/ppermute | solution.py:23
  58.1 4.3 %collective-permute-start.7 = (bf16[64,384]{1,0:T(8,128)(2,1)S(1)}, bf16[64,384]{1,0:T(8,128)(2,1)S(1)}, u32[]{:S(2)}, u32[]{:S(2)}) collective-permute-start(bf16[64,384]{1,0:T(8,128)(2,1)S(1)} %add_convert_fusion.1), channel_id=1, source_target_pairs={{0,24},{8,0},{16,8},{24,16},{1,25},{9,1},{17,9},{25,17},{2,26},{10... | collective-permute-start | bytes 147464 | tf_op jit(solution)/shard_map/ppermute | solution.py:23
  58.4 16.8 %collective-permute-start.6 = (bf16[64,384]{1,0:T(8,128)(2,1)S(1)}, bf16[64,384]{1,0:T(8,128)(2,1)S(1)}, u32[]{:S(2)}, u32[]{:S(2)}) collective-permute-start(bf16[64,384]{1,0:T(8,128)(2,1)S(1)} %add_convert_fusion.1), channel_id=1, source_target_pairs={{0,16},{8,24},{16,0},{24,8},{1,17},{9,25},{17,1},{25,9},{2,18},{10... | collective-permute-start | bytes 147464 | tf_op jit(solution)/shard_map/ppermute | solution.py:23
  62.1 15.3 %collective-permute-start.5 = (bf16[64,384]{1,0:T(8,128)(2,1)S(1)}, bf16[64,384]{1,0:T(8,128)(2,1)S(1)}, u32[]{:S(2)}, u32[]{:S(2)}) collective-permute-start(bf16[64,384]{1,0:T(8,128)(2,1)S(1)} %add_convert_fusion.1), channel_id=1, source_target_pairs={{0,8},{8,16},{16,24},{24,0},{1,9},{9,17},{17,25},{25,1},{2,10},{10... | collective-permute-start | bytes 147464 | tf_op jit(solution)/shard_map/ppermute | solution.py:23
  78.2 4.2 %collective-permute-start.10 = (bf16[64,384]{1,0:T(8,128)(2,1)S(1)}, bf16[64,384]{1,0:T(8,128)(2,1)S(1)}, u32[]{:S(2)}, u32[]{:S(2)}) collective-permute-start(bf16[64,384]{1,0:T(8,128)(2,1)S(1)} %fusion.56.refs_0_), channel_id=1, source_target_pairs={{0,32},{32,64},{64,96},{96,0},{1,33},{33,65},{65,97},{97,1},{2,34}... | collective-permute-start | bytes 147464 | tf_op jit(solution)/shard_map/ppermute | solution.py:23
  78.7 4.4 %collective-permute-start.9 = (bf16[64,384]{1,0:T(8,128)(2,1)S(1)}, bf16[64,384]{1,0:T(8,128)(2,1)S(1)}, u32[]{:S(2)}, u32[]{:S(2)}) collective-permute-start(bf16[64,384]{1,0:T(8,128)(2,1)S(1)} %fusion.56.refs_0_), channel_id=1, source_target_pairs={{0,64},{32,96},{64,0},{96,32},{1,65},{33,97},{65,1},{97,33},{2,66}... | collective-permute-start | bytes 147464 | tf_op jit(solution)/shard_map/ppermute | solution.py:23
  80.4 3.2 %collective-permute-start.8 = (bf16[64,384]{1,0:T(8,128)(2,1)S(1)}, bf16[64,384]{1,0:T(8,128)(2,1)S(1)}, u32[]{:S(2)}, u32[]{:S(2)}) collective-permute-start(bf16[64,384]{1,0:T(8,128)(2,1)S(1)} %fusion.56.refs_0_), channel_id=1, source_target_pairs={{0,96},{32,0},{64,32},{96,64},{1,97},{33,1},{65,33},{97,65},{2,98}... | collective-permute-start | bytes 147464 | tf_op jit(solution)/shard_map/ppermute | solution.py:23
  83.6 4.2 %collective-permute-start.11 = (bf16[64,1536]{1,0:T(8,128)(2,1)S(1)}, bf16[64,1536]{1,0:T(8,128)(2,1)S(1)}, u32[]{:S(2)}, u32[]{:S(2)}) collective-permute-start(bf16[64,1536]{1,0:T(8,128)(2,1)S(1)} %assemble.2.own_ref), channel_id=1, source_target_pairs={{0,128},{128,0},{1,129},{129,1},{2,130},{130,2},{3,131},{131,3},{4... | collective-permute-start | bytes 589832 | tf_op jit(solution)/shard_map/ppermute | solution.py:23
  89.4 3.5 %collective-permute-start.12 = (bf16[2,128,384]{2,1,0:T(8,128)(2,1)}, bf16[2,128,384]{2,1,0:T(8,128)(2,1)S(1)}, u32[]{:S(2)}, u32[]{:S(2)}) collective-permute-start(bf16[2,128,384]{2,1,0:T(8,128)(2,1)} %picked.2), channel_id=1, source_target_pairs={{128,0},{129,1},{130,2},{131,3},{132,4},{133,5},{134,6},{135,7},{1... | collective-permute-start | bytes 589832 | tf_op jit(solution)/shard_map/ppermute | solution.py:27
  97.1 53.2 %all-to-all-start.2 = ((bf16[8,960,128]{2,1,0:T(8,128)(2,1)}), bf16[8,960,128]{2,1,0:T(8,128)(2,1)}, u32[]{:S(2)}, u32[]{:S(2)}) async-start(bf16[8,960,128]{2,1,0:T(8,128)(2,1)} %packed.3), calls=%async_computation.2 | async-start | bytes 3932160 | tf_op jit(solution)/shard_map/all_to_all | solution.py:31
  104.8 3.6 %collective-permute-start.14 = (bf16[64,1536]{1,0:T(8,128)(2,1)S(1)}, bf16[64,1536]{1,0:T(8,128)(2,1)S(1)}, u32[]{:S(2)}, u32[]{:S(2)}) collective-permute-start(bf16[64,1536]{1,0:T(8,128)(2,1)S(1)} %slice.27), channel_id=1, source_target_pairs={{128,0},{129,1},{130,2},{131,3},{132,4},{133,5},{134,6},{135,7},{1... | collective-permute-start | bytes 589832 | tf_op jit(solution)/shard_map/ppermute | solution.py:27
  108.4 4.6 %collective-permute-start.15 = (bf16[64,384]{1,0:T(8,128)(2,1)S(1)}, bf16[64,384]{1,0:T(8,128)(2,1)S(1)}, u32[]{:S(2)}, u32[]{:S(2)}) collective-permute-start(bf16[64,384]{1,0:T(8,128)(2,1)S(1)} %get-tuple-element.25), channel_id=1, source_target_pairs={{0,32},{32,64},{64,96},{96,0},{1,33},{33,65},{65,97},{97,1},{2,34}... | collective-permute-start | bytes 147464 | tf_op jit(solution)/shard_map/ppermute | solution.py:23
  109.7 3.3 %collective-permute-start.17 = (bf16[64,384]{1,0:T(8,128)(2,1)S(1)}, bf16[64,384]{1,0:T(8,128)(2,1)S(1)}, u32[]{:S(2)}, u32[]{:S(2)}) collective-permute-start(bf16[64,384]{1,0:T(8,128)(2,1)S(1)} %get-tuple-element.26), channel_id=1, source_target_pairs={{0,96},{32,0},{64,32},{96,64},{1,97},{33,1},{65,33},{97,65},{2,98}... | collective-permute-start | bytes 147464 | tf_op jit(solution)/shard_map/ppermute | solution.py:23
  111.2 4.8 %collective-permute-start.16 = (bf16[64,384]{1,0:T(8,128)(2,1)S(1)}, bf16[64,384]{1,0:T(8,128)(2,1)S(1)}, u32[]{:S(2)}, u32[]{:S(2)}) collective-permute-start(bf16[64,384]{1,0:T(8,128)(2,1)S(1)} %get-tuple-element.27), channel_id=1, source_target_pairs={{0,64},{32,96},{64,0},{96,32},{1,65},{33,97},{65,1},{97,33},{2,66}... | collective-permute-start | bytes 147464 | tf_op jit(solution)/shard_map/ppermute | solution.py:23
  116.1 7.2 %collective-permute-start.20 = (bf16[64,384]{1,0:T(8,128)(2,1)S(1)}, bf16[64,384]{1,0:T(8,128)(2,1)S(1)}, u32[]{:S(2)}, u32[]{:S(2)}) collective-permute-start(bf16[64,384]{1,0:T(8,128)(2,1)S(1)} %add_convert_fusion), channel_id=1, source_target_pairs={{0,24},{8,0},{16,8},{24,16},{1,25},{9,1},{17,9},{25,17},{2,26},{10... | collective-permute-start | bytes 147464 | tf_op jit(solution)/shard_map/ppermute | solution.py:23
  120.0 10.0 %collective-permute-start.19 = (bf16[64,384]{1,0:T(8,128)(2,1)S(1)}, bf16[64,384]{1,0:T(8,128)(2,1)S(1)}, u32[]{:S(2)}, u32[]{:S(2)}) collective-permute-start(bf16[64,384]{1,0:T(8,128)(2,1)S(1)} %add_convert_fusion), channel_id=1, source_target_pairs={{0,16},{8,24},{16,0},{24,8},{1,17},{9,25},{17,1},{25,9},{2,18},{10... | collective-permute-start | bytes 147464 | tf_op jit(solution)/shard_map/ppermute | solution.py:23
  121.1 10.4 %collective-permute-start.18 = (bf16[64,384]{1,0:T(8,128)(2,1)S(1)}, bf16[64,384]{1,0:T(8,128)(2,1)S(1)}, u32[]{:S(2)}, u32[]{:S(2)}) collective-permute-start(bf16[64,384]{1,0:T(8,128)(2,1)S(1)} %add_convert_fusion), channel_id=1, source_target_pairs={{0,8},{8,16},{16,24},{24,0},{1,9},{9,17},{17,25},{25,1},{2,10},{10... | collective-permute-start | bytes 147464 | tf_op jit(solution)/shard_map/ppermute | solution.py:23
  132.4 4.2 %collective-permute-start.23 = (bf16[64,384]{1,0:T(8,128)(2,1)S(1)}, bf16[64,384]{1,0:T(8,128)(2,1)S(1)}, u32[]{:S(2)}, u32[]{:S(2)}) collective-permute-start(bf16[64,384]{1,0:T(8,128)(2,1)S(1)} %fusion.55.refs_0_), channel_id=1, source_target_pairs={{0,32},{32,64},{64,96},{96,0},{1,33},{33,65},{65,97},{97,1},{2,34}... | collective-permute-start | bytes 147464 | tf_op jit(solution)/shard_map/ppermute | solution.py:23
  133.3 4.4 %collective-permute-start.22 = (bf16[64,384]{1,0:T(8,128)(2,1)S(1)}, bf16[64,384]{1,0:T(8,128)(2,1)S(1)}, u32[]{:S(2)}, u32[]{:S(2)}) collective-permute-start(bf16[64,384]{1,0:T(8,128)(2,1)S(1)} %fusion.55.refs_0_), channel_id=1, source_target_pairs={{0,64},{32,96},{64,0},{96,32},{1,65},{33,97},{65,1},{97,33},{2,66}... | collective-permute-start | bytes 147464 | tf_op jit(solution)/shard_map/ppermute | solution.py:23
  135.4 3.2 %collective-permute-start.21 = (bf16[64,384]{1,0:T(8,128)(2,1)S(1)}, bf16[64,384]{1,0:T(8,128)(2,1)S(1)}, u32[]{:S(2)}, u32[]{:S(2)}) collective-permute-start(bf16[64,384]{1,0:T(8,128)(2,1)S(1)} %fusion.55.refs_0_), channel_id=1, source_target_pairs={{0,96},{32,0},{64,32},{96,64},{1,97},{33,1},{65,33},{97,65},{2,98}... | collective-permute-start | bytes 147464 | tf_op jit(solution)/shard_map/ppermute | solution.py:23
  138.7 4.6 %collective-permute-start.24 = (bf16[64,1536]{1,0:T(8,128)(2,1)S(1)}, bf16[64,1536]{1,0:T(8,128)(2,1)S(1)}, u32[]{:S(2)}, u32[]{:S(2)}) collective-permute-start(bf16[64,1536]{1,0:T(8,128)(2,1)S(1)} %assemble.3.own_ref), channel_id=1, source_target_pairs={{0,128},{128,0},{1,129},{129,1},{2,130},{130,2},{3,131},{131,3},{4... | collective-permute-start | bytes 589832 | tf_op jit(solution)/shard_map/ppermute | solution.py:23
  144.3 3.2 %collective-permute-start.25 = (bf16[1,128,384]{2,1,0:T(8,128)(2,1)S(1)}, bf16[1,128,384]{2,1,0:T(8,128)(2,1)S(1)}, u32[]{:S(2)}, u32[]{:S(2)}) collective-permute-start(bf16[1,128,384]{2,1,0:T(8,128)(2,1)S(1)} %slice_bitcast_fusion), channel_id=1, source_target_pairs={{0,128},{1,129},{2,130},{3,131},{4,132},{5,133},{6,134},{7,135},{8... | collective-permute-start | bytes 294920 | tf_op jit(solution)/shard_map/ppermute | solution.py:27
  150.3 22.2 %all-to-all-start.3 = ((bf16[8,576,128]{2,1,0:T(8,128)(2,1)}), bf16[8,576,128]{2,1,0:T(8,128)(2,1)S(1)}, u32[]{:S(2)}, u32[]{:S(2)}) async-start(bf16[8,576,128]{2,1,0:T(8,128)(2,1)} %packed.5), calls=%async_computation.3 | async-start | bytes 2359296 | tf_op jit(solution)/shard_map/all_to_all | solution.py:31
  157.2 1.9 %collective-permute-start.26 = (bf16[8,192,128]{2,1,0:T(8,128)(2,1)S(1)}, bf16[8,192,128]{2,1,0:T(8,128)(2,1)S(1)}, u32[]{:S(2)}, u32[]{:S(2)}) collective-permute-start(bf16[8,192,128]{2,1,0:T(8,128)(2,1)S(1)} %slice.29), channel_id=1, source_target_pairs={{0,128},{128,0},{1,129},{129,1},{2,130},{130,2},{3,131},{131,3},{4... | collective-permute-start | bytes 1179656 | tf_op jit(solution)/shard_map/ppermute | solution.py:23
  165.1 15.2 %collective-permute-start.28 = (bf16[3,192,384]{2,1,0:T(8,128)(2,1)}, bf16[3,192,384]{2,1,0:T(8,128)(2,1)}, u32[]{:S(2)}, u32[]{:S(2)}) collective-permute-start(bf16[3,192,384]{2,1,0:T(8,128)(2,1)} %get-tuple-element.21), channel_id=1, source_target_pairs={{0,128},{1,129},{2,130},{3,131},{4,132},{5,133},{6,134},{7,135},{8... | collective-permute-start | bytes 1327112 | tf_op jit(solution)/shard_map/ppermute | solution.py:27
  177.5 4.1 %collective-permute-start.27 = (bf16[3,192,384]{2,1,0:T(8,128)(2,1)S(1)}, bf16[3,192,384]{2,1,0:T(8,128)(2,1)S(1)}, u32[]{:S(2)}, u32[]{:S(2)}) collective-permute-start(bf16[3,192,384]{2,1,0:T(8,128)(2,1)S(1)} %get-tuple-element.20), channel_id=1, source_target_pairs={{128,0},{129,1},{130,2},{131,3},{132,4},{133,5},{134,6},{135,7},{1... | collective-permute-start | bytes 1327112 | tf_op jit(solution)/shard_map/ppermute | solution.py:27
  (12 other events, 153.2 us)

commit v4 on v3

--- a/solution.py
+++ b/solution.py
@@ -23,6 +23,13 @@
     return lax.ppermute(value, axis, [(i, (i + distance) % size) for i in range(size)])
 
 
+def shifted_on(value, core, axis, distance):
+    size = lax.axis_size(axis)
+    first = core * size
+    pairs = [(first + i, first + (i + distance) % size) for i in range(size)]
+    return lax.ppermute(value, ("segment", axis), pairs)
+
+
 def one_way(value, source):
     return lax.ppermute(value, "segment", [(source, 1 - source)])
 
@@ -86,25 +93,6 @@
         compiler_params=limits(2),
         name="assemble",
     )(x, *blocks)
-
-
-def merge(own, other, core):
-    rows, width = own.shape
-
-    def body(core_ref, own_ref, other_ref, out_ref):
-        start = pl.multiple_of(core_ref[0] * rows, 16)
-        out_ref[pl.ds(start, rows), :] = own_ref[...]
-        start = pl.multiple_of((1 - core_ref[0]) * rows, 16)
-        out_ref[pl.ds(start, rows), :] = other_ref[...]
-
-    return pl.pallas_call(
-        body,
-        in_specs=[whole(pltpu.SMEM), whole(), whole()],
-        out_specs=whole(),
-        out_shape=jax.ShapeDtypeStruct((rows * CORES, width), BF16),
-        compiler_params=limits(2),
-        name="merge",
-    )(core, own, other)
 
 
 def picked(by_core, core):
@@ -139,36 +127,65 @@
 
 
 def packed(choices, given, acts, core):
-    rows, width = choices[0][0].shape
-    half = width // CORES
+    rows = choices[0][0].shape[0]
+    half = choices[0][0].shape[1] // (1 if given is None else CORES)
     tiles = half // LANES
-    shard = acts.shape[0] // PEERS
+    turned = isinstance(acts, tuple)
+    features = acts[0].shape[1] if turned else acts.shape[0]
+    shard = features // PEERS
     count = len(choices)
     height = count * tiles * rows + shard
+    values = [choice[0] for choice in choices]
+    specs = [pl.BlockSpec(value.shape, lambda p: (0, 0)) for value in values]
+    if given is not None:
+        values.append(given)
+        specs.append(pl.BlockSpec(given.shape, lambda p: (0, 0, 0)))
+    if turned:
+        values += acts[:2]
+        specs += [pl.BlockSpec(acts[0].shape, lambda p: (0, 0))] * 2
+    else:
+        values.append(acts)
+        specs.append(pl.BlockSpec((shard, rows), lambda p: (p, 0)))
 
     def body(core_ref, *refs):
-        given_ref, acts_ref, out_ref = refs[count:]
+        given_ref = None if given is None else refs[count]
+        out_ref = refs[len(values)]
+        peer = pl.program_id(0)
         for c, (_, source, slot) in enumerate(choices):
             for t in range(tiles):
                 base = (c * tiles + t) * rows
-                first = source * half + t * LANES
-                own = refs[c][:, first : first + LANES]
-                other = given_ref[slot, :, t * LANES : (t + 1) * LANES]
-                out_ref[0, base : base + rows, :] = jnp.where(core_ref[0] == source, own, other)
-        out_ref[0, count * tiles * rows :, :] = acts_ref[...]
+                first = (source or 0) * half + t * LANES
+                tile = refs[c][:, first : first + LANES]
+                if source is not None:
+                    other = given_ref[slot, :, t * LANES : (t + 1) * LANES]
+                    tile = jnp.where(core_ref[0] == source, tile, other)
+                out_ref[0, base : base + rows, :] = tile
+        if turned:
+            own_ref, received_ref = refs[len(values) - 2 : len(values)]
+            turned_ref = refs[-1]
+
+            @pl.when(peer == 0)
+            def _():
+                for t in range(features // LANES):
+                    at = slice(t * LANES, (t + 1) * LANES)
+                    tile = jnp.where(core_ref[0] == acts[2], own_ref[:, at], received_ref[:, at])
+                    turned_ref[at, :] = tile.T
+
+            start = pl.multiple_of(peer * shard, 64)
+            out_ref[0, count * tiles * rows :, :] = turned_ref[pl.ds(start, shard), :]
+        else:
+            out_ref[0, count * tiles * rows :, :] = refs[len(values) - 1][...]
 
     return pl.pallas_call(
         body,
         grid=(PEERS,),
-        in_specs=[whole(pltpu.SMEM)]
-        + [pl.BlockSpec((rows, width), lambda p: (0, 0))] * count
-        + [pl.BlockSpec(given.shape, lambda p: (0, 0, 0))]
-        + [pl.BlockSpec((shard, rows), lambda p: (p, 0))],
+        in_specs=[whole(pltpu.SMEM)] + specs,
         out_specs=pl.BlockSpec((1, height, rows), lambda p: (p, 0, 0)),
-        out_shape=pltpu.HBM((PEERS, height, rows), BF16),
+        out_shape=jax.ShapeDtypeStruct((PEERS, height, rows), BF16),
+        scratch_shapes=[pltpu.VMEM((features, rows), BF16)] if turned else [],
         compiler_params=limits(8),
         name="packed",
-    )(core, *[choice[0] for choice in choices], given, acts)
+    )(core, *values)
 
 
 def weight_grads(stored, d_hidden, acts, upstream, core):
@@ -283,29 +300,25 @@
     )(core, own_0, own_1, got_0, got_1)
 
 
-def crossing(partial, residual, source, core, x, core_id, x_id):
-    split = partial.shape[0] // CORES
-    halves = [partial[:split], partial[split:]]
-    received = one_way(halves[1 - source], source)
-    mine = jnp.where(core == source, halves[source], received)
-    width = mine.shape[1] // XS
+def crossing(partial, residual, source, x, x_id):
+    width = partial.shape[1] // XS
     pieces = [
-        shifted(columns_at(mine, (x + k) % XS, width), "x", k) for k in range(1, XS)
+        shifted_on(columns_at(partial, (x + k) % XS, width), source, "x", k)
+        for k in range(1, XS)
     ]
-    total = columns_at(mine, x, width).astype(F32)
+    total = columns_at(partial, x, width).astype(F32)
     for piece in pieces:
         total = total + piece.astype(F32)
     summed = total.astype(BF16)
-    pieces = [shifted(summed, "zh", k) for k in range(1, ZH)]
+    pieces = [shifted_on(summed, source, "zh", k) for k in range(1, ZH)]
     total = summed.astype(F32)
     for piece in pieces:
         total = total + piece.astype(F32)
-    half_rows = lax.dynamic_slice(residual, (core * split, x * width), (split, width))
-    out = (half_rows.astype(F32) + total).astype(BF16)
-    blocks = [out] + [shifted(out, "x", XS - k) for k in range(1, XS)]
+    out = (columns_at(residual, x, width).astype(F32) + total).astype(BF16)
+    blocks = [out] + [shifted_on(out, source, "x", XS - k) for k in range(1, XS)]
     own = assemble(blocks, x_id)
-    other = shifted(own, "segment", 1)
-    return merge(own, other, core_id)
+    received = one_way(own, source)
+    return own, received
 
 
 def local(tokens, w_gate, w_up, w_down, cotangent):
@@ -321,6 +334,8 @@
     features, hidden = gate_w.shape
     half = hidden // CORES
 
+    lent = one_way(down_w[half:], 0)
+    down_half = lax.optimization_barrier(jnp.where(core == 0, down_w[:half], lent))
     own = jnp.where(core == 0, tokens.T, cotangent.T)
     gathered = exchanged(jnp.broadcast_to(own, (XS * ZH, *own.shape)), TENSOR)
     entered = gathered.reshape(features, rows)
@@ -329,10 +344,8 @@
     up_a = dot_tn(entered, up_w).astype(BF16)
     hidden_a = hidden_of(gate_a, up_a)
     partial_a = dot_nn(hidden_a, down_w).astype(BF16)
-    swapped = shifted(entered, "segment", 1)
-    tokens_t = jnp.where(core == 0, entered, swapped)
-    cot_t = jnp.where(core == 0, swapped, entered)
-    middle = crossing(partial_a, tokens_t.T, 0, core, x, core_id, x_id)
+    residual = entered.T
+    middle_own, middle = crossing(partial_a, residual, 0, x, x_id)
 
     d_hidden_a = lax.optimization_barrier(
         lax.dot_general(
@@ -341,7 +354,9 @@
     )
     outgoing = picked([[(gate_a, 1), (up_a, 1)], [(d_hidden_a, 0)]], core_id)
     given = shifted(outgoing, "segment", 1)
-    load = packed([(gate_a, 0, 0), (up_a, 0, 1), (d_hidden_a, 1, 0)], given, entered, core_id)
+    load = packed(
+        [(gate_a, 0, 0), (up_a, 0, 1), (d_hidden_a, 1, 0)], given, entered, core_id
+    )
     wide = exchanged(load, DP)
 
     wide_a = wide
@@ -352,19 +367,18 @@
     up_b = dot_nn(middle, up_w).astype(BF16)
     d_gate_b, d_up_b = gate_grads(d_hidden_a.astype(F32), gate_b, up_b)
     partial_b = (dot_nt(d_gate_b, gate_w) + dot_nt(d_up_b, up_w)).astype(BF16)
-    upstream = crossing(partial_b, cot_t.T, 1, core, x, core_id, x_id)
+    up_own, up_received = crossing(partial_b, residual, 1, x, x_id)
+    upstream = jnp.where(core == 1, up_own, up_received)
 
     picks = [(gate_b, 0), (up_b, 0)]
     outgoing = picked([picks, picks], core_id)
     given = one_way(outgoing, 1)
-    load = packed([(gate_b, 1, 0), (up_b, 1, 1)], given, middle.T, core_id)
+    load = packed([(gate_b, 1, 0), (up_b, 1, 1)], given, (middle_own, middle, 0), core_id)
     load, wide_a = lax.optimization_barrier((load, wide_a))
     wide_b = exchanged(load, DP)
 
-    d_hidden_b = dot_nt(upstream, down_w).astype(BF16)
-    outgoing = d_hidden_b[:, half:][None]
-    given = one_way(outgoing, 0)
-    load = packed([(d_hidden_b, 0, 0)], given, upstream.T, core_id)
+    d_hidden_b = dot_nt(upstream, down_half).astype(BF16)
+    load = packed([(d_hidden_b, None, 0)], None, (up_own, up_received, 1), core_id)
     load, wide_b = lax.optimization_barrier((load, wide_b))
     wide_c = exchanged(load, DP)
 

time: 185 us -> 192 us (1.038)
  waiting for transfers between devices: 51.9 us -> 63.8 us
  Pallas kernels: 21.6 us -> 13.3 us
  local copies, waits for them, and re-layouts: 6.97 us -> 10.3 us
    ppermute x6, waiting for transfers between devices: 4.47 us -> 43.4 us  [one_way(): return lax.ppermute(value, 'segment', [(source, 1 - source)])]
    ppermute x23 -> x2, waiting for transfers between devices: 41.2 us -> 2.62 us  [shifted(): lax.ppermute(value, axis, [(i, (i + distance) % size) for i in range(size)])]
    ppermute x0 -> x18, starting transfers between devices: none -> 34.1 us  [shifted_on(): return lax.ppermute(value, ('segment', axis), pairs)]
    ppermute x23 -> x2, starting transfers between devices: 36.1 us -> 2.57 us  [shifted(): lax.ppermute(value, axis, [(i, (i + distance) % size) for i in range(size)])]
    ppermute x0 -> x18, waiting for transfers between devices: none -> 11.6 us  [shifted_on(): return lax.ppermute(value, ('segment', axis), pairs)]
    pallas_call x5 -> x3, Pallas kernels: 9.43 us -> 1.81 us  [packed(): pl.pallas_call(body, grid=(PEERS,), in_specs=[whole(pltpu.SMEM)] + specs,...]
    slice x2 -> x1, local copies, waits for them, and re-layouts: 0.03 us -> 2.42 us  [step(): lent = one_way(down_w[half:], 0)]
    unnamed x24 -> x25, local copies, waits for them, and re-layouts: 4.49 us -> 6.7 us
  transfers between devices with their start and end apart: 32 -> 29, of which waited for: 25 -> 12; matrix products, arithmetic and copies ran while one was open for 6% -> 6% of each run, Pallas kernels for 9% -> 5%
where the time goes in v4:
time: 192 us; the launch traced here: 190 us
  waiting for transfers between devices  63.8 us (33%)
  starting transfers between devices  62.7 us (33%)
  blocking collectives  26.1 us (14%)
  Pallas kernels  13.3 us (7%)
  local copies, waits for them, and re-layouts  10.3 us (5%)
  matrix products  9.18 us (5%)
  other arithmetic  3.82 us (2%)
    ppermute x6, waiting for transfers between devices, one_way(): return lax.ppermute(value, 'segment', [(source, 1 - source)])  43.4 us
    ppermute x18, starting transfers between devices, shifted_on(): return lax.ppermute(value, ('segment', axis), pairs)  34.1 us
    all_to_all x1, blocking collectives, exchanged(): return lax.all_to_all(value, axes, 0, 0, tiled=True)  26.1 us
    all_to_all x3, starting transfers between devices, exchanged(): return lax.all_to_all(value, axes, 0, 0, tiled=True)  15.9 us
    ppermute x18, waiting for transfers between devices, shifted_on(): return lax.ppermute(value, ('segment', axis), pairs)  11.6 us
    ppermute x6, starting transfers between devices, one_way(): return lax.ppermute(value, 'segment', [(source, 1 - source)])  10.1 us
    pallas_call x2, Pallas kernels, weight_grads(): pl.pallas_call(body, grid=(PEERS // step,), in_specs=[whole(pltpu.SMEM)]...  9.04 us
    unnamed x25, local copies, waits for them, and re-layouts  6.7 us
  transfers between devices with their start and end apart: 29, of which 12 were waited for; matrix products, arithmetic and copies ran while one was open for 6% of the time, Pallas kernels for 5%

profile of v4, /device:TPU:1, one launch (start us, length us, event | category | flops | bytes accessed | tf_op | source)
XLA Modules:
  0.0 190.5 jit_solution(11426390078283108853)
XLA Ops:
  1.6 26.1 %all_to_all.20 = bf16[16,96,128]{2,1,0:T(8,128)(2,1)S(1)} all-to-all(bf16[16,96,128]{2,1,0:T(8,128)(2,1)S(1)} %broadcast_in_dim.20), channel_id=1, replica_groups=mesh['segment'=2,'x'=4,'zh'=4,'zl'=2,'y'=4] {'x','zh'}, dimensions={0} | all-to-all | bytes 786432 | tf_op jit(solution)/shard_map/all_to_all | solution.py:38
  27.7 2.3 %fusion.21.refs_1_ = bf16[128,768]{1,0:T(8,128)(2,1)S(1)} fusion(bf16[1536,128]{1,0:T(8,128)(2,1)S(1)} %bitcast.56, bf16[1,1536,768]{2,1,0:T(8,128)(2,1)} %param.7), kind=kOutput, calls=%fused_computation.21 | convolution fusion | flops 302088192 | bytes 2949120 | tf_op jit(solution)/shard_map/dot_general | solution.py:42
  31.6 2.3 %collective-permute-start.11 = (bf16[2,128,384]{2,1,0:T(8,128)(2,1)S(1)}, bf16[2,128,384]{2,1,0:T(8,128)(2,1)S(1)}, u32[]{:S(2)}, u32[]{:S(2)}) collective-permute-start(bf16[2,128,384]{2,1,0:T(8,128)(2,1)S(1)} %picked.3), channel_id=1, source_target_pairs={{0,128},{128,0},{1,129},{129,1},{2,130},{130,2},{3,131},{131,3},{4... | collective-permute-start | bytes 589832 | tf_op jit(solution)/shard_map/ppermute | solution.py:23
  37.1 4.7 %all-to-all-start.1 = ((bf16[8,1344,128]{2,1,0:T(8,128)(2,1)}), bf16[8,1344,128]{2,1,0:T(8,128)(2,1)}, u32[]{:S(2)}, u32[]{:S(2)}) async-start(bf16[8,1344,128]{2,1,0:T(8,128)(2,1)} %copy-done.1), calls=%async_computation.1 | async-start | bytes 5505024 | tf_op jit(solution)/shard_map/all_to_all | solution.py:38
  41.8 2.2 %convolution_convert_fusion = bf16[128,1536]{1,0:T(8,128)(2,1)S(1)} fusion(bf16[1,768,1536]{2,1,0:T(8,128)(2,1)} %param.8, bf16[128,768]{1,0:T(8,128)(2,1)S(1)} %fusion.21.refs_1_, bf16[128,768]{1,0:T(8,128)(2,1)S(1)} %fusion.15.refs_0_), kind=kOutput, calls=%fused_computation.2 | convolution fusion | flops 302972928 | bytes 3145728 | tf_op jit(solution)/shard_map/dot_general | solution.py:50
  53.6 41.0 %collective-permute-done.9.refs_4_ = bf16[128,1536]{1,0:T(8,128)(2,1)S(1)} collective-permute-done((bf16[128,1536]{1,0:T(8,128)(2,1)S(1)}, bf16[128,1536]{1,0:T(8,128)(2,1)S(1)}, u32[]{:S(2)}, u32[]{:S(2)}) %collective-permute-start.9) | collective-permute-done | bytes 393248 | tf_op jit(solution)/shard_map/ppermute | solution.py:34
  95.7 2.1 %collective-permute-start.10 = (bf16[2,128,384]{2,1,0:T(8,128)(2,1)S(1)}, bf16[2,128,384]{2,1,0:T(8,128)(2,1)S(1)}, u32[]{:S(2)}, u32[]{:S(2)}) collective-permute-start(bf16[2,128,384]{2,1,0:T(8,128)(2,1)S(1)} %picked.2), channel_id=1, source_target_pairs={{128,0},{129,1},{130,2},{131,3},{132,4},{133,5},{134,6},{135,7},{1... | collective-permute-start | bytes 589832 | tf_op jit(solution)/shard_map/ppermute | solution.py:34
  100.8 5.1 %all-to-all-start.2 = ((bf16[8,960,128]{2,1,0:T(8,128)(2,1)}), bf16[8,960,128]{2,1,0:T(8,128)(2,1)}, u32[]{:S(2)}, u32[]{:S(2)}) async-start(bf16[8,960,128]{2,1,0:T(8,128)(2,1)} %copy-done.2), calls=%async_computation.2 | async-start | bytes 3932160 | tf_op jit(solution)/shard_map/all_to_all | solution.py:38
  105.9 2.4 %slice_bitcast_fusion = bf16[384,1536]{1,0:T(8,128)(2,1)} fusion(bf16[1,768,1536]{2,1,0:T(8,128)(2,1)} %param.8), kind=kLoop, calls=%fused_computation.18 | loop fusion | bytes 2359296 | tf_op jit(solution)/shard_map/slice | solution.py:337
  111.6 2.4 %collective-permute-start.14 = (bf16[128,384]{1,0:T(8,128)(2,1)S(1)}, bf16[128,384]{1,0:T(8,128)(2,1)S(1)}, u32[]{:S(2)}, u32[]{:S(2)}) collective-permute-start(bf16[128,384]{1,0:T(8,128)(2,1)S(1)} %get-tuple-element.26), channel_id=1, source_target_pairs={{128,224},{160,128},{192,160},{224,192},{129,225},{161,129},{193,1... | collective-permute-start | bytes 294920 | tf_op jit(solution)/shard_map/ppermute | solution.py:30
  114.0 2.6 %collective-permute-start.13 = (bf16[128,384]{1,0:T(8,128)(2,1)S(1)}, bf16[128,384]{1,0:T(8,128)(2,1)S(1)}, u32[]{:S(2)}, u32[]{:S(2)}) collective-permute-start(bf16[128,384]{1,0:T(8,128)(2,1)S(1)} %get-tuple-element.27), channel_id=1, source_target_pairs={{128,192},{160,224},{192,128},{224,160},{129,193},{161,225},{193,1... | collective-permute-start | bytes 294920 | tf_op jit(solution)/shard_map/ppermute | solution.py:30
  116.7 2.8 %collective-permute-start.12 = (bf16[128,384]{1,0:T(8,128)(2,1)S(1)}, bf16[128,384]{1,0:T(8,128)(2,1)S(1)}, u32[]{:S(2)}, u32[]{:S(2)}) collective-permute-start(bf16[128,384]{1,0:T(8,128)(2,1)S(1)} %get-tuple-element.25), channel_id=1, source_target_pairs={{128,160},{160,192},{192,224},{224,128},{129,161},{161,193},{193,2... | collective-permute-start | bytes 294920 | tf_op jit(solution)/shard_map/ppermute | solution.py:30
  119.4 1.9 collective-permute-done.13
  121.3 2.3 %collective-permute-done.12 = bf16[128,384]{1,0:T(8,128)(2,1)S(1)} collective-permute-done((bf16[128,384]{1,0:T(8,128)(2,1)S(1)}, bf16[128,384]{1,0:T(8,128)(2,1)S(1)}, u32[]{:S(2)}, u32[]{:S(2)}) %collective-permute-start.12) | collective-permute-done | bytes 98336 | tf_op jit(solution)/shard_map/ppermute | solution.py:30
  123.7 4.8 %collective-permute-start.17 = (bf16[128,384]{1,0:T(8,128)(2,1)S(1)}, bf16[128,384]{1,0:T(8,128)(2,1)S(1)}, u32[]{:S(2)}, u32[]{:S(2)}) collective-permute-start(bf16[128,384]{1,0:T(8,128)(2,1)S(1)} %add_convert_fusion), channel_id=1, source_target_pairs={{128,152},{136,128},{144,136},{152,144},{129,153},{137,129},{145,1... | collective-permute-start | bytes 294920 | tf_op jit(solution)/shard_map/ppermute | solution.py:30
  128.5 3.3 %collective-permute-start.16 = (bf16[128,384]{1,0:T(8,128)(2,1)S(1)}, bf16[128,384]{1,0:T(8,128)(2,1)S(1)}, u32[]{:S(2)}, u32[]{:S(2)}) collective-permute-start(bf16[128,384]{1,0:T(8,128)(2,1)S(1)} %add_convert_fusion), channel_id=1, source_target_pairs={{128,144},{136,152},{144,128},{152,136},{129,145},{137,153},{145,1... | collective-permute-start | bytes 294920 | tf_op jit(solution)/shard_map/ppermute | solution.py:30
  131.9 4.1 %collective-permute-start.15 = (bf16[128,384]{1,0:T(8,128)(2,1)S(1)}, bf16[128,384]{1,0:T(8,128)(2,1)S(1)}, u32[]{:S(2)}, u32[]{:S(2)}) collective-permute-start(bf16[128,384]{1,0:T(8,128)(2,1)S(1)} %add_convert_fusion), channel_id=1, source_target_pairs={{128,136},{136,144},{144,152},{152,128},{129,137},{137,145},{145,1... | collective-permute-start | bytes 294920 | tf_op jit(solution)/shard_map/ppermute | solution.py:30
  136.0 1.8 collective-permute-done.16
  137.8 1.6 collective-permute-done.15
  139.5 3.4 %collective-permute-start.18 = (bf16[128,384]{1,0:T(8,128)(2,1)S(1)}, bf16[128,384]{1,0:T(8,128)(2,1)S(1)}, u32[]{:S(2)}, u32[]{:S(2)}) collective-permute-start(bf16[128,384]{1,0:T(8,128)(2,1)S(1)} %fusion.50.refs_0_), channel_id=1, source_target_pairs={{128,224},{160,128},{192,160},{224,192},{129,225},{161,129},{193,1... | collective-permute-start | bytes 294920 | tf_op jit(solution)/shard_map/ppermute | solution.py:30
  142.9 1.9 %collective-permute-start.19 = (bf16[128,384]{1,0:T(8,128)(2,1)S(1)}, bf16[128,384]{1,0:T(8,128)(2,1)S(1)}, u32[]{:S(2)}, u32[]{:S(2)}) collective-permute-start(bf16[128,384]{1,0:T(8,128)(2,1)S(1)} %fusion.50.refs_0_), channel_id=1, source_target_pairs={{128,192},{160,224},{192,128},{224,160},{129,193},{161,225},{193,1... | collective-permute-start | bytes 294920 | tf_op jit(solution)/shard_map/ppermute | solution.py:30
  144.8 2.6 %collective-permute-start.20 = (bf16[128,384]{1,0:T(8,128)(2,1)S(1)}, bf16[128,384]{1,0:T(8,128)(2,1)S(1)}, u32[]{:S(2)}, u32[]{:S(2)}) collective-permute-start(bf16[128,384]{1,0:T(8,128)(2,1)S(1)} %fusion.50.refs_0_), channel_id=1, source_target_pairs={{128,160},{160,192},{192,224},{224,128},{129,161},{161,193},{193,2... | collective-permute-start | bytes 294920 | tf_op jit(solution)/shard_map/ppermute | solution.py:30
  147.5 2.3 %collective-permute-done.19.refs_2_ = bf16[128,384]{1,0:T(8,128)(2,1)S(1)} collective-permute-done((bf16[128,384]{1,0:T(8,128)(2,1)S(1)}, bf16[128,384]{1,0:T(8,128)(2,1)S(1)}, u32[]{:S(2)}, u32[]{:S(2)}) %collective-permute-start.19) | collective-permute-done | bytes 98336 | tf_op jit(solution)/shard_map/ppermute | solution.py:30
  149.7 1.6 collective-permute-done.20.refs_3_
  152.8 1.8 bitcast_select_fusion
  156.6 6.1 %all-to-all-start.3 = ((bf16[8,576,128]{2,1,0:T(8,128)(2,1)}), bf16[8,576,128]{2,1,0:T(8,128)(2,1)S(1)}, u32[]{:S(2)}, u32[]{:S(2)}) async-start(bf16[8,576,128]{2,1,0:T(8,128)(2,1)} %copy-done.3), calls=%async_computation.3 | async-start | bytes 2359296 | tf_op jit(solution)/shard_map/all_to_all | solution.py:38
  163.9 1.5 collective-permute-done.23.refs_2_
  165.5 5.1 %shard_map.77 = (f32[3,192,384]{2,1,0:T(8,128)S(1)}, bf16[3,192,384]{2,1,0:T(8,128)(2,1)}) custom-call(s32[1]{0:T(128)} %bitcast.core_ref, bf16[8,960,128]{2,1,0:T(8,128)(2,1)} %all-to-all-done.2.refs_0_, bf16[8,1344,128]{2,1,0:T(8,128)(2,1)} %all-to-all-done.1.refs_0_.refs_1_, bf16[8,192,128]{2,1,0:T(8,128)(2,1)S(1)} %collective-permute-done.23.refs_2_), custom_call_target="tpu_custom_call" | custom-call | tf_op jit(solution)/shard_map/pallas_call | solution.py:261
  172.8 6.2 %all-to-all-done.3.refs_1_ = bf16[8,576,128]{2,1,0:T(8,128)(2,1)S(1)} async-done(((bf16[8,576,128]{2,1,0:T(8,128)(2,1)}), bf16[8,576,128]{2,1,0:T(8,128)(2,1)S(1)}, u32[]{:S(2)}, u32[]{:S(2)}) %all-to-all-start.3) | async-done | bytes 1179680 | tf_op jit(solution)/shard_map/all_to_all | solution.py:38
  180.0 4.0 %shard_map.76 = (f32[3,192,384]{2,1,0:T(8,128)S(1)}, bf16[3,192,384]{2,1,0:T(8,128)(2,1)S(1)}) custom-call(s32[1]{0:T(128)} %bitcast.core_ref, bf16[8,1344,128]{2,1,0:T(8,128)(2,1)} %all-to-all-done.1.refs_0_.refs_1_, bf16[8,576,128]{2,1,0:T(8,128)(2,1)S(1)} %all-to-all-done.3.refs_1_, bf16[8,192,128]{2,1,0:T(8,128)(2,1)S(1)} %copy-done.5), custom_call_target="tpu_custom_call" | custom-call | tf_op jit(solution)/shard_map/pallas_call | solution.py:261
  184.0 2.7 %collective-permute-start.24 = (bf16[3,192,384]{2,1,0:T(8,128)(2,1)S(1)}, bf16[3,192,384]{2,1,0:T(8,128)(2,1)S(1)}, u32[]{:S(2)}, u32[]{:S(2)}) collective-permute-start(bf16[3,192,384]{2,1,0:T(8,128)(2,1)S(1)} %get-tuple-element.20), channel_id=1, source_target_pairs={{128,0},{129,1},{130,2},{131,3},{132,4},{133,5},{134,6},{135,7},{1... | collective-permute-start | bytes 1327112 | tf_op jit(solution)/shard_map/ppermute | solution.py:34
  188.1 2.3 %finish.1 = (f32[192,768]{1,0:T(8,128)}, f32[192,768]{1,0:T(8,128)}, f32[192,768]{1,0:T(8,128)}) custom-call(s32[1]{0:T(128)} %bitcast.core_ref, f32[3,192,384]{2,1,0:T(8,128)S(1)} %get-tuple-element.17.own_0_ref, f32[3,192,384]{2,1,0:T(8,128)S(1)} %copy-done.7, bf16[3,192,384]{2,1,0:T(8,128)(2,1)S(1)} %collective-permute-done.24.got_0_ref, ...), custom_call_target="tpu_custom_call" | custom-call | tf_op jit(solution)/shard_map/finish/pallas_call | solution.py:293
  (83 shorter events, 31.8 us)
Async XLA Ops:
  0.6 29.4 %copy-start = (bf16[1,1536,768]{2,1,0:T(8,128)(2,1)S(1)}, bf16[1,1536,768]{2,1,0:T(8,128)(2,1)}, u32[]{:S(2)}) copy-start(bf16[1,1536,768]{2,1,0:T(8,128)(2,1)} %param.6) | copy-start | bytes 7077892
  31.6 3.4 %collective-permute-start.11 = (bf16[2,128,384]{2,1,0:T(8,128)(2,1)S(1)}, bf16[2,128,384]{2,1,0:T(8,128)(2,1)S(1)}, u32[]{:S(2)}, u32[]{:S(2)}) collective-permute-start(bf16[2,128,384]{2,1,0:T(8,128)(2,1)S(1)} %picked.3), channel_id=1, source_target_pairs={{0,128},{128,0},{1,129},{129,1},{2,130},{130,2},{3,131},{131,3},{4... | collective-permute-start | bytes 589832 | tf_op jit(solution)/shard_map/ppermute | solution.py:23
  37.1 63.6 %all-to-all-start.1 = ((bf16[8,1344,128]{2,1,0:T(8,128)(2,1)}), bf16[8,1344,128]{2,1,0:T(8,128)(2,1)}, u32[]{:S(2)}, u32[]{:S(2)}) async-start(bf16[8,1344,128]{2,1,0:T(8,128)(2,1)} %copy-done.1), calls=%async_computation.1 | async-start | bytes 5505024 | tf_op jit(solution)/shard_map/all_to_all | solution.py:38
  44.8 2.0 %collective-permute-start.2 = (bf16[128,384]{1,0:T(8,128)(2,1)S(1)}, bf16[128,384]{1,0:T(8,128)(2,1)S(1)}, u32[]{:S(2)}, u32[]{:S(2)}) collective-permute-start(bf16[128,384]{1,0:T(8,128)(2,1)S(1)} %get-tuple-element.29), channel_id=1, source_target_pairs={{0,96},{32,0},{64,32},{96,64},{1,97},{33,1},{65,33},{97,65},{2,98}... | collective-permute-start | bytes 294920 | tf_op jit(solution)/shard_map/ppermute | solution.py:30
  45.5 1.4 collective-permute-start.1
  46.1 0.7 collective-permute-start
  47.8 2.2 %collective-permute-start.5 = (bf16[128,384]{1,0:T(8,128)(2,1)S(1)}, bf16[128,384]{1,0:T(8,128)(2,1)S(1)}, u32[]{:S(2)}, u32[]{:S(2)}) collective-permute-start(bf16[128,384]{1,0:T(8,128)(2,1)S(1)} %add_convert_fusion.1), channel_id=1, source_target_pairs={{0,24},{8,0},{16,8},{24,16},{1,25},{9,1},{17,9},{25,17},{2,26},{10... | collective-permute-start | bytes 294920 | tf_op jit(solution)/shard_map/ppermute | solution.py:30
  48.5 1.5 collective-permute-start.4
  49.1 0.9 collective-permute-start.3
  50.0 45.1 %copy-start.8 = (bf16[1,1536,768]{2,1,0:T(8,128)(2,1)S(1)}, bf16[1,1536,768]{2,1,0:T(8,128)(2,1)}, u32[]{:S(2)}) copy-start(bf16[1,1536,768]{2,1,0:T(8,128)(2,1)} %param.7) | copy-start | bytes 7077892
  50.1 2.2 %collective-permute-start.6 = (bf16[128,384]{1,0:T(8,128)(2,1)S(1)}, bf16[128,384]{1,0:T(8,128)(2,1)S(1)}, u32[]{:S(2)}, u32[]{:S(2)}) collective-permute-start(bf16[128,384]{1,0:T(8,128)(2,1)S(1)} %fusion.49.refs_0_), channel_id=1, source_target_pairs={{0,96},{32,0},{64,32},{96,64},{1,97},{33,1},{65,33},{97,65},{2,98}... | collective-permute-start | bytes 294920 | tf_op jit(solution)/shard_map/ppermute | solution.py:30
  50.9 1.4 collective-permute-start.7
  51.6 0.7 collective-permute-start.8
  52.3 42.3 %collective-permute-start.9 = (bf16[128,1536]{1,0:T(8,128)(2,1)S(1)}, bf16[128,1536]{1,0:T(8,128)(2,1)S(1)}, u32[]{:S(2)}, u32[]{:S(2)}) collective-permute-start(bf16[128,1536]{1,0:T(8,128)(2,1)S(1)} %assemble.2.refs_3_), channel_id=1, source_target_pairs={{0,128},{1,129},{2,130},{3,131},{4,132},{5,133},{6,134},{7,135},{8... | collective-permute-start | bytes 1179656 | tf_op jit(solution)/shard_map/ppermute | solution.py:34
  95.7 3.1 %collective-permute-start.10 = (bf16[2,128,384]{2,1,0:T(8,128)(2,1)S(1)}, bf16[2,128,384]{2,1,0:T(8,128)(2,1)S(1)}, u32[]{:S(2)}, u32[]{:S(2)}) collective-permute-start(bf16[2,128,384]{2,1,0:T(8,128)(2,1)S(1)} %picked.2), channel_id=1, source_target_pairs={{128,0},{129,1},{130,2},{131,3},{132,4},{133,5},{134,6},{135,7},{1... | collective-permute-start | bytes 589832 | tf_op jit(solution)/shard_map/ppermute | solution.py:34
  100.8 55.8 %all-to-all-start.2 = ((bf16[8,960,128]{2,1,0:T(8,128)(2,1)}), bf16[8,960,128]{2,1,0:T(8,128)(2,1)}, u32[]{:S(2)}, u32[]{:S(2)}) async-start(bf16[8,960,128]{2,1,0:T(8,128)(2,1)} %copy-done.2), calls=%async_computation.2 | async-start | bytes 3932160 | tf_op jit(solution)/shard_map/all_to_all | solution.py:38
  108.3 44.4 %collective-permute-start.22 = (bf16[384,1536]{1,0:T(8,128)(2,1)}, bf16[384,1536]{1,0:T(8,128)(2,1)}, u32[]{:S(2)}, u32[]{:S(2)}) collective-permute-start(bf16[384,1536]{1,0:T(8,128)(2,1)} %slice_bitcast_fusion), channel_id=1, source_target_pairs={{0,128},{1,129},{2,130},{3,131},{4,132},{5,133},{6,134},{7,135},{8... | collective-permute-start | bytes 3538952 | tf_op jit(solution)/shard_map/ppermute | solution.py:34
  111.6 7.8 %collective-permute-start.14 = (bf16[128,384]{1,0:T(8,128)(2,1)S(1)}, bf16[128,384]{1,0:T(8,128)(2,1)S(1)}, u32[]{:S(2)}, u32[]{:S(2)}) collective-permute-start(bf16[128,384]{1,0:T(8,128)(2,1)S(1)} %get-tuple-element.26), channel_id=1, source_target_pairs={{128,224},{160,128},{192,160},{224,192},{129,225},{161,129},{193,1... | collective-permute-start | bytes 294920 | tf_op jit(solution)/shard_map/ppermute | solution.py:30
  114.0 7.3 %collective-permute-start.13 = (bf16[128,384]{1,0:T(8,128)(2,1)S(1)}, bf16[128,384]{1,0:T(8,128)(2,1)S(1)}, u32[]{:S(2)}, u32[]{:S(2)}) collective-permute-start(bf16[128,384]{1,0:T(8,128)(2,1)S(1)} %get-tuple-element.27), channel_id=1, source_target_pairs={{128,192},{160,224},{192,128},{224,160},{129,193},{161,225},{193,1... | collective-permute-start | bytes 294920 | tf_op jit(solution)/shard_map/ppermute | solution.py:30
  116.7 7.0 %collective-permute-start.12 = (bf16[128,384]{1,0:T(8,128)(2,1)S(1)}, bf16[128,384]{1,0:T(8,128)(2,1)S(1)}, u32[]{:S(2)}, u32[]{:S(2)}) collective-permute-start(bf16[128,384]{1,0:T(8,128)(2,1)S(1)} %get-tuple-element.25), channel_id=1, source_target_pairs={{128,160},{160,192},{192,224},{224,128},{129,161},{161,193},{193,2... | collective-permute-start | bytes 294920 | tf_op jit(solution)/shard_map/ppermute | solution.py:30
  123.7 12.3 %collective-permute-start.17 = (bf16[128,384]{1,0:T(8,128)(2,1)S(1)}, bf16[128,384]{1,0:T(8,128)(2,1)S(1)}, u32[]{:S(2)}, u32[]{:S(2)}) collective-permute-start(bf16[128,384]{1,0:T(8,128)(2,1)S(1)} %add_convert_fusion), channel_id=1, source_target_pairs={{128,152},{136,128},{144,136},{152,144},{129,153},{137,129},{145,1... | collective-permute-start | bytes 294920 | tf_op jit(solution)/shard_map/ppermute | solution.py:30
  128.5 9.3 %collective-permute-start.16 = (bf16[128,384]{1,0:T(8,128)(2,1)S(1)}, bf16[128,384]{1,0:T(8,128)(2,1)S(1)}, u32[]{:S(2)}, u32[]{:S(2)}) collective-permute-start(bf16[128,384]{1,0:T(8,128)(2,1)S(1)} %add_convert_fusion), channel_id=1, source_target_pairs={{128,144},{136,152},{144,128},{152,136},{129,145},{137,153},{145,1... | collective-permute-start | bytes 294920 | tf_op jit(solution)/shard_map/ppermute | solution.py:30
  131.9 7.6 %collective-permute-start.15 = (bf16[128,384]{1,0:T(8,128)(2,1)S(1)}, bf16[128,384]{1,0:T(8,128)(2,1)S(1)}, u32[]{:S(2)}, u32[]{:S(2)}) collective-permute-start(bf16[128,384]{1,0:T(8,128)(2,1)S(1)} %add_convert_fusion), channel_id=1, source_target_pairs={{128,136},{136,144},{144,152},{152,128},{129,137},{137,145},{145,1... | collective-permute-start | bytes 294920 | tf_op jit(solution)/shard_map/ppermute | solution.py:30
  139.5 8.0 %collective-permute-start.18 = (bf16[128,384]{1,0:T(8,128)(2,1)S(1)}, bf16[128,384]{1,0:T(8,128)(2,1)S(1)}, u32[]{:S(2)}, u32[]{:S(2)}) collective-permute-start(bf16[128,384]{1,0:T(8,128)(2,1)S(1)} %fusion.50.refs_0_), channel_id=1, source_target_pairs={{128,224},{160,128},{192,160},{224,192},{129,225},{161,129},{193,1... | collective-permute-start | bytes 294920 | tf_op jit(solution)/shard_map/ppermute | solution.py:30
  142.9 6.9 %collective-permute-start.19 = (bf16[128,384]{1,0:T(8,128)(2,1)S(1)}, bf16[128,384]{1,0:T(8,128)(2,1)S(1)}, u32[]{:S(2)}, u32[]{:S(2)}) collective-permute-start(bf16[128,384]{1,0:T(8,128)(2,1)S(1)} %fusion.50.refs_0_), channel_id=1, source_target_pairs={{128,192},{160,224},{192,128},{224,160},{129,193},{161,225},{193,1... | collective-permute-start | bytes 294920 | tf_op jit(solution)/shard_map/ppermute | solution.py:30
  144.8 6.6 %collective-permute-start.20 = (bf16[128,384]{1,0:T(8,128)(2,1)S(1)}, bf16[128,384]{1,0:T(8,128)(2,1)S(1)}, u32[]{:S(2)}, u32[]{:S(2)}) collective-permute-start(bf16[128,384]{1,0:T(8,128)(2,1)S(1)} %fusion.50.refs_0_), channel_id=1, source_target_pairs={{128,160},{160,192},{192,224},{224,128},{129,161},{161,193},{193,2... | collective-permute-start | bytes 294920 | tf_op jit(solution)/shard_map/ppermute | solution.py:30
  151.4 3.1 %collective-permute-start.21 = (bf16[128,1536]{1,0:T(8,128)(2,1)S(1)}, bf16[128,1536]{1,0:T(8,128)(2,1)S(1)}, u32[]{:S(2)}, u32[]{:S(2)}) collective-permute-start(bf16[128,1536]{1,0:T(8,128)(2,1)S(1)} %assemble.3.refs_1_), channel_id=1, source_target_pairs={{128,0},{129,1},{130,2},{131,3},{132,4},{133,5},{134,6},{135,7},{1... | collective-permute-start | bytes 1179656 | tf_op jit(solution)/shard_map/ppermute | solution.py:34
  156.6 22.4 %all-to-all-start.3 = ((bf16[8,576,128]{2,1,0:T(8,128)(2,1)}), bf16[8,576,128]{2,1,0:T(8,128)(2,1)S(1)}, u32[]{:S(2)}, u32[]{:S(2)}) async-start(bf16[8,576,128]{2,1,0:T(8,128)(2,1)} %copy-done.3), calls=%async_computation.3 | async-start | bytes 2359296 | tf_op jit(solution)/shard_map/all_to_all | solution.py:38
  163.7 1.8 collective-permute-start.23
  171.5 15.2 %collective-permute-start.25 = (bf16[3,192,384]{2,1,0:T(8,128)(2,1)}, bf16[3,192,384]{2,1,0:T(8,128)(2,1)}, u32[]{:S(2)}, u32[]{:S(2)}) collective-permute-start(bf16[3,192,384]{2,1,0:T(8,128)(2,1)} %get-tuple-element.21), channel_id=1, source_target_pairs={{0,128},{1,129},{2,130},{3,131},{4,132},{5,133},{6,134},{7,135},{8... | collective-permute-start | bytes 1327112 | tf_op jit(solution)/shard_map/ppermute | solution.py:34
  180.0 8.1 %copy-start.7 = (f32[3,192,384]{2,1,0:T(8,128)S(1)}, f32[3,192,384]{2,1,0:T(8,128)}, u32[]{:S(2)}) copy-start(f32[3,192,384]{2,1,0:T(8,128)} %copy-done.6) | copy-start | bytes 2654212
  184.0 4.1 %collective-permute-start.24 = (bf16[3,192,384]{2,1,0:T(8,128)(2,1)S(1)}, bf16[3,192,384]{2,1,0:T(8,128)(2,1)S(1)}, u32[]{:S(2)}, u32[]{:S(2)}) collective-permute-start(bf16[3,192,384]{2,1,0:T(8,128)(2,1)S(1)} %get-tuple-element.20), channel_id=1, source_target_pairs={{128,0},{129,1},{130,2},{131,3},{132,4},{133,5},{134,6},{135,7},{1... | collective-permute-start | bytes 1327112 | tf_op jit(solution)/shard_map/ppermute | solution.py:34
  (9 other events, 16.8 us)

commit v5 on v4

--- a/solution.py
+++ b/solution.py
@@ -23,13 +23,6 @@
     return lax.ppermute(value, axis, [(i, (i + distance) % size) for i in range(size)])
 
 
-def shifted_on(value, core, axis, distance):
-    size = lax.axis_size(axis)
-    first = core * size
-    pairs = [(first + i, first + (i + distance) % size) for i in range(size)]
-    return lax.ppermute(value, ("segment", axis), pairs)
-
-
 def one_way(value, source):
     return lax.ppermute(value, "segment", [(source, 1 - source)])
 
@@ -93,6 +86,25 @@
         compiler_params=limits(2),
         name="assemble",
     )(x, *blocks)
+
+
+def merge(own, other, core):
+    rows, width = own.shape
+
+    def body(core_ref, own_ref, other_ref, out_ref):
+        start = pl.multiple_of(core_ref[0] * rows, 16)
+        out_ref[pl.ds(start, rows), :] = own_ref[...]
+        start = pl.multiple_of((1 - core_ref[0]) * rows, 16)
+        out_ref[pl.ds(start, rows), :] = other_ref[...]
+
+    return pl.pallas_call(
+        body,
+        in_specs=[whole(pltpu.SMEM), whole(), whole()],
+        out_specs=whole(),
+        out_shape=jax.ShapeDtypeStruct((rows * CORES, width), BF16),
+        compiler_params=limits(2),
+        name="merge",
+    )(core, own, other)
 
 
 def picked(by_core, core):
@@ -141,8 +153,8 @@
         values.append(given)
         specs.append(pl.BlockSpec(given.shape, lambda p: (0, 0, 0)))
     if turned:
-        values += acts[:2]
-        specs += [pl.BlockSpec(acts[0].shape, lambda p: (0, 0))] * 2
+        values.append(acts[0])
+        specs.append(pl.BlockSpec(acts[0].shape, lambda p: (0, 0)))
     else:
         values.append(acts)
         specs.append(pl.BlockSpec((shard, rows), lambda p: (p, 0)))
@@ -161,15 +173,14 @@
                     tile = jnp.where(core_ref[0] == source, tile, other)
                 out_ref[0, base : base + rows, :] = tile
         if turned:
-            own_ref, received_ref = refs[len(values) - 2 : len(values)]
+            acts_ref = refs[len(values) - 1]
             turned_ref = refs[-1]
 
             @pl.when(peer == 0)
             def _():
                 for t in range(features // LANES):
                     at = slice(t * LANES, (t + 1) * LANES)
-                    tile = jnp.where(core_ref[0] == acts[2], own_ref[:, at], received_ref[:, at])
-                    turned_ref[at, :] = tile.T
+                    turned_ref[at, :] = acts_ref[:, at].T
 
             start = pl.multiple_of(peer * shard, 64)
             out_ref[0, count * tiles * rows :, :] = turned_ref[pl.ds(start, shard), :]
@@ -273,15 +284,105 @@
     )(core, *arrays)
 
 
-def finish(own_0, own_1, got_0, got_1, core):
+def coefficients(stored, other, core):
+    peers, height, lanes = stored.shape
+    shard = other.shape[1]
+    half = 3 * lanes
+    base = height - shard
+
+    def body(core_ref, stored_ref, other_ref, first_ref, second_ref, hidden_ref, acts_ref):
+        for t in range(3):
+            at = slice(t * lanes, (t + 1) * lanes)
+            gate = stored_ref[0, t * lanes : (t + 1) * lanes, :].astype(F32)
+            up = stored_ref[0, half + t * lanes : half + (t + 1) * lanes, :].astype(F32)
+            sigma = jax.nn.sigmoid(gate)
+            silu = gate * sigma
+            first_ref[0, :, at] = (up * sigma * (1.0 + gate * (1.0 - sigma))).astype(BF16)
+            second_ref[0, :, at] = silu.astype(BF16)
+            hidden_ref[0, :, at] = (silu * up).astype(BF16)
+        acts_ref[0] = jnp.where(core_ref[0] == 0, stored_ref[0, base:, :], other_ref[0])
+
+    def block(rows, width):
+        return pl.BlockSpec((1, rows, width), lambda p: (p, 0, 0))
+
+    return pl.pallas_call(
+        body,
+        grid=(peers,),
+        in_specs=[whole(pltpu.SMEM), block(height, lanes), block(shard, lanes)],
+        out_specs=[block(lanes, half)] * 3 + [block(shard, lanes)],
+        out_shape=[
+            jax.ShapeDtypeStruct((peers, lanes, half), BF16),
+            jax.ShapeDtypeStruct((peers, lanes, half), BF16),
+            jax.ShapeDtypeStruct((peers, lanes, half), BF16),
+            jax.ShapeDtypeStruct((peers, shard, lanes), BF16),
+        ],
+        compiler_params=limits(8),
+        name="coefficients",
+    )(core, stored, other)
+
+
+def last_grads(first, second, hidden, acts, late):
+    peers, _, lanes = late.shape
+    shard = acts.shape[1]
+    half = 3 * lanes
+    step = 2
+
+    def body(first_ref, second_ref, hidden_ref, acts_ref, late_ref, out_ref, low_ref):
+        index = pl.program_id(0)
+
+        @pl.when(index == 0)
+        def _():
+            out_ref[...] = jnp.zeros_like(out_ref)
+
+        def pair(ref):
+            return jnp.concatenate([ref[r] for r in range(step)], axis=0)
+
+        def turned(ref, base):
+            return jnp.concatenate(
+                [ref[r, base : base + shard, :] for r in range(step)], axis=1
+            )
+
+        grad = jnp.concatenate(
+            [
+                jnp.concatenate(
+                    [late_ref[r, t * lanes : (t + 1) * lanes, :] for t in range(3)], axis=1
+                )
+                for r in range(step)
+            ],
+            axis=0,
+        ).astype(F32)
+        acts_t = turned(acts_ref, 0)
+        out_ref[0] += dot_nn(acts_t, (grad * pair(first_ref).astype(F32)).astype(BF16))
+        out_ref[1] += dot_nn(acts_t, (grad * pair(second_ref).astype(F32)).astype(BF16))
+        out_ref[2] += dot_nn(turned(late_ref, half), pair(hidden_ref))
+
+        @pl.when(index == peers // step - 1)
+        def _():
+            low_ref[...] = out_ref[...].astype(BF16)
+
+    shape = (3, shard, half)
+    return pl.pallas_call(
+        body,
+        grid=(peers // step,),
+        in_specs=[
+            pl.BlockSpec((step, *a.shape[1:]), lambda p: (p, 0, 0))
+            for a in (first, second, hidden, acts, late)
+        ],
+        out_specs=[pl.BlockSpec(shape, lambda p: (0, 0, 0))] * 2,
+        out_shape=[jax.ShapeDtypeStruct(shape, F32), jax.ShapeDtypeStruct(shape, BF16)],
+        compiler_params=limits(16),
+        name="last_grads",
+    )(*[pltpu.with_memory_space_constraint(a, pltpu.HBM) for a in (first, second, hidden, acts, late)])
+
+
+def early_out(own_0, own_1, got_1, core):
     count, shard, half = own_0.shape
 
-    def body(core_ref, own_0_ref, own_1_ref, got_0_ref, got_1_ref, *outs):
+    def body(core_ref, own_0_ref, own_1_ref, got_1_ref, *outs):
         @pl.when(core_ref[0] == 0)
         def _():
             for i in range(count):
                 outs[i][:, :half] = own_0_ref[i]
-                outs[i][:, half:] = got_0_ref[i].astype(F32)
 
         @pl.when(core_ref[0] != 0)
         def _():
@@ -292,33 +393,73 @@
     shape = jax.ShapeDtypeStruct((shard, half * CORES), F32)
     return pl.pallas_call(
         body,
-        in_specs=[whole(pltpu.SMEM)] + [whole()] * 4,
+        in_specs=[whole(pltpu.SMEM)] + [whole()] * 3,
         out_specs=[whole()] * count,
         out_shape=[shape] * count,
         compiler_params=limits(8),
-        name="finish",
-    )(core, own_0, own_1, got_0, got_1)
-
-
-def crossing(partial, residual, source, x, x_id):
+        name="early_out",
+    )(core, own_0, own_1, got_1)
+
+
+def late_out(outs, got_0, core):
+    count, shard, half = got_0.shape
+
+    def body(core_ref, got_ref, *refs):
+        wide_ref, sems = refs[-2:]
+        targets = refs[count : 2 * count]
+
+        @pl.when(core_ref[0] == 0)
+        def _():
+            copies = []
+            for i in range(count):
+                wide_ref[i] = got_ref[i].astype(F32)
+                copy = pltpu.make_async_copy(
+                    wide_ref.at[i], targets[i].at[:, half:], sems.at[i]
+                )
+                copy.start()
+                copies.append(copy)
+            for copy in copies:
+                copy.wait()
+
+    return pl.pallas_call(
+        body,
+        in_specs=[whole(pltpu.SMEM), whole()] + [whole(pl.ANY)] * count,
+        out_specs=[whole(pl.ANY)] * count,
+        out_shape=[jax.ShapeDtypeStruct(o.shape, o.dtype) for o in outs],
+        scratch_shapes=[
+            pltpu.VMEM((count, shard, half), F32),
+            pltpu.SemaphoreType.DMA((count,)),
+        ],
+        input_output_aliases={2 + i: i for i in range(count)},
+        compiler_params=limits(8),
+        name="late_out",
+    )(core, got_0, *outs)
+
+
+def crossing(partial, residual, source, core, x, core_id, x_id):
     width = partial.shape[1] // XS
+    split = partial.shape[0] // CORES
+    own = columns_at(partial, x, width)
     pieces = [
-        shifted_on(columns_at(partial, (x + k) % XS, width), source, "x", k)
-        for k in range(1, XS)
+        shifted(columns_at(partial, (x + k) % XS, width), "x", k) for k in range(1, XS)
     ]
-    total = columns_at(partial, x, width).astype(F32)
+
+    total = own.astype(F32)
     for piece in pieces:
         total = total + piece.astype(F32)
-    summed = total.astype(BF16)
-    pieces = [shifted_on(summed, source, "zh", k) for k in range(1, ZH)]
-    total = summed.astype(F32)
+    summed = lax.optimization_barrier(total.astype(BF16))
+    halves = [summed[:split], summed[split:]]
+    received = one_way(halves[1 - source], source)
+    mine = jnp.where(core == source, halves[source], received)
+    pieces = [shifted(mine, "zh", k) for k in range(1, ZH)]
+    total = mine.astype(F32)
     for piece in pieces:
         total = total + piece.astype(F32)
-    out = (columns_at(residual, x, width).astype(F32) + total).astype(BF16)
-    blocks = [out] + [shifted_on(out, source, "x", XS - k) for k in range(1, XS)]
-    own = assemble(blocks, x_id)
-    received = one_way(own, source)
-    return own, received
+    out = (residual.astype(F32) + total).astype(BF16)
+    blocks = [out] + [shifted(out, "x", XS - k) for k in range(1, XS)]
+    gathered = assemble(blocks, x_id)
+    other = shifted(gathered, "segment", 1)
+    return merge(gathered, other, core_id)
 
 
 def local(tokens, w_gate, w_up, w_down, cotangent):
@@ -344,8 +485,12 @@
     up_a = dot_tn(entered, up_w).astype(BF16)
     hidden_a = hidden_of(gate_a, up_a)
     partial_a = dot_nn(hidden_a, down_w).astype(BF16)
-    residual = entered.T
-    middle_own, middle = crossing(partial_a, residual, 0, x, x_id)
+    block = lax.dynamic_slice_in_dim(entered, x * (features // XS), features // XS, 0).T
+    first, second = block[: rows // CORES], block[rows // CORES :]
+    other = shifted(jnp.where(core == 0, second, first), "segment", 1)
+    residual_1 = jnp.where(core == 0, first, other)
+    residual_2 = jnp.where(core == 0, other, second)
+    middle = crossing(partial_a, residual_1, 0, core, x, core_id, x_id)
 
     d_hidden_a = lax.optimization_barrier(
         lax.dot_general(
@@ -367,18 +512,17 @@
     up_b = dot_nn(middle, up_w).astype(BF16)
     d_gate_b, d_up_b = gate_grads(d_hidden_a.astype(F32), gate_b, up_b)
     partial_b = (dot_nt(d_gate_b, gate_w) + dot_nt(d_up_b, up_w)).astype(BF16)
-    up_own, up_received = crossing(partial_b, residual, 1, x, x_id)
-    upstream = jnp.where(core == 1, up_own, up_received)
+    upstream = crossing(partial_b, residual_2, 1, core, x, core_id, x_id)
 
     picks = [(gate_b, 0), (up_b, 0)]
     outgoing = picked([picks, picks], core_id)
     given = one_way(outgoing, 1)
-    load = packed([(gate_b, 1, 0), (up_b, 1, 1)], given, (middle_own, middle, 0), core_id)
+    load = packed([(gate_b, 1, 0), (up_b, 1, 1)], given, (middle,), core_id)
     load, wide_a = lax.optimization_barrier((load, wide_a))
     wide_b = exchanged(load, DP)
 
     d_hidden_b = dot_nt(upstream, down_half).astype(BF16)
-    load = packed([(d_hidden_b, None, 0)], None, (up_own, up_received, 1), core_id)
+    load = packed([(d_hidden_b, None, 0)], None, (upstream,), core_id)
     load, wide_b = lax.optimization_barrier((load, wide_b))
     wide_c = exchanged(load, DP)
 
@@ -390,15 +534,11 @@
         core_id,
     )
     got_1 = one_way(low_1, 0)
-    own_0, low_0 = weight_grads(
-        (wide_a, 0),
-        (wide_c, 0),
-        ("pick", 0, wide_a, 3 * half, entered_other),
-        ("own", wide_c, half),
-        core_id,
-    )
+    first, second, hidden_0, tokens_all = coefficients(wide_a, entered_other, core_id)
+    own_0, low_0 = last_grads(first, second, hidden_0, tokens_all, wide_c)
     got_0 = one_way(low_0, 1)
-    grad_gate, grad_up, grad_down = finish(own_0, own_1, got_0, got_1, core_id)
+    outs = early_out(own_0, own_1, got_1, core_id)
+    grad_gate, grad_up, grad_down = late_out(outs, got_0, core_id)
     return (grad_gate[None], grad_up[None], grad_down.T[None])
 
 

time: 192 us -> 177 us (0.922)
  waiting for transfers between devices: 63.8 us -> 38.6 us
  Pallas kernels: 13.3 us -> 20.2 us
  starting transfers between devices: 62.7 us -> 66.2 us
    ppermute x6, waiting for transfers between devices: 43.4 us -> 2.49 us  [one_way(): return lax.ppermute(value, 'segment', [(source, 1 - source)])]
    ppermute x18 -> x0, starting transfers between devices: 34.1 us -> none  [shifted_on(): return lax.ppermute(value, ('segment', axis), pairs)]
    ppermute x2 -> x23, waiting for transfers between devices: 2.62 us -> 36.1 us  [shifted(): lax.ppermute(value, axis, [(i, (i + distance) % size) for i in range(size)])]
    ppermute x2 -> x23, starting transfers between devices: 2.57 us -> 35.7 us  [shifted(): lax.ppermute(value, axis, [(i, (i + distance) % size) for i in range(size)])]
    ppermute x18 -> x0, waiting for transfers between devices: 11.6 us -> none  [shifted_on(): return lax.ppermute(value, ('segment', axis), pairs)]
    pallas_call x1 -> x6, Pallas kernels: 2.33 us -> 10.8 us  [the longest x1 4.6 us: coefficients(): pl.pallas_call(body, grid=(peers,), in_specs=[whole(pltpu.SMEM), block(he...]
    all_to_all x3, waiting for transfers between devices: 6.24 us -> 0.01 us  [exchanged(): return lax.all_to_all(value, axes, 0, 0, tiled=True)]
    ppermute x6, starting transfers between devices: 10.1 us -> 15.1 us  [one_way(): return lax.ppermute(value, 'segment', [(source, 1 - source)])]
  transfers between devices with their start and end apart: 29 -> 32, of which waited for: 12 -> 20; matrix products, arithmetic and copies ran while one was open for 6% -> 7% of each run, Pallas kernels for 5% -> 11%
where the time goes in v5:
time: 177 us; the launch traced here: 176 us
  starting transfers between devices  66.2 us (37%)
  waiting for transfers between devices  38.6 us (22%)
  blocking collectives  26.1 us (15%)
  Pallas kernels  20.2 us (11%)
  local copies, waits for them, and re-layouts  10.8 us (6%)
  matrix products  9.18 us (5%)
  other arithmetic  3.79 us (2%)
    ppermute x23, waiting for transfers between devices, shifted(): lax.ppermute(value, axis, [(i, (i + distance) % size) for i in range(size)])  36.1 us
    ppermute x23, starting transfers between devices, shifted(): lax.ppermute(value, axis, [(i, (i + distance) % size) for i in range(size)])  35.7 us
    all_to_all x1, blocking collectives, exchanged(): return lax.all_to_all(value, axes, 0, 0, tiled=True)  26.1 us
    all_to_all x3, starting transfers between devices, exchanged(): return lax.all_to_all(value, axes, 0, 0, tiled=True)  15.4 us
    ppermute x6, starting transfers between devices, one_way(): return lax.ppermute(value, 'segment', [(source, 1 - source)])  15.1 us
    unnamed x23, local copies, waits for them, and re-layouts  6.47 us
    pallas_call x1, Pallas kernels, weight_grads(): pl.pallas_call(body, grid=(PEERS // step,), in_specs=[whole(pltpu.SMEM)]...  4.92 us
    pallas_call x1, Pallas kernels, coefficients(): pl.pallas_call(body, grid=(peers,), in_specs=[whole(pltpu.SMEM), block(he...  4.6 us
  transfers between devices with their start and end apart: 32, of which 20 were waited for; matrix products, arithmetic and copies ran while one was open for 7% of the time, Pallas kernels for 11%

profile of v5, /device:TPU:1, one launch (start us, length us, event | category | flops | bytes accessed | tf_op | source)
XLA Modules:
  0.0 176.1 jit_solution(18151348283897247658)
XLA Ops:
  1.6 26.1 %all_to_all.20 = bf16[16,96,128]{2,1,0:T(8,128)(2,1)S(1)} all-to-all(bf16[16,96,128]{2,1,0:T(8,128)(2,1)S(1)} %broadcast_in_dim.20), channel_id=1, replica_groups=mesh['segment'=2,'x'=4,'zh'=4,'zl'=2,'y'=4] {'x','zh'}, dimensions={0} | all-to-all | bytes 786432 | tf_op jit(solution)/shard_map/all_to_all | solution.py:31
  27.7 2.3 %fusion.21.refs_1_ = bf16[128,768]{1,0:T(8,128)(2,1)S(1)} fusion(bf16[1536,128]{1,0:T(8,128)(2,1)S(1)} %bitcast.51, bf16[1,1536,768]{2,1,0:T(8,128)(2,1)} %param.7), kind=kOutput, calls=%fused_computation.21 | convolution fusion | flops 302088192 | bytes 2949120 | tf_op jit(solution)/shard_map/dot_general | solution.py:35
  31.6 2.3 %collective-permute-start.13 = (bf16[2,128,384]{2,1,0:T(8,128)(2,1)S(1)}, bf16[2,128,384]{2,1,0:T(8,128)(2,1)S(1)}, u32[]{:S(2)}, u32[]{:S(2)}) collective-permute-start(bf16[2,128,384]{2,1,0:T(8,128)(2,1)S(1)} %picked.3), channel_id=1, source_target_pairs={{0,128},{128,0},{1,129},{129,1},{2,130},{130,2},{3,131},{131,3},{4... | collective-permute-start | bytes 589832 | tf_op jit(solution)/shard_map/ppermute | solution.py:23
  37.2 4.7 %all-to-all-start.1 = ((bf16[8,1344,128]{2,1,0:T(8,128)(2,1)}), bf16[8,1344,128]{2,1,0:T(8,128)(2,1)}, u32[]{:S(2)}, u32[]{:S(2)}) async-start(bf16[8,1344,128]{2,1,0:T(8,128)(2,1)} %copy-done.1), calls=%async_computation.1 | async-start | bytes 5505024 | tf_op jit(solution)/shard_map/all_to_all | solution.py:31
  41.9 2.2 %convolution_convert_fusion = bf16[128,1536]{1,0:T(8,128)(2,1)S(1)} fusion(bf16[1,768,1536]{2,1,0:T(8,128)(2,1)} %param.8, bf16[128,768]{1,0:T(8,128)(2,1)S(1)} %fusion.21.refs_1_, bf16[128,768]{1,0:T(8,128)(2,1)S(1)} %fusion.15.refs_0_), kind=kOutput, calls=%fused_computation.2 | convolution fusion | flops 302972928 | bytes 3145728 | tf_op jit(solution)/shard_map/dot_general | solution.py:43
  44.9 2.7 %collective-permute-start.3 = (bf16[128,384]{1,0:T(8,128)(2,1)}, bf16[128,384]{1,0:T(8,128)(2,1)S(1)}, u32[]{:S(2)}, u32[]{:S(2)}) collective-permute-start(bf16[128,384]{1,0:T(8,128)(2,1)} %get-tuple-element.43), channel_id=1, source_target_pairs={{0,96},{32,0},{64,32},{96,64},{1,97},{33,1},{65,33},{97,65},{2,98}... | collective-permute-start | bytes 294920 | tf_op jit(solution)/shard_map/ppermute | solution.py:23
  47.7 2.5 %collective-permute-done.1 = bf16[128,384]{1,0:T(8,128)(2,1)S(1)} collective-permute-done((bf16[128,384]{1,0:T(8,128)(2,1)}, bf16[128,384]{1,0:T(8,128)(2,1)S(1)}, u32[]{:S(2)}, u32[]{:S(2)}) %collective-permute-start.1) | collective-permute-done | bytes 98336 | tf_op jit(solution)/shard_map/ppermute | solution.py:23
  55.2 2.0 %collective-permute-start = (bf16[64,384]{1,0:T(8,128)(2,1)S(1)}, bf16[64,384]{1,0:T(8,128)(2,1)S(1)}, u32[]{:S(2)}, u32[]{:S(2)}) collective-permute-start(bf16[64,384]{1,0:T(8,128)(2,1)S(1)} %broadcast_select_fusion), channel_id=1, source_target_pairs={{0,128},{128,0},{1,129},{129,1},{2,130},{130,2},{3,131},{131,3},{4... | collective-permute-start | bytes 147464 | tf_op jit(solution)/shard_map/ppermute | solution.py:23
  58.1 3.7 %collective-permute-start.6 = (bf16[64,384]{1,0:T(8,128)(2,1)S(1)}, bf16[64,384]{1,0:T(8,128)(2,1)S(1)}, u32[]{:S(2)}, u32[]{:S(2)}) collective-permute-start(bf16[64,384]{1,0:T(8,128)(2,1)S(1)} %slice_select_fusion.1), channel_id=1, source_target_pairs={{0,16},{8,24},{16,0},{24,8},{1,17},{9,25},{17,1},{25,9},{2,18},{10... | collective-permute-start | bytes 147464 | tf_op jit(solution)/shard_map/ppermute | solution.py:23
  62.2 11.9 %collective-permute-done.6 = bf16[64,384]{1,0:T(8,128)(2,1)S(1)} collective-permute-done((bf16[64,384]{1,0:T(8,128)(2,1)S(1)}, bf16[64,384]{1,0:T(8,128)(2,1)S(1)}, u32[]{:S(2)}, u32[]{:S(2)}) %collective-permute-start.6) | collective-permute-done | bytes 49184 | tf_op jit(solution)/shard_map/ppermute | solution.py:23
  74.1 2.1 %collective-permute-done.5 = bf16[64,384]{1,0:T(8,128)(2,1)S(1)} collective-permute-done((bf16[64,384]{1,0:T(8,128)(2,1)S(1)}, bf16[64,384]{1,0:T(8,128)(2,1)S(1)}, u32[]{:S(2)}, u32[]{:S(2)}) %collective-permute-start.5) | collective-permute-done | bytes 49184 | tf_op jit(solution)/shard_map/ppermute | solution.py:23
  81.6 3.1 %collective-permute-start.11 = (bf16[64,1536]{1,0:T(8,128)(2,1)S(1)}, bf16[64,1536]{1,0:T(8,128)(2,1)S(1)}, u32[]{:S(2)}, u32[]{:S(2)}) collective-permute-start(bf16[64,1536]{1,0:T(8,128)(2,1)S(1)} %assemble.2.own_ref), channel_id=1, source_target_pairs={{0,128},{128,0},{1,129},{129,1},{2,130},{130,2},{3,131},{131,3},{4... | collective-permute-start | bytes 589832 | tf_op jit(solution)/shard_map/ppermute | solution.py:23
  86.8 2.3 %collective-permute-start.12 = (bf16[2,128,384]{2,1,0:T(8,128)(2,1)S(1)}, bf16[2,128,384]{2,1,0:T(8,128)(2,1)S(1)}, u32[]{:S(2)}, u32[]{:S(2)}) collective-permute-start(bf16[2,128,384]{2,1,0:T(8,128)(2,1)S(1)} %picked.2), channel_id=1, source_target_pairs={{128,0},{129,1},{130,2},{131,3},{132,4},{133,5},{134,6},{135,7},{1... | collective-permute-start | bytes 589832 | tf_op jit(solution)/shard_map/ppermute | solution.py:27
  92.2 5.0 %all-to-all-start.2 = ((bf16[8,960,128]{2,1,0:T(8,128)(2,1)}), bf16[8,960,128]{2,1,0:T(8,128)(2,1)}, u32[]{:S(2)}, u32[]{:S(2)}) async-start(bf16[8,960,128]{2,1,0:T(8,128)(2,1)} %copy-done.2), calls=%async_computation.2 | async-start | bytes 3932160 | tf_op jit(solution)/shard_map/all_to_all | solution.py:31
  97.2 2.4 %slice_bitcast_fusion = bf16[384,1536]{1,0:T(8,128)(2,1)} fusion(bf16[1,768,1536]{2,1,0:T(8,128)(2,1)} %param.8), kind=kLoop, calls=%fused_computation.18 | loop fusion | bytes 2359296 | tf_op jit(solution)/shard_map/slice | solution.py:478
  108.1 3.4 %collective-permute-done.16 = bf16[128,384]{1,0:T(8,128)(2,1)S(1)} collective-permute-done((bf16[128,384]{1,0:T(8,128)(2,1)S(1)}, bf16[128,384]{1,0:T(8,128)(2,1)S(1)}, u32[]{:S(2)}, u32[]{:S(2)}) %collective-permute-start.16) | collective-permute-done | bytes 98336 | tf_op jit(solution)/shard_map/ppermute | solution.py:23
  111.5 5.0 %collective-permute-start.18 = (bf16[64,384]{1,0:T(8,128)(2,1)S(1)}, bf16[64,384]{1,0:T(8,128)(2,1)S(1)}, u32[]{:S(2)}, u32[]{:S(2)}) collective-permute-start(bf16[64,384]{1,0:T(8,128)(2,1)S(1)} %slice.50), channel_id=1, source_target_pairs={{128,0},{129,1},{130,2},{131,3},{132,4},{133,5},{134,6},{135,7},{1... | collective-permute-start | bytes 147464 | tf_op jit(solution)/shard_map/ppermute | solution.py:27
  117.4 3.9 %collective-permute-start.21 = (bf16[64,384]{1,0:T(8,128)(2,1)S(1)}, bf16[64,384]{1,0:T(8,128)(2,1)S(1)}, u32[]{:S(2)}, u32[]{:S(2)}) collective-permute-start(bf16[64,384]{1,0:T(8,128)(2,1)S(1)} %slice_select_fusion), channel_id=1, source_target_pairs={{0,24},{8,0},{16,8},{24,16},{1,25},{9,1},{17,9},{25,17},{2,26},{10... | collective-permute-start | bytes 147464 | tf_op jit(solution)/shard_map/ppermute | solution.py:23
  122.4 2.2 %collective-permute-start.19 = (bf16[64,384]{1,0:T(8,128)(2,1)S(1)}, bf16[64,384]{1,0:T(8,128)(2,1)S(1)}, u32[]{:S(2)}, u32[]{:S(2)}) collective-permute-start(bf16[64,384]{1,0:T(8,128)(2,1)S(1)} %slice_select_fusion), channel_id=1, source_target_pairs={{0,8},{8,16},{16,24},{24,0},{1,9},{9,17},{17,25},{25,1},{2,10},{10... | collective-permute-start | bytes 147464 | tf_op jit(solution)/shard_map/ppermute | solution.py:23
  124.7 3.5 %collective-permute-done.20 = bf16[64,384]{1,0:T(8,128)(2,1)S(1)} collective-permute-done((bf16[64,384]{1,0:T(8,128)(2,1)S(1)}, bf16[64,384]{1,0:T(8,128)(2,1)S(1)}, u32[]{:S(2)}, u32[]{:S(2)}) %collective-permute-start.20) | collective-permute-done | bytes 49184 | tf_op jit(solution)/shard_map/ppermute | solution.py:23
  128.3 2.5 %collective-permute-start.23 = (bf16[64,384]{1,0:T(8,128)(2,1)S(1)}, bf16[64,384]{1,0:T(8,128)(2,1)S(1)}, u32[]{:S(2)}, u32[]{:S(2)}) collective-permute-start(bf16[64,384]{1,0:T(8,128)(2,1)S(1)} %add_convert_fusion.2.refs_0_), channel_id=1, source_target_pairs={{0,64},{32,96},{64,0},{96,32},{1,65},{33,97},{65,1},{97,33},{2,66}... | collective-permute-start | bytes 147464 | tf_op jit(solution)/shard_map/ppermute | solution.py:23
  131.2 1.8 %collective-permute-done.24.refs_3_ = bf16[64,384]{1,0:T(8,128)(2,1)S(1)} collective-permute-done((bf16[64,384]{1,0:T(8,128)(2,1)S(1)}, bf16[64,384]{1,0:T(8,128)(2,1)S(1)}, u32[]{:S(2)}, u32[]{:S(2)}) %collective-permute-start.24) | collective-permute-done | bytes 49184 | tf_op jit(solution)/shard_map/ppermute | solution.py:23
  133.8 3.9 %collective-permute-start.25 = (bf16[64,1536]{1,0:T(8,128)(2,1)S(1)}, bf16[64,1536]{1,0:T(8,128)(2,1)S(1)}, u32[]{:S(2)}, u32[]{:S(2)}) collective-permute-start(bf16[64,1536]{1,0:T(8,128)(2,1)S(1)} %assemble.3.own_ref), channel_id=1, source_target_pairs={{0,128},{128,0},{1,129},{129,1},{2,130},{130,2},{3,131},{131,3},{4... | collective-permute-start | bytes 589832 | tf_op jit(solution)/shard_map/ppermute | solution.py:23
  137.7 1.8 bitcast_select_fusion
  140.1 3.0 %packed.5 = bf16[8,576,128]{2,1,0:T(8,128)(2,1)} custom-call(s32[1]{0:T(128)} %bitcast.core_ref, bf16[128,384]{1,0:T(8,128)(2,1)S(1)} %convolution_convert_fusion.1.refs_0_, bf16[128,1536]{1,0:T(8,128)(2,1)S(1)} %merge.3.refs_1_), custom_call_target="tpu_custom_call" | custom-call | tf_op jit(solution)/shard_map/packed/pallas_call | solution.py:190
  143.0 5.7 %all-to-all-start.3 = ((bf16[8,576,128]{2,1,0:T(8,128)(2,1)}), bf16[8,576,128]{2,1,0:T(8,128)(2,1)}, u32[]{:S(2)}, u32[]{:S(2)}) async-start(bf16[8,576,128]{2,1,0:T(8,128)(2,1)} %packed.5), calls=%async_computation.3 | async-start | bytes 2359296 | tf_op jit(solution)/shard_map/all_to_all | solution.py:31
  149.9 1.7 collective-permute-done.14.other_ref.refs_2_
  151.6 4.6 %coefficients.1 = (bf16[8,128,384]{2,1,0:T(8,128)(2,1)S(1)}, bf16[8,128,384]{2,1,0:T(8,128)(2,1)S(1)}, bf16[8,128,384]{2,1,0:T(8,128)(2,1)S(1)}, bf16[8,192,128]{2,1,0:T(8,128)(2,1)S(1)}) custom-call(s32[1]{0:T(128)} %bitcast.core_ref, bf16[8,1344,128]{2,1,0:T(8,128)(2,1)} %all-to-all-done.1.stored_ref.refs_1_, ...), custom_call_target="tpu_custom_call" | custom-call | tf_op jit(solution)/shard_map/coefficients/pallas_call | solution.py:308
  159.7 4.9 %shard_map.76 = (f32[3,192,384]{2,1,0:T(8,128)S(1)}, bf16[3,192,384]{2,1,0:T(8,128)(2,1)}) custom-call(s32[1]{0:T(128)} %bitcast.core_ref, bf16[8,960,128]{2,1,0:T(8,128)(2,1)} %all-to-all-done.2.refs_0_, bf16[8,1344,128]{2,1,0:T(8,128)(2,1)} %all-to-all-done.1.stored_ref.refs_1_, bf16[8,192,128]{2,1,0:T(8,128)(2,1)S(1)} %collective-permute-done.14.other_ref.refs_2_), custom_call_target="tpu_custom_call" | custom-call | tf_op jit(solution)/shard_map/pallas_call | solution.py:272
  165.9 3.8 %last_grads.1 = (f32[3,192,384]{2,1,0:T(8,128)S(1)}, bf16[3,192,384]{2,1,0:T(8,128)(2,1)S(1)}) custom-call(bf16[8,128,384]{2,1,0:T(8,128)(2,1)} %copy-done.3, bf16[8,128,384]{2,1,0:T(8,128)(2,1)} %copy-done.4, bf16[8,128,384]{2,1,0:T(8,128)(2,1)} %copy-done.5, bf16[8,192,128]{2,1,0:T(8,128)(2,1)} %copy-done.6, bf16[8,576,128]{2,1,0:T(8,128)(2,1)} %all-to-all-done.3.late_ref), custom_call_target="tpu_custom_call" | custom-call | tf_op jit(solution)/shard_map/last_grads/pallas_call | solution.py:364
  169.7 3.8 %collective-permute-start.27 = (bf16[3,192,384]{2,1,0:T(8,128)(2,1)S(1)}, bf16[3,192,384]{2,1,0:T(8,128)(2,1)S(1)}, u32[]{:S(2)}, u32[]{:S(2)}) collective-permute-start(bf16[3,192,384]{2,1,0:T(8,128)(2,1)S(1)} %get-tuple-element.28), channel_id=1, source_target_pairs={{128,0},{129,1},{130,2},{131,3},{132,4},{133,5},{134,6},{135,7},{1... | collective-permute-start | bytes 1327112 | tf_op jit(solution)/shard_map/ppermute | solution.py:27
  173.5 2.3 %early_out.1 = (f32[192,768]{1,0:T(8,128)}, f32[192,768]{1,0:T(8,128)}, f32[192,768]{1,0:T(8,128)}) custom-call(s32[1]{0:T(128)} %bitcast.core_ref, f32[3,192,384]{2,1,0:T(8,128)S(1)} %get-tuple-element.29.own_0_ref, f32[3,192,384]{2,1,0:T(8,128)S(1)} %get-tuple-element.31.own_1_ref, bf16[3,192,384]{2,1,0:T(8,128)(2,1)} %collective-permute-done.28.got_1_ref), custom_call_target="tpu_custom_call" | custom-call | tf_op jit(solution)/shard_map/early_out/pallas_call | solution.py:394
  (96 shorter events, 41.7 us)
Async XLA Ops:
  31.6 3.4 %collective-permute-start.13 = (bf16[2,128,384]{2,1,0:T(8,128)(2,1)S(1)}, bf16[2,128,384]{2,1,0:T(8,128)(2,1)S(1)}, u32[]{:S(2)}, u32[]{:S(2)}) collective-permute-start(bf16[2,128,384]{2,1,0:T(8,128)(2,1)S(1)} %picked.3), channel_id=1, source_target_pairs={{0,128},{128,0},{1,129},{129,1},{2,130},{130,2},{3,131},{131,3},{4... | collective-permute-start | bytes 589832 | tf_op jit(solution)/shard_map/ppermute | solution.py:23
  37.2 55.0 %all-to-all-start.1 = ((bf16[8,1344,128]{2,1,0:T(8,128)(2,1)}), bf16[8,1344,128]{2,1,0:T(8,128)(2,1)}, u32[]{:S(2)}, u32[]{:S(2)}) async-start(bf16[8,1344,128]{2,1,0:T(8,128)(2,1)} %copy-done.1), calls=%async_computation.1 | async-start | bytes 5505024 | tf_op jit(solution)/shard_map/all_to_all | solution.py:31
  44.9 5.3 %collective-permute-start.1 = (bf16[128,384]{1,0:T(8,128)(2,1)}, bf16[128,384]{1,0:T(8,128)(2,1)S(1)}, u32[]{:S(2)}, u32[]{:S(2)}) collective-permute-start(bf16[128,384]{1,0:T(8,128)(2,1)} %get-tuple-element.42), channel_id=1, source_target_pairs={{0,32},{32,64},{64,96},{96,0},{1,33},{33,65},{65,97},{97,1},{2,34}... | collective-permute-start | bytes 294920 | tf_op jit(solution)/shard_map/ppermute | solution.py:23
  44.9 6.8 %collective-permute-start.3 = (bf16[128,384]{1,0:T(8,128)(2,1)}, bf16[128,384]{1,0:T(8,128)(2,1)S(1)}, u32[]{:S(2)}, u32[]{:S(2)}) collective-permute-start(bf16[128,384]{1,0:T(8,128)(2,1)} %get-tuple-element.43), channel_id=1, source_target_pairs={{0,96},{32,0},{64,32},{96,64},{1,97},{33,1},{65,33},{97,65},{2,98}... | collective-permute-start | bytes 294920 | tf_op jit(solution)/shard_map/ppermute | solution.py:23
  47.5 5.4 %collective-permute-start.2 = (bf16[128,384]{1,0:T(8,128)(2,1)S(1)}, bf16[128,384]{1,0:T(8,128)(2,1)S(1)}, u32[]{:S(2)}, u32[]{:S(2)}) collective-permute-start(bf16[128,384]{1,0:T(8,128)(2,1)S(1)} %get-tuple-element.44), channel_id=1, source_target_pairs={{0,64},{32,96},{64,0},{96,32},{1,65},{33,97},{65,1},{97,33},{2,66}... | collective-permute-start | bytes 294920 | tf_op jit(solution)/shard_map/ppermute | solution.py:23
  53.9 4.0 %collective-permute-start.4 = (bf16[64,384]{1,0:T(8,128)(2,1)S(1)}, bf16[64,384]{1,0:T(8,128)(2,1)S(1)}, u32[]{:S(2)}, u32[]{:S(2)}) collective-permute-start(bf16[64,384]{1,0:T(8,128)(2,1)S(1)} %slice.47), channel_id=1, source_target_pairs={{0,128},{1,129},{2,130},{3,131},{4,132},{5,133},{6,134},{7,135},{8... | collective-permute-start | bytes 147464 | tf_op jit(solution)/shard_map/ppermute | solution.py:27
  55.2 6.6 %collective-permute-start = (bf16[64,384]{1,0:T(8,128)(2,1)S(1)}, bf16[64,384]{1,0:T(8,128)(2,1)S(1)}, u32[]{:S(2)}, u32[]{:S(2)}) collective-permute-start(bf16[64,384]{1,0:T(8,128)(2,1)S(1)} %broadcast_select_fusion), channel_id=1, source_target_pairs={{0,128},{128,0},{1,129},{129,1},{2,130},{130,2},{3,131},{131,3},{4... | collective-permute-start | bytes 147464 | tf_op jit(solution)/shard_map/ppermute | solution.py:23
  57.9 4.3 %collective-permute-start.7 = (bf16[64,384]{1,0:T(8,128)(2,1)S(1)}, bf16[64,384]{1,0:T(8,128)(2,1)S(1)}, u32[]{:S(2)}, u32[]{:S(2)}) collective-permute-start(bf16[64,384]{1,0:T(8,128)(2,1)S(1)} %slice_select_fusion.1), channel_id=1, source_target_pairs={{0,24},{8,0},{16,8},{24,16},{1,25},{9,1},{17,9},{25,17},{2,26},{10... | collective-permute-start | bytes 147464 | tf_op jit(solution)/shard_map/ppermute | solution.py:23
  58.1 16.0 %collective-permute-start.6 = (bf16[64,384]{1,0:T(8,128)(2,1)S(1)}, bf16[64,384]{1,0:T(8,128)(2,1)S(1)}, u32[]{:S(2)}, u32[]{:S(2)}) collective-permute-start(bf16[64,384]{1,0:T(8,128)(2,1)S(1)} %slice_select_fusion.1), channel_id=1, source_target_pairs={{0,16},{8,24},{16,0},{24,8},{1,17},{9,25},{17,1},{25,9},{2,18},{10... | collective-permute-start | bytes 147464 | tf_op jit(solution)/shard_map/ppermute | solution.py:23
  61.8 14.4 %collective-permute-start.5 = (bf16[64,384]{1,0:T(8,128)(2,1)S(1)}, bf16[64,384]{1,0:T(8,128)(2,1)S(1)}, u32[]{:S(2)}, u32[]{:S(2)}) collective-permute-start(bf16[64,384]{1,0:T(8,128)(2,1)S(1)} %slice_select_fusion.1), channel_id=1, source_target_pairs={{0,8},{8,16},{16,24},{24,0},{1,9},{9,17},{17,25},{25,1},{2,10},{10... | collective-permute-start | bytes 147464 | tf_op jit(solution)/shard_map/ppermute | solution.py:23
  76.3 4.2 %collective-permute-start.10 = (bf16[64,384]{1,0:T(8,128)(2,1)S(1)}, bf16[64,384]{1,0:T(8,128)(2,1)S(1)}, u32[]{:S(2)}, u32[]{:S(2)}) collective-permute-start(bf16[64,384]{1,0:T(8,128)(2,1)S(1)} %add_convert_fusion.3.refs_0_), channel_id=1, source_target_pairs={{0,32},{32,64},{64,96},{96,0},{1,33},{33,65},{65,97},{97,1},{2,34}... | collective-permute-start | bytes 147464 | tf_op jit(solution)/shard_map/ppermute | solution.py:23
  76.8 4.4 %collective-permute-start.9 = (bf16[64,384]{1,0:T(8,128)(2,1)S(1)}, bf16[64,384]{1,0:T(8,128)(2,1)S(1)}, u32[]{:S(2)}, u32[]{:S(2)}) collective-permute-start(bf16[64,384]{1,0:T(8,128)(2,1)S(1)} %add_convert_fusion.3.refs_0_), channel_id=1, source_target_pairs={{0,64},{32,96},{64,0},{96,32},{1,65},{33,97},{65,1},{97,33},{2,66}... | collective-permute-start | bytes 147464 | tf_op jit(solution)/shard_map/ppermute | solution.py:23
  78.4 3.2 %collective-permute-start.8 = (bf16[64,384]{1,0:T(8,128)(2,1)S(1)}, bf16[64,384]{1,0:T(8,128)(2,1)S(1)}, u32[]{:S(2)}, u32[]{:S(2)}) collective-permute-start(bf16[64,384]{1,0:T(8,128)(2,1)S(1)} %add_convert_fusion.3.refs_0_), channel_id=1, source_target_pairs={{0,96},{32,0},{64,32},{96,64},{1,97},{33,1},{65,33},{97,65},{2,98}... | collective-permute-start | bytes 147464 | tf_op jit(solution)/shard_map/ppermute | solution.py:23
  81.6 4.2 %collective-permute-start.11 = (bf16[64,1536]{1,0:T(8,128)(2,1)S(1)}, bf16[64,1536]{1,0:T(8,128)(2,1)S(1)}, u32[]{:S(2)}, u32[]{:S(2)}) collective-permute-start(bf16[64,1536]{1,0:T(8,128)(2,1)S(1)} %assemble.2.own_ref), channel_id=1, source_target_pairs={{0,128},{128,0},{1,129},{129,1},{2,130},{130,2},{3,131},{131,3},{4... | collective-permute-start | bytes 589832 | tf_op jit(solution)/shard_map/ppermute | solution.py:23
  86.8 3.3 %collective-permute-start.12 = (bf16[2,128,384]{2,1,0:T(8,128)(2,1)S(1)}, bf16[2,128,384]{2,1,0:T(8,128)(2,1)S(1)}, u32[]{:S(2)}, u32[]{:S(2)}) collective-permute-start(bf16[2,128,384]{2,1,0:T(8,128)(2,1)S(1)} %picked.2), channel_id=1, source_target_pairs={{128,0},{129,1},{130,2},{131,3},{132,4},{133,5},{134,6},{135,7},{1... | collective-permute-start | bytes 589832 | tf_op jit(solution)/shard_map/ppermute | solution.py:27
  92.2 50.9 %all-to-all-start.2 = ((bf16[8,960,128]{2,1,0:T(8,128)(2,1)}), bf16[8,960,128]{2,1,0:T(8,128)(2,1)}, u32[]{:S(2)}, u32[]{:S(2)}) async-start(bf16[8,960,128]{2,1,0:T(8,128)(2,1)} %copy-done.2), calls=%async_computation.2 | async-start | bytes 3932160 | tf_op jit(solution)/shard_map/all_to_all | solution.py:31
  99.6 38.1 %collective-permute-start.26 = (bf16[384,1536]{1,0:T(8,128)(2,1)}, bf16[384,1536]{1,0:T(8,128)(2,1)}, u32[]{:S(2)}, u32[]{:S(2)}) collective-permute-start(bf16[384,1536]{1,0:T(8,128)(2,1)} %slice_bitcast_fusion), channel_id=1, source_target_pairs={{0,128},{1,129},{2,130},{3,131},{4,132},{5,133},{6,134},{7,135},{8... | collective-permute-start | bytes 3538952 | tf_op jit(solution)/shard_map/ppermute | solution.py:27
  102.9 5.2 %collective-permute-start.15 = (bf16[128,384]{1,0:T(8,128)(2,1)S(1)}, bf16[128,384]{1,0:T(8,128)(2,1)S(1)}, u32[]{:S(2)}, u32[]{:S(2)}) collective-permute-start(bf16[128,384]{1,0:T(8,128)(2,1)S(1)} %get-tuple-element.39), channel_id=1, source_target_pairs={{0,32},{32,64},{64,96},{96,0},{1,33},{33,65},{65,97},{97,1},{2,34}... | collective-permute-start | bytes 294920 | tf_op jit(solution)/shard_map/ppermute | solution.py:23
  104.2 3.9 %collective-permute-start.17 = (bf16[128,384]{1,0:T(8,128)(2,1)S(1)}, bf16[128,384]{1,0:T(8,128)(2,1)S(1)}, u32[]{:S(2)}, u32[]{:S(2)}) collective-permute-start(bf16[128,384]{1,0:T(8,128)(2,1)S(1)} %get-tuple-element.40), channel_id=1, source_target_pairs={{0,96},{32,0},{64,32},{96,64},{1,97},{33,1},{65,33},{97,65},{2,98}... | collective-permute-start | bytes 294920 | tf_op jit(solution)/shard_map/ppermute | solution.py:23
  105.6 5.8 %collective-permute-start.16 = (bf16[128,384]{1,0:T(8,128)(2,1)S(1)}, bf16[128,384]{1,0:T(8,128)(2,1)S(1)}, u32[]{:S(2)}, u32[]{:S(2)}) collective-permute-start(bf16[128,384]{1,0:T(8,128)(2,1)S(1)} %get-tuple-element.41), channel_id=1, source_target_pairs={{0,64},{32,96},{64,0},{96,32},{1,65},{33,97},{65,1},{97,33},{2,66}... | collective-permute-start | bytes 294920 | tf_op jit(solution)/shard_map/ppermute | solution.py:23
  111.5 5.9 %collective-permute-start.18 = (bf16[64,384]{1,0:T(8,128)(2,1)S(1)}, bf16[64,384]{1,0:T(8,128)(2,1)S(1)}, u32[]{:S(2)}, u32[]{:S(2)}) collective-permute-start(bf16[64,384]{1,0:T(8,128)(2,1)S(1)} %slice.50), channel_id=1, source_target_pairs={{128,0},{129,1},{130,2},{131,3},{132,4},{133,5},{134,6},{135,7},{1... | collective-permute-start | bytes 147464 | tf_op jit(solution)/shard_map/ppermute | solution.py:27
  117.4 7.2 %collective-permute-start.21 = (bf16[64,384]{1,0:T(8,128)(2,1)S(1)}, bf16[64,384]{1,0:T(8,128)(2,1)S(1)}, u32[]{:S(2)}, u32[]{:S(2)}) collective-permute-start(bf16[64,384]{1,0:T(8,128)(2,1)S(1)} %slice_select_fusion), channel_id=1, source_target_pairs={{0,24},{8,0},{16,8},{24,16},{1,25},{9,1},{17,9},{25,17},{2,26},{10... | collective-permute-start | bytes 147464 | tf_op jit(solution)/shard_map/ppermute | solution.py:23
  121.3 6.9 %collective-permute-start.20 = (bf16[64,384]{1,0:T(8,128)(2,1)S(1)}, bf16[64,384]{1,0:T(8,128)(2,1)S(1)}, u32[]{:S(2)}, u32[]{:S(2)}) collective-permute-start(bf16[64,384]{1,0:T(8,128)(2,1)S(1)} %slice_select_fusion), channel_id=1, source_target_pairs={{0,16},{8,24},{16,0},{24,8},{1,17},{9,25},{17,1},{25,9},{2,18},{10... | collective-permute-start | bytes 147464 | tf_op jit(solution)/shard_map/ppermute | solution.py:23
  122.4 5.8 %collective-permute-start.19 = (bf16[64,384]{1,0:T(8,128)(2,1)S(1)}, bf16[64,384]{1,0:T(8,128)(2,1)S(1)}, u32[]{:S(2)}, u32[]{:S(2)}) collective-permute-start(bf16[64,384]{1,0:T(8,128)(2,1)S(1)} %slice_select_fusion), channel_id=1, source_target_pairs={{0,8},{8,16},{16,24},{24,0},{1,9},{9,17},{17,25},{25,1},{2,10},{10... | collective-permute-start | bytes 147464 | tf_op jit(solution)/shard_map/ppermute | solution.py:23
  128.2 4.8 %collective-permute-start.24 = (bf16[64,384]{1,0:T(8,128)(2,1)S(1)}, bf16[64,384]{1,0:T(8,128)(2,1)S(1)}, u32[]{:S(2)}, u32[]{:S(2)}) collective-permute-start(bf16[64,384]{1,0:T(8,128)(2,1)S(1)} %add_convert_fusion.2.refs_0_), channel_id=1, source_target_pairs={{0,32},{32,64},{64,96},{96,0},{1,33},{33,65},{65,97},{97,1},{2,34}... | collective-permute-start | bytes 147464 | tf_op jit(solution)/shard_map/ppermute | solution.py:23
  128.3 4.7 %collective-permute-start.23 = (bf16[64,384]{1,0:T(8,128)(2,1)S(1)}, bf16[64,384]{1,0:T(8,128)(2,1)S(1)}, u32[]{:S(2)}, u32[]{:S(2)}) collective-permute-start(bf16[64,384]{1,0:T(8,128)(2,1)S(1)} %add_convert_fusion.2.refs_0_), channel_id=1, source_target_pairs={{0,64},{32,96},{64,0},{96,32},{1,65},{33,97},{65,1},{97,33},{2,66}... | collective-permute-start | bytes 147464 | tf_op jit(solution)/shard_map/ppermute | solution.py:23
  130.8 2.9 %collective-permute-start.22 = (bf16[64,384]{1,0:T(8,128)(2,1)S(1)}, bf16[64,384]{1,0:T(8,128)(2,1)S(1)}, u32[]{:S(2)}, u32[]{:S(2)}) collective-permute-start(bf16[64,384]{1,0:T(8,128)(2,1)S(1)} %add_convert_fusion.2.refs_0_), channel_id=1, source_target_pairs={{0,96},{32,0},{64,32},{96,64},{1,97},{33,1},{65,33},{97,65},{2,98}... | collective-permute-start | bytes 147464 | tf_op jit(solution)/shard_map/ppermute | solution.py:23
  133.8 5.7 %collective-permute-start.25 = (bf16[64,1536]{1,0:T(8,128)(2,1)S(1)}, bf16[64,1536]{1,0:T(8,128)(2,1)S(1)}, u32[]{:S(2)}, u32[]{:S(2)}) collective-permute-start(bf16[64,1536]{1,0:T(8,128)(2,1)S(1)} %assemble.3.own_ref), channel_id=1, source_target_pairs={{0,128},{128,0},{1,129},{129,1},{2,130},{130,2},{3,131},{131,3},{4... | collective-permute-start | bytes 589832 | tf_op jit(solution)/shard_map/ppermute | solution.py:23
  143.0 22.9 %all-to-all-start.3 = ((bf16[8,576,128]{2,1,0:T(8,128)(2,1)}), bf16[8,576,128]{2,1,0:T(8,128)(2,1)}, u32[]{:S(2)}, u32[]{:S(2)}) async-start(bf16[8,576,128]{2,1,0:T(8,128)(2,1)} %packed.5), calls=%async_computation.3 | async-start | bytes 2359296 | tf_op jit(solution)/shard_map/all_to_all | solution.py:31
  149.8 1.8 %collective-permute-start.14 = (bf16[8,192,128]{2,1,0:T(8,128)(2,1)S(1)}, bf16[8,192,128]{2,1,0:T(8,128)(2,1)S(1)}, u32[]{:S(2)}, u32[]{:S(2)}) collective-permute-start(bf16[8,192,128]{2,1,0:T(8,128)(2,1)S(1)} %slice.48), channel_id=1, source_target_pairs={{0,128},{128,0},{1,129},{129,1},{2,130},{130,2},{3,131},{131,3},{4... | collective-permute-start | bytes 1179656 | tf_op jit(solution)/shard_map/ppermute | solution.py:23
  164.6 8.9 %collective-permute-start.28 = (bf16[3,192,384]{2,1,0:T(8,128)(2,1)}, bf16[3,192,384]{2,1,0:T(8,128)(2,1)}, u32[]{:S(2)}, u32[]{:S(2)}) collective-permute-start(bf16[3,192,384]{2,1,0:T(8,128)(2,1)} %get-tuple-element.32), channel_id=1, source_target_pairs={{0,128},{1,129},{2,130},{3,131},{4,132},{5,133},{6,134},{7,135},{8... | collective-permute-start | bytes 1327112 | tf_op jit(solution)/shard_map/ppermute | solution.py:27
  169.7 6.2 %collective-permute-start.27 = (bf16[3,192,384]{2,1,0:T(8,128)(2,1)S(1)}, bf16[3,192,384]{2,1,0:T(8,128)(2,1)S(1)}, u32[]{:S(2)}, u32[]{:S(2)}) collective-permute-start(bf16[3,192,384]{2,1,0:T(8,128)(2,1)S(1)} %get-tuple-element.28), channel_id=1, source_target_pairs={{128,0},{129,1},{130,2},{131,3},{132,4},{133,5},{134,6},{135,7},{1... | collective-permute-start | bytes 1327112 | tf_op jit(solution)/shard_map/ppermute | solution.py:27
  (11 other events, 75.5 us)

commit v6 on v5

--- a/solution.py
+++ b/solution.py
@@ -199,180 +199,77 @@
     )(core, *values)
 
 
-def weight_grads(stored, d_hidden, acts, upstream, core):
-    arrays = []
-
-    def ref_of(array):
-        for i, known in enumerate(arrays):
-            if known is array:
-                return i
-        arrays.append(array)
-        return len(arrays) - 1
-
+def weight_grads(gate, up, d_hidden, acts, upstream, core):
     step = 2
-    lanes = stored[0].shape[2]
+    lanes = gate[0].shape[2]
     half = 3 * lanes
     shard = 192
-    stored_at = ref_of(stored[0])
-    grad_at = ref_of(d_hidden[0])
-    plans = []
-    for plan in (acts, upstream):
-        if plan[0] == "own":
-            plans.append((ref_of(plan[1]), plan[2], None, None))
-        else:
-            plans.append((ref_of(plan[2]), plan[3], plan[1], ref_of(plan[4])))
+    values = []
+    specs = []
+
+    def add(value, rows, index):
+        values.append(value)
+        specs.append(pl.BlockSpec((step, rows, lanes), lambda p: (p, index, 0)))
+
+    for value, index in (gate, up, d_hidden):
+        add(value, half, index)
+    for operand in (acts, upstream):
+        add(operand[0], shard, operand[1])
+        if len(operand) > 2:
+            add(operand[3], shard, 0)
 
     def body(core_ref, *refs):
-        ins = refs[: len(arrays)]
-        out_ref, low_ref, acc_ref = refs[len(arrays) :]
+        ins = list(refs[: len(values)])
+        out_ref, low_ref = refs[len(values) :]
         index = pl.program_id(0)
 
         @pl.when(index == 0)
         def _():
-            acc_ref[...] = jnp.zeros_like(acc_ref)
-
-        def wide(ref, base):
+            out_ref[...] = jnp.zeros_like(out_ref)
+
+        def wide(ref):
             rows = [
                 jnp.concatenate(
-                    [ref[r, base + t * lanes : base + (t + 1) * lanes, :] for t in range(3)],
-                    axis=1,
+                    [ref[r, t * lanes : (t + 1) * lanes, :] for t in range(3)], axis=1
                 )
                 for r in range(step)
             ]
             return jnp.concatenate(rows, axis=0)
 
-        def features(plan):
-            at, base, when, other = plan
-            blocks = []
-            for r in range(step):
-                block = ins[at][r, base : base + shard, :]
-                if other is not None:
-                    block = jnp.where(core_ref[0] == when, block, ins[other][r])
-                blocks.append(block)
+        def features(operand):
+            ref = ins.pop(0)
+            blocks = [ref[r] for r in range(step)]
+            if len(operand) > 2:
+                other = ins.pop(0)
+                mine = core_ref[0] == operand[2]
+                blocks = [jnp.where(mine, blocks[r], other[r]) for r in range(step)]
             return jnp.concatenate(blocks, axis=1)
 
-        gate = wide(ins[stored_at], stored[1]).astype(F32)
-        up = wide(ins[stored_at], stored[1] + half).astype(F32)
-        grad = wide(ins[grad_at], d_hidden[1]).astype(F32)
-        sigma = jax.nn.sigmoid(gate)
-        silu = gate * sigma
-        d_gate = (grad * up * sigma * (1.0 + gate * (1.0 - sigma))).astype(BF16)
+        gate_v = wide(ins.pop(0)).astype(F32)
+        up_v = wide(ins.pop(0)).astype(F32)
+        grad = wide(ins.pop(0)).astype(F32)
+        sigma = jax.nn.sigmoid(gate_v)
+        silu = gate_v * sigma
+        d_gate = (grad * up_v * sigma * (1.0 + gate_v * (1.0 - sigma))).astype(BF16)
         d_up = (grad * silu).astype(BF16)
-        acts_t = features(plans[0])
-        acc_ref[0] += dot_nn(acts_t, d_gate)
-        acc_ref[1] += dot_nn(acts_t, d_up)
-        acc_ref[2] += dot_nn(features(plans[1]), (silu * up).astype(BF16))
+        acts_t = features(acts)
+        out_ref[0] += dot_nn(acts_t, d_gate)
+        out_ref[1] += dot_nn(acts_t, d_up)
+        out_ref[2] += dot_nn(features(upstream), (silu * up_v).astype(BF16))
 
         @pl.when(index == PEERS // step - 1)
         def _():
-            out_ref[...] = acc_ref[...]
-            low_ref[...] = acc_ref[...].astype(BF16)
+            low_ref[...] = out_ref[...].astype(BF16)
 
     shape = (3, shard, half)
     return pl.pallas_call(
         body,
         grid=(PEERS // step,),
-        in_specs=[whole(pltpu.SMEM)]
-        + [pl.BlockSpec((step, *a.shape[1:]), lambda p: (p, 0, 0)) for a in arrays],
-        out_specs=[
-            pl.BlockSpec(shape, lambda p: (0, 0, 0)),
-            pl.BlockSpec(shape, lambda p: (0, 0, 0)),
-        ],
-        out_shape=[jax.ShapeDtypeStruct(shape, F32), jax.ShapeDtypeStruct(shape, BF16)],
-        scratch_shapes=[pltpu.VMEM(shape, F32)],
-        compiler_params=limits(16),
-    )(core, *arrays)
-
-
-def coefficients(stored, other, core):
-    peers, height, lanes = stored.shape
-    shard = other.shape[1]
-    half = 3 * lanes
-    base = height - shard
-
-    def body(core_ref, stored_ref, other_ref, first_ref, second_ref, hidden_ref, acts_ref):
-        for t in range(3):
-            at = slice(t * lanes, (t + 1) * lanes)
-            gate = stored_ref[0, t * lanes : (t + 1) * lanes, :].astype(F32)
-            up = stored_ref[0, half + t * lanes : half + (t + 1) * lanes, :].astype(F32)
-            sigma = jax.nn.sigmoid(gate)
-            silu = gate * sigma
-            first_ref[0, :, at] = (up * sigma * (1.0 + gate * (1.0 - sigma))).astype(BF16)
-            second_ref[0, :, at] = silu.astype(BF16)
-            hidden_ref[0, :, at] = (silu * up).astype(BF16)
-        acts_ref[0] = jnp.where(core_ref[0] == 0, stored_ref[0, base:, :], other_ref[0])
-
-    def block(rows, width):
-        return pl.BlockSpec((1, rows, width), lambda p: (p, 0, 0))
-
-    return pl.pallas_call(
-        body,
-        grid=(peers,),
-        in_specs=[whole(pltpu.SMEM), block(height, lanes), block(shard, lanes)],
-        out_specs=[block(lanes, half)] * 3 + [block(shard, lanes)],
-        out_shape=[
-            jax.ShapeDtypeStruct((peers, lanes, half), BF16),
-            jax.ShapeDtypeStruct((peers, lanes, half), BF16),
-            jax.ShapeDtypeStruct((peers, lanes, half), BF16),
-            jax.ShapeDtypeStruct((peers, shard, lanes), BF16),
-        ],
-        compiler_params=limits(8),
-        name="coefficients",
-    )(core, stored, other)
-
-
-def last_grads(first, second, hidden, acts, late):
-    peers, _, lanes = late.shape
-    shard = acts.shape[1]
-    half = 3 * lanes
-    step = 2
-
-    def body(first_ref, second_ref, hidden_ref, acts_ref, late_ref, out_ref, low_ref):
-        index = pl.program_id(0)
-
-        @pl.when(index == 0)
-        def _():
-            out_ref[...] = jnp.zeros_like(out_ref)
-
-        def pair(ref):
-            return jnp.concatenate([ref[r] for r in range(step)], axis=0)
-
-        def turned(ref, base):
-            return jnp.concatenate(
-                [ref[r, base : base + shard, :] for r in range(step)], axis=1
-            )
-
-        grad = jnp.concatenate(
-            [
-                jnp.concatenate(
-                    [late_ref[r, t * lanes : (t + 1) * lanes, :] for t in range(3)], axis=1
-                )
-                for r in range(step)
-            ],
-            axis=0,
-        ).astype(F32)
-        acts_t = turned(acts_ref, 0)
-        out_ref[0] += dot_nn(acts_t, (grad * pair(first_ref).astype(F32)).astype(BF16))
-        out_ref[1] += dot_nn(acts_t, (grad * pair(second_ref).astype(F32)).astype(BF16))
-        out_ref[2] += dot_nn(turned(late_ref, half), pair(hidden_ref))
-
-        @pl.when(index == peers // step - 1)
-        def _():
-            low_ref[...] = out_ref[...].astype(BF16)
-
-    shape = (3, shard, half)
-    return pl.pallas_call(
-        body,
-        grid=(peers // step,),
-        in_specs=[
-            pl.BlockSpec((step, *a.shape[1:]), lambda p: (p, 0, 0))
-            for a in (first, second, hidden, acts, late)
-        ],
+        in_specs=[whole(pltpu.SMEM)] + specs,
         out_specs=[pl.BlockSpec(shape, lambda p: (0, 0, 0))] * 2,
         out_shape=[jax.ShapeDtypeStruct(shape, F32), jax.ShapeDtypeStruct(shape, BF16)],
         compiler_params=limits(16),
-        name="last_grads",
-    )(*[pltpu.with_memory_space_constraint(a, pltpu.HBM) for a in (first, second, hidden, acts, late)])
+    )(core, *[pltpu.with_memory_space_constraint(v, pltpu.HBM) for v in values])
 
 
 def early_out(own_0, own_1, got_1, core):
@@ -492,11 +389,10 @@
     residual_2 = jnp.where(core == 0, other, second)
     middle = crossing(partial_a, residual_1, 0, core, x, core_id, x_id)
 
-    d_hidden_a = lax.optimization_barrier(
-        lax.dot_general(
-            entered, down_w, (((0,), (1,)), ((), ())), preferred_element_type=F32
-        ).astype(BF16)
-    )
+    d_hidden_a = lax.dot_general(
+        entered, down_w, (((0,), (1,)), ((), ())), preferred_element_type=F32
+    ).astype(BF16)
+    d_hidden_a = lax.optimization_barrier(d_hidden_a)
     outgoing = picked([[(gate_a, 1), (up_a, 1)], [(d_hidden_a, 0)]], core_id)
     given = shifted(outgoing, "segment", 1)
     load = packed(
@@ -522,20 +418,27 @@
     wide_b = exchanged(load, DP)
 
     d_hidden_b = dot_nt(upstream, down_half).astype(BF16)
+    d_hidden_b, wide_b = lax.optimization_barrier((d_hidden_b, wide_b))
     load = packed([(d_hidden_b, None, 0)], None, (upstream,), core_id)
-    load, wide_b = lax.optimization_barrier((load, wide_b))
     wide_c = exchanged(load, DP)
 
     own_1, low_1 = weight_grads(
         (wide_b, 0),
-        (wide_a, 2 * half),
-        ("own", wide_b, 2 * half),
-        ("pick", 1, wide_a, 3 * half, entered_other),
+        (wide_b, 1),
+        (wide_a, 2),
+        (wide_b, 4),
+        (wide_a, 6, 1, entered_other),
         core_id,
     )
     got_1 = one_way(low_1, 0)
-    first, second, hidden_0, tokens_all = coefficients(wide_a, entered_other, core_id)
-    own_0, low_0 = last_grads(first, second, hidden_0, tokens_all, wide_c)
+    own_0, low_0 = weight_grads(
+        (wide_a, 0),
+        (wide_a, 1),
+        (wide_c, 0),
+        (wide_a, 6, 0, entered_other),
+        (wide_c, 2),
+        core_id,
+    )
     got_0 = one_way(low_0, 1)
     outs = early_out(own_0, own_1, got_1, core_id)
     grad_gate, grad_up, grad_down = late_out(outs, got_0, core_id)

time: 177 us -> 175 us (0.989)
  waiting for transfers between devices: 38.6 us -> 45.3 us
  Pallas kernels: 20.2 us -> 15.8 us
  local copies, waits for them, and re-layouts: 10.8 us -> 8.14 us
    pallas_call x2 -> x0, Pallas kernels: 8.39 us -> none  [the longest x1 4.6 us: coefficients(): pl.pallas_call(body, grid=(peers,), in_specs=[whole(pltpu.SMEM), block(he...]
    all_to_all x3, waiting for transfers between devices: 0.01 us -> 6.8 us  [exchanged(): return lax.all_to_all(value, axes, 0, 0, tiled=True)]
    pallas_call x1 -> x2, Pallas kernels: 4.92 us -> 8.92 us  [weight_grads(): pl.pallas_call(body, grid=(PEERS // step,), in_specs=[whole(pltpu.SMEM)]...]
    unnamed x23 -> x17, local copies, waits for them, and re-layouts: 6.47 us -> 3.77 us
  transfers between devices with their start and end apart: 32 -> 32, of which waited for: 20 -> 21; matrix products, arithmetic and copies ran while one was open for 7% -> 7% of each run, Pallas kernels for 11% -> 7%
where the time goes in v6:
time: 175 us
  starting transfers between devices  65.1 us (37%)
  waiting for transfers between devices  45.3 us (26%)
  blocking collectives  26.1 us (15%)
  Pallas kernels  15.8 us (9%)
  matrix products  9.18 us (5%)
  local copies, waits for them, and re-layouts  8.14 us (5%)
  other arithmetic  3.79 us (2%)
    ppermute x23, waiting for transfers between devices, shifted(): lax.ppermute(value, axis, [(i, (i + distance) % size) for i in range(size)])  36.1 us
    ppermute x23, starting transfers between devices, shifted(): lax.ppermute(value, axis, [(i, (i + distance) % size) for i in range(size)])  35.7 us
    all_to_all x1, blocking collectives, exchanged(): return lax.all_to_all(value, axes, 0, 0, tiled=True)  26.1 us
    all_to_all x3, starting transfers between devices, exchanged(): return lax.all_to_all(value, axes, 0, 0, tiled=True)  15.4 us
    ppermute x6, starting transfers between devices, one_way(): return lax.ppermute(value, 'segment', [(source, 1 - source)])  14 us
    pallas_call x2, Pallas kernels, weight_grads(): pl.pallas_call(body, grid=(PEERS // step,), in_specs=[whole(pltpu.SMEM)]...  8.92 us
    all_to_all x3, waiting for transfers between devices, exchanged(): return lax.all_to_all(value, axes, 0, 0, tiled=True)  6.8 us
    pallas_call x3, Pallas kernels, packed(): pl.pallas_call(body, grid=(PEERS,), in_specs=[whole(pltpu.SMEM)] + specs,...  4.3 us
  transfers between devices with their start and end apart: 32, of which 21 were waited for; matrix products, arithmetic and copies ran while one was open for 7% of the time, Pallas kernels for 7%

profile of v6, /device:TPU:1, one launch (start us, length us, event | category | flops | bytes accessed | tf_op | source)
XLA Modules:
  0.0 174.6 jit_solution(11329549641434671892)
XLA Ops:
  1.6 26.1 %all_to_all.20 = bf16[16,96,128]{2,1,0:T(8,128)(2,1)S(1)} all-to-all(bf16[16,96,128]{2,1,0:T(8,128)(2,1)S(1)} %broadcast_in_dim.20), channel_id=1, replica_groups=mesh['segment'=2,'x'=4,'zh'=4,'zl'=2,'y'=4] {'x','zh'}, dimensions={0} | all-to-all | bytes 786432 | tf_op jit(solution)/shard_map/all_to_all | solution.py:31
  27.7 2.3 %fusion.21.refs_1_ = bf16[128,768]{1,0:T(8,128)(2,1)S(1)} fusion(bf16[1536,128]{1,0:T(8,128)(2,1)S(1)} %bitcast.51, bf16[1,1536,768]{2,1,0:T(8,128)(2,1)} %param.7), kind=kOutput, calls=%fused_computation.21 | convolution fusion | flops 302088192 | bytes 2949120 | tf_op jit(solution)/shard_map/dot_general | solution.py:35
  31.6 2.3 %collective-permute-start.13 = (bf16[2,128,384]{2,1,0:T(8,128)(2,1)S(1)}, bf16[2,128,384]{2,1,0:T(8,128)(2,1)S(1)}, u32[]{:S(2)}, u32[]{:S(2)}) collective-permute-start(bf16[2,128,384]{2,1,0:T(8,128)(2,1)S(1)} %picked.3), channel_id=1, source_target_pairs={{0,128},{128,0},{1,129},{129,1},{2,130},{130,2},{3,131},{131,3},{4... | collective-permute-start | bytes 589832 | tf_op jit(solution)/shard_map/ppermute | solution.py:23
  37.2 4.7 %all-to-all-start.1 = ((bf16[8,1344,128]{2,1,0:T(8,128)(2,1)}), bf16[8,1344,128]{2,1,0:T(8,128)(2,1)}, u32[]{:S(2)}, u32[]{:S(2)}) async-start(bf16[8,1344,128]{2,1,0:T(8,128)(2,1)} %copy-done.1), calls=%async_computation.1 | async-start | bytes 5505024 | tf_op jit(solution)/shard_map/all_to_all | solution.py:31
  41.9 2.2 %convolution_convert_fusion = bf16[128,1536]{1,0:T(8,128)(2,1)S(1)} fusion(bf16[1,768,1536]{2,1,0:T(8,128)(2,1)} %param.8, bf16[128,768]{1,0:T(8,128)(2,1)S(1)} %fusion.21.refs_1_, bf16[128,768]{1,0:T(8,128)(2,1)S(1)} %fusion.15.refs_0_), kind=kOutput, calls=%fused_computation.2 | convolution fusion | flops 302972928 | bytes 3145728 | tf_op jit(solution)/shard_map/dot_general | solution.py:43
  44.9 2.7 %collective-permute-start.3 = (bf16[128,384]{1,0:T(8,128)(2,1)}, bf16[128,384]{1,0:T(8,128)(2,1)S(1)}, u32[]{:S(2)}, u32[]{:S(2)}) collective-permute-start(bf16[128,384]{1,0:T(8,128)(2,1)} %get-tuple-element.35), channel_id=1, source_target_pairs={{0,96},{32,0},{64,32},{96,64},{1,97},{33,1},{65,33},{97,65},{2,98}... | collective-permute-start | bytes 294920 | tf_op jit(solution)/shard_map/ppermute | solution.py:23
  47.7 2.5 %collective-permute-done.1 = bf16[128,384]{1,0:T(8,128)(2,1)S(1)} collective-permute-done((bf16[128,384]{1,0:T(8,128)(2,1)}, bf16[128,384]{1,0:T(8,128)(2,1)S(1)}, u32[]{:S(2)}, u32[]{:S(2)}) %collective-permute-start.1) | collective-permute-done | bytes 98336 | tf_op jit(solution)/shard_map/ppermute | solution.py:23
  55.2 2.0 %collective-permute-start = (bf16[64,384]{1,0:T(8,128)(2,1)S(1)}, bf16[64,384]{1,0:T(8,128)(2,1)S(1)}, u32[]{:S(2)}, u32[]{:S(2)}) collective-permute-start(bf16[64,384]{1,0:T(8,128)(2,1)S(1)} %broadcast_select_fusion), channel_id=1, source_target_pairs={{0,128},{128,0},{1,129},{129,1},{2,130},{130,2},{3,131},{131,3},{4... | collective-permute-start | bytes 147464 | tf_op jit(solution)/shard_map/ppermute | solution.py:23
  58.2 3.7 %collective-permute-start.6 = (bf16[64,384]{1,0:T(8,128)(2,1)S(1)}, bf16[64,384]{1,0:T(8,128)(2,1)S(1)}, u32[]{:S(2)}, u32[]{:S(2)}) collective-permute-start(bf16[64,384]{1,0:T(8,128)(2,1)S(1)} %slice_select_fusion.1), channel_id=1, source_target_pairs={{0,16},{8,24},{16,0},{24,8},{1,17},{9,25},{17,1},{25,9},{2,18},{10... | collective-permute-start | bytes 147464 | tf_op jit(solution)/shard_map/ppermute | solution.py:23
  62.2 11.9 %collective-permute-done.6 = bf16[64,384]{1,0:T(8,128)(2,1)S(1)} collective-permute-done((bf16[64,384]{1,0:T(8,128)(2,1)S(1)}, bf16[64,384]{1,0:T(8,128)(2,1)S(1)}, u32[]{:S(2)}, u32[]{:S(2)}) %collective-permute-start.6) | collective-permute-done | bytes 49184 | tf_op jit(solution)/shard_map/ppermute | solution.py:23
  74.1 2.1 %collective-permute-done.5 = bf16[64,384]{1,0:T(8,128)(2,1)S(1)} collective-permute-done((bf16[64,384]{1,0:T(8,128)(2,1)S(1)}, bf16[64,384]{1,0:T(8,128)(2,1)S(1)}, u32[]{:S(2)}, u32[]{:S(2)}) %collective-permute-start.5) | collective-permute-done | bytes 49184 | tf_op jit(solution)/shard_map/ppermute | solution.py:23
  81.6 3.1 %collective-permute-start.11 = (bf16[64,1536]{1,0:T(8,128)(2,1)S(1)}, bf16[64,1536]{1,0:T(8,128)(2,1)S(1)}, u32[]{:S(2)}, u32[]{:S(2)}) collective-permute-start(bf16[64,1536]{1,0:T(8,128)(2,1)S(1)} %assemble.2.own_ref), channel_id=1, source_target_pairs={{0,128},{128,0},{1,129},{129,1},{2,130},{130,2},{3,131},{131,3},{4... | collective-permute-start | bytes 589832 | tf_op jit(solution)/shard_map/ppermute | solution.py:23
  86.8 2.3 %collective-permute-start.12 = (bf16[2,128,384]{2,1,0:T(8,128)(2,1)S(1)}, bf16[2,128,384]{2,1,0:T(8,128)(2,1)S(1)}, u32[]{:S(2)}, u32[]{:S(2)}) collective-permute-start(bf16[2,128,384]{2,1,0:T(8,128)(2,1)S(1)} %picked.2), channel_id=1, source_target_pairs={{128,0},{129,1},{130,2},{131,3},{132,4},{133,5},{134,6},{135,7},{1... | collective-permute-start | bytes 589832 | tf_op jit(solution)/shard_map/ppermute | solution.py:27
  92.2 5.0 %all-to-all-start.2 = ((bf16[8,960,128]{2,1,0:T(8,128)(2,1)}), bf16[8,960,128]{2,1,0:T(8,128)(2,1)}, u32[]{:S(2)}, u32[]{:S(2)}) async-start(bf16[8,960,128]{2,1,0:T(8,128)(2,1)} %copy-done.2), calls=%async_computation.2 | async-start | bytes 3932160 | tf_op jit(solution)/shard_map/all_to_all | solution.py:31
  97.2 2.4 %slice_bitcast_fusion = bf16[384,1536]{1,0:T(8,128)(2,1)} fusion(bf16[1,768,1536]{2,1,0:T(8,128)(2,1)} %param.8), kind=kLoop, calls=%fused_computation.18 | loop fusion | bytes 2359296 | tf_op jit(solution)/shard_map/slice | solution.py:375
  108.1 3.4 %collective-permute-done.15 = bf16[128,384]{1,0:T(8,128)(2,1)S(1)} collective-permute-done((bf16[128,384]{1,0:T(8,128)(2,1)S(1)}, bf16[128,384]{1,0:T(8,128)(2,1)S(1)}, u32[]{:S(2)}, u32[]{:S(2)}) %collective-permute-start.15) | collective-permute-done | bytes 98336 | tf_op jit(solution)/shard_map/ppermute | solution.py:23
  111.5 5.0 %collective-permute-start.17 = (bf16[64,384]{1,0:T(8,128)(2,1)S(1)}, bf16[64,384]{1,0:T(8,128)(2,1)S(1)}, u32[]{:S(2)}, u32[]{:S(2)}) collective-permute-start(bf16[64,384]{1,0:T(8,128)(2,1)S(1)} %slice.49), channel_id=1, source_target_pairs={{128,0},{129,1},{130,2},{131,3},{132,4},{133,5},{134,6},{135,7},{1... | collective-permute-start | bytes 147464 | tf_op jit(solution)/shard_map/ppermute | solution.py:27
  117.4 3.9 %collective-permute-start.20 = (bf16[64,384]{1,0:T(8,128)(2,1)S(1)}, bf16[64,384]{1,0:T(8,128)(2,1)S(1)}, u32[]{:S(2)}, u32[]{:S(2)}) collective-permute-start(bf16[64,384]{1,0:T(8,128)(2,1)S(1)} %slice_select_fusion), channel_id=1, source_target_pairs={{0,24},{8,0},{16,8},{24,16},{1,25},{9,1},{17,9},{25,17},{2,26},{10... | collective-permute-start | bytes 147464 | tf_op jit(solution)/shard_map/ppermute | solution.py:23
  122.4 2.2 %collective-permute-start.18 = (bf16[64,384]{1,0:T(8,128)(2,1)S(1)}, bf16[64,384]{1,0:T(8,128)(2,1)S(1)}, u32[]{:S(2)}, u32[]{:S(2)}) collective-permute-start(bf16[64,384]{1,0:T(8,128)(2,1)S(1)} %slice_select_fusion), channel_id=1, source_target_pairs={{0,8},{8,16},{16,24},{24,0},{1,9},{9,17},{17,25},{25,1},{2,10},{10... | collective-permute-start | bytes 147464 | tf_op jit(solution)/shard_map/ppermute | solution.py:23
  124.7 3.5 %collective-permute-done.19 = bf16[64,384]{1,0:T(8,128)(2,1)S(1)} collective-permute-done((bf16[64,384]{1,0:T(8,128)(2,1)S(1)}, bf16[64,384]{1,0:T(8,128)(2,1)S(1)}, u32[]{:S(2)}, u32[]{:S(2)}) %collective-permute-start.19) | collective-permute-done | bytes 49184 | tf_op jit(solution)/shard_map/ppermute | solution.py:23
  128.4 2.5 %collective-permute-start.22 = (bf16[64,384]{1,0:T(8,128)(2,1)S(1)}, bf16[64,384]{1,0:T(8,128)(2,1)S(1)}, u32[]{:S(2)}, u32[]{:S(2)}) collective-permute-start(bf16[64,384]{1,0:T(8,128)(2,1)S(1)} %add_convert_fusion.2.refs_0_), channel_id=1, source_target_pairs={{0,64},{32,96},{64,0},{96,32},{1,65},{33,97},{65,1},{97,33},{2,66}... | collective-permute-start | bytes 147464 | tf_op jit(solution)/shard_map/ppermute | solution.py:23
  131.2 1.8 %collective-permute-done.23.refs_3_ = bf16[64,384]{1,0:T(8,128)(2,1)S(1)} collective-permute-done((bf16[64,384]{1,0:T(8,128)(2,1)S(1)}, bf16[64,384]{1,0:T(8,128)(2,1)S(1)}, u32[]{:S(2)}, u32[]{:S(2)}) %collective-permute-start.23) | collective-permute-done | bytes 49184 | tf_op jit(solution)/shard_map/ppermute | solution.py:23
  133.8 3.9 %collective-permute-start.24 = (bf16[64,1536]{1,0:T(8,128)(2,1)S(1)}, bf16[64,1536]{1,0:T(8,128)(2,1)S(1)}, u32[]{:S(2)}, u32[]{:S(2)}) collective-permute-start(bf16[64,1536]{1,0:T(8,128)(2,1)S(1)} %assemble.3.own_ref), channel_id=1, source_target_pairs={{0,128},{128,0},{1,129},{129,1},{2,130},{130,2},{3,131},{131,3},{4... | collective-permute-start | bytes 589832 | tf_op jit(solution)/shard_map/ppermute | solution.py:23
  137.8 1.8 %bitcast_select_fusion = bf16[384,1536]{1,0:T(8,128)(2,1)S(1)} fusion(bf16[384,1536]{1,0:T(8,128)(2,1)} %collective-permute-done.25, bf16[1,768,1536]{2,1,0:T(8,128)(2,1)} %param.8, pred[]{:T(512)S(6)} %eq.18), kind=kLoop, calls=%fused_computation.17 | loop fusion | flops 589824 | bytes 3538945 | tf_op jit(solution)/shard_map/jit(_where)/select_n | solution.py:376
  140.1 2.9 %packed.5 = bf16[8,576,128]{2,1,0:T(8,128)(2,1)} custom-call(s32[1]{0:T(128)} %bitcast.core_ref, bf16[128,384]{1,0:T(8,128)(2,1)S(1)} %convolution_convert_fusion.1.refs_0_, bf16[128,1536]{1,0:T(8,128)(2,1)S(1)} %merge.3.refs_1_), custom_call_target="tpu_custom_call" | custom-call | tf_op jit(solution)/shard_map/packed/pallas_call | solution.py:190
  143.0 5.7 %all-to-all-start.3 = ((bf16[8,576,128]{2,1,0:T(8,128)(2,1)}), bf16[8,576,128]{2,1,0:T(8,128)(2,1)}, u32[]{:S(2)}, u32[]{:S(2)}) async-start(bf16[8,576,128]{2,1,0:T(8,128)(2,1)} %packed.5), calls=%async_computation.3 | async-start | bytes 2359296 | tf_op jit(solution)/shard_map/all_to_all | solution.py:31
  149.9 1.7 collective-permute-done.26.refs_4_.refs_5_
  152.3 4.8 %shard_map.77 = (f32[3,192,384]{2,1,0:T(8,128)S(1)}, bf16[3,192,384]{2,1,0:T(8,128)(2,1)}) custom-call(s32[1]{0:T(128)} %bitcast.core_ref, bf16[8,960,128]{2,1,0:T(8,128)(2,1)} %all-to-all-done.2.refs_0_.refs_1_.refs_3_, bf16[8,960,128]{2,1,0:T(8,128)(2,1)} %all-to-all-done.2.refs_0_.refs_1_.refs_3_, ...), custom_call_target="tpu_custom_call" | custom-call | tf_op jit(solution)/shard_map/pallas_call | solution.py:265
  158.4 6.8 %all-to-all-done.3.refs_2_.refs_5_ = bf16[8,576,128]{2,1,0:T(8,128)(2,1)} async-done(((bf16[8,576,128]{2,1,0:T(8,128)(2,1)}), bf16[8,576,128]{2,1,0:T(8,128)(2,1)}, u32[]{:S(2)}, u32[]{:S(2)}) %all-to-all-start.3) | async-done | bytes 1179680 | tf_op jit(solution)/shard_map/all_to_all | solution.py:31
  165.2 4.1 %shard_map.76 = (f32[3,192,384]{2,1,0:T(8,128)S(1)}, bf16[3,192,384]{2,1,0:T(8,128)(2,1)S(1)}) custom-call(s32[1]{0:T(128)} %bitcast.core_ref, bf16[8,1344,128]{2,1,0:T(8,128)(2,1)} %all-to-all-done.1.refs_0_.refs_1_.refs_3_.refs_2_.refs_4_, bf16[8,1344,128]{2,1,0:T(8,128)(2,1)} %all-to-all-done.1.refs_0_.refs_1_.refs_3_.refs_2_.refs_4_, ...), custom_call_target="tpu_custom_call" | custom-call | tf_op jit(solution)/shard_map/pallas_call | solution.py:265
  169.4 2.7 %collective-permute-start.27 = (bf16[3,192,384]{2,1,0:T(8,128)(2,1)S(1)}, bf16[3,192,384]{2,1,0:T(8,128)(2,1)S(1)}, u32[]{:S(2)}, u32[]{:S(2)}) collective-permute-start(bf16[3,192,384]{2,1,0:T(8,128)(2,1)S(1)} %get-tuple-element.20), channel_id=1, source_target_pairs={{128,0},{129,1},{130,2},{131,3},{132,4},{133,5},{134,6},{135,7},{1... | collective-permute-start | bytes 1327112 | tf_op jit(solution)/shard_map/ppermute | solution.py:27
  172.1 2.3 %early_out.1 = (f32[192,768]{1,0:T(8,128)}, f32[192,768]{1,0:T(8,128)}, f32[192,768]{1,0:T(8,128)}) custom-call(s32[1]{0:T(128)} %bitcast.core_ref, f32[3,192,384]{2,1,0:T(8,128)S(1)} %get-tuple-element.21.own_0_ref, f32[3,192,384]{2,1,0:T(8,128)S(1)} %get-tuple-element.23.own_1_ref, bf16[3,192,384]{2,1,0:T(8,128)(2,1)} %collective-permute-done.28.got_1_ref), custom_call_target="tpu_custom_call" | custom-call | tf_op jit(solution)/shard_map/early_out/pallas_call | solution.py:291
  (89 shorter events, 39.0 us)
Async XLA Ops:
  31.6 3.4 %collective-permute-start.13 = (bf16[2,128,384]{2,1,0:T(8,128)(2,1)S(1)}, bf16[2,128,384]{2,1,0:T(8,128)(2,1)S(1)}, u32[]{:S(2)}, u32[]{:S(2)}) collective-permute-start(bf16[2,128,384]{2,1,0:T(8,128)(2,1)S(1)} %picked.3), channel_id=1, source_target_pairs={{0,128},{128,0},{1,129},{129,1},{2,130},{130,2},{3,131},{131,3},{4... | collective-permute-start | bytes 589832 | tf_op jit(solution)/shard_map/ppermute | solution.py:23
  37.2 55.0 %all-to-all-start.1 = ((bf16[8,1344,128]{2,1,0:T(8,128)(2,1)}), bf16[8,1344,128]{2,1,0:T(8,128)(2,1)}, u32[]{:S(2)}, u32[]{:S(2)}) async-start(bf16[8,1344,128]{2,1,0:T(8,128)(2,1)} %copy-done.1), calls=%async_computation.1 | async-start | bytes 5505024 | tf_op jit(solution)/shard_map/all_to_all | solution.py:31
  44.9 5.3 %collective-permute-start.1 = (bf16[128,384]{1,0:T(8,128)(2,1)}, bf16[128,384]{1,0:T(8,128)(2,1)S(1)}, u32[]{:S(2)}, u32[]{:S(2)}) collective-permute-start(bf16[128,384]{1,0:T(8,128)(2,1)} %get-tuple-element.34), channel_id=1, source_target_pairs={{0,32},{32,64},{64,96},{96,0},{1,33},{33,65},{65,97},{97,1},{2,34}... | collective-permute-start | bytes 294920 | tf_op jit(solution)/shard_map/ppermute | solution.py:23
  44.9 6.8 %collective-permute-start.3 = (bf16[128,384]{1,0:T(8,128)(2,1)}, bf16[128,384]{1,0:T(8,128)(2,1)S(1)}, u32[]{:S(2)}, u32[]{:S(2)}) collective-permute-start(bf16[128,384]{1,0:T(8,128)(2,1)} %get-tuple-element.35), channel_id=1, source_target_pairs={{0,96},{32,0},{64,32},{96,64},{1,97},{33,1},{65,33},{97,65},{2,98}... | collective-permute-start | bytes 294920 | tf_op jit(solution)/shard_map/ppermute | solution.py:23
  47.6 5.4 %collective-permute-start.2 = (bf16[128,384]{1,0:T(8,128)(2,1)S(1)}, bf16[128,384]{1,0:T(8,128)(2,1)S(1)}, u32[]{:S(2)}, u32[]{:S(2)}) collective-permute-start(bf16[128,384]{1,0:T(8,128)(2,1)S(1)} %get-tuple-element.36), channel_id=1, source_target_pairs={{0,64},{32,96},{64,0},{96,32},{1,65},{33,97},{65,1},{97,33},{2,66}... | collective-permute-start | bytes 294920 | tf_op jit(solution)/shard_map/ppermute | solution.py:23
  53.9 4.0 %collective-permute-start.4 = (bf16[64,384]{1,0:T(8,128)(2,1)S(1)}, bf16[64,384]{1,0:T(8,128)(2,1)S(1)}, u32[]{:S(2)}, u32[]{:S(2)}) collective-permute-start(bf16[64,384]{1,0:T(8,128)(2,1)S(1)} %slice.47), channel_id=1, source_target_pairs={{0,128},{1,129},{2,130},{3,131},{4,132},{5,133},{6,134},{7,135},{8... | collective-permute-start | bytes 147464 | tf_op jit(solution)/shard_map/ppermute | solution.py:27
  55.2 6.6 %collective-permute-start = (bf16[64,384]{1,0:T(8,128)(2,1)S(1)}, bf16[64,384]{1,0:T(8,128)(2,1)S(1)}, u32[]{:S(2)}, u32[]{:S(2)}) collective-permute-start(bf16[64,384]{1,0:T(8,128)(2,1)S(1)} %broadcast_select_fusion), channel_id=1, source_target_pairs={{0,128},{128,0},{1,129},{129,1},{2,130},{130,2},{3,131},{131,3},{4... | collective-permute-start | bytes 147464 | tf_op jit(solution)/shard_map/ppermute | solution.py:23
  57.9 4.3 %collective-permute-start.7 = (bf16[64,384]{1,0:T(8,128)(2,1)S(1)}, bf16[64,384]{1,0:T(8,128)(2,1)S(1)}, u32[]{:S(2)}, u32[]{:S(2)}) collective-permute-start(bf16[64,384]{1,0:T(8,128)(2,1)S(1)} %slice_select_fusion.1), channel_id=1, source_target_pairs={{0,24},{8,0},{16,8},{24,16},{1,25},{9,1},{17,9},{25,17},{2,26},{10... | collective-permute-start | bytes 147464 | tf_op jit(solution)/shard_map/ppermute | solution.py:23
  58.2 16.0 %collective-permute-start.6 = (bf16[64,384]{1,0:T(8,128)(2,1)S(1)}, bf16[64,384]{1,0:T(8,128)(2,1)S(1)}, u32[]{:S(2)}, u32[]{:S(2)}) collective-permute-start(bf16[64,384]{1,0:T(8,128)(2,1)S(1)} %slice_select_fusion.1), channel_id=1, source_target_pairs={{0,16},{8,24},{16,0},{24,8},{1,17},{9,25},{17,1},{25,9},{2,18},{10... | collective-permute-start | bytes 147464 | tf_op jit(solution)/shard_map/ppermute | solution.py:23
  61.8 14.4 %collective-permute-start.5 = (bf16[64,384]{1,0:T(8,128)(2,1)S(1)}, bf16[64,384]{1,0:T(8,128)(2,1)S(1)}, u32[]{:S(2)}, u32[]{:S(2)}) collective-permute-start(bf16[64,384]{1,0:T(8,128)(2,1)S(1)} %slice_select_fusion.1), channel_id=1, source_target_pairs={{0,8},{8,16},{16,24},{24,0},{1,9},{9,17},{17,25},{25,1},{2,10},{10... | collective-permute-start | bytes 147464 | tf_op jit(solution)/shard_map/ppermute | solution.py:23
  76.3 4.2 %collective-permute-start.10 = (bf16[64,384]{1,0:T(8,128)(2,1)S(1)}, bf16[64,384]{1,0:T(8,128)(2,1)S(1)}, u32[]{:S(2)}, u32[]{:S(2)}) collective-permute-start(bf16[64,384]{1,0:T(8,128)(2,1)S(1)} %add_convert_fusion.3.refs_0_), channel_id=1, source_target_pairs={{0,32},{32,64},{64,96},{96,0},{1,33},{33,65},{65,97},{97,1},{2,34}... | collective-permute-start | bytes 147464 | tf_op jit(solution)/shard_map/ppermute | solution.py:23
  76.8 4.4 %collective-permute-start.9 = (bf16[64,384]{1,0:T(8,128)(2,1)S(1)}, bf16[64,384]{1,0:T(8,128)(2,1)S(1)}, u32[]{:S(2)}, u32[]{:S(2)}) collective-permute-start(bf16[64,384]{1,0:T(8,128)(2,1)S(1)} %add_convert_fusion.3.refs_0_), channel_id=1, source_target_pairs={{0,64},{32,96},{64,0},{96,32},{1,65},{33,97},{65,1},{97,33},{2,66}... | collective-permute-start | bytes 147464 | tf_op jit(solution)/shard_map/ppermute | solution.py:23
  78.4 3.2 %collective-permute-start.8 = (bf16[64,384]{1,0:T(8,128)(2,1)S(1)}, bf16[64,384]{1,0:T(8,128)(2,1)S(1)}, u32[]{:S(2)}, u32[]{:S(2)}) collective-permute-start(bf16[64,384]{1,0:T(8,128)(2,1)S(1)} %add_convert_fusion.3.refs_0_), channel_id=1, source_target_pairs={{0,96},{32,0},{64,32},{96,64},{1,97},{33,1},{65,33},{97,65},{2,98}... | collective-permute-start | bytes 147464 | tf_op jit(solution)/shard_map/ppermute | solution.py:23
  81.6 4.2 %collective-permute-start.11 = (bf16[64,1536]{1,0:T(8,128)(2,1)S(1)}, bf16[64,1536]{1,0:T(8,128)(2,1)S(1)}, u32[]{:S(2)}, u32[]{:S(2)}) collective-permute-start(bf16[64,1536]{1,0:T(8,128)(2,1)S(1)} %assemble.2.own_ref), channel_id=1, source_target_pairs={{0,128},{128,0},{1,129},{129,1},{2,130},{130,2},{3,131},{131,3},{4... | collective-permute-start | bytes 589832 | tf_op jit(solution)/shard_map/ppermute | solution.py:23
  86.8 3.3 %collective-permute-start.12 = (bf16[2,128,384]{2,1,0:T(8,128)(2,1)S(1)}, bf16[2,128,384]{2,1,0:T(8,128)(2,1)S(1)}, u32[]{:S(2)}, u32[]{:S(2)}) collective-permute-start(bf16[2,128,384]{2,1,0:T(8,128)(2,1)S(1)} %picked.2), channel_id=1, source_target_pairs={{128,0},{129,1},{130,2},{131,3},{132,4},{133,5},{134,6},{135,7},{1... | collective-permute-start | bytes 589832 | tf_op jit(solution)/shard_map/ppermute | solution.py:27
  92.2 47.9 %all-to-all-start.2 = ((bf16[8,960,128]{2,1,0:T(8,128)(2,1)}), bf16[8,960,128]{2,1,0:T(8,128)(2,1)}, u32[]{:S(2)}, u32[]{:S(2)}) async-start(bf16[8,960,128]{2,1,0:T(8,128)(2,1)} %copy-done.2), calls=%async_computation.2 | async-start | bytes 3932160 | tf_op jit(solution)/shard_map/all_to_all | solution.py:31
  99.6 38.2 %collective-permute-start.25 = (bf16[384,1536]{1,0:T(8,128)(2,1)}, bf16[384,1536]{1,0:T(8,128)(2,1)}, u32[]{:S(2)}, u32[]{:S(2)}) collective-permute-start(bf16[384,1536]{1,0:T(8,128)(2,1)} %slice_bitcast_fusion), channel_id=1, source_target_pairs={{0,128},{1,129},{2,130},{3,131},{4,132},{5,133},{6,134},{7,135},{8... | collective-permute-start | bytes 3538952 | tf_op jit(solution)/shard_map/ppermute | solution.py:27
  102.9 5.2 %collective-permute-start.14 = (bf16[128,384]{1,0:T(8,128)(2,1)S(1)}, bf16[128,384]{1,0:T(8,128)(2,1)S(1)}, u32[]{:S(2)}, u32[]{:S(2)}) collective-permute-start(bf16[128,384]{1,0:T(8,128)(2,1)S(1)} %get-tuple-element.31), channel_id=1, source_target_pairs={{0,32},{32,64},{64,96},{96,0},{1,33},{33,65},{65,97},{97,1},{2,34}... | collective-permute-start | bytes 294920 | tf_op jit(solution)/shard_map/ppermute | solution.py:23
  104.2 3.9 %collective-permute-start.16 = (bf16[128,384]{1,0:T(8,128)(2,1)S(1)}, bf16[128,384]{1,0:T(8,128)(2,1)S(1)}, u32[]{:S(2)}, u32[]{:S(2)}) collective-permute-start(bf16[128,384]{1,0:T(8,128)(2,1)S(1)} %get-tuple-element.32), channel_id=1, source_target_pairs={{0,96},{32,0},{64,32},{96,64},{1,97},{33,1},{65,33},{97,65},{2,98}... | collective-permute-start | bytes 294920 | tf_op jit(solution)/shard_map/ppermute | solution.py:23
  105.7 5.8 %collective-permute-start.15 = (bf16[128,384]{1,0:T(8,128)(2,1)S(1)}, bf16[128,384]{1,0:T(8,128)(2,1)S(1)}, u32[]{:S(2)}, u32[]{:S(2)}) collective-permute-start(bf16[128,384]{1,0:T(8,128)(2,1)S(1)} %get-tuple-element.33), channel_id=1, source_target_pairs={{0,64},{32,96},{64,0},{96,32},{1,65},{33,97},{65,1},{97,33},{2,66}... | collective-permute-start | bytes 294920 | tf_op jit(solution)/shard_map/ppermute | solution.py:23
  111.5 5.9 %collective-permute-start.17 = (bf16[64,384]{1,0:T(8,128)(2,1)S(1)}, bf16[64,384]{1,0:T(8,128)(2,1)S(1)}, u32[]{:S(2)}, u32[]{:S(2)}) collective-permute-start(bf16[64,384]{1,0:T(8,128)(2,1)S(1)} %slice.49), channel_id=1, source_target_pairs={{128,0},{129,1},{130,2},{131,3},{132,4},{133,5},{134,6},{135,7},{1... | collective-permute-start | bytes 147464 | tf_op jit(solution)/shard_map/ppermute | solution.py:27
  117.4 7.2 %collective-permute-start.20 = (bf16[64,384]{1,0:T(8,128)(2,1)S(1)}, bf16[64,384]{1,0:T(8,128)(2,1)S(1)}, u32[]{:S(2)}, u32[]{:S(2)}) collective-permute-start(bf16[64,384]{1,0:T(8,128)(2,1)S(1)} %slice_select_fusion), channel_id=1, source_target_pairs={{0,24},{8,0},{16,8},{24,16},{1,25},{9,1},{17,9},{25,17},{2,26},{10... | collective-permute-start | bytes 147464 | tf_op jit(solution)/shard_map/ppermute | solution.py:23
  121.3 6.9 %collective-permute-start.19 = (bf16[64,384]{1,0:T(8,128)(2,1)S(1)}, bf16[64,384]{1,0:T(8,128)(2,1)S(1)}, u32[]{:S(2)}, u32[]{:S(2)}) collective-permute-start(bf16[64,384]{1,0:T(8,128)(2,1)S(1)} %slice_select_fusion), channel_id=1, source_target_pairs={{0,16},{8,24},{16,0},{24,8},{1,17},{9,25},{17,1},{25,9},{2,18},{10... | collective-permute-start | bytes 147464 | tf_op jit(solution)/shard_map/ppermute | solution.py:23
  122.4 5.8 %collective-permute-start.18 = (bf16[64,384]{1,0:T(8,128)(2,1)S(1)}, bf16[64,384]{1,0:T(8,128)(2,1)S(1)}, u32[]{:S(2)}, u32[]{:S(2)}) collective-permute-start(bf16[64,384]{1,0:T(8,128)(2,1)S(1)} %slice_select_fusion), channel_id=1, source_target_pairs={{0,8},{8,16},{16,24},{24,0},{1,9},{9,17},{17,25},{25,1},{2,10},{10... | collective-permute-start | bytes 147464 | tf_op jit(solution)/shard_map/ppermute | solution.py:23
  128.3 4.8 %collective-permute-start.23 = (bf16[64,384]{1,0:T(8,128)(2,1)S(1)}, bf16[64,384]{1,0:T(8,128)(2,1)S(1)}, u32[]{:S(2)}, u32[]{:S(2)}) collective-permute-start(bf16[64,384]{1,0:T(8,128)(2,1)S(1)} %add_convert_fusion.2.refs_0_), channel_id=1, source_target_pairs={{0,32},{32,64},{64,96},{96,0},{1,33},{33,65},{65,97},{97,1},{2,34}... | collective-permute-start | bytes 147464 | tf_op jit(solution)/shard_map/ppermute | solution.py:23
  128.4 4.7 %collective-permute-start.22 = (bf16[64,384]{1,0:T(8,128)(2,1)S(1)}, bf16[64,384]{1,0:T(8,128)(2,1)S(1)}, u32[]{:S(2)}, u32[]{:S(2)}) collective-permute-start(bf16[64,384]{1,0:T(8,128)(2,1)S(1)} %add_convert_fusion.2.refs_0_), channel_id=1, source_target_pairs={{0,64},{32,96},{64,0},{96,32},{1,65},{33,97},{65,1},{97,33},{2,66}... | collective-permute-start | bytes 147464 | tf_op jit(solution)/shard_map/ppermute | solution.py:23
  130.9 2.9 %collective-permute-start.21 = (bf16[64,384]{1,0:T(8,128)(2,1)S(1)}, bf16[64,384]{1,0:T(8,128)(2,1)S(1)}, u32[]{:S(2)}, u32[]{:S(2)}) collective-permute-start(bf16[64,384]{1,0:T(8,128)(2,1)S(1)} %add_convert_fusion.2.refs_0_), channel_id=1, source_target_pairs={{0,96},{32,0},{64,32},{96,64},{1,97},{33,1},{65,33},{97,65},{2,98}... | collective-permute-start | bytes 147464 | tf_op jit(solution)/shard_map/ppermute | solution.py:23
  133.8 5.7 %collective-permute-start.24 = (bf16[64,1536]{1,0:T(8,128)(2,1)S(1)}, bf16[64,1536]{1,0:T(8,128)(2,1)S(1)}, u32[]{:S(2)}, u32[]{:S(2)}) collective-permute-start(bf16[64,1536]{1,0:T(8,128)(2,1)S(1)} %assemble.3.own_ref), channel_id=1, source_target_pairs={{0,128},{128,0},{1,129},{129,1},{2,130},{130,2},{3,131},{131,3},{4... | collective-permute-start | bytes 589832 | tf_op jit(solution)/shard_map/ppermute | solution.py:23
  143.0 22.2 %all-to-all-start.3 = ((bf16[8,576,128]{2,1,0:T(8,128)(2,1)}), bf16[8,576,128]{2,1,0:T(8,128)(2,1)}, u32[]{:S(2)}, u32[]{:S(2)}) async-start(bf16[8,576,128]{2,1,0:T(8,128)(2,1)} %packed.5), calls=%async_computation.3 | async-start | bytes 2359296 | tf_op jit(solution)/shard_map/all_to_all | solution.py:31
  149.8 1.8 %collective-permute-start.26 = (bf16[8,192,128]{2,1,0:T(8,128)(2,1)S(1)}, bf16[8,192,128]{2,1,0:T(8,128)(2,1)S(1)}, u32[]{:S(2)}, u32[]{:S(2)}) collective-permute-start(bf16[8,192,128]{2,1,0:T(8,128)(2,1)S(1)} %slice.50), channel_id=1, source_target_pairs={{0,128},{128,0},{1,129},{129,1},{2,130},{130,2},{3,131},{131,3},{4... | collective-permute-start | bytes 1179656 | tf_op jit(solution)/shard_map/ppermute | solution.py:23
  157.2 14.9 %collective-permute-start.28 = (bf16[3,192,384]{2,1,0:T(8,128)(2,1)}, bf16[3,192,384]{2,1,0:T(8,128)(2,1)}, u32[]{:S(2)}, u32[]{:S(2)}) collective-permute-start(bf16[3,192,384]{2,1,0:T(8,128)(2,1)} %get-tuple-element.24), channel_id=1, source_target_pairs={{0,128},{1,129},{2,130},{3,131},{4,132},{5,133},{6,134},{7,135},{8... | collective-permute-start | bytes 1327112 | tf_op jit(solution)/shard_map/ppermute | solution.py:27
  169.4 5.1 %collective-permute-start.27 = (bf16[3,192,384]{2,1,0:T(8,128)(2,1)S(1)}, bf16[3,192,384]{2,1,0:T(8,128)(2,1)S(1)}, u32[]{:S(2)}, u32[]{:S(2)}) collective-permute-start(bf16[3,192,384]{2,1,0:T(8,128)(2,1)S(1)} %get-tuple-element.20), channel_id=1, source_target_pairs={{128,0},{129,1},{130,2},{131,3},{132,4},{133,5},{134,6},{135,7},{1... | collective-permute-start | bytes 1327112 | tf_op jit(solution)/shard_map/ppermute | solution.py:27
  (8 other events, 72.9 us)

commit v7 on v6

--- a/solution.py
+++ b/solution.py
@@ -142,6 +142,7 @@
     rows = choices[0][0].shape[0]
     half = choices[0][0].shape[1] // (1 if given is None else CORES)
     tiles = half // LANES
+    group = 4
     turned = isinstance(acts, tuple)
     features = acts[0].shape[1] if turned else acts.shape[0]
     shard = features // PEERS
@@ -157,12 +158,12 @@
         specs.append(pl.BlockSpec(acts[0].shape, lambda p: (0, 0)))
     else:
         values.append(acts)
-        specs.append(pl.BlockSpec((shard, rows), lambda p: (p, 0)))
+        specs.append(pl.BlockSpec((group * shard, rows), lambda p: (p, 0)))
 
     def body(core_ref, *refs):
         given_ref = None if given is None else refs[count]
         out_ref = refs[len(values)]
-        peer = pl.program_id(0)
+        index = pl.program_id(0)
         for c, (_, source, slot) in enumerate(choices):
             for t in range(tiles):
                 base = (c * tiles + t) * rows
@@ -171,27 +172,32 @@
                 if source is not None:
                     other = given_ref[slot, :, t * LANES : (t + 1) * LANES]
                     tile = jnp.where(core_ref[0] == source, tile, other)
-                out_ref[0, base : base + rows, :] = tile
+                for g in range(group):
+                    out_ref[g, base : base + rows, :] = tile
         if turned:
             acts_ref = refs[len(values) - 1]
             turned_ref = refs[-1]
 
-            @pl.when(peer == 0)
+            @pl.when(index == 0)
             def _():
                 for t in range(features // LANES):
                     at = slice(t * LANES, (t + 1) * LANES)
                     turned_ref[at, :] = acts_ref[:, at].T
 
-            start = pl.multiple_of(peer * shard, 64)
-            out_ref[0, count * tiles * rows :, :] = turned_ref[pl.ds(start, shard), :]
+            for g in range(group):
+                start = pl.multiple_of((index * group + g) * shard, 64)
+                out_ref[g, count * tiles * rows :, :] = turned_ref[pl.ds(start, shard), :]
         else:
-            out_ref[0, count * tiles * rows :, :] = refs[len(values) - 1][...]
-
-    return pl.pallas_call(
-        body,
-        grid=(PEERS,),
+            acts_ref = refs[len(values) - 1]
+            for g in range(group):
+                at = slice(g * shard, (g + 1) * shard)
+                out_ref[g, count * tiles * rows :, :] = acts_ref[at, :]
+
+    return pl.pallas_call(
+        body,
+        grid=(PEERS // group,),
         in_specs=[whole(pltpu.SMEM)] + specs,
-        out_specs=pl.BlockSpec((1, height, rows), lambda p: (p, 0, 0)),
+        out_specs=pl.BlockSpec((group, height, rows), lambda p: (p, 0, 0)),
         out_shape=jax.ShapeDtypeStruct((PEERS, height, rows), BF16),
         scratch_shapes=[pltpu.VMEM((features, rows), BF16)] if turned else [],
         compiler_params=limits(8),

time: 175 us -> 173 us (0.989)
  Pallas kernels: 15.8 us -> 13.5 us
    pallas_call x3, Pallas kernels: 4.3 us -> 2 us  [packed(): pl.pallas_call(body, grid=(PEERS // group,), in_specs=[whole(pltpu.SMEM)]...]
where the time goes in v7:
time: 173 us; the launch traced here: 172 us
  starting transfers between devices  65.3 us (38%)
  waiting for transfers between devices  45.2 us (26%)
  blocking collectives  26.1 us (15%)
  Pallas kernels  13.5 us (8%)
  matrix products  9.19 us (5%)
  local copies, waits for them, and re-layouts  8.14 us (5%)
  other arithmetic  3.79 us (2%)
    ppermute x23, waiting for transfers between devices, shifted(): lax.ppermute(value, axis, [(i, (i + distance) % size) for i in range(size)])  36 us
    ppermute x23, starting transfers between devices, shifted(): lax.ppermute(value, axis, [(i, (i + distance) % size) for i in range(size)])  35.7 us
    all_to_all x1, blocking collectives, exchanged(): return lax.all_to_all(value, axes, 0, 0, tiled=True)  26.1 us
    all_to_all x3, starting transfers between devices, exchanged(): return lax.all_to_all(value, axes, 0, 0, tiled=True)  15.4 us
    ppermute x6, starting transfers between devices, one_way(): return lax.ppermute(value, 'segment', [(source, 1 - source)])  14.2 us
    pallas_call x2, Pallas kernels, weight_grads(): pl.pallas_call(body, grid=(PEERS // step,), in_specs=[whole(pltpu.SMEM)]...  8.92 us
    all_to_all x3, waiting for transfers between devices, exchanged(): return lax.all_to_all(value, axes, 0, 0, tiled=True)  6.8 us
    unnamed x17, local copies, waits for them, and re-layouts  3.77 us
  transfers between devices with their start and end apart: 32, of which 21 were waited for; matrix products, arithmetic and copies ran while one was open for 7% of the time, Pallas kernels for 7%

profile of v7, /device:TPU:1, one launch (start us, length us, event | category | flops | bytes accessed | tf_op | source)
XLA Modules:
  0.0 172.3 jit_solution(8589182833330921198)
XLA Ops:
  1.6 26.1 %all_to_all.20 = bf16[16,96,128]{2,1,0:T(8,128)(2,1)S(1)} all-to-all(bf16[16,96,128]{2,1,0:T(8,128)(2,1)S(1)} %broadcast_in_dim.20), channel_id=1, replica_groups=mesh['segment'=2,'x'=4,'zh'=4,'zl'=2,'y'=4] {'x','zh'}, dimensions={0} | all-to-all | bytes 786432 | tf_op jit(solution)/shard_map/all_to_all | solution.py:31
  27.7 2.3 %fusion.21.refs_1_ = bf16[128,768]{1,0:T(8,128)(2,1)S(1)} fusion(bf16[1536,128]{1,0:T(8,128)(2,1)S(1)} %bitcast.51, bf16[1,1536,768]{2,1,0:T(8,128)(2,1)} %param.7), kind=kOutput, calls=%fused_computation.21 | convolution fusion | flops 302088192 | bytes 2949120 | tf_op jit(solution)/shard_map/dot_general | solution.py:35
  31.6 2.3 %collective-permute-start.13 = (bf16[2,128,384]{2,1,0:T(8,128)(2,1)S(1)}, bf16[2,128,384]{2,1,0:T(8,128)(2,1)S(1)}, u32[]{:S(2)}, u32[]{:S(2)}) collective-permute-start(bf16[2,128,384]{2,1,0:T(8,128)(2,1)S(1)} %picked.3), channel_id=1, source_target_pairs={{0,128},{128,0},{1,129},{129,1},{2,130},{130,2},{3,131},{131,3},{4... | collective-permute-start | bytes 589832 | tf_op jit(solution)/shard_map/ppermute | solution.py:23
  36.9 4.7 %all-to-all-start.1 = ((bf16[8,1344,128]{2,1,0:T(8,128)(2,1)}), bf16[8,1344,128]{2,1,0:T(8,128)(2,1)}, u32[]{:S(2)}, u32[]{:S(2)}) async-start(bf16[8,1344,128]{2,1,0:T(8,128)(2,1)} %copy-done.1), calls=%async_computation.1 | async-start | bytes 5505024 | tf_op jit(solution)/shard_map/all_to_all | solution.py:31
  41.6 2.2 %convolution_convert_fusion = bf16[128,1536]{1,0:T(8,128)(2,1)S(1)} fusion(bf16[1,768,1536]{2,1,0:T(8,128)(2,1)} %param.8, bf16[128,768]{1,0:T(8,128)(2,1)S(1)} %fusion.21.refs_1_, bf16[128,768]{1,0:T(8,128)(2,1)S(1)} %fusion.15.refs_0_), kind=kOutput, calls=%fused_computation.2 | convolution fusion | flops 302972928 | bytes 3145728 | tf_op jit(solution)/shard_map/dot_general | solution.py:43
  44.6 2.7 %collective-permute-start.3 = (bf16[128,384]{1,0:T(8,128)(2,1)}, bf16[128,384]{1,0:T(8,128)(2,1)S(1)}, u32[]{:S(2)}, u32[]{:S(2)}) collective-permute-start(bf16[128,384]{1,0:T(8,128)(2,1)} %get-tuple-element.35), channel_id=1, source_target_pairs={{0,96},{32,0},{64,32},{96,64},{1,97},{33,1},{65,33},{97,65},{2,98}... | collective-permute-start | bytes 294920 | tf_op jit(solution)/shard_map/ppermute | solution.py:23
  47.4 2.5 %collective-permute-done.1 = bf16[128,384]{1,0:T(8,128)(2,1)S(1)} collective-permute-done((bf16[128,384]{1,0:T(8,128)(2,1)}, bf16[128,384]{1,0:T(8,128)(2,1)S(1)}, u32[]{:S(2)}, u32[]{:S(2)}) %collective-permute-start.1) | collective-permute-done | bytes 98336 | tf_op jit(solution)/shard_map/ppermute | solution.py:23
  54.9 2.0 %collective-permute-start = (bf16[64,384]{1,0:T(8,128)(2,1)S(1)}, bf16[64,384]{1,0:T(8,128)(2,1)S(1)}, u32[]{:S(2)}, u32[]{:S(2)}) collective-permute-start(bf16[64,384]{1,0:T(8,128)(2,1)S(1)} %broadcast_select_fusion), channel_id=1, source_target_pairs={{0,128},{128,0},{1,129},{129,1},{2,130},{130,2},{3,131},{131,3},{4... | collective-permute-start | bytes 147464 | tf_op jit(solution)/shard_map/ppermute | solution.py:23
  57.9 3.7 %collective-permute-start.6 = (bf16[64,384]{1,0:T(8,128)(2,1)S(1)}, bf16[64,384]{1,0:T(8,128)(2,1)S(1)}, u32[]{:S(2)}, u32[]{:S(2)}) collective-permute-start(bf16[64,384]{1,0:T(8,128)(2,1)S(1)} %slice_select_fusion.1), channel_id=1, source_target_pairs={{0,16},{8,24},{16,0},{24,8},{1,17},{9,25},{17,1},{25,9},{2,18},{10... | collective-permute-start | bytes 147464 | tf_op jit(solution)/shard_map/ppermute | solution.py:23
  61.9 11.9 %collective-permute-done.6 = bf16[64,384]{1,0:T(8,128)(2,1)S(1)} collective-permute-done((bf16[64,384]{1,0:T(8,128)(2,1)S(1)}, bf16[64,384]{1,0:T(8,128)(2,1)S(1)}, u32[]{:S(2)}, u32[]{:S(2)}) %collective-permute-start.6) | collective-permute-done | bytes 49184 | tf_op jit(solution)/shard_map/ppermute | solution.py:23
  73.8 2.1 %collective-permute-done.5 = bf16[64,384]{1,0:T(8,128)(2,1)S(1)} collective-permute-done((bf16[64,384]{1,0:T(8,128)(2,1)S(1)}, bf16[64,384]{1,0:T(8,128)(2,1)S(1)}, u32[]{:S(2)}, u32[]{:S(2)}) %collective-permute-start.5) | collective-permute-done | bytes 49184 | tf_op jit(solution)/shard_map/ppermute | solution.py:23
  78.1 1.6 collective-permute-start.8
  81.3 3.1 %collective-permute-start.11 = (bf16[64,1536]{1,0:T(8,128)(2,1)S(1)}, bf16[64,1536]{1,0:T(8,128)(2,1)S(1)}, u32[]{:S(2)}, u32[]{:S(2)}) collective-permute-start(bf16[64,1536]{1,0:T(8,128)(2,1)S(1)} %assemble.2.own_ref), channel_id=1, source_target_pairs={{0,128},{128,0},{1,129},{129,1},{2,130},{130,2},{3,131},{131,3},{4... | collective-permute-start | bytes 589832 | tf_op jit(solution)/shard_map/ppermute | solution.py:23
  86.6 2.5 %collective-permute-start.12 = (bf16[2,128,384]{2,1,0:T(8,128)(2,1)S(1)}, bf16[2,128,384]{2,1,0:T(8,128)(2,1)S(1)}, u32[]{:S(2)}, u32[]{:S(2)}) collective-permute-start(bf16[2,128,384]{2,1,0:T(8,128)(2,1)S(1)} %picked.2), channel_id=1, source_target_pairs={{128,0},{129,1},{130,2},{131,3},{132,4},{133,5},{134,6},{135,7},{1... | collective-permute-start | bytes 589832 | tf_op jit(solution)/shard_map/ppermute | solution.py:27
  91.6 5.0 %all-to-all-start.2 = ((bf16[8,960,128]{2,1,0:T(8,128)(2,1)}), bf16[8,960,128]{2,1,0:T(8,128)(2,1)}, u32[]{:S(2)}, u32[]{:S(2)}) async-start(bf16[8,960,128]{2,1,0:T(8,128)(2,1)} %copy-done.2), calls=%async_computation.2 | async-start | bytes 3932160 | tf_op jit(solution)/shard_map/all_to_all | solution.py:31
  96.6 2.4 %slice_bitcast_fusion = bf16[384,1536]{1,0:T(8,128)(2,1)} fusion(bf16[1,768,1536]{2,1,0:T(8,128)(2,1)} %param.8), kind=kLoop, calls=%fused_computation.18 | loop fusion | bytes 2359296 | tf_op jit(solution)/shard_map/slice | solution.py:381
  107.5 3.4 %collective-permute-done.15 = bf16[128,384]{1,0:T(8,128)(2,1)S(1)} collective-permute-done((bf16[128,384]{1,0:T(8,128)(2,1)S(1)}, bf16[128,384]{1,0:T(8,128)(2,1)S(1)}, u32[]{:S(2)}, u32[]{:S(2)}) %collective-permute-start.15) | collective-permute-done | bytes 98336 | tf_op jit(solution)/shard_map/ppermute | solution.py:23
  110.9 5.0 %collective-permute-start.17 = (bf16[64,384]{1,0:T(8,128)(2,1)S(1)}, bf16[64,384]{1,0:T(8,128)(2,1)S(1)}, u32[]{:S(2)}, u32[]{:S(2)}) collective-permute-start(bf16[64,384]{1,0:T(8,128)(2,1)S(1)} %slice.49), channel_id=1, source_target_pairs={{128,0},{129,1},{130,2},{131,3},{132,4},{133,5},{134,6},{135,7},{1... | collective-permute-start | bytes 147464 | tf_op jit(solution)/shard_map/ppermute | solution.py:27
  116.9 3.9 %collective-permute-start.20 = (bf16[64,384]{1,0:T(8,128)(2,1)S(1)}, bf16[64,384]{1,0:T(8,128)(2,1)S(1)}, u32[]{:S(2)}, u32[]{:S(2)}) collective-permute-start(bf16[64,384]{1,0:T(8,128)(2,1)S(1)} %slice_select_fusion), channel_id=1, source_target_pairs={{0,24},{8,0},{16,8},{24,16},{1,25},{9,1},{17,9},{25,17},{2,26},{10... | collective-permute-start | bytes 147464 | tf_op jit(solution)/shard_map/ppermute | solution.py:23
  121.8 2.3 %collective-permute-start.18 = (bf16[64,384]{1,0:T(8,128)(2,1)S(1)}, bf16[64,384]{1,0:T(8,128)(2,1)S(1)}, u32[]{:S(2)}, u32[]{:S(2)}) collective-permute-start(bf16[64,384]{1,0:T(8,128)(2,1)S(1)} %slice_select_fusion), channel_id=1, source_target_pairs={{0,8},{8,16},{16,24},{24,0},{1,9},{9,17},{17,25},{25,1},{2,10},{10... | collective-permute-start | bytes 147464 | tf_op jit(solution)/shard_map/ppermute | solution.py:23
  124.1 3.5 %collective-permute-done.19 = bf16[64,384]{1,0:T(8,128)(2,1)S(1)} collective-permute-done((bf16[64,384]{1,0:T(8,128)(2,1)S(1)}, bf16[64,384]{1,0:T(8,128)(2,1)S(1)}, u32[]{:S(2)}, u32[]{:S(2)}) %collective-permute-start.19) | collective-permute-done | bytes 49184 | tf_op jit(solution)/shard_map/ppermute | solution.py:23
  127.8 2.5 %collective-permute-start.22 = (bf16[64,384]{1,0:T(8,128)(2,1)S(1)}, bf16[64,384]{1,0:T(8,128)(2,1)S(1)}, u32[]{:S(2)}, u32[]{:S(2)}) collective-permute-start(bf16[64,384]{1,0:T(8,128)(2,1)S(1)} %add_convert_fusion.2.refs_0_), channel_id=1, source_target_pairs={{0,64},{32,96},{64,0},{96,32},{1,65},{33,97},{65,1},{97,33},{2,66}... | collective-permute-start | bytes 147464 | tf_op jit(solution)/shard_map/ppermute | solution.py:23
  130.6 1.8 %collective-permute-done.23.refs_3_ = bf16[64,384]{1,0:T(8,128)(2,1)S(1)} collective-permute-done((bf16[64,384]{1,0:T(8,128)(2,1)S(1)}, bf16[64,384]{1,0:T(8,128)(2,1)S(1)}, u32[]{:S(2)}, u32[]{:S(2)}) %collective-permute-start.23) | collective-permute-done | bytes 49184 | tf_op jit(solution)/shard_map/ppermute | solution.py:23
  133.3 3.9 %collective-permute-start.24 = (bf16[64,1536]{1,0:T(8,128)(2,1)S(1)}, bf16[64,1536]{1,0:T(8,128)(2,1)S(1)}, u32[]{:S(2)}, u32[]{:S(2)}) collective-permute-start(bf16[64,1536]{1,0:T(8,128)(2,1)S(1)} %assemble.3.own_ref), channel_id=1, source_target_pairs={{0,128},{128,0},{1,129},{129,1},{2,130},{130,2},{3,131},{131,3},{4... | collective-permute-start | bytes 589832 | tf_op jit(solution)/shard_map/ppermute | solution.py:23
  137.2 1.8 %bitcast_select_fusion = bf16[384,1536]{1,0:T(8,128)(2,1)S(1)} fusion(bf16[384,1536]{1,0:T(8,128)(2,1)} %collective-permute-done.25, bf16[1,768,1536]{2,1,0:T(8,128)(2,1)} %param.8, pred[]{:T(512)S(6)} %eq.18), kind=kLoop, calls=%fused_computation.17 | loop fusion | flops 589824 | bytes 3538945 | tf_op jit(solution)/shard_map/jit(_where)/select_n | solution.py:382
  140.7 5.7 %all-to-all-start.3 = ((bf16[8,576,128]{2,1,0:T(8,128)(2,1)}), bf16[8,576,128]{2,1,0:T(8,128)(2,1)}, u32[]{:S(2)}, u32[]{:S(2)}) async-start(bf16[8,576,128]{2,1,0:T(8,128)(2,1)} %packed.5), calls=%async_computation.3 | async-start | bytes 2359296 | tf_op jit(solution)/shard_map/all_to_all | solution.py:31
  147.6 1.7 collective-permute-done.26.refs_4_.refs_5_
  150.0 4.8 %shard_map.77 = (f32[3,192,384]{2,1,0:T(8,128)S(1)}, bf16[3,192,384]{2,1,0:T(8,128)(2,1)}) custom-call(s32[1]{0:T(128)} %bitcast.core_ref, bf16[8,960,128]{2,1,0:T(8,128)(2,1)} %all-to-all-done.2.refs_0_.refs_1_.refs_3_, bf16[8,960,128]{2,1,0:T(8,128)(2,1)} %all-to-all-done.2.refs_0_.refs_1_.refs_3_, ...), custom_call_target="tpu_custom_call" | custom-call | tf_op jit(solution)/shard_map/pallas_call | solution.py:271
  156.1 6.8 %all-to-all-done.3.refs_2_.refs_5_ = bf16[8,576,128]{2,1,0:T(8,128)(2,1)} async-done(((bf16[8,576,128]{2,1,0:T(8,128)(2,1)}), bf16[8,576,128]{2,1,0:T(8,128)(2,1)}, u32[]{:S(2)}, u32[]{:S(2)}) %all-to-all-start.3) | async-done | bytes 1179680 | tf_op jit(solution)/shard_map/all_to_all | solution.py:31
  162.9 4.1 %shard_map.76 = (f32[3,192,384]{2,1,0:T(8,128)S(1)}, bf16[3,192,384]{2,1,0:T(8,128)(2,1)S(1)}) custom-call(s32[1]{0:T(128)} %bitcast.core_ref, bf16[8,1344,128]{2,1,0:T(8,128)(2,1)} %all-to-all-done.1.refs_0_.refs_1_.refs_3_.refs_2_.refs_4_, bf16[8,1344,128]{2,1,0:T(8,128)(2,1)} %all-to-all-done.1.refs_0_.refs_1_.refs_3_.refs_2_.refs_4_, ...), custom_call_target="tpu_custom_call" | custom-call | tf_op jit(solution)/shard_map/pallas_call | solution.py:271
  167.1 2.7 %collective-permute-start.27 = (bf16[3,192,384]{2,1,0:T(8,128)(2,1)S(1)}, bf16[3,192,384]{2,1,0:T(8,128)(2,1)S(1)}, u32[]{:S(2)}, u32[]{:S(2)}) collective-permute-start(bf16[3,192,384]{2,1,0:T(8,128)(2,1)S(1)} %get-tuple-element.20), channel_id=1, source_target_pairs={{128,0},{129,1},{130,2},{131,3},{132,4},{133,5},{134,6},{135,7},{1... | collective-permute-start | bytes 1327112 | tf_op jit(solution)/shard_map/ppermute | solution.py:27
  169.8 2.3 %early_out.1 = (f32[192,768]{1,0:T(8,128)}, f32[192,768]{1,0:T(8,128)}, f32[192,768]{1,0:T(8,128)}) custom-call(s32[1]{0:T(128)} %bitcast.core_ref, f32[3,192,384]{2,1,0:T(8,128)S(1)} %get-tuple-element.21.own_0_ref, f32[3,192,384]{2,1,0:T(8,128)S(1)} %get-tuple-element.23.own_1_ref, bf16[3,192,384]{2,1,0:T(8,128)(2,1)} %collective-permute-done.28.got_1_ref), custom_call_target="tpu_custom_call" | custom-call | tf_op jit(solution)/shard_map/early_out/pallas_call | solution.py:297
  (89 shorter events, 37.8 us)
Async XLA Ops:
  31.6 3.4 %collective-permute-start.13 = (bf16[2,128,384]{2,1,0:T(8,128)(2,1)S(1)}, bf16[2,128,384]{2,1,0:T(8,128)(2,1)S(1)}, u32[]{:S(2)}, u32[]{:S(2)}) collective-permute-start(bf16[2,128,384]{2,1,0:T(8,128)(2,1)S(1)} %picked.3), channel_id=1, source_target_pairs={{0,128},{128,0},{1,129},{129,1},{2,130},{130,2},{3,131},{131,3},{4... | collective-permute-start | bytes 589832 | tf_op jit(solution)/shard_map/ppermute | solution.py:23
  36.9 54.7 %all-to-all-start.1 = ((bf16[8,1344,128]{2,1,0:T(8,128)(2,1)}), bf16[8,1344,128]{2,1,0:T(8,128)(2,1)}, u32[]{:S(2)}, u32[]{:S(2)}) async-start(bf16[8,1344,128]{2,1,0:T(8,128)(2,1)} %copy-done.1), calls=%async_computation.1 | async-start | bytes 5505024 | tf_op jit(solution)/shard_map/all_to_all | solution.py:31
  44.6 5.3 %collective-permute-start.1 = (bf16[128,384]{1,0:T(8,128)(2,1)}, bf16[128,384]{1,0:T(8,128)(2,1)S(1)}, u32[]{:S(2)}, u32[]{:S(2)}) collective-permute-start(bf16[128,384]{1,0:T(8,128)(2,1)} %get-tuple-element.34), channel_id=1, source_target_pairs={{0,32},{32,64},{64,96},{96,0},{1,33},{33,65},{65,97},{97,1},{2,34}... | collective-permute-start | bytes 294920 | tf_op jit(solution)/shard_map/ppermute | solution.py:23
  44.6 6.8 %collective-permute-start.3 = (bf16[128,384]{1,0:T(8,128)(2,1)}, bf16[128,384]{1,0:T(8,128)(2,1)S(1)}, u32[]{:S(2)}, u32[]{:S(2)}) collective-permute-start(bf16[128,384]{1,0:T(8,128)(2,1)} %get-tuple-element.35), channel_id=1, source_target_pairs={{0,96},{32,0},{64,32},{96,64},{1,97},{33,1},{65,33},{97,65},{2,98}... | collective-permute-start | bytes 294920 | tf_op jit(solution)/shard_map/ppermute | solution.py:23
  47.3 5.4 %collective-permute-start.2 = (bf16[128,384]{1,0:T(8,128)(2,1)S(1)}, bf16[128,384]{1,0:T(8,128)(2,1)S(1)}, u32[]{:S(2)}, u32[]{:S(2)}) collective-permute-start(bf16[128,384]{1,0:T(8,128)(2,1)S(1)} %get-tuple-element.36), channel_id=1, source_target_pairs={{0,64},{32,96},{64,0},{96,32},{1,65},{33,97},{65,1},{97,33},{2,66}... | collective-permute-start | bytes 294920 | tf_op jit(solution)/shard_map/ppermute | solution.py:23
  53.6 4.0 %collective-permute-start.4 = (bf16[64,384]{1,0:T(8,128)(2,1)S(1)}, bf16[64,384]{1,0:T(8,128)(2,1)S(1)}, u32[]{:S(2)}, u32[]{:S(2)}) collective-permute-start(bf16[64,384]{1,0:T(8,128)(2,1)S(1)} %slice.47), channel_id=1, source_target_pairs={{0,128},{1,129},{2,130},{3,131},{4,132},{5,133},{6,134},{7,135},{8... | collective-permute-start | bytes 147464 | tf_op jit(solution)/shard_map/ppermute | solution.py:27
  54.9 6.6 %collective-permute-start = (bf16[64,384]{1,0:T(8,128)(2,1)S(1)}, bf16[64,384]{1,0:T(8,128)(2,1)S(1)}, u32[]{:S(2)}, u32[]{:S(2)}) collective-permute-start(bf16[64,384]{1,0:T(8,128)(2,1)S(1)} %broadcast_select_fusion), channel_id=1, source_target_pairs={{0,128},{128,0},{1,129},{129,1},{2,130},{130,2},{3,131},{131,3},{4... | collective-permute-start | bytes 147464 | tf_op jit(solution)/shard_map/ppermute | solution.py:23
  57.6 4.3 %collective-permute-start.7 = (bf16[64,384]{1,0:T(8,128)(2,1)S(1)}, bf16[64,384]{1,0:T(8,128)(2,1)S(1)}, u32[]{:S(2)}, u32[]{:S(2)}) collective-permute-start(bf16[64,384]{1,0:T(8,128)(2,1)S(1)} %slice_select_fusion.1), channel_id=1, source_target_pairs={{0,24},{8,0},{16,8},{24,16},{1,25},{9,1},{17,9},{25,17},{2,26},{10... | collective-permute-start | bytes 147464 | tf_op jit(solution)/shard_map/ppermute | solution.py:23
  57.9 16.0 %collective-permute-start.6 = (bf16[64,384]{1,0:T(8,128)(2,1)S(1)}, bf16[64,384]{1,0:T(8,128)(2,1)S(1)}, u32[]{:S(2)}, u32[]{:S(2)}) collective-permute-start(bf16[64,384]{1,0:T(8,128)(2,1)S(1)} %slice_select_fusion.1), channel_id=1, source_target_pairs={{0,16},{8,24},{16,0},{24,8},{1,17},{9,25},{17,1},{25,9},{2,18},{10... | collective-permute-start | bytes 147464 | tf_op jit(solution)/shard_map/ppermute | solution.py:23
  61.5 14.4 %collective-permute-start.5 = (bf16[64,384]{1,0:T(8,128)(2,1)S(1)}, bf16[64,384]{1,0:T(8,128)(2,1)S(1)}, u32[]{:S(2)}, u32[]{:S(2)}) collective-permute-start(bf16[64,384]{1,0:T(8,128)(2,1)S(1)} %slice_select_fusion.1), channel_id=1, source_target_pairs={{0,8},{8,16},{16,24},{24,0},{1,9},{9,17},{17,25},{25,1},{2,10},{10... | collective-permute-start | bytes 147464 | tf_op jit(solution)/shard_map/ppermute | solution.py:23
  76.0 4.2 %collective-permute-start.10 = (bf16[64,384]{1,0:T(8,128)(2,1)S(1)}, bf16[64,384]{1,0:T(8,128)(2,1)S(1)}, u32[]{:S(2)}, u32[]{:S(2)}) collective-permute-start(bf16[64,384]{1,0:T(8,128)(2,1)S(1)} %add_convert_fusion.3.refs_0_), channel_id=1, source_target_pairs={{0,32},{32,64},{64,96},{96,0},{1,33},{33,65},{65,97},{97,1},{2,34}... | collective-permute-start | bytes 147464 | tf_op jit(solution)/shard_map/ppermute | solution.py:23
  76.5 4.4 %collective-permute-start.9 = (bf16[64,384]{1,0:T(8,128)(2,1)S(1)}, bf16[64,384]{1,0:T(8,128)(2,1)S(1)}, u32[]{:S(2)}, u32[]{:S(2)}) collective-permute-start(bf16[64,384]{1,0:T(8,128)(2,1)S(1)} %add_convert_fusion.3.refs_0_), channel_id=1, source_target_pairs={{0,64},{32,96},{64,0},{96,32},{1,65},{33,97},{65,1},{97,33},{2,66}... | collective-permute-start | bytes 147464 | tf_op jit(solution)/shard_map/ppermute | solution.py:23
  78.1 3.2 %collective-permute-start.8 = (bf16[64,384]{1,0:T(8,128)(2,1)S(1)}, bf16[64,384]{1,0:T(8,128)(2,1)S(1)}, u32[]{:S(2)}, u32[]{:S(2)}) collective-permute-start(bf16[64,384]{1,0:T(8,128)(2,1)S(1)} %add_convert_fusion.3.refs_0_), channel_id=1, source_target_pairs={{0,96},{32,0},{64,32},{96,64},{1,97},{33,1},{65,33},{97,65},{2,98}... | collective-permute-start | bytes 147464 | tf_op jit(solution)/shard_map/ppermute | solution.py:23
  81.3 4.2 %collective-permute-start.11 = (bf16[64,1536]{1,0:T(8,128)(2,1)S(1)}, bf16[64,1536]{1,0:T(8,128)(2,1)S(1)}, u32[]{:S(2)}, u32[]{:S(2)}) collective-permute-start(bf16[64,1536]{1,0:T(8,128)(2,1)S(1)} %assemble.2.own_ref), channel_id=1, source_target_pairs={{0,128},{128,0},{1,129},{129,1},{2,130},{130,2},{3,131},{131,3},{4... | collective-permute-start | bytes 589832 | tf_op jit(solution)/shard_map/ppermute | solution.py:23
  86.6 3.3 %collective-permute-start.12 = (bf16[2,128,384]{2,1,0:T(8,128)(2,1)S(1)}, bf16[2,128,384]{2,1,0:T(8,128)(2,1)S(1)}, u32[]{:S(2)}, u32[]{:S(2)}) collective-permute-start(bf16[2,128,384]{2,1,0:T(8,128)(2,1)S(1)} %picked.2), channel_id=1, source_target_pairs={{128,0},{129,1},{130,2},{131,3},{132,4},{133,5},{134,6},{135,7},{1... | collective-permute-start | bytes 589832 | tf_op jit(solution)/shard_map/ppermute | solution.py:27
  91.6 47.9 %all-to-all-start.2 = ((bf16[8,960,128]{2,1,0:T(8,128)(2,1)}), bf16[8,960,128]{2,1,0:T(8,128)(2,1)}, u32[]{:S(2)}, u32[]{:S(2)}) async-start(bf16[8,960,128]{2,1,0:T(8,128)(2,1)} %copy-done.2), calls=%async_computation.2 | async-start | bytes 3932160 | tf_op jit(solution)/shard_map/all_to_all | solution.py:31
  99.0 38.2 %collective-permute-start.25 = (bf16[384,1536]{1,0:T(8,128)(2,1)}, bf16[384,1536]{1,0:T(8,128)(2,1)}, u32[]{:S(2)}, u32[]{:S(2)}) collective-permute-start(bf16[384,1536]{1,0:T(8,128)(2,1)} %slice_bitcast_fusion), channel_id=1, source_target_pairs={{0,128},{1,129},{2,130},{3,131},{4,132},{5,133},{6,134},{7,135},{8... | collective-permute-start | bytes 3538952 | tf_op jit(solution)/shard_map/ppermute | solution.py:27
  102.3 5.2 %collective-permute-start.14 = (bf16[128,384]{1,0:T(8,128)(2,1)S(1)}, bf16[128,384]{1,0:T(8,128)(2,1)S(1)}, u32[]{:S(2)}, u32[]{:S(2)}) collective-permute-start(bf16[128,384]{1,0:T(8,128)(2,1)S(1)} %get-tuple-element.31), channel_id=1, source_target_pairs={{0,32},{32,64},{64,96},{96,0},{1,33},{33,65},{65,97},{97,1},{2,34}... | collective-permute-start | bytes 294920 | tf_op jit(solution)/shard_map/ppermute | solution.py:23
  103.6 3.9 %collective-permute-start.16 = (bf16[128,384]{1,0:T(8,128)(2,1)S(1)}, bf16[128,384]{1,0:T(8,128)(2,1)S(1)}, u32[]{:S(2)}, u32[]{:S(2)}) collective-permute-start(bf16[128,384]{1,0:T(8,128)(2,1)S(1)} %get-tuple-element.32), channel_id=1, source_target_pairs={{0,96},{32,0},{64,32},{96,64},{1,97},{33,1},{65,33},{97,65},{2,98}... | collective-permute-start | bytes 294920 | tf_op jit(solution)/shard_map/ppermute | solution.py:23
  105.1 5.8 %collective-permute-start.15 = (bf16[128,384]{1,0:T(8,128)(2,1)S(1)}, bf16[128,384]{1,0:T(8,128)(2,1)S(1)}, u32[]{:S(2)}, u32[]{:S(2)}) collective-permute-start(bf16[128,384]{1,0:T(8,128)(2,1)S(1)} %get-tuple-element.33), channel_id=1, source_target_pairs={{0,64},{32,96},{64,0},{96,32},{1,65},{33,97},{65,1},{97,33},{2,66}... | collective-permute-start | bytes 294920 | tf_op jit(solution)/shard_map/ppermute | solution.py:23
  110.9 5.9 %collective-permute-start.17 = (bf16[64,384]{1,0:T(8,128)(2,1)S(1)}, bf16[64,384]{1,0:T(8,128)(2,1)S(1)}, u32[]{:S(2)}, u32[]{:S(2)}) collective-permute-start(bf16[64,384]{1,0:T(8,128)(2,1)S(1)} %slice.49), channel_id=1, source_target_pairs={{128,0},{129,1},{130,2},{131,3},{132,4},{133,5},{134,6},{135,7},{1... | collective-permute-start | bytes 147464 | tf_op jit(solution)/shard_map/ppermute | solution.py:27
  116.9 7.2 %collective-permute-start.20 = (bf16[64,384]{1,0:T(8,128)(2,1)S(1)}, bf16[64,384]{1,0:T(8,128)(2,1)S(1)}, u32[]{:S(2)}, u32[]{:S(2)}) collective-permute-start(bf16[64,384]{1,0:T(8,128)(2,1)S(1)} %slice_select_fusion), channel_id=1, source_target_pairs={{0,24},{8,0},{16,8},{24,16},{1,25},{9,1},{17,9},{25,17},{2,26},{10... | collective-permute-start | bytes 147464 | tf_op jit(solution)/shard_map/ppermute | solution.py:23
  120.7 6.9 %collective-permute-start.19 = (bf16[64,384]{1,0:T(8,128)(2,1)S(1)}, bf16[64,384]{1,0:T(8,128)(2,1)S(1)}, u32[]{:S(2)}, u32[]{:S(2)}) collective-permute-start(bf16[64,384]{1,0:T(8,128)(2,1)S(1)} %slice_select_fusion), channel_id=1, source_target_pairs={{0,16},{8,24},{16,0},{24,8},{1,17},{9,25},{17,1},{25,9},{2,18},{10... | collective-permute-start | bytes 147464 | tf_op jit(solution)/shard_map/ppermute | solution.py:23
  121.8 5.8 %collective-permute-start.18 = (bf16[64,384]{1,0:T(8,128)(2,1)S(1)}, bf16[64,384]{1,0:T(8,128)(2,1)S(1)}, u32[]{:S(2)}, u32[]{:S(2)}) collective-permute-start(bf16[64,384]{1,0:T(8,128)(2,1)S(1)} %slice_select_fusion), channel_id=1, source_target_pairs={{0,8},{8,16},{16,24},{24,0},{1,9},{9,17},{17,25},{25,1},{2,10},{10... | collective-permute-start | bytes 147464 | tf_op jit(solution)/shard_map/ppermute | solution.py:23
  127.7 4.8 %collective-permute-start.23 = (bf16[64,384]{1,0:T(8,128)(2,1)S(1)}, bf16[64,384]{1,0:T(8,128)(2,1)S(1)}, u32[]{:S(2)}, u32[]{:S(2)}) collective-permute-start(bf16[64,384]{1,0:T(8,128)(2,1)S(1)} %add_convert_fusion.2.refs_0_), channel_id=1, source_target_pairs={{0,32},{32,64},{64,96},{96,0},{1,33},{33,65},{65,97},{97,1},{2,34}... | collective-permute-start | bytes 147464 | tf_op jit(solution)/shard_map/ppermute | solution.py:23
  127.8 4.7 %collective-permute-start.22 = (bf16[64,384]{1,0:T(8,128)(2,1)S(1)}, bf16[64,384]{1,0:T(8,128)(2,1)S(1)}, u32[]{:S(2)}, u32[]{:S(2)}) collective-permute-start(bf16[64,384]{1,0:T(8,128)(2,1)S(1)} %add_convert_fusion.2.refs_0_), channel_id=1, source_target_pairs={{0,64},{32,96},{64,0},{96,32},{1,65},{33,97},{65,1},{97,33},{2,66}... | collective-permute-start | bytes 147464 | tf_op jit(solution)/shard_map/ppermute | solution.py:23
  130.3 2.9 %collective-permute-start.21 = (bf16[64,384]{1,0:T(8,128)(2,1)S(1)}, bf16[64,384]{1,0:T(8,128)(2,1)S(1)}, u32[]{:S(2)}, u32[]{:S(2)}) collective-permute-start(bf16[64,384]{1,0:T(8,128)(2,1)S(1)} %add_convert_fusion.2.refs_0_), channel_id=1, source_target_pairs={{0,96},{32,0},{64,32},{96,64},{1,97},{33,1},{65,33},{97,65},{2,98}... | collective-permute-start | bytes 147464 | tf_op jit(solution)/shard_map/ppermute | solution.py:23
  133.3 5.7 %collective-permute-start.24 = (bf16[64,1536]{1,0:T(8,128)(2,1)S(1)}, bf16[64,1536]{1,0:T(8,128)(2,1)S(1)}, u32[]{:S(2)}, u32[]{:S(2)}) collective-permute-start(bf16[64,1536]{1,0:T(8,128)(2,1)S(1)} %assemble.3.own_ref), channel_id=1, source_target_pairs={{0,128},{128,0},{1,129},{129,1},{2,130},{130,2},{3,131},{131,3},{4... | collective-permute-start | bytes 589832 | tf_op jit(solution)/shard_map/ppermute | solution.py:23
  140.7 22.2 %all-to-all-start.3 = ((bf16[8,576,128]{2,1,0:T(8,128)(2,1)}), bf16[8,576,128]{2,1,0:T(8,128)(2,1)}, u32[]{:S(2)}, u32[]{:S(2)}) async-start(bf16[8,576,128]{2,1,0:T(8,128)(2,1)} %packed.5), calls=%async_computation.3 | async-start | bytes 2359296 | tf_op jit(solution)/shard_map/all_to_all | solution.py:31
  147.5 1.8 %collective-permute-start.26 = (bf16[8,192,128]{2,1,0:T(8,128)(2,1)S(1)}, bf16[8,192,128]{2,1,0:T(8,128)(2,1)S(1)}, u32[]{:S(2)}, u32[]{:S(2)}) collective-permute-start(bf16[8,192,128]{2,1,0:T(8,128)(2,1)S(1)} %slice.50), channel_id=1, source_target_pairs={{0,128},{128,0},{1,129},{129,1},{2,130},{130,2},{3,131},{131,3},{4... | collective-permute-start | bytes 1179656 | tf_op jit(solution)/shard_map/ppermute | solution.py:23
  154.9 14.9 %collective-permute-start.28 = (bf16[3,192,384]{2,1,0:T(8,128)(2,1)}, bf16[3,192,384]{2,1,0:T(8,128)(2,1)}, u32[]{:S(2)}, u32[]{:S(2)}) collective-permute-start(bf16[3,192,384]{2,1,0:T(8,128)(2,1)} %get-tuple-element.24), channel_id=1, source_target_pairs={{0,128},{1,129},{2,130},{3,131},{4,132},{5,133},{6,134},{7,135},{8... | collective-permute-start | bytes 1327112 | tf_op jit(solution)/shard_map/ppermute | solution.py:27
  167.1 5.1 %collective-permute-start.27 = (bf16[3,192,384]{2,1,0:T(8,128)(2,1)S(1)}, bf16[3,192,384]{2,1,0:T(8,128)(2,1)S(1)}, u32[]{:S(2)}, u32[]{:S(2)}) collective-permute-start(bf16[3,192,384]{2,1,0:T(8,128)(2,1)S(1)} %get-tuple-element.20), channel_id=1, source_target_pairs={{128,0},{129,1},{130,2},{131,3},{132,4},{133,5},{134,6},{135,7},{1... | collective-permute-start | bytes 1327112 | tf_op jit(solution)/shard_map/ppermute | solution.py:27
  (8 other events, 72.9 us)

commit v8 on v7

--- a/solution.py
+++ b/solution.py
@@ -69,6 +69,25 @@
     return lax.dynamic_slice_in_dim(value, index * width, width, 1)
 
 
+def spread(first, second, core):
+    def body(core_ref, first_ref, second_ref, out_ref):
+        value = jnp.where(core_ref[0] == 0, first_ref[...], second_ref[...])
+        for i in range(XS * ZH):
+            out_ref[i] = value
+
+    shape = (XS * ZH, *first.shape)
+    values = [pltpu.with_memory_space_constraint(v, pltpu.HBM) for v in (first, second)]
+    return pl.pallas_call(
+        body,
+        grid=(1,),
+        in_specs=[whole(pltpu.SMEM)] + [pl.BlockSpec(first.shape, lambda i: (0, 0))] * 2,
+        out_specs=pl.BlockSpec(shape, lambda i: (0, 0, 0)),
+        out_shape=jax.ShapeDtypeStruct(shape, BF16),
+        compiler_params=limits(2),
+        name="spread",
+    )(core, *values)
+
+
 def assemble(blocks, x):
     rows, width = blocks[0].shape
 
@@ -138,7 +157,7 @@
     )(core, *values)
 
 
-def packed(choices, given, acts, core):
+def packed(choices, given, acts, core, shared=False):
     rows = choices[0][0].shape[0]
     half = choices[0][0].shape[1] // (1 if given is None else CORES)
     tiles = half // LANES
@@ -147,7 +166,8 @@
     features = acts[0].shape[1] if turned else acts.shape[0]
     shard = features // PEERS
     count = len(choices)
-    height = count * tiles * rows + shard
+    part = shard // CORES if shared else shard
+    height = count * tiles * rows + part
     values = [choice[0] for choice in choices]
     specs = [pl.BlockSpec(value.shape, lambda p: (0, 0)) for value in values]
     if given is not None:
@@ -185,8 +205,11 @@
                     turned_ref[at, :] = acts_ref[:, at].T
 
             for g in range(group):
-                start = pl.multiple_of((index * group + g) * shard, 64)
-                out_ref[g, count * tiles * rows :, :] = turned_ref[pl.ds(start, shard), :]
+                start = (index * group + g) * shard
+                if shared:
+                    start = start + core_ref[0] * part
+                start = pl.multiple_of(start, 32)
+                out_ref[g, count * tiles * rows :, :] = turned_ref[pl.ds(start, part), :]
         else:
             acts_ref = refs[len(values) - 1]
             for g in range(group):
@@ -220,9 +243,10 @@
     for value, index in (gate, up, d_hidden):
         add(value, half, index)
     for operand in (acts, upstream):
-        add(operand[0], shard, operand[1])
+        height = shard // CORES if len(operand) > 2 and operand[2] is None else shard
+        add(operand[0], height, operand[1])
         if len(operand) > 2:
-            add(operand[3], shard, 0)
+            add(operand[3], height, 0)
 
     def body(core_ref, *refs):
         ins = list(refs[: len(values)])
@@ -247,8 +271,12 @@
             blocks = [ref[r] for r in range(step)]
             if len(operand) > 2:
                 other = ins.pop(0)
-                mine = core_ref[0] == operand[2]
-                blocks = [jnp.where(mine, blocks[r], other[r]) for r in range(step)]
+                first = core_ref[0] == (operand[2] or 0)
+                heads = [jnp.where(first, blocks[r], other[r]) for r in range(step)]
+                if operand[2] is None:
+                    tails = [jnp.where(first, other[r], blocks[r]) for r in range(step)]
+                    heads = [jnp.concatenate(pair, axis=0) for pair in zip(heads, tails)]
+                blocks = heads
             return jnp.concatenate(blocks, axis=1)
 
         gate_v = wide(ins.pop(0)).astype(F32)
@@ -380,8 +408,8 @@
 
     lent = one_way(down_w[half:], 0)
     down_half = lax.optimization_barrier(jnp.where(core == 0, down_w[:half], lent))
-    own = jnp.where(core == 0, tokens.T, cotangent.T)
-    gathered = exchanged(jnp.broadcast_to(own, (XS * ZH, *own.shape)), TENSOR)
+    own = spread(tokens.T, cotangent.T, core_id)
+    gathered = exchanged(own, TENSOR)
     entered = gathered.reshape(features, rows)
 
     gate_a = dot_tn(entered, gate_w).astype(BF16)
@@ -419,20 +447,21 @@
     picks = [(gate_b, 0), (up_b, 0)]
     outgoing = picked([picks, picks], core_id)
     given = one_way(outgoing, 1)
-    load = packed([(gate_b, 1, 0), (up_b, 1, 1)], given, (middle,), core_id)
+    load = packed([(gate_b, 1, 0), (up_b, 1, 1)], given, (middle,), core_id, True)
     load, wide_a = lax.optimization_barrier((load, wide_a))
     wide_b = exchanged(load, DP)
 
     d_hidden_b = dot_nt(upstream, down_half).astype(BF16)
-    d_hidden_b, wide_b = lax.optimization_barrier((d_hidden_b, wide_b))
     load = packed([(d_hidden_b, None, 0)], None, (upstream,), core_id)
+    load, wide_b = lax.optimization_barrier((load, wide_b))
     wide_c = exchanged(load, DP)
 
+    middle_other = shifted(wide_b[:, 2 * half :], "segment", 1)
     own_1, low_1 = weight_grads(
         (wide_b, 0),
         (wide_b, 1),
         (wide_a, 2),
-        (wide_b, 4),
+        (wide_b, 8, None, middle_other),
         (wide_a, 6, 1, entered_other),
         core_id,
     )

time: 173 us -> 173 us (level)
  starting transfers between devices: 65.3 us -> 59.4 us
  waiting for transfers between devices: 45.2 us -> 50.5 us
    ppermute x23 -> x24, starting transfers between devices: 35.7 us -> 29.6 us  [shifted(): lax.ppermute(value, axis, [(i, (i + distance) % size) for i in range(size)])]
    ppermute x23 -> x24, waiting for transfers between devices: 36 us -> 42.1 us  [shifted(): lax.ppermute(value, axis, [(i, (i + distance) % size) for i in range(size)])]
    unnamed x17 -> x19, local copies, waits for them, and re-layouts: 3.77 us -> 3.68 us
  transfers between devices with their start and end apart: 32 -> 33, of which waited for: 21 -> 24; matrix products, arithmetic and copies ran while one was open for 7% -> 8% of each run, Pallas kernels for 7% -> 8%
where the time goes in v8:
time: 173 us
  starting transfers between devices  59.4 us (34%)
  waiting for transfers between devices  50.5 us (29%)
  blocking collectives  26.1 us (15%)
  Pallas kernels  14.5 us (8%)
  matrix products  9.18 us (5%)
  local copies, waits for them, and re-layouts  8.89 us (5%)
  other arithmetic  2.88 us (2%)
    ppermute x24, waiting for transfers between devices, shifted(): lax.ppermute(value, axis, [(i, (i + distance) % size) for i in range(size)])  42.1 us
    ppermute x24, starting transfers between devices, shifted(): lax.ppermute(value, axis, [(i, (i + distance) % size) for i in range(size)])  29.6 us
    all_to_all x1, blocking collectives, exchanged(): return lax.all_to_all(value, axes, 0, 0, tiled=True)  26.1 us
    all_to_all x3, starting transfers between devices, exchanged(): return lax.all_to_all(value, axes, 0, 0, tiled=True)  15.7 us
    ppermute x6, starting transfers between devices, one_way(): return lax.ppermute(value, 'segment', [(source, 1 - source)])  14.1 us
    pallas_call x2, Pallas kernels, weight_grads(): pl.pallas_call(body, grid=(PEERS // step,), in_specs=[whole(pltpu.SMEM)]...  8.98 us
    all_to_all x3, waiting for transfers between devices, exchanged(): return lax.all_to_all(value, axes, 0, 0, tiled=True)  5.92 us
    unnamed x19, local copies, waits for them, and re-layouts  3.68 us
  transfers between devices with their start and end apart: 33, of which 24 were waited for; matrix products, arithmetic and copies ran while one was open for 8% of the time, Pallas kernels for 8%

profile of v8, /device:TPU:1, one launch (start us, length us, event | category | flops | bytes accessed | tf_op | source)
XLA Modules:
  0.0 172.6 jit_solution(3570995662168531612)
XLA Ops:
  1.6 26.1 %all_to_all.20 = bf16[16,96,128]{2,1,0:T(8,128)(2,1)S(1)} all-to-all(bf16[16,96,128]{2,1,0:T(8,128)(2,1)S(1)} %spread.1), channel_id=1, replica_groups=mesh['segment'=2,'x'=4,'zh'=4,'zl'=2,'y'=4] {'x','zh'}, dimensions={0} | all-to-all | bytes 786432 | tf_op jit(solution)/shard_map/all_to_all | solution.py:31
  27.7 2.3 %fusion.21.refs_1_ = bf16[128,768]{1,0:T(8,128)(2,1)S(1)} fusion(bf16[1536,128]{1,0:T(8,128)(2,1)S(1)} %bitcast.51, bf16[1,1536,768]{2,1,0:T(8,128)(2,1)} %param.7), kind=kOutput, calls=%fused_computation.21 | convolution fusion | flops 302088192 | bytes 2949120 | tf_op jit(solution)/shard_map/dot_general | solution.py:35
  31.5 2.3 %collective-permute-start.13 = (bf16[2,128,384]{2,1,0:T(8,128)(2,1)S(1)}, bf16[2,128,384]{2,1,0:T(8,128)(2,1)S(1)}, u32[]{:S(2)}, u32[]{:S(2)}) collective-permute-start(bf16[2,128,384]{2,1,0:T(8,128)(2,1)S(1)} %picked.3), channel_id=1, source_target_pairs={{0,128},{128,0},{1,129},{129,1},{2,130},{130,2},{3,131},{131,3},{4... | collective-permute-start | bytes 589832 | tf_op jit(solution)/shard_map/ppermute | solution.py:23
  35.3 1.6 copy-done.1
  36.9 4.8 %all-to-all-start.1 = ((bf16[8,1344,128]{2,1,0:T(8,128)(2,1)}), bf16[8,1344,128]{2,1,0:T(8,128)(2,1)}, u32[]{:S(2)}, u32[]{:S(2)}) async-start(bf16[8,1344,128]{2,1,0:T(8,128)(2,1)} %copy-done.1), calls=%async_computation.1 | async-start | bytes 5505024 | tf_op jit(solution)/shard_map/all_to_all | solution.py:31
  41.7 2.2 %convolution_convert_fusion = bf16[128,1536]{1,0:T(8,128)(2,1)S(1)} fusion(bf16[1,768,1536]{2,1,0:T(8,128)(2,1)} %param.8, bf16[128,768]{1,0:T(8,128)(2,1)S(1)} %fusion.21.refs_1_, bf16[128,768]{1,0:T(8,128)(2,1)S(1)} %fusion.15.refs_0_), kind=kOutput, calls=%fused_computation.2 | convolution fusion | flops 302972928 | bytes 3145728 | tf_op jit(solution)/shard_map/dot_general | solution.py:43
  46.3 2.5 %collective-permute-done.3 = bf16[128,384]{1,0:T(8,128)(2,1)S(1)} collective-permute-done((bf16[128,384]{1,0:T(8,128)(2,1)}, bf16[128,384]{1,0:T(8,128)(2,1)S(1)}, u32[]{:S(2)}, u32[]{:S(2)}) %collective-permute-start.3) | collective-permute-done | bytes 98336 | tf_op jit(solution)/shard_map/ppermute | solution.py:23
  48.8 2.1 %collective-permute-done.2 = bf16[128,384]{1,0:T(8,128)(2,1)S(1)} collective-permute-done((bf16[128,384]{1,0:T(8,128)(2,1)}, bf16[128,384]{1,0:T(8,128)(2,1)S(1)}, u32[]{:S(2)}, u32[]{:S(2)}) %collective-permute-start.2) | collective-permute-done | bytes 98336 | tf_op jit(solution)/shard_map/ppermute | solution.py:23
  50.9 2.6 %collective-permute-done.1 = bf16[128,384]{1,0:T(8,128)(2,1)S(1)} collective-permute-done((bf16[128,384]{1,0:T(8,128)(2,1)S(1)}, bf16[128,384]{1,0:T(8,128)(2,1)S(1)}, u32[]{:S(2)}, u32[]{:S(2)}) %collective-permute-start.1) | collective-permute-done | bytes 98336 | tf_op jit(solution)/shard_map/ppermute | solution.py:23
  57.8 3.8 %collective-permute-start.6 = (bf16[64,384]{1,0:T(8,128)(2,1)S(1)}, bf16[64,384]{1,0:T(8,128)(2,1)S(1)}, u32[]{:S(2)}, u32[]{:S(2)}) collective-permute-start(bf16[64,384]{1,0:T(8,128)(2,1)S(1)} %slice_select_fusion.1), channel_id=1, source_target_pairs={{0,16},{8,24},{16,0},{24,8},{1,17},{9,25},{17,1},{25,9},{2,18},{10... | collective-permute-start | bytes 147464 | tf_op jit(solution)/shard_map/ppermute | solution.py:23
  61.9 11.9 %collective-permute-done.6 = bf16[64,384]{1,0:T(8,128)(2,1)S(1)} collective-permute-done((bf16[64,384]{1,0:T(8,128)(2,1)S(1)}, bf16[64,384]{1,0:T(8,128)(2,1)S(1)}, u32[]{:S(2)}, u32[]{:S(2)}) %collective-permute-start.6) | collective-permute-done | bytes 49184 | tf_op jit(solution)/shard_map/ppermute | solution.py:23
  73.8 2.1 %collective-permute-done.5 = bf16[64,384]{1,0:T(8,128)(2,1)S(1)} collective-permute-done((bf16[64,384]{1,0:T(8,128)(2,1)S(1)}, bf16[64,384]{1,0:T(8,128)(2,1)S(1)}, u32[]{:S(2)}, u32[]{:S(2)}) %collective-permute-start.5) | collective-permute-done | bytes 49184 | tf_op jit(solution)/shard_map/ppermute | solution.py:23
  79.0 2.4 %collective-permute-done.9.refs_2_ = bf16[64,384]{1,0:T(8,128)(2,1)S(1)} collective-permute-done((bf16[64,384]{1,0:T(8,128)(2,1)S(1)}, bf16[64,384]{1,0:T(8,128)(2,1)S(1)}, u32[]{:S(2)}, u32[]{:S(2)}) %collective-permute-start.9) | collective-permute-done | bytes 49184 | tf_op jit(solution)/shard_map/ppermute | solution.py:23
  82.5 3.3 %collective-permute-start.11 = (bf16[64,1536]{1,0:T(8,128)(2,1)S(1)}, bf16[64,1536]{1,0:T(8,128)(2,1)S(1)}, u32[]{:S(2)}, u32[]{:S(2)}) collective-permute-start(bf16[64,1536]{1,0:T(8,128)(2,1)S(1)} %assemble.2.own_ref), channel_id=1, source_target_pairs={{0,128},{128,0},{1,129},{129,1},{2,130},{130,2},{3,131},{131,3},{4... | collective-permute-start | bytes 589832 | tf_op jit(solution)/shard_map/ppermute | solution.py:23
  87.9 2.3 %collective-permute-start.12 = (bf16[2,128,384]{2,1,0:T(8,128)(2,1)S(1)}, bf16[2,128,384]{2,1,0:T(8,128)(2,1)S(1)}, u32[]{:S(2)}, u32[]{:S(2)}) collective-permute-start(bf16[2,128,384]{2,1,0:T(8,128)(2,1)S(1)} %picked.2), channel_id=1, source_target_pairs={{128,0},{129,1},{130,2},{131,3},{132,4},{133,5},{134,6},{135,7},{1... | collective-permute-start | bytes 589832 | tf_op jit(solution)/shard_map/ppermute | solution.py:27
  92.9 4.6 %all-to-all-start.2 = ((bf16[8,864,128]{2,1,0:T(8,128)(2,1)}), bf16[8,864,128]{2,1,0:T(8,128)(2,1)}, u32[]{:S(2)}, u32[]{:S(2)}) async-start(bf16[8,864,128]{2,1,0:T(8,128)(2,1)} %copy-done.2), calls=%async_computation.2 | async-start | bytes 3538944 | tf_op jit(solution)/shard_map/all_to_all | solution.py:31
  97.6 2.4 %slice_bitcast_fusion = bf16[384,1536]{1,0:T(8,128)(2,1)} fusion(bf16[1,768,1536]{2,1,0:T(8,128)(2,1)} %param.8), kind=kLoop, calls=%fused_computation.18 | loop fusion | bytes 2359296 | tf_op jit(solution)/shard_map/slice | solution.py:409
  105.0 2.2 %collective-permute-done.16 = bf16[128,384]{1,0:T(8,128)(2,1)S(1)} collective-permute-done((bf16[128,384]{1,0:T(8,128)(2,1)S(1)}, bf16[128,384]{1,0:T(8,128)(2,1)S(1)}, u32[]{:S(2)}, u32[]{:S(2)}) %collective-permute-start.16) | collective-permute-done | bytes 98336 | tf_op jit(solution)/shard_map/ppermute | solution.py:23
  107.2 2.5 %collective-permute-done.15 = bf16[128,384]{1,0:T(8,128)(2,1)S(1)} collective-permute-done((bf16[128,384]{1,0:T(8,128)(2,1)S(1)}, bf16[128,384]{1,0:T(8,128)(2,1)S(1)}, u32[]{:S(2)}, u32[]{:S(2)}) %collective-permute-start.15) | collective-permute-done | bytes 98336 | tf_op jit(solution)/shard_map/ppermute | solution.py:23
  110.8 5.2 %collective-permute-start.17 = (bf16[64,384]{1,0:T(8,128)(2,1)S(1)}, bf16[64,384]{1,0:T(8,128)(2,1)S(1)}, u32[]{:S(2)}, u32[]{:S(2)}) collective-permute-start(bf16[64,384]{1,0:T(8,128)(2,1)S(1)} %slice.53), channel_id=1, source_target_pairs={{128,0},{129,1},{130,2},{131,3},{132,4},{133,5},{134,6},{135,7},{1... | collective-permute-start | bytes 147464 | tf_op jit(solution)/shard_map/ppermute | solution.py:27
  116.9 3.9 %collective-permute-start.20 = (bf16[64,384]{1,0:T(8,128)(2,1)S(1)}, bf16[64,384]{1,0:T(8,128)(2,1)S(1)}, u32[]{:S(2)}, u32[]{:S(2)}) collective-permute-start(bf16[64,384]{1,0:T(8,128)(2,1)S(1)} %slice_select_fusion), channel_id=1, source_target_pairs={{0,24},{8,0},{16,8},{24,16},{1,25},{9,1},{17,9},{25,17},{2,26},{10... | collective-permute-start | bytes 147464 | tf_op jit(solution)/shard_map/ppermute | solution.py:23
  121.9 2.3 %collective-permute-start.18 = (bf16[64,384]{1,0:T(8,128)(2,1)S(1)}, bf16[64,384]{1,0:T(8,128)(2,1)S(1)}, u32[]{:S(2)}, u32[]{:S(2)}) collective-permute-start(bf16[64,384]{1,0:T(8,128)(2,1)S(1)} %slice_select_fusion), channel_id=1, source_target_pairs={{0,8},{8,16},{16,24},{24,0},{1,9},{9,17},{17,25},{25,1},{2,10},{10... | collective-permute-start | bytes 147464 | tf_op jit(solution)/shard_map/ppermute | solution.py:23
  124.2 3.4 %collective-permute-done.19 = bf16[64,384]{1,0:T(8,128)(2,1)S(1)} collective-permute-done((bf16[64,384]{1,0:T(8,128)(2,1)S(1)}, bf16[64,384]{1,0:T(8,128)(2,1)S(1)}, u32[]{:S(2)}, u32[]{:S(2)}) %collective-permute-start.19) | collective-permute-done | bytes 49184 | tf_op jit(solution)/shard_map/ppermute | solution.py:23
  130.7 2.6 %collective-permute-done.22.refs_2_ = bf16[64,384]{1,0:T(8,128)(2,1)S(1)} collective-permute-done((bf16[64,384]{1,0:T(8,128)(2,1)S(1)}, bf16[64,384]{1,0:T(8,128)(2,1)S(1)}, u32[]{:S(2)}, u32[]{:S(2)}) %collective-permute-start.22) | collective-permute-done | bytes 49184 | tf_op jit(solution)/shard_map/ppermute | solution.py:23
  133.8 3.2 %collective-permute-start.24 = (bf16[64,1536]{1,0:T(8,128)(2,1)S(1)}, bf16[64,1536]{1,0:T(8,128)(2,1)S(1)}, u32[]{:S(2)}, u32[]{:S(2)}) collective-permute-start(bf16[64,1536]{1,0:T(8,128)(2,1)S(1)} %assemble.3.own_ref), channel_id=1, source_target_pairs={{0,128},{128,0},{1,129},{129,1},{2,130},{130,2},{3,131},{131,3},{4... | collective-permute-start | bytes 589832 | tf_op jit(solution)/shard_map/ppermute | solution.py:23
  137.0 1.8 %bitcast_select_fusion = bf16[384,1536]{1,0:T(8,128)(2,1)S(1)} fusion(bf16[384,1536]{1,0:T(8,128)(2,1)} %collective-permute-done.25, bf16[1,768,1536]{2,1,0:T(8,128)(2,1)} %param.8, pred[]{:T(512)S(6)} %eq.17), kind=kLoop, calls=%fused_computation.17 | loop fusion | flops 589824 | bytes 3538945 | tf_op jit(solution)/shard_map/jit(_where)/select_n | solution.py:410
  140.5 6.2 %all-to-all-start.3 = ((bf16[8,576,128]{2,1,0:T(8,128)(2,1)}), bf16[8,576,128]{2,1,0:T(8,128)(2,1)}, u32[]{:S(2)}, u32[]{:S(2)}) async-start(bf16[8,576,128]{2,1,0:T(8,128)(2,1)} %packed.5), calls=%async_computation.3 | async-start | bytes 2359296 | tf_op jit(solution)/shard_map/all_to_all | solution.py:31
  151.2 4.9 %shard_map.77 = (f32[3,192,384]{2,1,0:T(8,128)S(1)}, bf16[3,192,384]{2,1,0:T(8,128)(2,1)}) custom-call(s32[1]{0:T(128)} %bitcast.core_ref, bf16[8,864,128]{2,1,0:T(8,128)(2,1)} %all-to-all-done.2.refs_0_.refs_1_.refs_3_, bf16[8,864,128]{2,1,0:T(8,128)(2,1)} %all-to-all-done.2.refs_0_.refs_1_.refs_3_, ...), custom_call_target="tpu_custom_call" | custom-call | tf_op jit(solution)/shard_map/pallas_call | solution.py:299
  157.3 5.9 %all-to-all-done.3.refs_2_.refs_5_ = bf16[8,576,128]{2,1,0:T(8,128)(2,1)} async-done(((bf16[8,576,128]{2,1,0:T(8,128)(2,1)}), bf16[8,576,128]{2,1,0:T(8,128)(2,1)}, u32[]{:S(2)}, u32[]{:S(2)}) %all-to-all-start.3) | async-done | bytes 1179680 | tf_op jit(solution)/shard_map/all_to_all | solution.py:31
  163.2 4.1 %shard_map.76 = (f32[3,192,384]{2,1,0:T(8,128)S(1)}, bf16[3,192,384]{2,1,0:T(8,128)(2,1)S(1)}) custom-call(s32[1]{0:T(128)} %bitcast.core_ref, bf16[8,1344,128]{2,1,0:T(8,128)(2,1)} %all-to-all-done.1.refs_0_.refs_1_.refs_3_.refs_2_.refs_5_, bf16[8,1344,128]{2,1,0:T(8,128)(2,1)} %all-to-all-done.1.refs_0_.refs_1_.refs_3_.refs_2_.refs_5_, ...), custom_call_target="tpu_custom_call" | custom-call | tf_op jit(solution)/shard_map/pallas_call | solution.py:299
  167.3 2.7 %collective-permute-start.27 = (bf16[3,192,384]{2,1,0:T(8,128)(2,1)S(1)}, bf16[3,192,384]{2,1,0:T(8,128)(2,1)S(1)}, u32[]{:S(2)}, u32[]{:S(2)}) collective-permute-start(bf16[3,192,384]{2,1,0:T(8,128)(2,1)S(1)} %get-tuple-element.20), channel_id=1, source_target_pairs={{128,0},{129,1},{130,2},{131,3},{132,4},{133,5},{134,6},{135,7},{1... | collective-permute-start | bytes 1327112 | tf_op jit(solution)/shard_map/ppermute | solution.py:27
  170.1 2.3 %early_out.1 = (f32[192,768]{1,0:T(8,128)}, f32[192,768]{1,0:T(8,128)}, f32[192,768]{1,0:T(8,128)}) custom-call(s32[1]{0:T(128)} %bitcast.core_ref, f32[3,192,384]{2,1,0:T(8,128)S(1)} %get-tuple-element.21.own_0_ref, f32[3,192,384]{2,1,0:T(8,128)S(1)} %get-tuple-element.23.own_1_ref, bf16[3,192,384]{2,1,0:T(8,128)(2,1)} %collective-permute-done.29.got_1_ref), custom_call_target="tpu_custom_call" | custom-call | tf_op jit(solution)/shard_map/early_out/pallas_call | solution.py:325
  (93 shorter events, 39.1 us)
Async XLA Ops:
  31.5 3.4 %collective-permute-start.13 = (bf16[2,128,384]{2,1,0:T(8,128)(2,1)S(1)}, bf16[2,128,384]{2,1,0:T(8,128)(2,1)S(1)}, u32[]{:S(2)}, u32[]{:S(2)}) collective-permute-start(bf16[2,128,384]{2,1,0:T(8,128)(2,1)S(1)} %picked.3), channel_id=1, source_target_pairs={{0,128},{128,0},{1,129},{129,1},{2,130},{130,2},{3,131},{131,3},{4... | collective-permute-start | bytes 589832 | tf_op jit(solution)/shard_map/ppermute | solution.py:23
  36.9 56.0 %all-to-all-start.1 = ((bf16[8,1344,128]{2,1,0:T(8,128)(2,1)}), bf16[8,1344,128]{2,1,0:T(8,128)(2,1)}, u32[]{:S(2)}, u32[]{:S(2)}) async-start(bf16[8,1344,128]{2,1,0:T(8,128)(2,1)} %copy-done.1), calls=%async_computation.1 | async-start | bytes 5505024 | tf_op jit(solution)/shard_map/all_to_all | solution.py:31
  44.7 4.1 %collective-permute-start.3 = (bf16[128,384]{1,0:T(8,128)(2,1)}, bf16[128,384]{1,0:T(8,128)(2,1)S(1)}, u32[]{:S(2)}, u32[]{:S(2)}) collective-permute-start(bf16[128,384]{1,0:T(8,128)(2,1)} %get-tuple-element.35), channel_id=1, source_target_pairs={{0,96},{32,0},{64,32},{96,64},{1,97},{33,1},{65,33},{97,65},{2,98}... | collective-permute-start | bytes 294920 | tf_op jit(solution)/shard_map/ppermute | solution.py:23
  45.3 5.6 %collective-permute-start.2 = (bf16[128,384]{1,0:T(8,128)(2,1)}, bf16[128,384]{1,0:T(8,128)(2,1)S(1)}, u32[]{:S(2)}, u32[]{:S(2)}) collective-permute-start(bf16[128,384]{1,0:T(8,128)(2,1)} %get-tuple-element.36), channel_id=1, source_target_pairs={{0,64},{32,96},{64,0},{96,32},{1,65},{33,97},{65,1},{97,33},{2,66}... | collective-permute-start | bytes 294920 | tf_op jit(solution)/shard_map/ppermute | solution.py:23
  45.8 7.7 %collective-permute-start.1 = (bf16[128,384]{1,0:T(8,128)(2,1)S(1)}, bf16[128,384]{1,0:T(8,128)(2,1)S(1)}, u32[]{:S(2)}, u32[]{:S(2)}) collective-permute-start(bf16[128,384]{1,0:T(8,128)(2,1)S(1)} %get-tuple-element.34), channel_id=1, source_target_pairs={{0,32},{32,64},{64,96},{96,0},{1,33},{33,65},{65,97},{97,1},{2,34}... | collective-permute-start | bytes 294920 | tf_op jit(solution)/shard_map/ppermute | solution.py:23
  54.5 3.1 %collective-permute-start.4 = (bf16[64,384]{1,0:T(8,128)(2,1)S(1)}, bf16[64,384]{1,0:T(8,128)(2,1)S(1)}, u32[]{:S(2)}, u32[]{:S(2)}) collective-permute-start(bf16[64,384]{1,0:T(8,128)(2,1)S(1)} %slice.51), channel_id=1, source_target_pairs={{0,128},{1,129},{2,130},{3,131},{4,132},{5,133},{6,134},{7,135},{8... | collective-permute-start | bytes 147464 | tf_op jit(solution)/shard_map/ppermute | solution.py:27
  55.8 5.8 %collective-permute-start = (bf16[64,384]{1,0:T(8,128)(2,1)S(1)}, bf16[64,384]{1,0:T(8,128)(2,1)S(1)}, u32[]{:S(2)}, u32[]{:S(2)}) collective-permute-start(bf16[64,384]{1,0:T(8,128)(2,1)S(1)} %broadcast_select_fusion), channel_id=1, source_target_pairs={{0,128},{128,0},{1,129},{129,1},{2,130},{130,2},{3,131},{131,3},{4... | collective-permute-start | bytes 147464 | tf_op jit(solution)/shard_map/ppermute | solution.py:23
  57.6 4.3 %collective-permute-start.7 = (bf16[64,384]{1,0:T(8,128)(2,1)S(1)}, bf16[64,384]{1,0:T(8,128)(2,1)S(1)}, u32[]{:S(2)}, u32[]{:S(2)}) collective-permute-start(bf16[64,384]{1,0:T(8,128)(2,1)S(1)} %slice_select_fusion.1), channel_id=1, source_target_pairs={{0,24},{8,0},{16,8},{24,16},{1,25},{9,1},{17,9},{25,17},{2,26},{10... | collective-permute-start | bytes 147464 | tf_op jit(solution)/shard_map/ppermute | solution.py:23
  57.8 16.0 %collective-permute-start.6 = (bf16[64,384]{1,0:T(8,128)(2,1)S(1)}, bf16[64,384]{1,0:T(8,128)(2,1)S(1)}, u32[]{:S(2)}, u32[]{:S(2)}) collective-permute-start(bf16[64,384]{1,0:T(8,128)(2,1)S(1)} %slice_select_fusion.1), channel_id=1, source_target_pairs={{0,16},{8,24},{16,0},{24,8},{1,17},{9,25},{17,1},{25,9},{2,18},{10... | collective-permute-start | bytes 147464 | tf_op jit(solution)/shard_map/ppermute | solution.py:23
  61.6 14.4 %collective-permute-start.5 = (bf16[64,384]{1,0:T(8,128)(2,1)S(1)}, bf16[64,384]{1,0:T(8,128)(2,1)S(1)}, u32[]{:S(2)}, u32[]{:S(2)}) collective-permute-start(bf16[64,384]{1,0:T(8,128)(2,1)S(1)} %slice_select_fusion.1), channel_id=1, source_target_pairs={{0,8},{8,16},{16,24},{24,0},{1,9},{9,17},{17,25},{25,1},{2,10},{10... | collective-permute-start | bytes 147464 | tf_op jit(solution)/shard_map/ppermute | solution.py:23
  76.0 3.0 %collective-permute-start.8 = (bf16[64,384]{1,0:T(8,128)(2,1)S(1)}, bf16[64,384]{1,0:T(8,128)(2,1)S(1)}, u32[]{:S(2)}, u32[]{:S(2)}) collective-permute-start(bf16[64,384]{1,0:T(8,128)(2,1)S(1)} %add_convert_fusion.3.refs_0_), channel_id=1, source_target_pairs={{0,96},{32,0},{64,32},{96,64},{1,97},{33,1},{65,33},{97,65},{2,98}... | collective-permute-start | bytes 147464 | tf_op jit(solution)/shard_map/ppermute | solution.py:23
  77.0 4.4 %collective-permute-start.9 = (bf16[64,384]{1,0:T(8,128)(2,1)S(1)}, bf16[64,384]{1,0:T(8,128)(2,1)S(1)}, u32[]{:S(2)}, u32[]{:S(2)}) collective-permute-start(bf16[64,384]{1,0:T(8,128)(2,1)S(1)} %add_convert_fusion.3.refs_0_), channel_id=1, source_target_pairs={{0,64},{32,96},{64,0},{96,32},{1,65},{33,97},{65,1},{97,33},{2,66}... | collective-permute-start | bytes 147464 | tf_op jit(solution)/shard_map/ppermute | solution.py:23
  78.3 4.2 %collective-permute-start.10 = (bf16[64,384]{1,0:T(8,128)(2,1)S(1)}, bf16[64,384]{1,0:T(8,128)(2,1)S(1)}, u32[]{:S(2)}, u32[]{:S(2)}) collective-permute-start(bf16[64,384]{1,0:T(8,128)(2,1)S(1)} %add_convert_fusion.3.refs_0_), channel_id=1, source_target_pairs={{0,32},{32,64},{64,96},{96,0},{1,33},{33,65},{65,97},{97,1},{2,34}... | collective-permute-start | bytes 147464 | tf_op jit(solution)/shard_map/ppermute | solution.py:23
  82.5 4.4 %collective-permute-start.11 = (bf16[64,1536]{1,0:T(8,128)(2,1)S(1)}, bf16[64,1536]{1,0:T(8,128)(2,1)S(1)}, u32[]{:S(2)}, u32[]{:S(2)}) collective-permute-start(bf16[64,1536]{1,0:T(8,128)(2,1)S(1)} %assemble.2.own_ref), channel_id=1, source_target_pairs={{0,128},{128,0},{1,129},{129,1},{2,130},{130,2},{3,131},{131,3},{4... | collective-permute-start | bytes 589832 | tf_op jit(solution)/shard_map/ppermute | solution.py:23
  87.9 3.3 %collective-permute-start.12 = (bf16[2,128,384]{2,1,0:T(8,128)(2,1)S(1)}, bf16[2,128,384]{2,1,0:T(8,128)(2,1)S(1)}, u32[]{:S(2)}, u32[]{:S(2)}) collective-permute-start(bf16[2,128,384]{2,1,0:T(8,128)(2,1)S(1)} %picked.2), channel_id=1, source_target_pairs={{128,0},{129,1},{130,2},{131,3},{132,4},{133,5},{134,6},{135,7},{1... | collective-permute-start | bytes 589832 | tf_op jit(solution)/shard_map/ppermute | solution.py:27
  92.9 47.6 %all-to-all-start.2 = ((bf16[8,864,128]{2,1,0:T(8,128)(2,1)}), bf16[8,864,128]{2,1,0:T(8,128)(2,1)}, u32[]{:S(2)}, u32[]{:S(2)}) async-start(bf16[8,864,128]{2,1,0:T(8,128)(2,1)} %copy-done.2), calls=%async_computation.2 | async-start | bytes 3538944 | tf_op jit(solution)/shard_map/all_to_all | solution.py:31
  99.9 37.0 %collective-permute-start.25 = (bf16[384,1536]{1,0:T(8,128)(2,1)}, bf16[384,1536]{1,0:T(8,128)(2,1)}, u32[]{:S(2)}, u32[]{:S(2)}) collective-permute-start(bf16[384,1536]{1,0:T(8,128)(2,1)} %slice_bitcast_fusion), channel_id=1, source_target_pairs={{0,128},{1,129},{2,130},{3,131},{4,132},{5,133},{6,134},{7,135},{8... | collective-permute-start | bytes 3538952 | tf_op jit(solution)/shard_map/ppermute | solution.py:27
  103.2 3.9 %collective-permute-start.16 = (bf16[128,384]{1,0:T(8,128)(2,1)S(1)}, bf16[128,384]{1,0:T(8,128)(2,1)S(1)}, u32[]{:S(2)}, u32[]{:S(2)}) collective-permute-start(bf16[128,384]{1,0:T(8,128)(2,1)S(1)} %get-tuple-element.32), channel_id=1, source_target_pairs={{0,96},{32,0},{64,32},{96,64},{1,97},{33,1},{65,33},{97,65},{2,98}... | collective-permute-start | bytes 294920 | tf_op jit(solution)/shard_map/ppermute | solution.py:23
  104.3 5.4 %collective-permute-start.15 = (bf16[128,384]{1,0:T(8,128)(2,1)S(1)}, bf16[128,384]{1,0:T(8,128)(2,1)S(1)}, u32[]{:S(2)}, u32[]{:S(2)}) collective-permute-start(bf16[128,384]{1,0:T(8,128)(2,1)S(1)} %get-tuple-element.33), channel_id=1, source_target_pairs={{0,64},{32,96},{64,0},{96,32},{1,65},{33,97},{65,1},{97,33},{2,66}... | collective-permute-start | bytes 294920 | tf_op jit(solution)/shard_map/ppermute | solution.py:23
  104.9 5.8 %collective-permute-start.14 = (bf16[128,384]{1,0:T(8,128)(2,1)S(1)}, bf16[128,384]{1,0:T(8,128)(2,1)S(1)}, u32[]{:S(2)}, u32[]{:S(2)}) collective-permute-start(bf16[128,384]{1,0:T(8,128)(2,1)S(1)} %get-tuple-element.31), channel_id=1, source_target_pairs={{0,32},{32,64},{64,96},{96,0},{1,33},{33,65},{65,97},{97,1},{2,34}... | collective-permute-start | bytes 294920 | tf_op jit(solution)/shard_map/ppermute | solution.py:23
  110.8 6.0 %collective-permute-start.17 = (bf16[64,384]{1,0:T(8,128)(2,1)S(1)}, bf16[64,384]{1,0:T(8,128)(2,1)S(1)}, u32[]{:S(2)}, u32[]{:S(2)}) collective-permute-start(bf16[64,384]{1,0:T(8,128)(2,1)S(1)} %slice.53), channel_id=1, source_target_pairs={{128,0},{129,1},{130,2},{131,3},{132,4},{133,5},{134,6},{135,7},{1... | collective-permute-start | bytes 147464 | tf_op jit(solution)/shard_map/ppermute | solution.py:27
  116.9 7.3 %collective-permute-start.20 = (bf16[64,384]{1,0:T(8,128)(2,1)S(1)}, bf16[64,384]{1,0:T(8,128)(2,1)S(1)}, u32[]{:S(2)}, u32[]{:S(2)}) collective-permute-start(bf16[64,384]{1,0:T(8,128)(2,1)S(1)} %slice_select_fusion), channel_id=1, source_target_pairs={{0,24},{8,0},{16,8},{24,16},{1,25},{9,1},{17,9},{25,17},{2,26},{10... | collective-permute-start | bytes 147464 | tf_op jit(solution)/shard_map/ppermute | solution.py:23
  120.7 6.9 %collective-permute-start.19 = (bf16[64,384]{1,0:T(8,128)(2,1)S(1)}, bf16[64,384]{1,0:T(8,128)(2,1)S(1)}, u32[]{:S(2)}, u32[]{:S(2)}) collective-permute-start(bf16[64,384]{1,0:T(8,128)(2,1)S(1)} %slice_select_fusion), channel_id=1, source_target_pairs={{0,16},{8,24},{16,0},{24,8},{1,17},{9,25},{17,1},{25,9},{2,18},{10... | collective-permute-start | bytes 147464 | tf_op jit(solution)/shard_map/ppermute | solution.py:23
  121.9 5.7 %collective-permute-start.18 = (bf16[64,384]{1,0:T(8,128)(2,1)S(1)}, bf16[64,384]{1,0:T(8,128)(2,1)S(1)}, u32[]{:S(2)}, u32[]{:S(2)}) collective-permute-start(bf16[64,384]{1,0:T(8,128)(2,1)S(1)} %slice_select_fusion), channel_id=1, source_target_pairs={{0,8},{8,16},{16,24},{24,0},{1,9},{9,17},{17,25},{25,1},{2,10},{10... | collective-permute-start | bytes 147464 | tf_op jit(solution)/shard_map/ppermute | solution.py:23
  127.7 3.0 %collective-permute-start.21 = (bf16[64,384]{1,0:T(8,128)(2,1)S(1)}, bf16[64,384]{1,0:T(8,128)(2,1)S(1)}, u32[]{:S(2)}, u32[]{:S(2)}) collective-permute-start(bf16[64,384]{1,0:T(8,128)(2,1)S(1)} %add_convert_fusion.2.refs_0_), channel_id=1, source_target_pairs={{0,96},{32,0},{64,32},{96,64},{1,97},{33,1},{65,33},{97,65},{2,98}... | collective-permute-start | bytes 147464 | tf_op jit(solution)/shard_map/ppermute | solution.py:23
  128.8 4.5 %collective-permute-start.22 = (bf16[64,384]{1,0:T(8,128)(2,1)S(1)}, bf16[64,384]{1,0:T(8,128)(2,1)S(1)}, u32[]{:S(2)}, u32[]{:S(2)}) collective-permute-start(bf16[64,384]{1,0:T(8,128)(2,1)S(1)} %add_convert_fusion.2.refs_0_), channel_id=1, source_target_pairs={{0,64},{32,96},{64,0},{96,32},{1,65},{33,97},{65,1},{97,33},{2,66}... | collective-permute-start | bytes 147464 | tf_op jit(solution)/shard_map/ppermute | solution.py:23
  129.4 4.4 %collective-permute-start.23 = (bf16[64,384]{1,0:T(8,128)(2,1)S(1)}, bf16[64,384]{1,0:T(8,128)(2,1)S(1)}, u32[]{:S(2)}, u32[]{:S(2)}) collective-permute-start(bf16[64,384]{1,0:T(8,128)(2,1)S(1)} %add_convert_fusion.2.refs_0_), channel_id=1, source_target_pairs={{0,32},{32,64},{64,96},{96,0},{1,33},{33,65},{65,97},{97,1},{2,34}... | collective-permute-start | bytes 147464 | tf_op jit(solution)/shard_map/ppermute | solution.py:23
  133.8 4.9 %collective-permute-start.24 = (bf16[64,1536]{1,0:T(8,128)(2,1)S(1)}, bf16[64,1536]{1,0:T(8,128)(2,1)S(1)}, u32[]{:S(2)}, u32[]{:S(2)}) collective-permute-start(bf16[64,1536]{1,0:T(8,128)(2,1)S(1)} %assemble.3.own_ref), channel_id=1, source_target_pairs={{0,128},{128,0},{1,129},{129,1},{2,130},{130,2},{3,131},{131,3},{4... | collective-permute-start | bytes 589832 | tf_op jit(solution)/shard_map/ppermute | solution.py:23
  140.5 22.7 %all-to-all-start.3 = ((bf16[8,576,128]{2,1,0:T(8,128)(2,1)}), bf16[8,576,128]{2,1,0:T(8,128)(2,1)}, u32[]{:S(2)}, u32[]{:S(2)}) async-start(bf16[8,576,128]{2,1,0:T(8,128)(2,1)} %packed.5), calls=%async_computation.3 | async-start | bytes 2359296 | tf_op jit(solution)/shard_map/all_to_all | solution.py:31
  147.8 1.8 %collective-permute-start.26 = (bf16[8,192,128]{2,1,0:T(8,128)(2,1)S(1)}, bf16[8,192,128]{2,1,0:T(8,128)(2,1)S(1)}, u32[]{:S(2)}, u32[]{:S(2)}) collective-permute-start(bf16[8,192,128]{2,1,0:T(8,128)(2,1)S(1)} %slice.54), channel_id=1, source_target_pairs={{0,128},{128,0},{1,129},{129,1},{2,130},{130,2},{3,131},{131,3},{4... | collective-permute-start | bytes 1179656 | tf_op jit(solution)/shard_map/ppermute | solution.py:23
  156.0 14.1 %collective-permute-start.29 = (bf16[3,192,384]{2,1,0:T(8,128)(2,1)}, bf16[3,192,384]{2,1,0:T(8,128)(2,1)}, u32[]{:S(2)}, u32[]{:S(2)}) collective-permute-start(bf16[3,192,384]{2,1,0:T(8,128)(2,1)} %get-tuple-element.24), channel_id=1, source_target_pairs={{0,128},{1,129},{2,130},{3,131},{4,132},{5,133},{6,134},{7,135},{8... | collective-permute-start | bytes 1327112 | tf_op jit(solution)/shard_map/ppermute | solution.py:27
  167.3 5.1 %collective-permute-start.27 = (bf16[3,192,384]{2,1,0:T(8,128)(2,1)S(1)}, bf16[3,192,384]{2,1,0:T(8,128)(2,1)S(1)}, u32[]{:S(2)}, u32[]{:S(2)}) collective-permute-start(bf16[3,192,384]{2,1,0:T(8,128)(2,1)S(1)} %get-tuple-element.20), channel_id=1, source_target_pairs={{128,0},{129,1},{130,2},{131,3},{132,4},{133,5},{134,6},{135,7},{1... | collective-permute-start | bytes 1327112 | tf_op jit(solution)/shard_map/ppermute | solution.py:27
  (10 other events, 74.6 us)

commit v9 on v8

--- a/solution.py
+++ b/solution.py
@@ -21,6 +21,13 @@
 def shifted(value, axis, distance):
     size = lax.axis_size(axis)
     return lax.ppermute(value, axis, [(i, (i + distance) % size) for i in range(size)])
+
+
+def fanned(value_of, axis, distance_of):
+    out = []
+    for k in range(1, lax.axis_size(axis)):
+        out.append(shifted(value_of(k), axis, distance_of(k)))
+    return out
 
 
 def one_way(value, source):
@@ -371,9 +378,9 @@
     width = partial.shape[1] // XS
     split = partial.shape[0] // CORES
     own = columns_at(partial, x, width)
-    pieces = [
-        shifted(columns_at(partial, (x + k) % XS, width), "x", k) for k in range(1, XS)
-    ]
+    pieces = fanned(
+        lambda k: columns_at(partial, (x + k) % XS, width), "x", lambda k: k
+    )
 
     total = own.astype(F32)
     for piece in pieces:
@@ -382,12 +389,12 @@
     halves = [summed[:split], summed[split:]]
     received = one_way(halves[1 - source], source)
     mine = jnp.where(core == source, halves[source], received)
-    pieces = [shifted(mine, "zh", k) for k in range(1, ZH)]
+    pieces = fanned(lambda k: mine, "zh", lambda k: k)
     total = mine.astype(F32)
     for piece in pieces:
         total = total + piece.astype(F32)
     out = (residual.astype(F32) + total).astype(BF16)
-    blocks = [out] + [shifted(out, "x", XS - k) for k in range(1, XS)]
+    blocks = [out] + fanned(lambda k: out, "x", lambda k: XS - k)
     gathered = assemble(blocks, x_id)
     other = shifted(gathered, "segment", 1)
     return merge(gathered, other, core_id)

time: 173 us -> 173 us (level)
  no operation moved by 1% of the time
where the time goes in v9:
time: 173 us
  starting transfers between devices  59.4 us (34%)
  waiting for transfers between devices  50.5 us (29%)
  blocking collectives  26.1 us (15%)
  Pallas kernels  14.5 us (8%)
  matrix products  9.18 us (5%)
  local copies, waits for them, and re-layouts  8.89 us (5%)
  other arithmetic  2.88 us (2%)
    ppermute x24, waiting for transfers between devices, shifted(): lax.ppermute(value, axis, [(i, (i + distance) % size) for i in range(size)])  42.1 us
    ppermute x24, starting transfers between devices, shifted(): lax.ppermute(value, axis, [(i, (i + distance) % size) for i in range(size)])  29.6 us
    all_to_all x1, blocking collectives, exchanged(): return lax.all_to_all(value, axes, 0, 0, tiled=True)  26.1 us
    all_to_all x3, starting transfers between devices, exchanged(): return lax.all_to_all(value, axes, 0, 0, tiled=True)  15.7 us
    ppermute x6, starting transfers between devices, one_way(): return lax.ppermute(value, 'segment', [(source, 1 - source)])  14.1 us
    pallas_call x2, Pallas kernels, weight_grads(): pl.pallas_call(body, grid=(PEERS // step,), in_specs=[whole(pltpu.SMEM)]...  8.98 us
    all_to_all x3, waiting for transfers between devices, exchanged(): return lax.all_to_all(value, axes, 0, 0, tiled=True)  5.92 us
    unnamed x19, local copies, waits for them, and re-layouts  3.68 us
  transfers between devices with their start and end apart: 33, of which 24 were waited for; matrix products, arithmetic and copies ran while one was open for 8% of the time, Pallas kernels for 8%

profile of v9, /device:TPU:1, one launch (start us, length us, event | category | flops | bytes accessed | tf_op | source)
XLA Modules:
  0.0 172.6 jit_solution(3570995662168531612)
XLA Ops:
  1.6 26.1 %all_to_all.20 = bf16[16,96,128]{2,1,0:T(8,128)(2,1)S(1)} all-to-all(bf16[16,96,128]{2,1,0:T(8,128)(2,1)S(1)} %spread.1), channel_id=1, replica_groups=mesh['segment'=2,'x'=4,'zh'=4,'zl'=2,'y'=4] {'x','zh'}, dimensions={0} | all-to-all | bytes 786432 | tf_op jit(solution)/shard_map/all_to_all | solution.py:38
  27.7 2.3 %fusion.21.refs_1_ = bf16[128,768]{1,0:T(8,128)(2,1)S(1)} fusion(bf16[1536,128]{1,0:T(8,128)(2,1)S(1)} %bitcast.51, bf16[1,1536,768]{2,1,0:T(8,128)(2,1)} %param.7), kind=kOutput, calls=%fused_computation.21 | convolution fusion | flops 302088192 | bytes 2949120 | tf_op jit(solution)/shard_map/dot_general | solution.py:42
  31.5 2.3 %collective-permute-start.13 = (bf16[2,128,384]{2,1,0:T(8,128)(2,1)S(1)}, bf16[2,128,384]{2,1,0:T(8,128)(2,1)S(1)}, u32[]{:S(2)}, u32[]{:S(2)}) collective-permute-start(bf16[2,128,384]{2,1,0:T(8,128)(2,1)S(1)} %picked.3), channel_id=1, source_target_pairs={{0,128},{128,0},{1,129},{129,1},{2,130},{130,2},{3,131},{131,3},{4... | collective-permute-start | bytes 589832 | tf_op jit(solution)/shard_map/ppermute | solution.py:23
  35.3 1.6 copy-done.1
  36.9 4.8 %all-to-all-start.1 = ((bf16[8,1344,128]{2,1,0:T(8,128)(2,1)}), bf16[8,1344,128]{2,1,0:T(8,128)(2,1)}, u32[]{:S(2)}, u32[]{:S(2)}) async-start(bf16[8,1344,128]{2,1,0:T(8,128)(2,1)} %copy-done.1), calls=%async_computation.1 | async-start | bytes 5505024 | tf_op jit(solution)/shard_map/all_to_all | solution.py:38
  41.7 2.2 %convolution_convert_fusion = bf16[128,1536]{1,0:T(8,128)(2,1)S(1)} fusion(bf16[1,768,1536]{2,1,0:T(8,128)(2,1)} %param.8, bf16[128,768]{1,0:T(8,128)(2,1)S(1)} %fusion.21.refs_1_, bf16[128,768]{1,0:T(8,128)(2,1)S(1)} %fusion.15.refs_0_), kind=kOutput, calls=%fused_computation.2 | convolution fusion | flops 302972928 | bytes 3145728 | tf_op jit(solution)/shard_map/dot_general | solution.py:50
  46.3 2.5 %collective-permute-done.3 = bf16[128,384]{1,0:T(8,128)(2,1)S(1)} collective-permute-done((bf16[128,384]{1,0:T(8,128)(2,1)}, bf16[128,384]{1,0:T(8,128)(2,1)S(1)}, u32[]{:S(2)}, u32[]{:S(2)}) %collective-permute-start.3) | collective-permute-done | bytes 98336 | tf_op jit(solution)/shard_map/ppermute | solution.py:23
  48.8 2.1 %collective-permute-done.2 = bf16[128,384]{1,0:T(8,128)(2,1)S(1)} collective-permute-done((bf16[128,384]{1,0:T(8,128)(2,1)}, bf16[128,384]{1,0:T(8,128)(2,1)S(1)}, u32[]{:S(2)}, u32[]{:S(2)}) %collective-permute-start.2) | collective-permute-done | bytes 98336 | tf_op jit(solution)/shard_map/ppermute | solution.py:23
  50.9 2.6 %collective-permute-done.1 = bf16[128,384]{1,0:T(8,128)(2,1)S(1)} collective-permute-done((bf16[128,384]{1,0:T(8,128)(2,1)S(1)}, bf16[128,384]{1,0:T(8,128)(2,1)S(1)}, u32[]{:S(2)}, u32[]{:S(2)}) %collective-permute-start.1) | collective-permute-done | bytes 98336 | tf_op jit(solution)/shard_map/ppermute | solution.py:23
  57.8 3.8 %collective-permute-start.6 = (bf16[64,384]{1,0:T(8,128)(2,1)S(1)}, bf16[64,384]{1,0:T(8,128)(2,1)S(1)}, u32[]{:S(2)}, u32[]{:S(2)}) collective-permute-start(bf16[64,384]{1,0:T(8,128)(2,1)S(1)} %slice_select_fusion.1), channel_id=1, source_target_pairs={{0,16},{8,24},{16,0},{24,8},{1,17},{9,25},{17,1},{25,9},{2,18},{10... | collective-permute-start | bytes 147464 | tf_op jit(solution)/shard_map/ppermute | solution.py:23
  61.9 11.9 %collective-permute-done.6 = bf16[64,384]{1,0:T(8,128)(2,1)S(1)} collective-permute-done((bf16[64,384]{1,0:T(8,128)(2,1)S(1)}, bf16[64,384]{1,0:T(8,128)(2,1)S(1)}, u32[]{:S(2)}, u32[]{:S(2)}) %collective-permute-start.6) | collective-permute-done | bytes 49184 | tf_op jit(solution)/shard_map/ppermute | solution.py:23
  73.8 2.1 %collective-permute-done.5 = bf16[64,384]{1,0:T(8,128)(2,1)S(1)} collective-permute-done((bf16[64,384]{1,0:T(8,128)(2,1)S(1)}, bf16[64,384]{1,0:T(8,128)(2,1)S(1)}, u32[]{:S(2)}, u32[]{:S(2)}) %collective-permute-start.5) | collective-permute-done | bytes 49184 | tf_op jit(solution)/shard_map/ppermute | solution.py:23
  79.0 2.4 %collective-permute-done.9.refs_2_ = bf16[64,384]{1,0:T(8,128)(2,1)S(1)} collective-permute-done((bf16[64,384]{1,0:T(8,128)(2,1)S(1)}, bf16[64,384]{1,0:T(8,128)(2,1)S(1)}, u32[]{:S(2)}, u32[]{:S(2)}) %collective-permute-start.9) | collective-permute-done | bytes 49184 | tf_op jit(solution)/shard_map/ppermute | solution.py:23
  82.5 3.3 %collective-permute-start.11 = (bf16[64,1536]{1,0:T(8,128)(2,1)S(1)}, bf16[64,1536]{1,0:T(8,128)(2,1)S(1)}, u32[]{:S(2)}, u32[]{:S(2)}) collective-permute-start(bf16[64,1536]{1,0:T(8,128)(2,1)S(1)} %assemble.2.own_ref), channel_id=1, source_target_pairs={{0,128},{128,0},{1,129},{129,1},{2,130},{130,2},{3,131},{131,3},{4... | collective-permute-start | bytes 589832 | tf_op jit(solution)/shard_map/ppermute | solution.py:23
  87.9 2.3 %collective-permute-start.12 = (bf16[2,128,384]{2,1,0:T(8,128)(2,1)S(1)}, bf16[2,128,384]{2,1,0:T(8,128)(2,1)S(1)}, u32[]{:S(2)}, u32[]{:S(2)}) collective-permute-start(bf16[2,128,384]{2,1,0:T(8,128)(2,1)S(1)} %picked.2), channel_id=1, source_target_pairs={{128,0},{129,1},{130,2},{131,3},{132,4},{133,5},{134,6},{135,7},{1... | collective-permute-start | bytes 589832 | tf_op jit(solution)/shard_map/ppermute | solution.py:34
  92.9 4.6 %all-to-all-start.2 = ((bf16[8,864,128]{2,1,0:T(8,128)(2,1)}), bf16[8,864,128]{2,1,0:T(8,128)(2,1)}, u32[]{:S(2)}, u32[]{:S(2)}) async-start(bf16[8,864,128]{2,1,0:T(8,128)(2,1)} %copy-done.2), calls=%async_computation.2 | async-start | bytes 3538944 | tf_op jit(solution)/shard_map/all_to_all | solution.py:38
  97.6 2.4 %slice_bitcast_fusion = bf16[384,1536]{1,0:T(8,128)(2,1)} fusion(bf16[1,768,1536]{2,1,0:T(8,128)(2,1)} %param.8), kind=kLoop, calls=%fused_computation.18 | loop fusion | bytes 2359296 | tf_op jit(solution)/shard_map/slice | solution.py:416
  105.0 2.2 %collective-permute-done.16 = bf16[128,384]{1,0:T(8,128)(2,1)S(1)} collective-permute-done((bf16[128,384]{1,0:T(8,128)(2,1)S(1)}, bf16[128,384]{1,0:T(8,128)(2,1)S(1)}, u32[]{:S(2)}, u32[]{:S(2)}) %collective-permute-start.16) | collective-permute-done | bytes 98336 | tf_op jit(solution)/shard_map/ppermute | solution.py:23
  107.2 2.5 %collective-permute-done.15 = bf16[128,384]{1,0:T(8,128)(2,1)S(1)} collective-permute-done((bf16[128,384]{1,0:T(8,128)(2,1)S(1)}, bf16[128,384]{1,0:T(8,128)(2,1)S(1)}, u32[]{:S(2)}, u32[]{:S(2)}) %collective-permute-start.15) | collective-permute-done | bytes 98336 | tf_op jit(solution)/shard_map/ppermute | solution.py:23
  110.8 5.2 %collective-permute-start.17 = (bf16[64,384]{1,0:T(8,128)(2,1)S(1)}, bf16[64,384]{1,0:T(8,128)(2,1)S(1)}, u32[]{:S(2)}, u32[]{:S(2)}) collective-permute-start(bf16[64,384]{1,0:T(8,128)(2,1)S(1)} %slice.53), channel_id=1, source_target_pairs={{128,0},{129,1},{130,2},{131,3},{132,4},{133,5},{134,6},{135,7},{1... | collective-permute-start | bytes 147464 | tf_op jit(solution)/shard_map/ppermute | solution.py:34
  116.9 3.9 %collective-permute-start.20 = (bf16[64,384]{1,0:T(8,128)(2,1)S(1)}, bf16[64,384]{1,0:T(8,128)(2,1)S(1)}, u32[]{:S(2)}, u32[]{:S(2)}) collective-permute-start(bf16[64,384]{1,0:T(8,128)(2,1)S(1)} %slice_select_fusion), channel_id=1, source_target_pairs={{0,24},{8,0},{16,8},{24,16},{1,25},{9,1},{17,9},{25,17},{2,26},{10... | collective-permute-start | bytes 147464 | tf_op jit(solution)/shard_map/ppermute | solution.py:23
  121.9 2.3 %collective-permute-start.18 = (bf16[64,384]{1,0:T(8,128)(2,1)S(1)}, bf16[64,384]{1,0:T(8,128)(2,1)S(1)}, u32[]{:S(2)}, u32[]{:S(2)}) collective-permute-start(bf16[64,384]{1,0:T(8,128)(2,1)S(1)} %slice_select_fusion), channel_id=1, source_target_pairs={{0,8},{8,16},{16,24},{24,0},{1,9},{9,17},{17,25},{25,1},{2,10},{10... | collective-permute-start | bytes 147464 | tf_op jit(solution)/shard_map/ppermute | solution.py:23
  124.2 3.4 %collective-permute-done.19 = bf16[64,384]{1,0:T(8,128)(2,1)S(1)} collective-permute-done((bf16[64,384]{1,0:T(8,128)(2,1)S(1)}, bf16[64,384]{1,0:T(8,128)(2,1)S(1)}, u32[]{:S(2)}, u32[]{:S(2)}) %collective-permute-start.19) | collective-permute-done | bytes 49184 | tf_op jit(solution)/shard_map/ppermute | solution.py:23
  130.7 2.6 %collective-permute-done.22.refs_2_ = bf16[64,384]{1,0:T(8,128)(2,1)S(1)} collective-permute-done((bf16[64,384]{1,0:T(8,128)(2,1)S(1)}, bf16[64,384]{1,0:T(8,128)(2,1)S(1)}, u32[]{:S(2)}, u32[]{:S(2)}) %collective-permute-start.22) | collective-permute-done | bytes 49184 | tf_op jit(solution)/shard_map/ppermute | solution.py:23
  133.8 3.2 %collective-permute-start.24 = (bf16[64,1536]{1,0:T(8,128)(2,1)S(1)}, bf16[64,1536]{1,0:T(8,128)(2,1)S(1)}, u32[]{:S(2)}, u32[]{:S(2)}) collective-permute-start(bf16[64,1536]{1,0:T(8,128)(2,1)S(1)} %assemble.3.own_ref), channel_id=1, source_target_pairs={{0,128},{128,0},{1,129},{129,1},{2,130},{130,2},{3,131},{131,3},{4... | collective-permute-start | bytes 589832 | tf_op jit(solution)/shard_map/ppermute | solution.py:23
  137.0 1.8 %bitcast_select_fusion = bf16[384,1536]{1,0:T(8,128)(2,1)S(1)} fusion(bf16[384,1536]{1,0:T(8,128)(2,1)} %collective-permute-done.25, bf16[1,768,1536]{2,1,0:T(8,128)(2,1)} %param.8, pred[]{:T(512)S(6)} %eq.17), kind=kLoop, calls=%fused_computation.17 | loop fusion | flops 589824 | bytes 3538945 | tf_op jit(solution)/shard_map/jit(_where)/select_n | solution.py:417
  140.5 6.2 %all-to-all-start.3 = ((bf16[8,576,128]{2,1,0:T(8,128)(2,1)}), bf16[8,576,128]{2,1,0:T(8,128)(2,1)}, u32[]{:S(2)}, u32[]{:S(2)}) async-start(bf16[8,576,128]{2,1,0:T(8,128)(2,1)} %packed.5), calls=%async_computation.3 | async-start | bytes 2359296 | tf_op jit(solution)/shard_map/all_to_all | solution.py:38
  151.2 4.9 %shard_map.77 = (f32[3,192,384]{2,1,0:T(8,128)S(1)}, bf16[3,192,384]{2,1,0:T(8,128)(2,1)}) custom-call(s32[1]{0:T(128)} %bitcast.core_ref, bf16[8,864,128]{2,1,0:T(8,128)(2,1)} %all-to-all-done.2.refs_0_.refs_1_.refs_3_, bf16[8,864,128]{2,1,0:T(8,128)(2,1)} %all-to-all-done.2.refs_0_.refs_1_.refs_3_, ...), custom_call_target="tpu_custom_call" | custom-call | tf_op jit(solution)/shard_map/pallas_call | solution.py:306
  157.3 5.9 %all-to-all-done.3.refs_2_.refs_5_ = bf16[8,576,128]{2,1,0:T(8,128)(2,1)} async-done(((bf16[8,576,128]{2,1,0:T(8,128)(2,1)}), bf16[8,576,128]{2,1,0:T(8,128)(2,1)}, u32[]{:S(2)}, u32[]{:S(2)}) %all-to-all-start.3) | async-done | bytes 1179680 | tf_op jit(solution)/shard_map/all_to_all | solution.py:38
  163.2 4.1 %shard_map.76 = (f32[3,192,384]{2,1,0:T(8,128)S(1)}, bf16[3,192,384]{2,1,0:T(8,128)(2,1)S(1)}) custom-call(s32[1]{0:T(128)} %bitcast.core_ref, bf16[8,1344,128]{2,1,0:T(8,128)(2,1)} %all-to-all-done.1.refs_0_.refs_1_.refs_3_.refs_2_.refs_5_, bf16[8,1344,128]{2,1,0:T(8,128)(2,1)} %all-to-all-done.1.refs_0_.refs_1_.refs_3_.refs_2_.refs_5_, ...), custom_call_target="tpu_custom_call" | custom-call | tf_op jit(solution)/shard_map/pallas_call | solution.py:306
  167.3 2.7 %collective-permute-start.27 = (bf16[3,192,384]{2,1,0:T(8,128)(2,1)S(1)}, bf16[3,192,384]{2,1,0:T(8,128)(2,1)S(1)}, u32[]{:S(2)}, u32[]{:S(2)}) collective-permute-start(bf16[3,192,384]{2,1,0:T(8,128)(2,1)S(1)} %get-tuple-element.20), channel_id=1, source_target_pairs={{128,0},{129,1},{130,2},{131,3},{132,4},{133,5},{134,6},{135,7},{1... | collective-permute-start | bytes 1327112 | tf_op jit(solution)/shard_map/ppermute | solution.py:34
  170.1 2.3 %early_out.1 = (f32[192,768]{1,0:T(8,128)}, f32[192,768]{1,0:T(8,128)}, f32[192,768]{1,0:T(8,128)}) custom-call(s32[1]{0:T(128)} %bitcast.core_ref, f32[3,192,384]{2,1,0:T(8,128)S(1)} %get-tuple-element.21.own_0_ref, f32[3,192,384]{2,1,0:T(8,128)S(1)} %get-tuple-element.23.own_1_ref, bf16[3,192,384]{2,1,0:T(8,128)(2,1)} %collective-permute-done.29.got_1_ref), custom_call_target="tpu_custom_call" | custom-call | tf_op jit(solution)/shard_map/early_out/pallas_call | solution.py:332
  (93 shorter events, 39.1 us)
Async XLA Ops:
  31.5 3.4 %collective-permute-start.13 = (bf16[2,128,384]{2,1,0:T(8,128)(2,1)S(1)}, bf16[2,128,384]{2,1,0:T(8,128)(2,1)S(1)}, u32[]{:S(2)}, u32[]{:S(2)}) collective-permute-start(bf16[2,128,384]{2,1,0:T(8,128)(2,1)S(1)} %picked.3), channel_id=1, source_target_pairs={{0,128},{128,0},{1,129},{129,1},{2,130},{130,2},{3,131},{131,3},{4... | collective-permute-start | bytes 589832 | tf_op jit(solution)/shard_map/ppermute | solution.py:23
  36.9 56.0 %all-to-all-start.1 = ((bf16[8,1344,128]{2,1,0:T(8,128)(2,1)}), bf16[8,1344,128]{2,1,0:T(8,128)(2,1)}, u32[]{:S(2)}, u32[]{:S(2)}) async-start(bf16[8,1344,128]{2,1,0:T(8,128)(2,1)} %copy-done.1), calls=%async_computation.1 | async-start | bytes 5505024 | tf_op jit(solution)/shard_map/all_to_all | solution.py:38
  44.7 4.1 %collective-permute-start.3 = (bf16[128,384]{1,0:T(8,128)(2,1)}, bf16[128,384]{1,0:T(8,128)(2,1)S(1)}, u32[]{:S(2)}, u32[]{:S(2)}) collective-permute-start(bf16[128,384]{1,0:T(8,128)(2,1)} %get-tuple-element.35), channel_id=1, source_target_pairs={{0,96},{32,0},{64,32},{96,64},{1,97},{33,1},{65,33},{97,65},{2,98}... | collective-permute-start | bytes 294920 | tf_op jit(solution)/shard_map/ppermute | solution.py:23
  45.3 5.6 %collective-permute-start.2 = (bf16[128,384]{1,0:T(8,128)(2,1)}, bf16[128,384]{1,0:T(8,128)(2,1)S(1)}, u32[]{:S(2)}, u32[]{:S(2)}) collective-permute-start(bf16[128,384]{1,0:T(8,128)(2,1)} %get-tuple-element.36), channel_id=1, source_target_pairs={{0,64},{32,96},{64,0},{96,32},{1,65},{33,97},{65,1},{97,33},{2,66}... | collective-permute-start | bytes 294920 | tf_op jit(solution)/shard_map/ppermute | solution.py:23
  45.8 7.7 %collective-permute-start.1 = (bf16[128,384]{1,0:T(8,128)(2,1)S(1)}, bf16[128,384]{1,0:T(8,128)(2,1)S(1)}, u32[]{:S(2)}, u32[]{:S(2)}) collective-permute-start(bf16[128,384]{1,0:T(8,128)(2,1)S(1)} %get-tuple-element.34), channel_id=1, source_target_pairs={{0,32},{32,64},{64,96},{96,0},{1,33},{33,65},{65,97},{97,1},{2,34}... | collective-permute-start | bytes 294920 | tf_op jit(solution)/shard_map/ppermute | solution.py:23
  54.5 3.1 %collective-permute-start.4 = (bf16[64,384]{1,0:T(8,128)(2,1)S(1)}, bf16[64,384]{1,0:T(8,128)(2,1)S(1)}, u32[]{:S(2)}, u32[]{:S(2)}) collective-permute-start(bf16[64,384]{1,0:T(8,128)(2,1)S(1)} %slice.51), channel_id=1, source_target_pairs={{0,128},{1,129},{2,130},{3,131},{4,132},{5,133},{6,134},{7,135},{8... | collective-permute-start | bytes 147464 | tf_op jit(solution)/shard_map/ppermute | solution.py:34
  55.8 5.8 %collective-permute-start = (bf16[64,384]{1,0:T(8,128)(2,1)S(1)}, bf16[64,384]{1,0:T(8,128)(2,1)S(1)}, u32[]{:S(2)}, u32[]{:S(2)}) collective-permute-start(bf16[64,384]{1,0:T(8,128)(2,1)S(1)} %broadcast_select_fusion), channel_id=1, source_target_pairs={{0,128},{128,0},{1,129},{129,1},{2,130},{130,2},{3,131},{131,3},{4... | collective-permute-start | bytes 147464 | tf_op jit(solution)/shard_map/ppermute | solution.py:23
  57.6 4.3 %collective-permute-start.7 = (bf16[64,384]{1,0:T(8,128)(2,1)S(1)}, bf16[64,384]{1,0:T(8,128)(2,1)S(1)}, u32[]{:S(2)}, u32[]{:S(2)}) collective-permute-start(bf16[64,384]{1,0:T(8,128)(2,1)S(1)} %slice_select_fusion.1), channel_id=1, source_target_pairs={{0,24},{8,0},{16,8},{24,16},{1,25},{9,1},{17,9},{25,17},{2,26},{10... | collective-permute-start | bytes 147464 | tf_op jit(solution)/shard_map/ppermute | solution.py:23
  57.8 16.0 %collective-permute-start.6 = (bf16[64,384]{1,0:T(8,128)(2,1)S(1)}, bf16[64,384]{1,0:T(8,128)(2,1)S(1)}, u32[]{:S(2)}, u32[]{:S(2)}) collective-permute-start(bf16[64,384]{1,0:T(8,128)(2,1)S(1)} %slice_select_fusion.1), channel_id=1, source_target_pairs={{0,16},{8,24},{16,0},{24,8},{1,17},{9,25},{17,1},{25,9},{2,18},{10... | collective-permute-start | bytes 147464 | tf_op jit(solution)/shard_map/ppermute | solution.py:23
  61.6 14.4 %collective-permute-start.5 = (bf16[64,384]{1,0:T(8,128)(2,1)S(1)}, bf16[64,384]{1,0:T(8,128)(2,1)S(1)}, u32[]{:S(2)}, u32[]{:S(2)}) collective-permute-start(bf16[64,384]{1,0:T(8,128)(2,1)S(1)} %slice_select_fusion.1), channel_id=1, source_target_pairs={{0,8},{8,16},{16,24},{24,0},{1,9},{9,17},{17,25},{25,1},{2,10},{10... | collective-permute-start | bytes 147464 | tf_op jit(solution)/shard_map/ppermute | solution.py:23
  76.0 3.0 %collective-permute-start.8 = (bf16[64,384]{1,0:T(8,128)(2,1)S(1)}, bf16[64,384]{1,0:T(8,128)(2,1)S(1)}, u32[]{:S(2)}, u32[]{:S(2)}) collective-permute-start(bf16[64,384]{1,0:T(8,128)(2,1)S(1)} %add_convert_fusion.3.refs_0_), channel_id=1, source_target_pairs={{0,96},{32,0},{64,32},{96,64},{1,97},{33,1},{65,33},{97,65},{2,98}... | collective-permute-start | bytes 147464 | tf_op jit(solution)/shard_map/ppermute | solution.py:23
  77.0 4.4 %collective-permute-start.9 = (bf16[64,384]{1,0:T(8,128)(2,1)S(1)}, bf16[64,384]{1,0:T(8,128)(2,1)S(1)}, u32[]{:S(2)}, u32[]{:S(2)}) collective-permute-start(bf16[64,384]{1,0:T(8,128)(2,1)S(1)} %add_convert_fusion.3.refs_0_), channel_id=1, source_target_pairs={{0,64},{32,96},{64,0},{96,32},{1,65},{33,97},{65,1},{97,33},{2,66}... | collective-permute-start | bytes 147464 | tf_op jit(solution)/shard_map/ppermute | solution.py:23
  78.3 4.2 %collective-permute-start.10 = (bf16[64,384]{1,0:T(8,128)(2,1)S(1)}, bf16[64,384]{1,0:T(8,128)(2,1)S(1)}, u32[]{:S(2)}, u32[]{:S(2)}) collective-permute-start(bf16[64,384]{1,0:T(8,128)(2,1)S(1)} %add_convert_fusion.3.refs_0_), channel_id=1, source_target_pairs={{0,32},{32,64},{64,96},{96,0},{1,33},{33,65},{65,97},{97,1},{2,34}... | collective-permute-start | bytes 147464 | tf_op jit(solution)/shard_map/ppermute | solution.py:23
  82.5 4.4 %collective-permute-start.11 = (bf16[64,1536]{1,0:T(8,128)(2,1)S(1)}, bf16[64,1536]{1,0:T(8,128)(2,1)S(1)}, u32[]{:S(2)}, u32[]{:S(2)}) collective-permute-start(bf16[64,1536]{1,0:T(8,128)(2,1)S(1)} %assemble.2.own_ref), channel_id=1, source_target_pairs={{0,128},{128,0},{1,129},{129,1},{2,130},{130,2},{3,131},{131,3},{4... | collective-permute-start | bytes 589832 | tf_op jit(solution)/shard_map/ppermute | solution.py:23
  87.9 3.3 %collective-permute-start.12 = (bf16[2,128,384]{2,1,0:T(8,128)(2,1)S(1)}, bf16[2,128,384]{2,1,0:T(8,128)(2,1)S(1)}, u32[]{:S(2)}, u32[]{:S(2)}) collective-permute-start(bf16[2,128,384]{2,1,0:T(8,128)(2,1)S(1)} %picked.2), channel_id=1, source_target_pairs={{128,0},{129,1},{130,2},{131,3},{132,4},{133,5},{134,6},{135,7},{1... | collective-permute-start | bytes 589832 | tf_op jit(solution)/shard_map/ppermute | solution.py:34
  92.9 47.6 %all-to-all-start.2 = ((bf16[8,864,128]{2,1,0:T(8,128)(2,1)}), bf16[8,864,128]{2,1,0:T(8,128)(2,1)}, u32[]{:S(2)}, u32[]{:S(2)}) async-start(bf16[8,864,128]{2,1,0:T(8,128)(2,1)} %copy-done.2), calls=%async_computation.2 | async-start | bytes 3538944 | tf_op jit(solution)/shard_map/all_to_all | solution.py:38
  99.9 37.0 %collective-permute-start.25 = (bf16[384,1536]{1,0:T(8,128)(2,1)}, bf16[384,1536]{1,0:T(8,128)(2,1)}, u32[]{:S(2)}, u32[]{:S(2)}) collective-permute-start(bf16[384,1536]{1,0:T(8,128)(2,1)} %slice_bitcast_fusion), channel_id=1, source_target_pairs={{0,128},{1,129},{2,130},{3,131},{4,132},{5,133},{6,134},{7,135},{8... | collective-permute-start | bytes 3538952 | tf_op jit(solution)/shard_map/ppermute | solution.py:34
  103.2 3.9 %collective-permute-start.16 = (bf16[128,384]{1,0:T(8,128)(2,1)S(1)}, bf16[128,384]{1,0:T(8,128)(2,1)S(1)}, u32[]{:S(2)}, u32[]{:S(2)}) collective-permute-start(bf16[128,384]{1,0:T(8,128)(2,1)S(1)} %get-tuple-element.32), channel_id=1, source_target_pairs={{0,96},{32,0},{64,32},{96,64},{1,97},{33,1},{65,33},{97,65},{2,98}... | collective-permute-start | bytes 294920 | tf_op jit(solution)/shard_map/ppermute | solution.py:23
  104.3 5.4 %collective-permute-start.15 = (bf16[128,384]{1,0:T(8,128)(2,1)S(1)}, bf16[128,384]{1,0:T(8,128)(2,1)S(1)}, u32[]{:S(2)}, u32[]{:S(2)}) collective-permute-start(bf16[128,384]{1,0:T(8,128)(2,1)S(1)} %get-tuple-element.33), channel_id=1, source_target_pairs={{0,64},{32,96},{64,0},{96,32},{1,65},{33,97},{65,1},{97,33},{2,66}... | collective-permute-start | bytes 294920 | tf_op jit(solution)/shard_map/ppermute | solution.py:23
  104.9 5.8 %collective-permute-start.14 = (bf16[128,384]{1,0:T(8,128)(2,1)S(1)}, bf16[128,384]{1,0:T(8,128)(2,1)S(1)}, u32[]{:S(2)}, u32[]{:S(2)}) collective-permute-start(bf16[128,384]{1,0:T(8,128)(2,1)S(1)} %get-tuple-element.31), channel_id=1, source_target_pairs={{0,32},{32,64},{64,96},{96,0},{1,33},{33,65},{65,97},{97,1},{2,34}... | collective-permute-start | bytes 294920 | tf_op jit(solution)/shard_map/ppermute | solution.py:23
  110.8 6.0 %collective-permute-start.17 = (bf16[64,384]{1,0:T(8,128)(2,1)S(1)}, bf16[64,384]{1,0:T(8,128)(2,1)S(1)}, u32[]{:S(2)}, u32[]{:S(2)}) collective-permute-start(bf16[64,384]{1,0:T(8,128)(2,1)S(1)} %slice.53), channel_id=1, source_target_pairs={{128,0},{129,1},{130,2},{131,3},{132,4},{133,5},{134,6},{135,7},{1... | collective-permute-start | bytes 147464 | tf_op jit(solution)/shard_map/ppermute | solution.py:34
  116.9 7.3 %collective-permute-start.20 = (bf16[64,384]{1,0:T(8,128)(2,1)S(1)}, bf16[64,384]{1,0:T(8,128)(2,1)S(1)}, u32[]{:S(2)}, u32[]{:S(2)}) collective-permute-start(bf16[64,384]{1,0:T(8,128)(2,1)S(1)} %slice_select_fusion), channel_id=1, source_target_pairs={{0,24},{8,0},{16,8},{24,16},{1,25},{9,1},{17,9},{25,17},{2,26},{10... | collective-permute-start | bytes 147464 | tf_op jit(solution)/shard_map/ppermute | solution.py:23
  120.7 6.9 %collective-permute-start.19 = (bf16[64,384]{1,0:T(8,128)(2,1)S(1)}, bf16[64,384]{1,0:T(8,128)(2,1)S(1)}, u32[]{:S(2)}, u32[]{:S(2)}) collective-permute-start(bf16[64,384]{1,0:T(8,128)(2,1)S(1)} %slice_select_fusion), channel_id=1, source_target_pairs={{0,16},{8,24},{16,0},{24,8},{1,17},{9,25},{17,1},{25,9},{2,18},{10... | collective-permute-start | bytes 147464 | tf_op jit(solution)/shard_map/ppermute | solution.py:23
  121.9 5.7 %collective-permute-start.18 = (bf16[64,384]{1,0:T(8,128)(2,1)S(1)}, bf16[64,384]{1,0:T(8,128)(2,1)S(1)}, u32[]{:S(2)}, u32[]{:S(2)}) collective-permute-start(bf16[64,384]{1,0:T(8,128)(2,1)S(1)} %slice_select_fusion), channel_id=1, source_target_pairs={{0,8},{8,16},{16,24},{24,0},{1,9},{9,17},{17,25},{25,1},{2,10},{10... | collective-permute-start | bytes 147464 | tf_op jit(solution)/shard_map/ppermute | solution.py:23
  127.7 3.0 %collective-permute-start.21 = (bf16[64,384]{1,0:T(8,128)(2,1)S(1)}, bf16[64,384]{1,0:T(8,128)(2,1)S(1)}, u32[]{:S(2)}, u32[]{:S(2)}) collective-permute-start(bf16[64,384]{1,0:T(8,128)(2,1)S(1)} %add_convert_fusion.2.refs_0_), channel_id=1, source_target_pairs={{0,96},{32,0},{64,32},{96,64},{1,97},{33,1},{65,33},{97,65},{2,98}... | collective-permute-start | bytes 147464 | tf_op jit(solution)/shard_map/ppermute | solution.py:23
  128.8 4.5 %collective-permute-start.22 = (bf16[64,384]{1,0:T(8,128)(2,1)S(1)}, bf16[64,384]{1,0:T(8,128)(2,1)S(1)}, u32[]{:S(2)}, u32[]{:S(2)}) collective-permute-start(bf16[64,384]{1,0:T(8,128)(2,1)S(1)} %add_convert_fusion.2.refs_0_), channel_id=1, source_target_pairs={{0,64},{32,96},{64,0},{96,32},{1,65},{33,97},{65,1},{97,33},{2,66}... | collective-permute-start | bytes 147464 | tf_op jit(solution)/shard_map/ppermute | solution.py:23
  129.4 4.4 %collective-permute-start.23 = (bf16[64,384]{1,0:T(8,128)(2,1)S(1)}, bf16[64,384]{1,0:T(8,128)(2,1)S(1)}, u32[]{:S(2)}, u32[]{:S(2)}) collective-permute-start(bf16[64,384]{1,0:T(8,128)(2,1)S(1)} %add_convert_fusion.2.refs_0_), channel_id=1, source_target_pairs={{0,32},{32,64},{64,96},{96,0},{1,33},{33,65},{65,97},{97,1},{2,34}... | collective-permute-start | bytes 147464 | tf_op jit(solution)/shard_map/ppermute | solution.py:23
  133.8 4.9 %collective-permute-start.24 = (bf16[64,1536]{1,0:T(8,128)(2,1)S(1)}, bf16[64,1536]{1,0:T(8,128)(2,1)S(1)}, u32[]{:S(2)}, u32[]{:S(2)}) collective-permute-start(bf16[64,1536]{1,0:T(8,128)(2,1)S(1)} %assemble.3.own_ref), channel_id=1, source_target_pairs={{0,128},{128,0},{1,129},{129,1},{2,130},{130,2},{3,131},{131,3},{4... | collective-permute-start | bytes 589832 | tf_op jit(solution)/shard_map/ppermute | solution.py:23
  140.5 22.7 %all-to-all-start.3 = ((bf16[8,576,128]{2,1,0:T(8,128)(2,1)}), bf16[8,576,128]{2,1,0:T(8,128)(2,1)}, u32[]{:S(2)}, u32[]{:S(2)}) async-start(bf16[8,576,128]{2,1,0:T(8,128)(2,1)} %packed.5), calls=%async_computation.3 | async-start | bytes 2359296 | tf_op jit(solution)/shard_map/all_to_all | solution.py:38
  147.8 1.8 %collective-permute-start.26 = (bf16[8,192,128]{2,1,0:T(8,128)(2,1)S(1)}, bf16[8,192,128]{2,1,0:T(8,128)(2,1)S(1)}, u32[]{:S(2)}, u32[]{:S(2)}) collective-permute-start(bf16[8,192,128]{2,1,0:T(8,128)(2,1)S(1)} %slice.54), channel_id=1, source_target_pairs={{0,128},{128,0},{1,129},{129,1},{2,130},{130,2},{3,131},{131,3},{4... | collective-permute-start | bytes 1179656 | tf_op jit(solution)/shard_map/ppermute | solution.py:23
  156.0 14.1 %collective-permute-start.29 = (bf16[3,192,384]{2,1,0:T(8,128)(2,1)}, bf16[3,192,384]{2,1,0:T(8,128)(2,1)}, u32[]{:S(2)}, u32[]{:S(2)}) collective-permute-start(bf16[3,192,384]{2,1,0:T(8,128)(2,1)} %get-tuple-element.24), channel_id=1, source_target_pairs={{0,128},{1,129},{2,130},{3,131},{4,132},{5,133},{6,134},{7,135},{8... | collective-permute-start | bytes 1327112 | tf_op jit(solution)/shard_map/ppermute | solution.py:34
  167.3 5.1 %collective-permute-start.27 = (bf16[3,192,384]{2,1,0:T(8,128)(2,1)S(1)}, bf16[3,192,384]{2,1,0:T(8,128)(2,1)S(1)}, u32[]{:S(2)}, u32[]{:S(2)}) collective-permute-start(bf16[3,192,384]{2,1,0:T(8,128)(2,1)S(1)} %get-tuple-element.20), channel_id=1, source_target_pairs={{128,0},{129,1},{130,2},{131,3},{132,4},{133,5},{134,6},{135,7},{1... | collective-permute-start | bytes 1327112 | tf_op jit(solution)/shard_map/ppermute | solution.py:34
  (10 other events, 74.6 us)

commit v10 on v9

--- a/solution.py
+++ b/solution.py
@@ -4,6 +4,7 @@
 from jax.experimental import pallas as pl
 from jax.experimental.pallas import tpu as pltpu
 from jax.sharding import Mesh, PartitionSpec as P
+
 
 CORES = 2
 XS = 4
@@ -313,6 +314,113 @@
     )(core, *[pltpu.with_memory_space_constraint(v, pltpu.HBM) for v in values])
 
 
+def packed_late(d_hidden, upstream, place):
+    rows, half = d_hidden.shape
+    features = upstream.shape[1]
+    shard = features // PEERS
+    tiles = half // LANES
+
+    def body(place_ref, grad_ref, up_ref, *refs):
+        outs = refs[:PEERS]
+        turned_ref = refs[PEERS]
+        for t in range(features // LANES):
+            at = slice(t * LANES, (t + 1) * LANES)
+            turned_ref[at, :] = up_ref[:, at].T
+        for k in range(PEERS):
+            for t in range(tiles):
+                outs[k][t * rows : (t + 1) * rows, :] = grad_ref[:, t * LANES : (t + 1) * LANES]
+            start = pl.multiple_of(((place_ref[1] + k) % PEERS) * shard, 64)
+            outs[k][tiles * rows :, :] = turned_ref[pl.ds(start, shard), :]
+
+    shape = jax.ShapeDtypeStruct((tiles * rows + shard, rows), BF16)
+    return pl.pallas_call(
+        body,
+        in_specs=[whole(pltpu.SMEM), whole(), whole()],
+        out_specs=[whole()] * PEERS,
+        out_shape=[shape] * PEERS,
+        scratch_shapes=[pltpu.VMEM((features, rows), BF16)],
+        compiler_params=limits(4),
+        name="packed_late",
+    )(place, d_hidden, upstream)
+
+
+def last_grads(wide, other, late, place):
+    peers, height, lanes = wide.shape
+    shard = other.shape[1]
+    half = 3 * lanes
+    step = 2
+
+    def at_place(index, k):
+        return lambda p, place_ref: ((place_ref[1] + 2 * peers - step * p - k) % peers, index, 0)
+
+    specs = []
+    values = []
+    for k in range(step):
+        for index in (0, 1):
+            specs.append(pl.BlockSpec((1, half, lanes), at_place(index, k)))
+            values.append(wide)
+        specs.append(pl.BlockSpec((1, shard, lanes), at_place((height - shard) // shard, k)))
+        values.append(wide)
+        specs.append(pl.BlockSpec((1, shard, lanes), at_place(0, k)))
+        values.append(other)
+    early = len(values)
+
+    def body(place_ref, *refs):
+        out_ref, low_ref = refs[early + peers :]
+        index = pl.program_id(0)
+
+        @pl.when(index == 0)
+        def _():
+            out_ref[...] = jnp.zeros_like(out_ref)
+
+        def flat(ref):
+            return jnp.concatenate(
+                [ref[t * lanes : (t + 1) * lanes, :] for t in range(3)], axis=1
+            )
+
+        def over(which):
+            return jnp.concatenate([flat(refs[4 * k + which].at[0]) for k in range(step)], axis=0)
+
+        gate = over(0).astype(F32)
+        up = over(1).astype(F32)
+        sigma = jax.nn.sigmoid(gate)
+        silu = gate * sigma
+        for_gate = up * sigma * (1.0 + gate * (1.0 - sigma))
+        hidden = (silu * up).astype(BF16)
+        mine = place_ref[0] == 0
+        acts = jnp.concatenate(
+            [jnp.where(mine, refs[4 * k + 2][0], refs[4 * k + 3][0]) for k in range(step)], axis=1
+        )
+        for turn in range(peers // step):
+
+            @pl.when(index == turn)
+            def _(turn=turn):
+                pair = refs[early + step * turn : early + step * (turn + 1)]
+                grad = jnp.concatenate([flat(ref) for ref in pair], axis=0).astype(F32)
+                upstream = jnp.concatenate([ref[half:, :] for ref in pair], axis=1)
+                out_ref[0] += dot_nn(acts, (grad * for_gate).astype(BF16))
+                out_ref[1] += dot_nn(acts, (grad * silu).astype(BF16))
+                out_ref[2] += dot_nn(upstream, hidden)
+
+        @pl.when(index == peers // step - 1)
+        def _():
+            low_ref[...] = out_ref[...].astype(BF16)
+
+    shape = (3, shard, half)
+    return pl.pallas_call(
+        body,
+        grid_spec=pltpu.PrefetchScalarGridSpec(
+            num_scalar_prefetch=1,
+            grid=(peers // step,),
+            in_specs=specs + [whole()] * peers,
+            out_specs=[pl.BlockSpec(shape, lambda p, place_ref: (0, 0, 0))] * 2,
+        ),
+        out_shape=[jax.ShapeDtypeStruct(shape, F32), jax.ShapeDtypeStruct(shape, BF16)],
+        compiler_params=limits(16),
+        name="last_grads",
+    )(place, *[pltpu.with_memory_space_constraint(v, pltpu.HBM) for v in values], *late)
+
+
 def early_out(own_0, own_1, got_1, core):
     count, shard, half = own_0.shape
 
@@ -409,6 +517,7 @@
     x = lax.axis_index("x")
     core_id = core.astype(jnp.int32)[None]
     x_id = x.astype(jnp.int32)[None]
+    place = jnp.stack([core, lax.axis_index(DP)]).astype(jnp.int32)
     rows = tokens.shape[0]
     features, hidden = gate_w.shape
     half = hidden // CORES
@@ -459,9 +568,9 @@
     wide_b = exchanged(load, DP)
 
     d_hidden_b = dot_nt(upstream, down_half).astype(BF16)
-    load = packed([(d_hidden_b, None, 0)], None, (upstream,), core_id)
-    load, wide_b = lax.optimization_barrier((load, wide_b))
-    wide_c = exchanged(load, DP)
+    late = list(packed_late(d_hidden_b, upstream, place))
+    for k in range(1, PEERS):
+        late[k] = shifted(late[k], DP, k)
 
     middle_other = shifted(wide_b[:, 2 * half :], "segment", 1)
     own_1, low_1 = weight_grads(
@@ -473,14 +582,7 @@
         core_id,
     )
     got_1 = one_way(low_1, 0)
-    own_0, low_0 = weight_grads(
-        (wide_a, 0),
-        (wide_a, 1),
-        (wide_c, 0),
-        (wide_a, 6, 0, entered_other),
-        (wide_c, 2),
-        core_id,
-    )
+    own_0, low_0 = last_grads(wide_a, entered_other, late, place)
     got_0 = one_way(low_0, 1)
     outs = early_out(own_0, own_1, got_1, core_id)
     grad_gate, grad_up, grad_down = late_out(outs, got_0, core_id)

time: 173 us -> 181 us (1.046)
  starting transfers between devices: 59.4 us -> 69.6 us
  waiting for transfers between devices: 50.5 us -> 47.1 us
    ppermute x24 -> x31, starting transfers between devices: 29.6 us -> 44.6 us  [shifted(): lax.ppermute(value, axis, [(i, (i + distance) % size) for i in range(size)])]
    all_to_all x3 -> x2, waiting for transfers between devices: 5.92 us -> 0.01 us  [exchanged(): return lax.all_to_all(value, axes, 0, 0, tiled=True)]
    pallas_call x0 -> x2, Pallas kernels: none -> 5.84 us  [the longest x1 5.05 us: last_grads(): pl.pallas_call(body, grid_spec=pltpu.PrefetchScalarGridSpec(num_scalar_pr...]
    all_to_all x3 -> x2, starting transfers between devices: 15.7 us -> 10.8 us  [exchanged(): return lax.all_to_all(value, axes, 0, 0, tiled=True)]
    pallas_call x2 -> x1, Pallas kernels: 8.98 us -> 4.13 us  [weight_grads(): pl.pallas_call(body, grid=(PEERS // step,), in_specs=[whole(pltpu.SMEM)]...]
    ppermute x24 -> x31, waiting for transfers between devices: 42.1 us -> 44.6 us  [shifted(): lax.ppermute(value, axis, [(i, (i + distance) % size) for i in range(size)])]
    unnamed x19 -> x21, local copies, waits for them, and re-layouts: 3.68 us -> 3.62 us
  transfers between devices with their start and end apart: 33 -> 39, of which waited for: 24 -> 20; matrix products, arithmetic and copies ran while one was open for 8% -> 9% of each run, Pallas kernels for 8% -> 7%
where the time goes in v10:
time: 181 us; the launch traced here: 180 us
  starting transfers between devices  69.6 us (38%)
  waiting for transfers between devices  47.1 us (26%)
  blocking collectives  26.2 us (14%)
  Pallas kernels  13.2 us (7%)
  local copies, waits for them, and re-layouts  9.66 us (5%)
  matrix products  8.63 us (5%)
  other arithmetic  4.07 us (2%)
    ppermute x31, starting transfers between devices, shifted(): lax.ppermute(value, axis, [(i, (i + distance) % size) for i in range(size)])  44.6 us
    ppermute x31, waiting for transfers between devices, shifted(): lax.ppermute(value, axis, [(i, (i + distance) % size) for i in range(size)])  44.6 us
    all_to_all x1, blocking collectives, exchanged(): return lax.all_to_all(value, axes, 0, 0, tiled=True)  26.2 us
    ppermute x6, starting transfers between devices, one_way(): return lax.ppermute(value, 'segment', [(source, 1 - source)])  14.2 us
    all_to_all x2, starting transfers between devices, exchanged(): return lax.all_to_all(value, axes, 0, 0, tiled=True)  10.8 us
    pallas_call x1, Pallas kernels, last_grads(): pl.pallas_call(body, grid_spec=pltpu.PrefetchScalarGridSpec(num_scalar_pr...  5.05 us
    pallas_call x1, Pallas kernels, weight_grads(): pl.pallas_call(body, grid=(PEERS // step,), in_specs=[whole(pltpu.SMEM)]...  4.13 us
  transfers between devices with their start and end apart: 39, of which 20 were waited for; matrix products, arithmetic and copies ran while one was open for 9% of the time, Pallas kernels for 7%

profile of v10, /device:TPU:1, one launch (start us, length us, event | category | flops | bytes accessed | tf_op | source)
XLA Modules:
  0.0 179.8 jit_solution(123850329952585237)
XLA Ops:
  1.6 26.2 %all_to_all.15 = bf16[16,96,128]{2,1,0:T(8,128)(2,1)S(1)} all-to-all(bf16[16,96,128]{2,1,0:T(8,128)(2,1)S(1)} %spread.1), channel_id=1, replica_groups=mesh['segment'=2,'x'=4,'zh'=4,'zl'=2,'y'=4] {'x','zh'}, dimensions={0} | all-to-all | bytes 786432 | tf_op jit(solution)/shard_map/all_to_all | solution.py:39
  30.5 2.3 %collective-permute-start.13 = (bf16[2,128,384]{2,1,0:T(8,128)(2,1)S(1)}, bf16[2,128,384]{2,1,0:T(8,128)(2,1)S(1)}, u32[]{:S(2)}, u32[]{:S(2)}) collective-permute-start(bf16[2,128,384]{2,1,0:T(8,128)(2,1)S(1)} %picked.3), channel_id=1, source_target_pairs={{0,128},{128,0},{1,129},{129,1},{2,130},{130,2},{3,131},{131,3},{4... | collective-permute-start | bytes 589832 | tf_op jit(solution)/shard_map/ppermute | solution.py:24
  35.8 4.8 %all-to-all-start.1 = ((bf16[8,1344,128]{2,1,0:T(8,128)(2,1)}), bf16[8,1344,128]{2,1,0:T(8,128)(2,1)}, u32[]{:S(2)}, u32[]{:S(2)}) async-start(bf16[8,1344,128]{2,1,0:T(8,128)(2,1)} %copy-done.1), calls=%async_computation.1 | async-start | bytes 5505024 | tf_op jit(solution)/shard_map/all_to_all | solution.py:39
  40.6 2.2 %convolution_convert_fusion = bf16[128,1536]{1,0:T(8,128)(2,1)S(1)} fusion(bf16[1,768,1536]{2,1,0:T(8,128)(2,1)} %param.8, bf16[128,768]{1,0:T(8,128)(2,1)S(1)} %fusion.21.refs_1_, bf16[128,768]{1,0:T(8,128)(2,1)S(1)} %fusion.15.refs_0_), kind=kOutput, calls=%fused_computation.2 | convolution fusion | flops 302972928 | bytes 3145728 | tf_op jit(solution)/shard_map/dot_general | solution.py:51
  43.6 1.8 collective-permute-start.2
  46.5 4.9 %collective-permute-done.1 = bf16[128,384]{1,0:T(8,128)(2,1)S(1)} collective-permute-done((bf16[128,384]{1,0:T(8,128)(2,1)}, bf16[128,384]{1,0:T(8,128)(2,1)S(1)}, u32[]{:S(2)}, u32[]{:S(2)}) %collective-permute-start.1) | collective-permute-done | bytes 98336 | tf_op jit(solution)/shard_map/ppermute | solution.py:24
  59.9 12.9 %collective-permute-done.5 = bf16[64,384]{1,0:T(8,128)(2,1)S(1)} collective-permute-done((bf16[64,384]{1,0:T(8,128)(2,1)S(1)}, bf16[64,384]{1,0:T(8,128)(2,1)S(1)}, u32[]{:S(2)}, u32[]{:S(2)}) %collective-permute-start.5) | collective-permute-done | bytes 49184 | tf_op jit(solution)/shard_map/ppermute | solution.py:24
  74.4 2.2 %collective-permute-start.8 = (bf16[64,384]{1,0:T(8,128)(2,1)S(1)}, bf16[64,384]{1,0:T(8,128)(2,1)S(1)}, u32[]{:S(2)}, u32[]{:S(2)}) collective-permute-start(bf16[64,384]{1,0:T(8,128)(2,1)S(1)} %add_convert_fusion.3.refs_0_), channel_id=1, source_target_pairs={{0,96},{32,0},{64,32},{96,64},{1,97},{33,1},{65,33},{97,65},{2,98}... | collective-permute-start | bytes 147464 | tf_op jit(solution)/shard_map/ppermute | solution.py:24
  78.2 3.0 %collective-permute-done.9.refs_2_ = bf16[64,384]{1,0:T(8,128)(2,1)S(1)} collective-permute-done((bf16[64,384]{1,0:T(8,128)(2,1)S(1)}, bf16[64,384]{1,0:T(8,128)(2,1)S(1)}, u32[]{:S(2)}, u32[]{:S(2)}) %collective-permute-start.9) | collective-permute-done | bytes 49184 | tf_op jit(solution)/shard_map/ppermute | solution.py:24
  81.2 3.8 %collective-permute-start.11 = (bf16[64,1536]{1,0:T(8,128)(2,1)S(1)}, bf16[64,1536]{1,0:T(8,128)(2,1)S(1)}, u32[]{:S(2)}, u32[]{:S(2)}) collective-permute-start(bf16[64,1536]{1,0:T(8,128)(2,1)S(1)} %assemble.2.own_ref), channel_id=1, source_target_pairs={{0,128},{128,0},{1,129},{129,1},{2,130},{130,2},{3,131},{131,3},{4... | collective-permute-start | bytes 589832 | tf_op jit(solution)/shard_map/ppermute | solution.py:24
  87.1 2.3 %collective-permute-start.12 = (bf16[2,128,384]{2,1,0:T(8,128)(2,1)S(1)}, bf16[2,128,384]{2,1,0:T(8,128)(2,1)S(1)}, u32[]{:S(2)}, u32[]{:S(2)}) collective-permute-start(bf16[2,128,384]{2,1,0:T(8,128)(2,1)S(1)} %picked.2), channel_id=1, source_target_pairs={{128,0},{129,1},{130,2},{131,3},{132,4},{133,5},{134,6},{135,7},{1... | collective-permute-start | bytes 589832 | tf_op jit(solution)/shard_map/ppermute | solution.py:35
  92.1 6.0 %all-to-all-start.2 = ((bf16[8,864,128]{2,1,0:T(8,128)(2,1)}), bf16[8,864,128]{2,1,0:T(8,128)(2,1)}, u32[]{:S(2)}, u32[]{:S(2)}) async-start(bf16[8,864,128]{2,1,0:T(8,128)(2,1)} %copy-done.2), calls=%async_computation.2 | async-start | bytes 3538944 | tf_op jit(solution)/shard_map/all_to_all | solution.py:39
  98.1 2.5 %slice_bitcast_fusion = bf16[384,1536]{1,0:T(8,128)(2,1)} fusion(bf16[1,768,1536]{2,1,0:T(8,128)(2,1)} %param.8), kind=kLoop, calls=%fused_computation.18 | loop fusion | bytes 2359296 | tf_op jit(solution)/shard_map/slice | solution.py:525
  106.6 3.5 %collective-permute-done.15 = bf16[128,384]{1,0:T(8,128)(2,1)S(1)} collective-permute-done((bf16[128,384]{1,0:T(8,128)(2,1)S(1)}, bf16[128,384]{1,0:T(8,128)(2,1)S(1)}, u32[]{:S(2)}, u32[]{:S(2)}) %collective-permute-start.15) | collective-permute-done | bytes 98336 | tf_op jit(solution)/shard_map/ppermute | solution.py:24
  110.8 5.1 %collective-permute-start.18 = (bf16[64,384]{1,0:T(8,128)(2,1)S(1)}, bf16[64,384]{1,0:T(8,128)(2,1)S(1)}, u32[]{:S(2)}, u32[]{:S(2)}) collective-permute-start(bf16[64,384]{1,0:T(8,128)(2,1)S(1)} %slice.54), channel_id=1, source_target_pairs={{128,0},{129,1},{130,2},{131,3},{132,4},{133,5},{134,6},{135,7},{1... | collective-permute-start | bytes 147464 | tf_op jit(solution)/shard_map/ppermute | solution.py:35
  117.8 4.2 %collective-permute-start.20 = (bf16[64,384]{1,0:T(8,128)(2,1)S(1)}, bf16[64,384]{1,0:T(8,128)(2,1)S(1)}, u32[]{:S(2)}, u32[]{:S(2)}) collective-permute-start(bf16[64,384]{1,0:T(8,128)(2,1)S(1)} %slice_select_fusion), channel_id=1, source_target_pairs={{0,16},{8,24},{16,0},{24,8},{1,17},{9,25},{17,1},{25,9},{2,18},{10... | collective-permute-start | bytes 147464 | tf_op jit(solution)/shard_map/ppermute | solution.py:24
  122.0 2.5 %collective-permute-start.21 = (bf16[64,384]{1,0:T(8,128)(2,1)S(1)}, bf16[64,384]{1,0:T(8,128)(2,1)S(1)}, u32[]{:S(2)}, u32[]{:S(2)}) collective-permute-start(bf16[64,384]{1,0:T(8,128)(2,1)S(1)} %slice_select_fusion), channel_id=1, source_target_pairs={{0,24},{8,0},{16,8},{24,16},{1,25},{9,1},{17,9},{25,17},{2,26},{10... | collective-permute-start | bytes 147464 | tf_op jit(solution)/shard_map/ppermute | solution.py:24
  124.8 4.3 %collective-permute-done.21 = bf16[64,384]{1,0:T(8,128)(2,1)S(1)} collective-permute-done((bf16[64,384]{1,0:T(8,128)(2,1)S(1)}, bf16[64,384]{1,0:T(8,128)(2,1)S(1)}, u32[]{:S(2)}, u32[]{:S(2)}) %collective-permute-start.21) | collective-permute-done | bytes 49184 | tf_op jit(solution)/shard_map/ppermute | solution.py:24
  129.2 2.2 %collective-permute-start.22 = (bf16[64,384]{1,0:T(8,128)(2,1)S(1)}, bf16[64,384]{1,0:T(8,128)(2,1)S(1)}, u32[]{:S(2)}, u32[]{:S(2)}) collective-permute-start(bf16[64,384]{1,0:T(8,128)(2,1)S(1)} %add_convert_fusion.2.refs_0_), channel_id=1, source_target_pairs={{0,96},{32,0},{64,32},{96,64},{1,97},{33,1},{65,33},{97,65},{2,98}... | collective-permute-start | bytes 147464 | tf_op jit(solution)/shard_map/ppermute | solution.py:24
  132.5 3.3 %collective-permute-done.23.refs_2_ = bf16[64,384]{1,0:T(8,128)(2,1)S(1)} collective-permute-done((bf16[64,384]{1,0:T(8,128)(2,1)S(1)}, bf16[64,384]{1,0:T(8,128)(2,1)S(1)}, u32[]{:S(2)}, u32[]{:S(2)}) %collective-permute-start.23) | collective-permute-done | bytes 49184 | tf_op jit(solution)/shard_map/ppermute | solution.py:24
  136.4 2.0 %collective-permute-start.25 = (bf16[64,1536]{1,0:T(8,128)(2,1)S(1)}, bf16[64,1536]{1,0:T(8,128)(2,1)S(1)}, u32[]{:S(2)}, u32[]{:S(2)}) collective-permute-start(bf16[64,1536]{1,0:T(8,128)(2,1)S(1)} %assemble.3.own_ref), channel_id=1, source_target_pairs={{0,128},{128,0},{1,129},{129,1},{2,130},{130,2},{3,131},{131,3},{4... | collective-permute-start | bytes 589832 | tf_op jit(solution)/shard_map/ppermute | solution.py:24
  138.4 2.9 %bitcast_select_fusion = bf16[384,1536]{1,0:T(8,128)(2,1)} fusion(bf16[384,1536]{1,0:T(8,128)(2,1)} %collective-permute-done.26, bf16[1,768,1536]{2,1,0:T(8,128)(2,1)} %param.8, pred[]{:T(512)S(6)} %eq.17), kind=kLoop, calls=%fused_computation.17 | loop fusion | flops 589824 | bytes 3538945 | tf_op jit(solution)/shard_map/jit(_where)/select_n | solution.py:526
  141.3 1.8 slice.52
  144.6 1.8 convolution_convert_fusion.1.grad_ref
  148.5 2.4 %collective-permute-start.28 = (bf16[576,128]{1,0:T(8,128)(2,1)S(1)}, bf16[576,128]{1,0:T(8,128)(2,1)S(1)}, u32[]{:S(2)}, u32[]{:S(2)}) collective-permute-start(bf16[576,128]{1,0:T(8,128)(2,1)S(1)} %get-tuple-element.26), channel_id=1, source_target_pairs={{0,2},{1,3},{2,4},{3,5},{4,6},{5,7},{6,0},{7,1},{8,10},{9,11},{10,... | collective-permute-start | bytes 442376 | tf_op jit(solution)/shard_map/ppermute | solution.py:24
  151.6 3.9 %collective-permute-done.27.refs_9_ = bf16[576,128]{1,0:T(8,128)(2,1)S(1)} collective-permute-done((bf16[576,128]{1,0:T(8,128)(2,1)S(1)}, bf16[576,128]{1,0:T(8,128)(2,1)S(1)}, u32[]{:S(2)}, u32[]{:S(2)}) %collective-permute-start.27) | collective-permute-done | bytes 147488 | tf_op jit(solution)/shard_map/ppermute | solution.py:24
  157.3 3.3 %collective-permute-start.31 = (bf16[576,128]{1,0:T(8,128)(2,1)S(1)}, bf16[576,128]{1,0:T(8,128)(2,1)S(1)}, u32[]{:S(2)}, u32[]{:S(2)}) collective-permute-start(bf16[576,128]{1,0:T(8,128)(2,1)S(1)} %get-tuple-element.29), channel_id=1, source_target_pairs={{0,5},{1,6},{2,7},{3,0},{4,1},{5,2},{6,3},{7,4},{8,13},{9,14},{10,... | collective-permute-start | bytes 442376 | tf_op jit(solution)/shard_map/ppermute | solution.py:24
  160.7 2.5 %collective-permute-start.33 = (bf16[576,128]{1,0:T(8,128)(2,1)S(1)}, bf16[576,128]{1,0:T(8,128)(2,1)S(1)}, u32[]{:S(2)}, u32[]{:S(2)}) collective-permute-start(bf16[576,128]{1,0:T(8,128)(2,1)S(1)} %get-tuple-element.31), channel_id=1, source_target_pairs={{0,7},{1,0},{2,1},{3,2},{4,3},{5,4},{6,5},{7,6},{8,15},{9,8},{10,9... | collective-permute-start | bytes 442376 | tf_op jit(solution)/shard_map/ppermute | solution.py:24
  163.1 4.1 %shard_map.76 = (f32[3,192,384]{2,1,0:T(8,128)S(1)}, bf16[3,192,384]{2,1,0:T(8,128)(2,1)S(1)}) custom-call(s32[1]{0:T(128)} %bitcast.core_ref, bf16[8,864,128]{2,1,0:T(8,128)(2,1)} %all-to-all-done.2.refs_0_.refs_1_.refs_3_, bf16[8,864,128]{2,1,0:T(8,128)(2,1)} %all-to-all-done.2.refs_0_.refs_1_.refs_3_, ...), custom_call_target="tpu_custom_call" | custom-call | tf_op jit(solution)/shard_map/pallas_call | solution.py:307
  168.6 1.7 collective-permute-done.32.refs_14_
  170.3 5.0 %last_grads.1 = (f32[3,192,384]{2,1,0:T(8,128)S(1)}, bf16[3,192,384]{2,1,0:T(8,128)(2,1)S(1)}) custom-call(s32[2]{0:T(128)S(1)} %pad_add_fusion.place_ref, bf16[8,1344,128]{2,1,0:T(8,128)(2,1)} %all-to-all-done.1.refs_0_.refs_1_.refs_2_.refs_4_.refs_5_.refs_6_, bf16[8,1344,128]{2,1,0:T(8,128)(2,1)} %all-to-all-done.1.refs_0_.refs_1_.refs_2_.refs_4_.refs_5_.refs_6_, ...), custom_call_target="tpu_custom_call" | custom-call | tf_op jit(solution)/shard_map/last_grads/pallas_call | solution.py:410
  175.4 2.8 %collective-permute-start.34 = (bf16[3,192,384]{2,1,0:T(8,128)(2,1)S(1)}, bf16[3,192,384]{2,1,0:T(8,128)(2,1)S(1)}, u32[]{:S(2)}, u32[]{:S(2)}) collective-permute-start(bf16[3,192,384]{2,1,0:T(8,128)(2,1)S(1)} %get-tuple-element.32), channel_id=1, source_target_pairs={{128,0},{129,1},{130,2},{131,3},{132,4},{133,5},{134,6},{135,7},{1... | collective-permute-start | bytes 1327112 | tf_op jit(solution)/shard_map/ppermute | solution.py:35
  (108 shorter events, 44.5 us)
Async XLA Ops:
  35.8 56.3 %all-to-all-start.1 = ((bf16[8,1344,128]{2,1,0:T(8,128)(2,1)}), bf16[8,1344,128]{2,1,0:T(8,128)(2,1)}, u32[]{:S(2)}, u32[]{:S(2)}) async-start(bf16[8,1344,128]{2,1,0:T(8,128)(2,1)} %copy-done.1), calls=%async_computation.1 | async-start | bytes 5505024 | tf_op jit(solution)/shard_map/all_to_all | solution.py:39
  43.6 7.7 %collective-permute-start.1 = (bf16[128,384]{1,0:T(8,128)(2,1)}, bf16[128,384]{1,0:T(8,128)(2,1)S(1)}, u32[]{:S(2)}, u32[]{:S(2)}) collective-permute-start(bf16[128,384]{1,0:T(8,128)(2,1)} %get-tuple-element.46), channel_id=1, source_target_pairs={{0,32},{32,64},{64,96},{96,0},{1,33},{33,65},{65,97},{97,1},{2,34}... | collective-permute-start | bytes 294920 | tf_op jit(solution)/shard_map/ppermute | solution.py:24
  43.6 7.7 %collective-permute-start.2 = (bf16[128,384]{1,0:T(8,128)(2,1)}, bf16[128,384]{1,0:T(8,128)(2,1)S(1)}, u32[]{:S(2)}, u32[]{:S(2)}) collective-permute-start(bf16[128,384]{1,0:T(8,128)(2,1)} %get-tuple-element.48), channel_id=1, source_target_pairs={{0,64},{32,96},{64,0},{96,32},{1,65},{33,97},{65,1},{97,33},{2,66}... | collective-permute-start | bytes 294920 | tf_op jit(solution)/shard_map/ppermute | solution.py:24
  45.4 6.0 %collective-permute-start.3 = (bf16[128,384]{1,0:T(8,128)(2,1)S(1)}, bf16[128,384]{1,0:T(8,128)(2,1)S(1)}, u32[]{:S(2)}, u32[]{:S(2)}) collective-permute-start(bf16[128,384]{1,0:T(8,128)(2,1)S(1)} %get-tuple-element.47), channel_id=1, source_target_pairs={{0,96},{32,0},{64,32},{96,64},{1,97},{33,1},{65,33},{97,65},{2,98}... | collective-permute-start | bytes 294920 | tf_op jit(solution)/shard_map/ppermute | solution.py:24
  53.7 6.2 %collective-permute-start = (bf16[64,384]{1,0:T(8,128)(2,1)S(1)}, bf16[64,384]{1,0:T(8,128)(2,1)S(1)}, u32[]{:S(2)}, u32[]{:S(2)}) collective-permute-start(bf16[64,384]{1,0:T(8,128)(2,1)S(1)} %broadcast_select_fusion), channel_id=1, source_target_pairs={{0,128},{128,0},{1,129},{129,1},{2,130},{130,2},{3,131},{131,3},{4... | collective-permute-start | bytes 147464 | tf_op jit(solution)/shard_map/ppermute | solution.py:24
  56.0 16.8 %collective-permute-start.5 = (bf16[64,384]{1,0:T(8,128)(2,1)S(1)}, bf16[64,384]{1,0:T(8,128)(2,1)S(1)}, u32[]{:S(2)}, u32[]{:S(2)}) collective-permute-start(bf16[64,384]{1,0:T(8,128)(2,1)S(1)} %slice_select_fusion.1), channel_id=1, source_target_pairs={{0,8},{8,16},{16,24},{24,0},{1,9},{9,17},{17,25},{25,1},{2,10},{10... | collective-permute-start | bytes 147464 | tf_op jit(solution)/shard_map/ppermute | solution.py:24
  56.5 17.3 %collective-permute-start.6 = (bf16[64,384]{1,0:T(8,128)(2,1)S(1)}, bf16[64,384]{1,0:T(8,128)(2,1)S(1)}, u32[]{:S(2)}, u32[]{:S(2)}) collective-permute-start(bf16[64,384]{1,0:T(8,128)(2,1)S(1)} %slice_select_fusion.1), channel_id=1, source_target_pairs={{0,16},{8,24},{16,0},{24,8},{1,17},{9,25},{17,1},{25,9},{2,18},{10... | collective-permute-start | bytes 147464 | tf_op jit(solution)/shard_map/ppermute | solution.py:24
  58.2 15.7 %collective-permute-start.7 = (bf16[64,384]{1,0:T(8,128)(2,1)S(1)}, bf16[64,384]{1,0:T(8,128)(2,1)S(1)}, u32[]{:S(2)}, u32[]{:S(2)}) collective-permute-start(bf16[64,384]{1,0:T(8,128)(2,1)S(1)} %slice_select_fusion.1), channel_id=1, source_target_pairs={{0,24},{8,0},{16,8},{24,16},{1,25},{9,1},{17,9},{25,17},{2,26},{10... | collective-permute-start | bytes 147464 | tf_op jit(solution)/shard_map/ppermute | solution.py:24
  76.7 4.5 %collective-permute-start.9 = (bf16[64,384]{1,0:T(8,128)(2,1)S(1)}, bf16[64,384]{1,0:T(8,128)(2,1)S(1)}, u32[]{:S(2)}, u32[]{:S(2)}) collective-permute-start(bf16[64,384]{1,0:T(8,128)(2,1)S(1)} %add_convert_fusion.3.refs_0_), channel_id=1, source_target_pairs={{0,64},{32,96},{64,0},{96,32},{1,65},{33,97},{65,1},{97,33},{2,66}... | collective-permute-start | bytes 147464 | tf_op jit(solution)/shard_map/ppermute | solution.py:24
  81.2 4.9 %collective-permute-start.11 = (bf16[64,1536]{1,0:T(8,128)(2,1)S(1)}, bf16[64,1536]{1,0:T(8,128)(2,1)S(1)}, u32[]{:S(2)}, u32[]{:S(2)}) collective-permute-start(bf16[64,1536]{1,0:T(8,128)(2,1)S(1)} %assemble.2.own_ref), channel_id=1, source_target_pairs={{0,128},{128,0},{1,129},{129,1},{2,130},{130,2},{3,131},{131,3},{4... | collective-permute-start | bytes 589832 | tf_op jit(solution)/shard_map/ppermute | solution.py:24
  92.1 50.9 %all-to-all-start.2 = ((bf16[8,864,128]{2,1,0:T(8,128)(2,1)}), bf16[8,864,128]{2,1,0:T(8,128)(2,1)}, u32[]{:S(2)}, u32[]{:S(2)}) async-start(bf16[8,864,128]{2,1,0:T(8,128)(2,1)} %copy-done.2), calls=%async_computation.2 | async-start | bytes 3538944 | tf_op jit(solution)/shard_map/all_to_all | solution.py:39
  100.6 37.8 %collective-permute-start.26 = (bf16[384,1536]{1,0:T(8,128)(2,1)}, bf16[384,1536]{1,0:T(8,128)(2,1)}, u32[]{:S(2)}, u32[]{:S(2)}) collective-permute-start(bf16[384,1536]{1,0:T(8,128)(2,1)} %slice_bitcast_fusion), channel_id=1, source_target_pairs={{0,128},{1,129},{2,130},{3,131},{4,132},{5,133},{6,134},{7,135},{8... | collective-permute-start | bytes 3538952 | tf_op jit(solution)/shard_map/ppermute | solution.py:35
  103.9 6.2 %collective-permute-start.15 = (bf16[128,384]{1,0:T(8,128)(2,1)S(1)}, bf16[128,384]{1,0:T(8,128)(2,1)S(1)}, u32[]{:S(2)}, u32[]{:S(2)}) collective-permute-start(bf16[128,384]{1,0:T(8,128)(2,1)S(1)} %get-tuple-element.43), channel_id=1, source_target_pairs={{0,32},{32,64},{64,96},{96,0},{1,33},{33,65},{65,97},{97,1},{2,34}... | collective-permute-start | bytes 294920 | tf_op jit(solution)/shard_map/ppermute | solution.py:24
  104.0 6.1 %collective-permute-start.16 = (bf16[128,384]{1,0:T(8,128)(2,1)S(1)}, bf16[128,384]{1,0:T(8,128)(2,1)S(1)}, u32[]{:S(2)}, u32[]{:S(2)}) collective-permute-start(bf16[128,384]{1,0:T(8,128)(2,1)S(1)} %get-tuple-element.45), channel_id=1, source_target_pairs={{0,64},{32,96},{64,0},{96,32},{1,65},{33,97},{65,1},{97,33},{2,66}... | collective-permute-start | bytes 294920 | tf_op jit(solution)/shard_map/ppermute | solution.py:24
  105.1 5.6 %collective-permute-start.17 = (bf16[128,384]{1,0:T(8,128)(2,1)S(1)}, bf16[128,384]{1,0:T(8,128)(2,1)S(1)}, u32[]{:S(2)}, u32[]{:S(2)}) collective-permute-start(bf16[128,384]{1,0:T(8,128)(2,1)S(1)} %get-tuple-element.44), channel_id=1, source_target_pairs={{0,96},{32,0},{64,32},{96,64},{1,97},{33,1},{65,33},{97,65},{2,98}... | collective-permute-start | bytes 294920 | tf_op jit(solution)/shard_map/ppermute | solution.py:24
  110.8 6.0 %collective-permute-start.18 = (bf16[64,384]{1,0:T(8,128)(2,1)S(1)}, bf16[64,384]{1,0:T(8,128)(2,1)S(1)}, u32[]{:S(2)}, u32[]{:S(2)}) collective-permute-start(bf16[64,384]{1,0:T(8,128)(2,1)S(1)} %slice.54), channel_id=1, source_target_pairs={{128,0},{129,1},{130,2},{131,3},{132,4},{133,5},{134,6},{135,7},{1... | collective-permute-start | bytes 147464 | tf_op jit(solution)/shard_map/ppermute | solution.py:35
  116.7 7.8 %collective-permute-start.19 = (bf16[64,384]{1,0:T(8,128)(2,1)S(1)}, bf16[64,384]{1,0:T(8,128)(2,1)S(1)}, u32[]{:S(2)}, u32[]{:S(2)}) collective-permute-start(bf16[64,384]{1,0:T(8,128)(2,1)S(1)} %slice_select_fusion), channel_id=1, source_target_pairs={{0,8},{8,16},{16,24},{24,0},{1,9},{9,17},{17,25},{25,1},{2,10},{10... | collective-permute-start | bytes 147464 | tf_op jit(solution)/shard_map/ppermute | solution.py:24
  117.8 7.0 %collective-permute-start.20 = (bf16[64,384]{1,0:T(8,128)(2,1)S(1)}, bf16[64,384]{1,0:T(8,128)(2,1)S(1)}, u32[]{:S(2)}, u32[]{:S(2)}) collective-permute-start(bf16[64,384]{1,0:T(8,128)(2,1)S(1)} %slice_select_fusion), channel_id=1, source_target_pairs={{0,16},{8,24},{16,0},{24,8},{1,17},{9,25},{17,1},{25,9},{2,18},{10... | collective-permute-start | bytes 147464 | tf_op jit(solution)/shard_map/ppermute | solution.py:24
  122.0 7.2 %collective-permute-start.21 = (bf16[64,384]{1,0:T(8,128)(2,1)S(1)}, bf16[64,384]{1,0:T(8,128)(2,1)S(1)}, u32[]{:S(2)}, u32[]{:S(2)}) collective-permute-start(bf16[64,384]{1,0:T(8,128)(2,1)S(1)} %slice_select_fusion), channel_id=1, source_target_pairs={{0,24},{8,0},{16,8},{24,16},{1,25},{9,1},{17,9},{25,17},{2,26},{10... | collective-permute-start | bytes 147464 | tf_op jit(solution)/shard_map/ppermute | solution.py:24
  131.4 4.5 %collective-permute-start.23 = (bf16[64,384]{1,0:T(8,128)(2,1)S(1)}, bf16[64,384]{1,0:T(8,128)(2,1)S(1)}, u32[]{:S(2)}, u32[]{:S(2)}) collective-permute-start(bf16[64,384]{1,0:T(8,128)(2,1)S(1)} %add_convert_fusion.2.refs_0_), channel_id=1, source_target_pairs={{0,64},{32,96},{64,0},{96,32},{1,65},{33,97},{65,1},{97,33},{2,66}... | collective-permute-start | bytes 147464 | tf_op jit(solution)/shard_map/ppermute | solution.py:24
  131.7 4.6 %collective-permute-start.24 = (bf16[64,384]{1,0:T(8,128)(2,1)S(1)}, bf16[64,384]{1,0:T(8,128)(2,1)S(1)}, u32[]{:S(2)}, u32[]{:S(2)}) collective-permute-start(bf16[64,384]{1,0:T(8,128)(2,1)S(1)} %add_convert_fusion.2.refs_0_), channel_id=1, source_target_pairs={{0,32},{32,64},{64,96},{96,0},{1,33},{33,65},{65,97},{97,1},{2,34}... | collective-permute-start | bytes 147464 | tf_op jit(solution)/shard_map/ppermute | solution.py:24
  136.4 4.9 %collective-permute-start.25 = (bf16[64,1536]{1,0:T(8,128)(2,1)S(1)}, bf16[64,1536]{1,0:T(8,128)(2,1)S(1)}, u32[]{:S(2)}, u32[]{:S(2)}) collective-permute-start(bf16[64,1536]{1,0:T(8,128)(2,1)S(1)} %assemble.3.own_ref), channel_id=1, source_target_pairs={{0,128},{128,0},{1,129},{129,1},{2,130},{130,2},{3,131},{131,3},{4... | collective-permute-start | bytes 589832 | tf_op jit(solution)/shard_map/ppermute | solution.py:24
  143.0 17.6 %collective-permute-start.14 = (bf16[8,192,128]{2,1,0:T(8,128)(2,1)}, bf16[8,192,128]{2,1,0:T(8,128)(2,1)S(1)}, u32[]{:S(2)}, u32[]{:S(2)}) collective-permute-start(bf16[8,192,128]{2,1,0:T(8,128)(2,1)} %slice.52), channel_id=1, source_target_pairs={{0,128},{128,0},{1,129},{129,1},{2,130},{130,2},{3,131},{131,3},{4... | collective-permute-start | bytes 1179656 | tf_op jit(solution)/shard_map/ppermute | solution.py:24
  144.0 16.6 %collective-permute-start.35 = (bf16[8,96,128]{2,1,0:T(8,128)(2,1)S(1)}, bf16[8,96,128]{2,1,0:T(8,128)(2,1)S(1)}, u32[]{:S(2)}, u32[]{:S(2)}) collective-permute-start(bf16[8,96,128]{2,1,0:T(8,128)(2,1)S(1)} %slice.55), channel_id=1, source_target_pairs={{0,128},{128,0},{1,129},{129,1},{2,130},{130,2},{3,131},{131,3},{4... | collective-permute-start | bytes 589832 | tf_op jit(solution)/shard_map/ppermute | solution.py:24
  147.2 8.4 %collective-permute-start.27 = (bf16[576,128]{1,0:T(8,128)(2,1)S(1)}, bf16[576,128]{1,0:T(8,128)(2,1)S(1)}, u32[]{:S(2)}, u32[]{:S(2)}) collective-permute-start(bf16[576,128]{1,0:T(8,128)(2,1)S(1)} %get-tuple-element.25), channel_id=1, source_target_pairs={{0,1},{1,2},{2,3},{3,4},{4,5},{5,6},{6,7},{7,0},{8,9},{9,10},{10,1... | collective-permute-start | bytes 442376 | tf_op jit(solution)/shard_map/ppermute | solution.py:24
  148.5 8.8 %collective-permute-start.28 = (bf16[576,128]{1,0:T(8,128)(2,1)S(1)}, bf16[576,128]{1,0:T(8,128)(2,1)S(1)}, u32[]{:S(2)}, u32[]{:S(2)}) collective-permute-start(bf16[576,128]{1,0:T(8,128)(2,1)S(1)} %get-tuple-element.26), channel_id=1, source_target_pairs={{0,2},{1,3},{2,4},{3,5},{4,6},{5,7},{6,0},{7,1},{8,10},{9,11},{10,... | collective-permute-start | bytes 442376 | tf_op jit(solution)/shard_map/ppermute | solution.py:24
  150.9 16.3 %collective-permute-start.29 = (bf16[576,128]{1,0:T(8,128)(2,1)S(1)}, bf16[576,128]{1,0:T(8,128)(2,1)S(1)}, u32[]{:S(2)}, u32[]{:S(2)}) collective-permute-start(bf16[576,128]{1,0:T(8,128)(2,1)S(1)} %get-tuple-element.27), channel_id=1, source_target_pairs={{0,3},{1,4},{2,5},{3,6},{4,7},{5,0},{6,1},{7,2},{8,11},{9,12},{10,... | collective-permute-start | bytes 442376 | tf_op jit(solution)/shard_map/ppermute | solution.py:24
  155.5 13.0 %collective-permute-start.30 = (bf16[576,128]{1,0:T(8,128)(2,1)S(1)}, bf16[576,128]{1,0:T(8,128)(2,1)S(1)}, u32[]{:S(2)}, u32[]{:S(2)}) collective-permute-start(bf16[576,128]{1,0:T(8,128)(2,1)S(1)} %get-tuple-element.28), channel_id=1, source_target_pairs={{0,4},{1,5},{2,6},{3,7},{4,0},{5,1},{6,2},{7,3},{8,12},{9,13},{10,... | collective-permute-start | bytes 442376 | tf_op jit(solution)/shard_map/ppermute | solution.py:24
  157.3 11.2 %collective-permute-start.31 = (bf16[576,128]{1,0:T(8,128)(2,1)S(1)}, bf16[576,128]{1,0:T(8,128)(2,1)S(1)}, u32[]{:S(2)}, u32[]{:S(2)}) collective-permute-start(bf16[576,128]{1,0:T(8,128)(2,1)S(1)} %get-tuple-element.29), channel_id=1, source_target_pairs={{0,5},{1,6},{2,7},{3,0},{4,1},{5,2},{6,3},{7,4},{8,13},{9,14},{10,... | collective-permute-start | bytes 442376 | tf_op jit(solution)/shard_map/ppermute | solution.py:24
  160.6 9.7 %collective-permute-start.32 = (bf16[576,128]{1,0:T(8,128)(2,1)S(1)}, bf16[576,128]{1,0:T(8,128)(2,1)S(1)}, u32[]{:S(2)}, u32[]{:S(2)}) collective-permute-start(bf16[576,128]{1,0:T(8,128)(2,1)S(1)} %get-tuple-element.30), channel_id=1, source_target_pairs={{0,6},{1,7},{2,0},{3,1},{4,2},{5,3},{6,4},{7,5},{8,14},{9,15},{10,... | collective-permute-start | bytes 442376 | tf_op jit(solution)/shard_map/ppermute | solution.py:24
  160.7 9.7 %collective-permute-start.33 = (bf16[576,128]{1,0:T(8,128)(2,1)S(1)}, bf16[576,128]{1,0:T(8,128)(2,1)S(1)}, u32[]{:S(2)}, u32[]{:S(2)}) collective-permute-start(bf16[576,128]{1,0:T(8,128)(2,1)S(1)} %get-tuple-element.31), channel_id=1, source_target_pairs={{0,7},{1,0},{2,1},{3,2},{4,3},{5,4},{6,5},{7,6},{8,15},{9,8},{10,9... | collective-permute-start | bytes 442376 | tf_op jit(solution)/shard_map/ppermute | solution.py:24
  167.3 11.0 %collective-permute-start.36 = (bf16[3,192,384]{2,1,0:T(8,128)(2,1)S(1)}, bf16[3,192,384]{2,1,0:T(8,128)(2,1)S(1)}, u32[]{:S(2)}, u32[]{:S(2)}) collective-permute-start(bf16[3,192,384]{2,1,0:T(8,128)(2,1)S(1)} %get-tuple-element.36), channel_id=1, source_target_pairs={{0,128},{1,129},{2,130},{3,131},{4,132},{5,133},{6,134},{7,135},{8... | collective-permute-start | bytes 1327112 | tf_op jit(solution)/shard_map/ppermute | solution.py:35
  (17 other events, 129.0 us)
